TPU v7x, 512 devices: a whole 4x8x8 slice. The times are simulated.
512 devices in a mesh: seq: 64 (over z_hi, y, core), head: 8 (over x, z_lo).
Axes of the slice: x: 4, y: 8, z: 8 (z_hi: 4, z_lo: 2; z = z_hi * 2 + z_lo), core: 2. Of those that a mesh axis runs over, the one named last changes fastest.
Arguments:
- tokens: bfloat16 [8192, 2880], P('seq'), may hold values from -80 to 80
- gain: float32 [2880], replicated, may hold values from 0.1 to 1.9
- w_query: bfloat16 [2880, 4096], P('seq', 'head'), may hold values from -4 to 4
- w_key: bfloat16 [2880, 512], P('seq', 'head'), may hold values from -1 to 1
- w_value: bfloat16 [2880, 512], P('seq', 'head'), may hold values from -0.109375 to 0.109375
- w_out: bfloat16 [2880, 4096], P('seq', 'head'), may hold values from -0.09375 to 0.09375
- w_gate: float32 [2880], replicated, may hold values from -0.109375 to 0.109375
- steering: bfloat16 [16, 2880], replicated, may hold values from -5 to 5
- segment_ids: int32 [8192], P('seq'), may hold values from 0 to 31, never falling along the last dimension, each value on 1 to 512 neighbouring positions
- steer_index: int32 [8192], P('seq'), may hold values from 0 to 15
- grad_out: bfloat16 [8192, 2880], P('seq'), may hold values from -6 to 6
Outputs:
- layer_out: bfloat16 [8192, 2880], P('seq', 'head')
- grad_tokens: bfloat16 [8192, 2880], P('seq', 'head')
- steer_grad: float32 [16, 2880], P(None, 'head')
Inputs may be any that keep to these rules, and one draw needn't show every extreme that they name: `segment_ids`: the ids never fall along the tokens; each id names one packed document of at most 512 tokens.
All inputs are finite; a program needn't handle non-finite values.
Results may differ from a plain program's by a relative error of at most 0.011.
Values may be sent and summed in bfloat16 or wider, within the bound.
No kernel may reach another device: no remote copies, remote signals or barrier semaphores. Data moves between devices by JAX's collectives and lax.ppermute only.
A program may use at most 64 MiB of HBM per device.

v0:
```python
import jax
import jax.numpy as jnp
from jax import lax
from jax.sharding import PartitionSpec as P

HD = 64
WIN = 128


EPSILON = 1e-05
HIGHEST = lax.Precision.HIGHEST


def shifted(value, axis, by):
    count = lax.axis_size(axis)
    pairs = [(i, i + by) for i in range(count) if 0 <= i + by < count]
    return lax.ppermute(value, axis, pairs)


def normalize(tokens, gain):
    tokens_f = tokens.astype(jnp.float32)
    inverse = lax.rsqrt(jnp.mean(tokens_f * tokens_f, axis=-1, keepdims=True) + EPSILON)
    unit_rows = tokens_f * inverse
    return (unit_rows, inverse, (unit_rows * gain).astype(jnp.bfloat16))


def contract(left, right):
    return lax.dot_general(
        left, right, (((1,), (1,)), ((), ())), preferred_element_type=jnp.float32
    )


def band_mask(query_seg, key_seg, offset):
    query_count = query_seg.shape[0]
    key_count = key_seg.shape[0]
    query_pos = lax.broadcasted_iota(jnp.int32, (query_count, key_count), 0)
    key_pos = lax.broadcasted_iota(jnp.int32, (query_count, key_count), 1) - offset
    distance = query_pos - key_pos
    return (distance >= 0) & (distance < WIN) & (query_seg[:, None] == key_seg[None, :])


def probabilities(query_three, key_rows, mask):
    scores = jnp.einsum(
        "rqd,kd->qrk", query_three, key_rows, preferred_element_type=jnp.float32
    ) * HD ** (-0.5)
    scores = jnp.where(mask[None], scores, -jnp.inf)
    highest = jnp.max(scores, axis=-1, keepdims=True)
    raised = jnp.exp(scores - highest)
    return raised / jnp.sum(raised, axis=-1, keepdims=True)


def attend(query_three, key_rows, value_rows, query_seg, key_seg, offset):
    probs = probabilities(query_three, key_rows, band_mask(query_seg, key_seg, offset))
    mixed = jnp.einsum(
        "qrk,kd->rqd", probs.astype(jnp.bfloat16), value_rows, preferred_element_type=jnp.float32
    )
    return mixed.astype(jnp.bfloat16)


def attend_back(query_three, key_rows, value_rows, query_seg, key_seg, offset, grad_three):
    probs = probabilities(query_three, key_rows, band_mask(query_seg, key_seg, offset))
    grad_values = jnp.einsum(
        "qrk,rqd->kd", probs.astype(jnp.bfloat16), grad_three, preferred_element_type=jnp.float32
    )
    grad_prob = jnp.einsum(
        "rqd,kd->qrk", grad_three, value_rows, preferred_element_type=jnp.float32
    )
    delta = jnp.sum(probs * grad_prob, axis=-1, keepdims=True)
    grad_scores = (probs * (grad_prob - delta) * HD ** (-0.5)).astype(jnp.bfloat16)
    grad_query = jnp.einsum(
        "qrk,kd->rqd", grad_scores, key_rows, preferred_element_type=jnp.float32
    ).astype(jnp.bfloat16)
    grad_keys = jnp.einsum(
        "qrk,rqd->kd", grad_scores, query_three, preferred_element_type=jnp.float32
    )
    return (grad_query, grad_keys, grad_values)


def shards(
    tokens,
    gain,
    w_query,
    w_key,
    w_value,
    w_out,
    w_gate,
    steering,
    segment_ids,
    steer_index,
    grad_out,
):
    row_count = tokens.shape[0]
    model_width = tokens.shape[1]
    head_count = lax.axis_size("head")
    slice_width = model_width // head_count
    slice_start = lax.axis_index("head") * slice_width
    query_weight, key_weight, value_weight, out_weight = (
        lax.all_gather(w_query, "seq", axis=0, tiled=True),
        lax.all_gather(w_key, "seq", axis=0, tiled=True),
        lax.all_gather(w_value, "seq", axis=0, tiled=True),
        lax.all_gather(w_out, "seq", axis=0, tiled=True),
    )
    head_dim = key_weight.shape[1]
    heads_here = query_weight.shape[1] // head_dim
    group_cols = heads_here * head_dim
    unit_rows, inverse, normed = normalize(tokens, gain)
    query_rows = jnp.dot(normed, query_weight, preferred_element_type=jnp.float32).astype(
        jnp.bfloat16
    )
    key_rows = jnp.dot(normed, key_weight, preferred_element_type=jnp.float32).astype(jnp.bfloat16)
    value_rows = jnp.dot(normed, value_weight, preferred_element_type=jnp.float32).astype(
        jnp.bfloat16
    )
    query_three = query_rows.reshape(row_count, heads_here, head_dim)
    sent_rows = jnp.concatenate([key_rows, value_rows], axis=1)
    halo_rows, halo_seg = shifted((sent_rows, segment_ids), "seq", 1)
    halo_seg = jnp.where(lax.axis_index("seq") > 0, halo_seg, -1)
    wide_keys = jnp.concatenate([halo_rows[:, :head_dim], key_rows], axis=0)
    wide_values = jnp.concatenate([halo_rows[:, head_dim:], value_rows], axis=0)
    wide_seg = jnp.concatenate([halo_seg, segment_ids], axis=0)
    mixed_three = attend(query_three, wide_keys, wide_values, segment_ids, wide_seg, WIN)
    mixed_rows = mixed_three.reshape(row_count, group_cols)
    attn_share = lax.psum_scatter(
        contract(mixed_rows, out_weight).astype(jnp.bfloat16),
        "head",
        scatter_dimension=1,
        tiled=True,
    ).astype(jnp.float32)
    token_share = lax.dynamic_slice_in_dim(tokens, slice_start, slice_width, 1).astype(jnp.float32)
    gate_value = jax.nn.sigmoid(jnp.dot(normed.astype(jnp.float32), w_gate, precision=HIGHEST))
    one_hot = (
        steer_index[:, None] == jnp.arange(steering.shape[0], dtype=jnp.int32)[None, :]
    ).astype(jnp.float32)
    steer_rows = jnp.dot(one_hot, steering.astype(jnp.float32), precision=HIGHEST)
    steer_share = lax.dynamic_slice_in_dim(steer_rows, slice_start, slice_width, 1)
    layer_out = (token_share + attn_share + gate_value[:, None] * steer_share).astype(jnp.bfloat16)
    grad_share = lax.dynamic_slice_in_dim(grad_out, slice_start, slice_width, 1).astype(jnp.float32)
    steer_part = jnp.dot(one_hot.T, gate_value[:, None] * grad_share, precision=HIGHEST)
    steer_grad = lax.psum(steer_part, "seq")
    grad_logit = (
        gate_value
        * (1.0 - gate_value)
        * jnp.sum(grad_out.astype(jnp.float32) * steer_rows, axis=-1)
    )
    grad_mixed = jnp.dot(grad_out, out_weight, preferred_element_type=jnp.float32).astype(
        jnp.bfloat16
    )
    grad_three = grad_mixed.reshape(row_count, heads_here, head_dim)
    grad_query, grad_keys, grad_values = attend_back(
        query_three, wide_keys, wide_values, segment_ids, wide_seg, WIN, grad_three
    )
    returned = shifted(
        jnp.concatenate([grad_keys[:WIN], grad_values[:WIN]], axis=1).astype(jnp.bfloat16),
        "seq",
        -1,
    ).astype(jnp.float32)
    key_grad = (
        grad_keys[WIN:].at[row_count - WIN :].add(returned[:, :head_dim]).astype(jnp.bfloat16)
    )
    value_grad = (
        grad_values[WIN:].at[row_count - WIN :].add(returned[:, head_dim:]).astype(jnp.bfloat16)
    )
    group_terms = contract(grad_query.reshape(row_count, group_cols), query_weight)
    group_terms = group_terms + contract(key_grad, key_weight)
    group_terms = group_terms + contract(value_grad, value_weight)
    gain_share = lax.dynamic_slice_in_dim(gain, slice_start, slice_width, 0)
    unit_share = lax.dynamic_slice_in_dim(unit_rows, slice_start, slice_width, 1)
    gate_share = lax.dynamic_slice_in_dim(w_gate, slice_start, slice_width, 0)
    total_share = (
        lax.psum_scatter(
            group_terms.astype(jnp.bfloat16), "head", scatter_dimension=1, tiled=True
        ).astype(jnp.float32)
        + grad_logit[:, None] * gate_share[None, :]
    )
    scaled = total_share * gain_share
    row_total = lax.psum(jnp.sum(scaled * unit_share, axis=-1), "head")
    grad_tokens = (
        grad_share + inverse * (scaled - unit_share * (row_total / model_width)[:, None])
    ).astype(jnp.bfloat16)
    return (layer_out, grad_tokens, steer_grad)


def solution(mesh):
    placed = (
        P("seq", None),
        P(),
        P("seq", "head"),
        P("seq", "head"),
        P("seq", "head"),
        P("seq", "head"),
        P(),
        P(),
        P("seq"),
        P("seq"),
        P("seq", None),
    )
    return jax.shard_map(
        shards,
        mesh=mesh,
        in_specs=placed,
        out_specs=(P("seq", "head"), P("seq", "head"), P(None, "head")),
        check_vma=False,
    )
```

profile of v0, /device:TPU:1, one launch (start us, length us, event | category | flops | bytes accessed | tf_op | source)
XLA Modules:
  0.0 523.9 jit_solution(6505114353116053724)
XLA Ops:
  7.2 0.7 all-gather.7.cloned.1.call-update
  8.0 0.7 all-gather.9.cloned.1.call-update
  8.7 4.6 collective-permute-start.1
  13.3 90.1 %all-gather = bf16[64,45,64]{2,1,0:T(8,128)(2,1)S(1)} all-gather(bf16[1,45,64]{2,1,0:T(8,128)(2,1)} %bitcast.98), channel_id=1, replica_groups=mesh['seq'=64,'head'=8] {'seq'}, dimensions={0}, use_global_device_ids=true | all-gather | bytes 374400 | tf_op jit(solution)/shard_map/all_gather | solution.py:99
  103.7 79.3 %all-gather.1 = bf16[64,45,64]{2,1,0:T(8,128)(2,1)S(1)} all-gather(bf16[1,45,64]{2,1,0:T(8,128)(2,1)S(1)} %bitcast.99), channel_id=1, replica_groups=mesh['seq'=64,'head'=8] {'seq'}, dimensions={0}, use_global_device_ids=true | all-gather | bytes 374400 | tf_op jit(solution)/shard_map/all_gather | solution.py:100
  183.3 0.4 fusion.4
  183.7 0.8 convolution_convert_fusion.6
  184.5 0.8 convolution_convert_fusion.5
  185.3 3.4 collective-permute-start
  188.9 0.8 collective-permute-done
  189.7 3.0 reshape.143
  192.8 2.4 convolution_convert_fusion.4
  195.3 4.6 reshape.145
  199.9 2.7 convolution_convert_fusion.3
  202.7 1.4 convolution_bitcast_fusion
  204.1 1.5 fusion.58
  205.5 0.7 convolution_convert_fusion.2
  206.2 3.7 convolution_convert_fusion
  209.9 0.7 convolution_bitcast_fusion.1
  210.7 2.6 convolution_bitcast_fusion.2
  213.4 1.9 collective-permute-start.2
  215.3 2.6 convolution_convert_fusion.1
  217.9 0.9 fusion.59
  219.5 0.8 copy-done.7
  220.3 1.2 fusion.2
  221.6 1.8 multiply_reduce_fusion
  223.5 0.8 fusion.44
  224.6 271.7 %psum.15 = f32[16,360]{1,0:T(8,128)} all-reduce(f32[16,360]{1,0:T(8,128)S(1)} %fusion.26), channel_id=1, replica_groups=mesh['seq'=64,'head'=8] {'seq'}, use_global_device_ids=true, to_apply=%region_9.10 | all-reduce | flops 5760 | bytes 46080 | tf_op jit(solution)/shard_map/psum | solution.py:139
  496.4 1.7 add_convert_fusion
  498.1 1.1 multiply_reduce_fusion.2
  499.1 16.5 %psum.14 = f32[128]{0:T(128)S(1)} all-reduce(f32[128]{0:T(128)S(1)} %multiply_reduce_fusion.2), channel_id=1, replica_groups=mesh['seq'=64,'head'=8] {'head'}, use_global_device_ids=true, to_apply=%region_8.9 | all-reduce | flops 128 | bytes 1024 | tf_op jit(solution)/shard_map/psum | solution.py:176
  515.7 1.7 fusion.25
  (59 shorter events, 2.5 us)
Async XLA Ops:
  7.2 214.4 %copy-start = (bf16[16,2880]{1,0:T(8,128)(2,1)S(1)}, bf16[16,2880]{1,0:T(8,128)(2,1)}, u32[]{:S(2)}) copy-start(bf16[16,2880]{1,0:T(8,128)(2,1)} %param.26) | copy-start | bytes 276484
  7.2 96.5 %copy-start.10 = (bf16[45,64]{1,0:T(8,128)(2,1)S(1)}, bf16[45,64]{1,0:T(8,128)(2,1)}, u32[]{:S(2)}) copy-start(bf16[45,64]{1,0:T(8,128)(2,1)} %param.23) | copy-start | bytes 17284
  7.2 182.5 %all-gather.7.cloned.1.call-start = ((), (), s32[]{:S(2)}) async-start(), calls=%async_computation.2 | async-start | bytes 3194880 | tf_op jit(solution)/shard_map/all_gather | solution.py:98
  7.9 187.4 %all-gather.9.cloned.1.call-start = ((), (), s32[]{:S(2)}) async-start(), calls=%async_computation.3 | async-start | bytes 3194880 | tf_op jit(solution)/shard_map/all_gather | solution.py:101
  8.7 487.7 %reduce-scatter.9.cloned.1.call-start = ((), (), s32[]{:S(2)}) async-start(), calls=%async_computation.4 | async-start | bytes 829440
  8.7 180.0 %collective-permute-start.1 = (s32[128]{0:T(128)}, s32[128]{0:T(128)S(1)}, u32[]{:S(2)}, u32[]{:S(2)}) collective-permute-start(s32[128]{0:T(128)} %param.27), channel_id=1, source_target_pairs={{0,8},{8,16},{16,24},{24,32},{32,40},{40,48},{48,56},{56,64},{64,7... | collective-permute-start | bytes 1544 | tf_op jit(solution)/shard_map/ppermute | solution.py:17
  103.7 80.0 %copy-start.4 = (bf16[2880,64]{1,0:T(8,128)(2,1)}, bf16[2880,64]{1,0:T(8,128)(2,1)S(1)}, u32[]{:S(2)}) copy-start(bf16[2880,64]{1,0:T(8,128)(2,1)S(1)} %reshape.152) | copy-start | bytes 1105924
  103.7 79.6 %copy-start.1 = (bf16[128,2880]{0,1:T(8,128)(2,1)S(1)}, bf16[128,2880]{0,1:T(8,128)(2,1)}, u32[]{:S(2)}) copy-start(bf16[128,2880]{0,1:T(8,128)(2,1)} %param.19) | copy-start | bytes 2211844
  103.7 80.0 %copy-start.8 = (f32[2880]{0:T(1024)S(1)}, f32[2880]{0:T(1024)}, u32[]{:S(2)}) copy-start(f32[2880]{0:T(1024)} %param.20) | copy-start | bytes 34564
  183.3 2.0 copy-start.6
  183.7 5.1 copy-start.11
  185.3 4.4 collective-permute-start
  209.9 288.2 %reduce-scatter.11.cloned.1.call-start = ((), (), s32[]{:S(2)}) async-start(), calls=%async_computation.5 | async-start | bytes 829440
  213.4 5.8 %collective-permute-start.2 = (bf16[128,128]{0,1:T(8,128)(2,1)S(1)}, bf16[128,128]{0,1:T(8,128)(2,1)S(1)}, u32[]{:S(2)}, u32[]{:S(2)}) collective-permute-start(bf16[128,128]{0,1:T(8,128)(2,1)S(1)} %pad_maximum_fusion.1), channel_id=1, source_target_pairs={{8,0},{16,8},{24,16},{32,24},{40,32},{48,40},{56,48},{64,56},{72,6... | collective-permute-start | bytes 98312 | tf_op jit(solution)/shard_map/ppermute | solution.py:17
  217.9 1.3 copy-start.5
  219.2 1.1 copy-start.7
  220.3 1.3 copy-start.3
  220.3 1.3 copy-start.12
  221.5 1.9 copy-start.9
  221.5 2.0 copy-start.2
Sparse Core Ops, SparseCore 0:
  11.3 91.9 all-gather.6
  106.7 82.3 all-gather.8
  210.0 35.4 reduce-scatter.8
  248.4 42.9 reduce-scatter.10
where the time goes:
time: 531 us; the launch traced here: 524 us
  blocking collectives  458 us (86%)
  matrix products  25.1 us (5%)
  between operations  14.1 us (3%)
  starting transfers between devices  10.1 us (2%)
  local copies, waits for them, and re-layouts  9.42 us (2%)
    psum x1, blocking collectives, shards(): steer_grad = lax.psum(steer_part, 'seq')  272 us
    all_gather x1, blocking collectives, shards(): lax.all_gather(w_key, 'seq', axis=0, tiled=True)  90.1 us
    all_gather x1, blocking collectives, shards(): lax.all_gather(w_value, 'seq', axis=0, tiled=True)  79.3 us
    psum x1, blocking collectives, shards(): row_total = lax.psum(jnp.sum(scaled * unit_share, axis=-1), 'head')  16.5 us
  transfers between devices with their start and end apart: 7, of which 2 were waited for; matrix products, arithmetic and copies ran while one was open for 4% of the time, Pallas kernels for 0%

commit v1 on v0

v1 whole, which is shorter than its diff:
```python
import jax
import jax.numpy as jnp
from jax import lax
from jax.sharding import Mesh, PartitionSpec as P

HD = 64
WIN = 128
EPSILON = 1e-05
HIGHEST = lax.Precision.HIGHEST
SEQ = ("zh", "y", "core")
HEAD = ("x", "zl")
F32 = jnp.float32
BF16 = jnp.bfloat16
PAD = 48


def shifted(value, by):
    count = lax.axis_size(SEQ)
    pairs = [(i, i + by) for i in range(count) if 0 <= i + by < count]
    return lax.ppermute(value, SEQ, pairs)


def gathered(value, axes):
    count = lax.axis_size(axes)
    spread = jnp.broadcast_to(value[None], (count,) + value.shape)
    return lax.all_to_all(spread, axes, 0, 0)


def dot(left, right, dims, **kw):
    return lax.dot_general(left, right, (dims, ((), ())), preferred_element_type=F32, **kw)


def blocked(rows):
    width = rows.shape[-1]
    parts = rows.reshape(4, 8, 2, -1, width).transpose(1, 0, 2, 3, 4)
    parts = jnp.pad(parts, ((0, 0), (0, 0), (0, 0), (0, PAD - parts.shape[3]), (0, 0)))
    return parts.reshape(-1, width)


def for_heads(rows):
    width = rows.shape[-1]
    parts = rows.reshape(2, 4, 4, 2, PAD, width).transpose(2, 0, 1, 3, 4, 5)
    return parts.reshape(8, -1, width)


def unpadded(rows, row_count):
    width = rows.shape[-1]
    return rows.reshape(8, PAD, width)[:, : row_count // 8].reshape(row_count, width)


def split3(value):
    high = lax.reduce_precision(value, 8, 7)
    rest = value - high
    mid = lax.reduce_precision(rest, 8, 7)
    low = lax.reduce_precision(rest - mid, 8, 7)
    return jnp.stack([high, mid, low])


def shards(
    tokens,
    gain,
    w_query,
    w_key,
    w_value,
    w_out,
    w_gate,
    steering,
    segment_ids,
    steer_index,
    grad_out,
):
    row_count, model_width = tokens.shape
    share = model_width // 8
    start = lax.axis_index(HEAD) * share

    padded = lambda w: jnp.pad(w, ((0, PAD - w.shape[0]), (0, 0)))
    both = jnp.stack([padded(w_query), padded(w_out)])
    half = both.shape[2] // 2
    both = both.reshape(2, PAD, 2, half).transpose(2, 0, 1, 3)
    sent = jnp.broadcast_to(both[None], (4,) + both.shape).reshape((8,) + both.shape[1:])
    near = lax.all_to_all(sent, ("zh", "core"), 0, 0)
    q_own = lax.all_gather(near[:, 0], "y", axis=0, tiled=True).reshape(-1, half)
    o_own = lax.all_gather(near[:, 1], "y", axis=0, tiled=True).reshape(-1, half)
    w_kv = padded(jnp.concatenate([w_key, w_value], axis=1))
    kv_near = lax.all_gather(w_kv, ("zh",), axis=0, tiled=False)
    kv_all = lax.all_gather(kv_near, ("y", "core"), axis=0, tiled=False)
    kv_all = kv_all.reshape(8, 2, 4, PAD, 2 * HD).transpose(0, 2, 1, 3, 4).reshape(-1, 2 * HD)
    flip = [(0, 1), (1, 0)]
    q_oth = lax.ppermute(q_own, "core", flip)
    o_oth = lax.ppermute(o_own, "core", flip)

    tok = tokens.T.astype(F32)
    inverse = lax.rsqrt(jnp.mean(tok * tok, axis=0, keepdims=True) + EPSILON)
    unit = tok * inverse
    normed = (unit * gain[:, None]).astype(BF16)
    normed_b = blocked(normed)
    unit_b = blocked(unit * gain[:, None])
    grad_t = grad_out.T
    grad_b = blocked(grad_t)
    gate = jax.nn.sigmoid(jnp.sum(normed.astype(F32) * w_gate[:, None], axis=0))
    one_hot = steer_index[None, :] == lax.broadcasted_iota(jnp.int32, (16, row_count), 0)
    products = dot(steering, grad_t, ((1,), (0,)))
    grad_logit = gate * (1.0 - gate) * jnp.sum(jnp.where(one_hot, products, 0.0), axis=0)
    steer_share = lax.dynamic_slice_in_dim(steering, start, share, 1)
    steer_rows = dot(steer_share, one_hot.astype(BF16), ((0,), (0,)))
    grad_share = lax.dynamic_slice_in_dim(grad_t, start, share, 0).astype(F32)
    steer_part = dot(
        one_hot.astype(F32), gate[None, :] * grad_share, ((1,), (1,)), precision=HIGHEST
    )
    steer_near = jnp.sum(gathered(steer_part, ("zh", "core")), axis=0)
    steer_grad = jnp.sum(gathered(steer_near, ("y",)), axis=0)

    halo_seg = shifted(segment_ids, 1)
    halo_seg = jnp.where(lax.axis_index(SEQ) > 0, halo_seg, -1)
    kv = dot(kv_all, normed_b, ((0,), (0,))).astype(BF16)
    kv_halo = shifted(kv, 1)
    wide = jnp.concatenate([kv_halo, kv], axis=1)
    keys, values = wide[:HD], wide[HD:]
    wide_seg = jnp.concatenate([halo_seg, segment_ids])
    query_pos = lax.broadcasted_iota(jnp.int32, (row_count, 2 * row_count), 0)
    key_pos = lax.broadcasted_iota(jnp.int32, (row_count, 2 * row_count), 1) - WIN
    distance = query_pos - key_pos
    mask = (distance >= 0) & (distance < WIN) & (segment_ids[:, None] == wide_seg[None, :])
    query = jnp.concatenate(
        [
            dot(q_own, normed_b, ((0,), (0,))).astype(BF16),
            dot(q_oth, normed_b, ((0,), (0,))).astype(BF16),
        ]
    ).reshape(8, HD, row_count)
    scores = jnp.einsum("hdq,dk->hqk", query, keys, preferred_element_type=F32) * HD**-0.5
    scores = jnp.where(mask[None], scores, -jnp.inf)
    raised = jnp.exp(scores - jnp.max(scores, axis=-1, keepdims=True))
    probs = raised / jnp.sum(raised, axis=-1, keepdims=True)
    probs_b = probs.astype(BF16)
    mixed = jnp.einsum("hqk,dk->hdq", probs_b, values, preferred_element_type=F32)
    mixed = mixed.astype(BF16).reshape(2, half, row_count)
    term = dot(o_own, mixed[0], ((1,), (0,))) + dot(o_oth, mixed[1], ((1,), (0,)))
    attn = lax.all_to_all(for_heads(term.astype(BF16)), HEAD, 0, 0)
    attn_share = unpadded(jnp.sum(attn.astype(F32), axis=0), share)
    token_share = lax.dynamic_slice_in_dim(tokens.T, start, share, 0).astype(F32)
    layer_out = (token_share + attn_share + gate[None, :] * steer_rows).astype(BF16)

    grad_mixed = jnp.concatenate(
        [
            dot(o_own, grad_b, ((0,), (0,))).astype(BF16),
            dot(o_oth, grad_b, ((0,), (0,))).astype(BF16),
        ]
    ).reshape(8, HD, row_count)
    grad_values = jnp.einsum("hqk,hdq->dk", probs_b, grad_mixed, preferred_element_type=F32)
    grad_prob = jnp.einsum("hdq,dk->hqk", grad_mixed, values, preferred_element_type=F32)
    delta = jnp.sum(probs * grad_prob, axis=-1, keepdims=True)
    grad_scores = (probs * (grad_prob - delta) * HD**-0.5).astype(BF16)
    grad_query = jnp.einsum("hqk,dk->hdq", grad_scores, keys, preferred_element_type=F32)
    grad_query = grad_query.astype(BF16).reshape(2, half, row_count)
    grad_keys = jnp.einsum("hqk,hdq->dk", grad_scores, query, preferred_element_type=F32)
    grad_kv = jnp.concatenate([grad_keys, grad_values])
    returned = shifted(grad_kv[:, :WIN].astype(BF16), -1)
    grad_kv = (grad_kv[:, WIN:] + returned.astype(F32)).astype(BF16)
    terms = (
        dot(q_own, grad_query[0], ((1,), (0,)))
        + dot(q_oth, grad_query[1], ((1,), (0,)))
        + dot(kv_all, grad_kv, ((1,), (0,)))
    ).astype(BF16)
    row_part = split3(jnp.sum(terms.astype(F32) * unit_b, axis=0)).astype(BF16)
    extra = jnp.broadcast_to(jnp.pad(row_part, ((0, 13), (0, 0)))[None], (8, 16, row_count))
    back = lax.all_to_all(jnp.concatenate([for_heads(terms), extra], axis=1), HEAD, 0, 0)
    back = jnp.sum(back.astype(F32), axis=0)
    gain_share = lax.dynamic_slice_in_dim(gain, start, share, 0)[:, None]
    gate_share = lax.dynamic_slice_in_dim(w_gate, start, share, 0)[:, None]
    total = unpadded(back[: 8 * PAD], share) + grad_logit[None, :] * gate_share
    gate_total = jnp.sum(unit * (gain * w_gate)[:, None], axis=0)
    row_total = jnp.sum(back[8 * PAD : 8 * PAD + 3], axis=0) + grad_logit * gate_total
    unit_share = token_share * inverse
    scaled = total * gain_share
    grad_tokens = (
        grad_share + inverse * (scaled - unit_share * (row_total / model_width)[None, :])
    ).astype(BF16)
    return (layer_out.T, grad_tokens.T, steer_grad)


def solution(mesh):
    split = Mesh(mesh.devices.reshape(4, 8, 2, 4, 2), SEQ + HEAD)
    placed = (
        P(SEQ, None),
        P(),
        P(SEQ, HEAD),
        P(SEQ, HEAD),
        P(SEQ, HEAD),
        P(SEQ, HEAD),
        P(),
        P(),
        P(SEQ),
        P(SEQ),
        P(SEQ, None),
    )
    return jax.shard_map(
        shards,
        mesh=split,
        in_specs=placed,
        out_specs=(P(SEQ, HEAD), P(SEQ, HEAD), P(None, HEAD)),
        check_vma=False,
    )
```

time: 531 us -> 242 us (0.46)
  blocking collectives: 458 us -> 60.9 us
  waiting for transfers between devices: 2.59 us -> 64.5 us
  starting transfers between devices: 10.1 us -> 38.2 us
  matrix products: 25.1 us -> 35.3 us
  local copies, waits for them, and re-layouts: 9.42 us -> 17 us
    psum x2 -> x0, blocking collectives: 288 us -> none  [the longest x1 272 us: shards(): steer_grad = lax.psum(steer_part, 'seq')]
    all_gather x2, blocking collectives: 169 us -> 34.3 us  [the longest x1 23.5 us: shards(): kv_all = lax.all_gather(kv_near, ('y', 'core'), axis=0, tiled=False)]
    all_to_all x0 -> x4, waiting for transfers between devices: none -> 31.7 us  [the longest x2 14.6 us: gathered(): return lax.all_to_all(spread, axes, 0, 0)]
    all_gather x2, waiting for transfers between devices: 0.02 us -> 29.6 us  [the longest x1 29.6 us: shards(): lax.all_gather(near[:, 0], 'y', axis=0, tiled=True).reshape(-1, half)]
    all_to_all x0 -> x1, blocking collectives: none -> 26.6 us  [shards(): near = lax.all_to_all(sent, ('zh', 'core'), 0, 0)]
    all_to_all x0 -> x4, starting transfers between devices: none -> 21.3 us  [the longest x2 12.6 us: gathered(): return lax.all_to_all(spread, axes, 0, 0)]
    dot_general x16 -> x18, matrix products: 23.6 us -> 33.7 us  [the longest x13 12.8 us: dot(): lax.dot_general(left, right, (dims, ((), ())), preferred_element_type=F32...]
    ppermute x3 -> x5, starting transfers between devices: 9.92 us -> 16.8 us  [the longest x3 7.92 us: shifted(): return lax.ppermute(value, SEQ, pairs)]
  transfers between devices with their start and end apart: 7 -> 11, of which waited for: 2 -> 6; matrix products, arithmetic and copies ran while one was open for 4% -> 13% of each run, Pallas kernels for 0% -> 0%
where the time goes in v1:
time: 242 us; the launch traced here: 240 us
  waiting for transfers between devices  64.5 us (27%)
  blocking collectives  60.9 us (25%)
  starting transfers between devices  38.2 us (16%)
  matrix products  35.3 us (15%)
  local copies, waits for them, and re-layouts  17 us (7%)
  between operations  14.7 us (6%)
  other arithmetic  9.35 us (4%)
    all_gather x1, waiting for transfers between devices, shards(): lax.all_gather(near[:, 0], 'y', axis=0, tiled=True).reshape(-1, half)  29.6 us
    all_to_all x1, blocking collectives, shards(): near = lax.all_to_all(sent, ('zh', 'core'), 0, 0)  26.6 us
    all_gather x1, blocking collectives, shards(): kv_all = lax.all_gather(kv_near, ('y', 'core'), axis=0, tiled=False)  23.5 us
    all_to_all x2, waiting for transfers between devices, gathered(): return lax.all_to_all(spread, axes, 0, 0)  14.6 us
    dot_general x13, matrix products, dot(): lax.dot_general(left, right, (dims, ((), ())), preferred_element_type=F32...  12.8 us
    all_to_all x2, starting transfers between devices, gathered(): return lax.all_to_all(spread, axes, 0, 0)  12.6 us
    all_to_all x1, waiting for transfers between devices, shards(): attn = lax.all_to_all(for_heads(term.astype(BF16)), HEAD, 0, 0)  11.4 us
    all_gather x1, blocking collectives, shards(): kv_near = lax.all_gather(w_kv, ('zh',), axis=0, tiled=False)  10.8 us
  transfers between devices with their start and end apart: 11, of which 6 were waited for; matrix products, arithmetic and copies ran while one was open for 13% of the time, Pallas kernels for 0%

profile of v1, /device:TPU:1, one launch (start us, length us, event | category | flops | bytes accessed | tf_op | source)
XLA Modules:
  0.0 240.0 jit_solution(13641125180174731504)
XLA Ops:
  9.2 26.6 %all_to_all.25 = bf16[8,2,48,256]{3,2,1,0:T(8,128)(2,1)S(1)} all-to-all(bf16[8,2,48,256]{3,2,1,0:T(8,128)(2,1)S(1)} %bitcast.165), channel_id=1, replica_groups=mesh['zh'=4,'y'=8,'core'=2,'x'=4,'zl'=2] {'zh','core'}, dimensions={0} | all-to-all | bytes 786432 | tf_op jit(solution)/shard_map/all_to_all | solution.py:81
  37.4 3.6 %collective-permute-start.1 = (s32[128]{0:T(128)S(1)}, s32[128]{0:T(128)S(1)}, u32[]{:S(2)}, u32[]{:S(2)}) collective-permute-start(s32[128]{0:T(128)S(1)} %copy-done.23), channel_id=1, source_target_pairs={{0,8},{8,16},{16,24},{24,32},{32,40},{40,48},{48,56},{56,64},{64,7... | collective-permute-start | bytes 1544 | tf_op jit(solution)/shard_map/ppermute | solution.py:20
  41.5 1.5 multiply_reduce_fusion
  43.8 10.8 %all-gather.1 = bf16[192,128]{1,0:T(8,128)(2,1)S(1)} all-gather(bf16[48,128]{1,0:T(8,128)(2,1)S(1)} %fusion.63), channel_id=3, replica_groups=mesh['zh'=4,'y'=8,'core'=2,'x'=4,'zl'=2] {'zh'}, dimensions={0}, use_global_device_ids=true | all-gather | bytes 61440 | tf_op jit(solution)/shard_map/all_gather | solution.py:85
  54.6 23.5 %all-gather.2 = bf16[64,48,128]{2,1,0:T(8,128)(2,1)S(1)} all-gather(bf16[4,48,128]{2,1,0:T(8,128)(2,1)S(1)} %bitcast.174), channel_id=4, replica_groups=mesh['zh'=4,'y'=8,'core'=2,'x'=4,'zl'=2] {'y','core'}, dimensions={0}, use_global_device_ids=true | all-gather | bytes 835584 | tf_op jit(solution)/shard_map/all_gather | solution.py:86
  78.1 2.1 collective-permute-start.3
  80.6 2.2 collective-permute-start
  82.8 3.2 %fusion.10 = (f32[128]{0:T(128)}, f32[2880,128]{1,0:T(8,128)}) fusion(bf16[128,2880]{0,1:T(8,128)(2,1)S(1)} %copy-done.1, f32[2880]{0:T(1024)S(1)} %mul.187, f32[128]{0:T(128)S(1)} %add_rsqrt_fusion, f32[2880]{0:T(1024)S(1)} %copy-done.13), kind=kLoop, calls=%fused_computation.17 | loop fusion | flops 1843072 | bytes 2235904 | tf_op jit(solution)/shard_map/reduce_sum | solution.py:171
  86.1 29.6 %all-gather.9.cloned.1.call-done = bf16[64,1,48,256]{3,2,1,0:T(8,128)(2,1)} async-done(((bf16[8,1,48,256]{3,2,1,0:T(8,128)(2,1)}), bf16[64,1,48,256]{3,2,1,0:T(8,128)(2,1)}) %all-gather.9.cloned.1.call-update) | async-done | bytes 1572880 | tf_op jit(solution)/shard_map/all_gather | solution.py:82
  115.6 6.8 %collective-permute-start.2 = (bf16[3072,256]{1,0:T(8,128)(2,1)}, bf16[3072,256]{1,0:T(8,128)(2,1)}, u32[]{:S(2)}, u32[]{:S(2)}) collective-permute-start(bf16[3072,256]{1,0:T(8,128)(2,1)} %bitcast.151), channel_id=1, source_target_pairs={{0,8},{8,0},{1,9},{9,1},{2,10},{10,2},{3,11},{11,3},{4,12},{12,4},... | collective-permute-start | bytes 4718600 | tf_op jit(solution)/shard_map/ppermute | solution.py:89
  124.1 2.5 %reshape.221 = f32[4,8,2,45,128]{4,3,2,1,0:T(8,128)} reshape(f32[2880,128]{1,0:T(8,128)} %get-tuple-element.9) | data formatting | bytes 2949120 | tf_op jit(solution)/shard_map/reshape | solution.py:35
  126.5 2.8 %copy.63 = f32[8,4,2,45,128]{4,3,2,1,0:T(8,128)} copy(f32[8,4,2,45,128]{4,3,2,0,1:T(8,128)} %bitcast.154) | data formatting | bytes 2949120
  129.3 2.8 %pad.31.clone = f32[8,4,2,48,128]{4,3,2,1,0:T(8,128)} pad(f32[8,4,2,45,128]{4,3,2,1,0:T(8,128)} %copy.63, f32[]{:T(128)} %constant.42.clone.1), padding=0_0x0_0x0_0x0_3x0_0 | pad | bytes 3047428 | tf_op jit(solution)/shard_map/jit(_pad)/pad | solution.py:36
  134.1 2.0 convolution_convert_fusion.2
  136.2 2.0 convolution_convert_fusion.4
  138.7 1.6 fusion.107
  140.3 7.2 %convolution_bitcast_fusion.2 = f32[64,256]{1,0:T(8,128)S(1)} fusion(bf16[8,64,128]{2,1,0:T(8,128)(2,1)S(1)} %bitcast.176, f32[8,128,256]{2,1,0:T(8,128)S(1)} %fusion.65, f32[8,128,256]{2,1,0:T(8,128)} %get-tuple-element.20, f32[8,128]{1,0:T(8,128)S(1)} %get-tuple-element.19), kind=kOutput, calls=%fused_computation.41 | convolution fusion | flops 35390720 | bytes 2297856 | tf_op jit(solution)/shard_map/hqk,hdq->dk/dot_general | solution.py:155
  147.5 7.3 %fusion.21 = bf16[8,64,128]{2,1,0:T(8,128)(2,1)S(1)} fusion(f32[8,128,256]{2,1,0:T(8,128)S(1)} %fusion.65, bf16[128,128]{0,1:T(8,128)(2,1)S(1)} %fusion.23, bf16[128,128]{0,1:T(8,128)(2,1)S(1)} %collective-permute-done, f32[8,128,256]{2,1,0:T(8,128)} %get-tuple-element.20, f32[8,128]{1,0:T(8,128)S(1)} %get-tuple-element.19), kind=kOutput, calls=%fused_computation.33 | convolution fusion | flops 35521792 | bytes 2297856 | tf_op jit(solution)/shard_map/hqk,dk->hdq/dot_general | solution.py:153
  154.9 3.0 %convolution_bitcast_fusion.1 = f32[64,256]{1,0:T(8,128)S(1)} fusion(bf16[8,64,128]{2,1,0:T(8,128)(2,1)S(1)} %bitcast.169, f32[8,128]{1,0:T(8,128)} %copy-done.25, bf16[8,64,128]{2,1,0:T(8,128)(2,1)} %bitcast.177, pred[128,256]{1,0:T(8,128)(4,1)} %copy-done.19, bf16[128,128]{0,1:T(8,128)(2,1)} %copy-done.15, bf16[128,128]{0,1:T(8,128)(2,1)} %copy-done.17), kind=kOutput, calls=%fused_computation.40 | convolution fusion | flops 68486400 | bytes 430080 | tf_op jit(solution)/shard_map/hqk,hdq->dk/dot_general | solution.py:149
  157.9 2.1 collective-permute-start.4
  160.6 2.5 %collective-permute-done.4 = bf16[128,128]{1,0:T(8,128)(2,1)S(1)} collective-permute-done((bf16[128,128]{1,0:T(8,128)(2,1)S(1)}, bf16[128,128]{1,0:T(8,128)(2,1)S(1)}, u32[]{:S(2)}, u32[]{:S(2)}) %collective-permute-start.4) | collective-permute-done | bytes 32800 | tf_op jit(solution)/shard_map/ppermute | solution.py:20
  163.5 2.3 fusion.7
  166.9 5.1 %all-to-all-start.2 = ((bf16[8,400,128]{2,1,0:T(8,128)(2,1)}), bf16[8,400,128]{2,1,0:T(8,128)(2,1)}, u32[]{:S(2)}, u32[]{:S(2)}) async-start(bf16[8,400,128]{2,1,0:T(8,128)(2,1)} %pad_maximum_fusion), calls=%async_computation.2 | async-start | bytes 1638400 | tf_op jit(solution)/shard_map/all_to_all | solution.py:166
  172.0 3.0 %fusion.20 = bf16[8,64,128]{2,1,0:T(8,128)(2,1)S(1)} fusion(bf16[128,128]{0,1:T(8,128)(2,1)S(1)} %copy-done.16, bf16[128,128]{0,1:T(8,128)(2,1)S(1)} %copy-done.18, f32[8,128]{1,0:T(8,128)S(1)} %copy-done.26, bf16[8,64,128]{2,1,0:T(8,128)(2,1)S(1)} %bitcast.178, pred[128,256]{1,0:T(8,128)(4,1)} %copy-done.19), kind=kOutput, calls=%fused_computation.32 | convolution fusion | flops 68617472 | bytes 430080 | tf_op jit(solution)/shard_map/hqk,dk->hdq/dot_general | solution.py:135
  175.6 2.0 fusion.3
  178.6 5.7 %all-to-all-done.2 = bf16[8,400,128]{2,1,0:T(8,128)(2,1)} async-done(((bf16[8,400,128]{2,1,0:T(8,128)(2,1)}), bf16[8,400,128]{2,1,0:T(8,128)(2,1)}, u32[]{:S(2)}, u32[]{:S(2)}) %all-to-all-start.2) | async-done | bytes 819232 | tf_op jit(solution)/shard_map/all_to_all | solution.py:166
  184.3 3.7 %all-to-all-start.1 = ((bf16[8,384,128]{2,1,0:T(8,128)(2,1)}), bf16[8,384,128]{2,1,0:T(8,128)(2,1)S(1)}, u32[]{:S(2)}, u32[]{:S(2)}) async-start(bf16[8,384,128]{2,1,0:T(8,128)(2,1)} %bitcast.21), calls=%async_computation.1 | async-start | bytes 1572864 | tf_op jit(solution)/shard_map/all_to_all | solution.py:138
  189.8 11.4 %all-to-all-done.1 = bf16[8,384,128]{2,1,0:T(8,128)(2,1)S(1)} async-done(((bf16[8,384,128]{2,1,0:T(8,128)(2,1)}), bf16[8,384,128]{2,1,0:T(8,128)(2,1)S(1)}, u32[]{:S(2)}, u32[]{:S(2)}) %all-to-all-start.1) | async-done | bytes 786464 | tf_op jit(solution)/shard_map/all_to_all | solution.py:138
  201.9 6.8 %all-to-all-start.3 = ((f32[8,16,360]{2,1,0:T(8,128)}), f32[8,16,360]{2,1,0:T(8,128)S(1)}, u32[]{:S(2)}, u32[]{:S(2)}) async-start(f32[8,16,360]{2,1,0:T(8,128)} %broadcast_in_dim.34), calls=%async_computation.3 | async-start | bytes 393216 | tf_op jit(solution)/shard_map/all_to_all | solution.py:26
  209.7 7.7 %all-to-all-done.3 = f32[8,16,360]{2,1,0:T(8,128)S(1)} async-done(((f32[8,16,360]{2,1,0:T(8,128)}), f32[8,16,360]{2,1,0:T(8,128)S(1)}, u32[]{:S(2)}, u32[]{:S(2)}) %all-to-all-start.3) | async-done | bytes 184352 | tf_op jit(solution)/shard_map/all_to_all | solution.py:26
  218.1 5.7 %all-to-all-start.4 = ((f32[8,16,360]{2,1,0:T(8,128)}), f32[8,16,360]{2,1,0:T(8,128)S(1)}, u32[]{:S(2)}, u32[]{:S(2)}) async-start(f32[8,16,360]{2,1,0:T(8,128)} %broadcast_in_dim.35), calls=%async_computation.4 | async-start | bytes 393216 | tf_op jit(solution)/shard_map/all_to_all | solution.py:26
  225.6 6.9 %all-to-all-done.4 = f32[8,16,360]{2,1,0:T(8,128)S(1)} async-done(((f32[8,16,360]{2,1,0:T(8,128)}), f32[8,16,360]{2,1,0:T(8,128)S(1)}, u32[]{:S(2)}, u32[]{:S(2)}) %all-to-all-start.4) | async-done | bytes 184352 | tf_op jit(solution)/shard_map/all_to_all | solution.py:26
  (121 shorter events, 19.2 us)
Async XLA Ops:
  7.2 180.8 %copy-start = (bf16[16,2880]{1,0:T(8,128)(2,1)S(1)}, bf16[16,2880]{1,0:T(8,128)(2,1)}, u32[]{:S(2)}) copy-start(bf16[16,2880]{1,0:T(8,128)(2,1)} %param.18) | copy-start | bytes 276484
  7.2 70.9 %all-gather.7.cloned.1.call-start = ((), (), s32[]{:S(2)}) async-start(), calls=%async_computation.5 | async-start | bytes 1769472 | tf_op jit(solution)/shard_map/all_gather | solution.py:83
  8.0 29.3 %copy-start.23 = (s32[128]{0:T(128)S(1)}, s32[128]{0:T(128)}, u32[]{:S(2)}) copy-start(s32[128]{0:T(128)} %param.19) | copy-start | bytes 1540
  8.0 33.0 %copy-start.1 = (bf16[128,2880]{0,1:T(8,128)(2,1)S(1)}, bf16[128,2880]{0,1:T(8,128)(2,1)}, u32[]{:S(2)}) copy-start(bf16[128,2880]{0,1:T(8,128)(2,1)} %param.11) | copy-start | bytes 2211844
  9.1 32.3 %copy-start.13 = (f32[2880]{0:T(1024)S(1)}, f32[2880]{0:T(1024)}, u32[]{:S(2)}) copy-start(f32[2880]{0:T(1024)} %param.12) | copy-start | bytes 34564
  9.1 32.3 %copy-start.14 = (f32[2880]{0:T(1024)S(1)}, f32[2880]{0:T(1024)}, u32[]{:S(2)}) copy-start(f32[2880]{0:T(1024)} %param.17) | copy-start | bytes 34564
  36.6 79.0 %all-gather.9.cloned.1.call-start = ((), (), s32[]{:S(2)}) async-start(), calls=%async_computation.6 | async-start | bytes 1769472 | tf_op jit(solution)/shard_map/all_gather | solution.py:82
  37.4 94.7 %collective-permute-start.1 = (s32[128]{0:T(128)S(1)}, s32[128]{0:T(128)S(1)}, u32[]{:S(2)}, u32[]{:S(2)}) collective-permute-start(s32[128]{0:T(128)S(1)} %copy-done.23), channel_id=1, source_target_pairs={{0,8},{8,16},{16,24},{24,32},{32,40},{40,48},{48,56},{56,64},{64,7... | collective-permute-start | bytes 1544 | tf_op jit(solution)/shard_map/ppermute | solution.py:20
  78.1 7.9 %copy-start.9 = (bf16[64,48,128]{2,1,0:T(8,128)(2,1)}, bf16[64,48,128]{2,1,0:T(8,128)(2,1)S(1)}, u32[]{:S(2)}) copy-start(bf16[64,48,128]{2,1,0:T(8,128)(2,1)S(1)} %all-gather.2) | copy-start | bytes 2359300
  78.1 56.0 %collective-permute-start.3 = (bf16[3072,256]{1,0:T(8,128)(2,1)}, bf16[3072,256]{1,0:T(8,128)(2,1)}, u32[]{:S(2)}, u32[]{:S(2)}) collective-permute-start(bf16[3072,256]{1,0:T(8,128)(2,1)} %bitcast.148), channel_id=1, source_target_pairs={{0,8},{8,0},{1,9},{9,1},{2,10},{10,2},{3,11},{11,3},{4,12},{12,4},... | collective-permute-start | bytes 4718600 | tf_op jit(solution)/shard_map/ppermute | solution.py:90
  80.6 66.9 %copy-start.15 = (bf16[128,128]{0,1:T(8,128)(2,1)}, bf16[128,128]{0,1:T(8,128)(2,1)S(1)}, u32[]{:S(2)}) copy-start(bf16[128,128]{0,1:T(8,128)(2,1)S(1)} %fusion.23) | copy-start | bytes 98308
  80.6 57.6 %collective-permute-start = (bf16[128,128]{0,1:T(8,128)(2,1)S(1)}, bf16[128,128]{0,1:T(8,128)(2,1)S(1)}, u32[]{:S(2)}, u32[]{:S(2)}) collective-permute-start(bf16[128,128]{0,1:T(8,128)(2,1)S(1)} %fusion.23), channel_id=1, source_target_pairs={{0,8},{8,16},{16,24},{24,32},{32,40},{40,48},{48,56},{56,64},{64,7... | collective-permute-start | bytes 98312 | tf_op jit(solution)/shard_map/ppermute | solution.py:20
  115.6 6.9 %copy-start.10 = (bf16[64,48,128]{2,1,0:T(8,128)(2,1)S(1)}, bf16[64,48,128]{2,1,0:T(8,128)(2,1)}, u32[]{:S(2)}) copy-start(bf16[64,48,128]{2,1,0:T(8,128)(2,1)} %copy-done.9) | copy-start | bytes 2359300
  115.6 20.6 %collective-permute-start.2 = (bf16[3072,256]{1,0:T(8,128)(2,1)}, bf16[3072,256]{1,0:T(8,128)(2,1)}, u32[]{:S(2)}, u32[]{:S(2)}) collective-permute-start(bf16[3072,256]{1,0:T(8,128)(2,1)} %bitcast.151), channel_id=1, source_target_pairs={{0,8},{8,0},{1,9},{9,1},{2,10},{10,2},{3,11},{11,3},{4,12},{12,4},... | collective-permute-start | bytes 4718600 | tf_op jit(solution)/shard_map/ppermute | solution.py:89
  132.2 6.4 %copy-start.19 = (pred[128,256]{1,0:T(8,128)(4,1)}, pred[128,256]{1,0:T(8,128)(4,1)S(1)}, u32[]{:S(2)}) copy-start(pred[128,256]{1,0:T(8,128)(4,1)S(1)} %fusion.43) | copy-start | bytes 98308
  138.2 16.6 %copy-start.11 = (bf16[512,128]{1,0:T(8,128)(2,1)}, bf16[512,128]{1,0:T(8,128)(2,1)S(1)}, u32[]{:S(2)}) copy-start(bf16[512,128]{1,0:T(8,128)(2,1)S(1)} %pad_maximum_fusion.1) | copy-start | bytes 393220
  138.3 9.2 %copy-start.17 = (bf16[128,128]{0,1:T(8,128)(2,1)}, bf16[128,128]{0,1:T(8,128)(2,1)S(1)}, u32[]{:S(2)}) copy-start(bf16[128,128]{0,1:T(8,128)(2,1)S(1)} %collective-permute-done) | copy-start | bytes 98308
  140.3 7.2 %copy-start.25 = (f32[8,128]{1,0:T(8,128)}, f32[8,128]{1,0:T(8,128)S(1)}, u32[]{:S(2)}) copy-start(f32[8,128]{1,0:T(8,128)S(1)} %get-tuple-element.19) | copy-start | bytes 12292
  154.9 5.2 %copy-start.5 = (bf16[64,1,48,256]{3,2,1,0:T(8,128)(2,1)S(1)}, bf16[64,1,48,256]{3,2,1,0:T(8,128)(2,1)}, u32[]{:S(2)}) copy-start(bf16[64,1,48,256]{3,2,1,0:T(8,128)(2,1)} %all-gather.9.cloned.1.call-done) | copy-start | bytes 4718596
  157.9 5.2 %collective-permute-start.4 = (bf16[128,128]{1,0:T(8,128)(2,1)S(1)}, bf16[128,128]{1,0:T(8,128)(2,1)S(1)}, u32[]{:S(2)}, u32[]{:S(2)}) collective-permute-start(bf16[128,128]{1,0:T(8,128)(2,1)S(1)} %fusion.50), channel_id=1, source_target_pairs={{8,0},{16,8},{24,16},{32,24},{40,32},{48,40},{56,48},{64,56},{72,6... | collective-permute-start | bytes 98312 | tf_op jit(solution)/shard_map/ppermute | solution.py:20
  160.0 3.1 %copy-start.8 = (bf16[8,2,4,48,128]{4,3,1,2,0:T(8,128)(2,1)S(1)}, bf16[8,2,4,48,128]{4,3,1,2,0:T(8,128)(2,1)}, u32[]{:S(2)}) copy-start(bf16[8,2,4,48,128]{4,3,1,2,0:T(8,128)(2,1)} %copy.43) | copy-start | bytes 2359300
  165.9 6.1 %copy-start.12 = (bf16[512,128]{1,0:T(8,128)(2,1)S(1)}, bf16[512,128]{1,0:T(8,128)(2,1)}, u32[]{:S(2)}) copy-start(bf16[512,128]{1,0:T(8,128)(2,1)} %copy-done.11) | copy-start | bytes 393220
  165.9 6.0 %copy-start.16 = (bf16[128,128]{0,1:T(8,128)(2,1)S(1)}, bf16[128,128]{0,1:T(8,128)(2,1)}, u32[]{:S(2)}) copy-start(bf16[128,128]{0,1:T(8,128)(2,1)} %copy-done.15) | copy-start | bytes 98308
  165.9 6.0 %copy-start.18 = (bf16[128,128]{0,1:T(8,128)(2,1)S(1)}, bf16[128,128]{0,1:T(8,128)(2,1)}, u32[]{:S(2)}) copy-start(bf16[128,128]{0,1:T(8,128)(2,1)} %copy-done.17) | copy-start | bytes 98308
  165.9 6.0 %copy-start.26 = (f32[8,128]{1,0:T(8,128)S(1)}, f32[8,128]{1,0:T(8,128)}, u32[]{:S(2)}) copy-start(f32[8,128]{1,0:T(8,128)} %copy-done.25) | copy-start | bytes 12292
  166.9 17.4 %all-to-all-start.2 = ((bf16[8,400,128]{2,1,0:T(8,128)(2,1)}), bf16[8,400,128]{2,1,0:T(8,128)(2,1)}, u32[]{:S(2)}, u32[]{:S(2)}) async-start(bf16[8,400,128]{2,1,0:T(8,128)(2,1)} %pad_maximum_fusion), calls=%async_computation.2 | async-start | bytes 1638400 | tf_op jit(solution)/shard_map/all_to_all | solution.py:166
  172.0 3.1 %copy-start.3 = (bf16[64,1,48,256]{3,2,1,0:T(8,128)(2,1)S(1)}, bf16[64,1,48,256]{3,2,1,0:T(8,128)(2,1)}, u32[]{:S(2)}) copy-start(bf16[64,1,48,256]{3,2,1,0:T(8,128)(2,1)} %all-gather.7.cloned.1.call-done) | copy-start | bytes 4718596
  177.6 10.4 %copy-start.22 = (s32[128]{0:T(128)S(1)}, s32[128]{0:T(128)}, u32[]{:S(2)}) copy-start(s32[128]{0:T(128)} %param.20) | copy-start | bytes 1540
  184.3 5.2 %copy-start.24 = (f32[128]{0:T(128)S(1)}, f32[128]{0:T(128)}, u32[]{:S(2)}) copy-start(f32[128]{0:T(128)} %get-tuple-element.8) | copy-start | bytes 1540
  184.3 16.9 %all-to-all-start.1 = ((bf16[8,384,128]{2,1,0:T(8,128)(2,1)}), bf16[8,384,128]{2,1,0:T(8,128)(2,1)S(1)}, u32[]{:S(2)}, u32[]{:S(2)}) async-start(bf16[8,384,128]{2,1,0:T(8,128)(2,1)} %bitcast.21), calls=%async_computation.1 | async-start | bytes 1572864 | tf_op jit(solution)/shard_map/all_to_all | solution.py:138
  201.9 15.5 %all-to-all-start.3 = ((f32[8,16,360]{2,1,0:T(8,128)}), f32[8,16,360]{2,1,0:T(8,128)S(1)}, u32[]{:S(2)}, u32[]{:S(2)}) async-start(f32[8,16,360]{2,1,0:T(8,128)} %broadcast_in_dim.34), calls=%async_computation.3 | async-start | bytes 393216 | tf_op jit(solution)/shard_map/all_to_all | solution.py:26
  218.1 14.5 %all-to-all-start.4 = ((f32[8,16,360]{2,1,0:T(8,128)}), f32[8,16,360]{2,1,0:T(8,128)S(1)}, u32[]{:S(2)}, u32[]{:S(2)}) async-start(f32[8,16,360]{2,1,0:T(8,128)} %broadcast_in_dim.35), calls=%async_computation.4 | async-start | bytes 393216 | tf_op jit(solution)/shard_map/all_to_all | solution.py:26
  (6 other events, 9.9 us)
Sparse Core Ops, SparseCore 0:
  36.7 35.8 all-gather.6
  74.7 40.8 all-gather.8

commit v2 on v1

--- a/solution.py
+++ b/solution.py
@@ -1,6 +1,8 @@
 import jax
 import jax.numpy as jnp
 from jax import lax
+from jax.experimental import pallas as pl
+from jax.experimental.pallas import tpu as pltpu
 from jax.sharding import Mesh, PartitionSpec as P
 
 HD = 64
@@ -54,6 +56,60 @@
     mid = lax.reduce_precision(rest, 8, 7)
     low = lax.reduce_precision(rest - mid, 8, 7)
     return jnp.stack([high, mid, low])
+
+
+def mm(left, right, left_dim, right_dim):
+    dims = (((left_dim,), (right_dim,)), ((), ()))
+    return lax.dot_general(left, right, dims, preferred_element_type=F32)
+
+
+def attend_kernel(q_own, q_oth, kv, halo, mask, mixed, probs):
+    keys = jnp.concatenate([halo[:HD, :], kv[:HD, :]], axis=1)
+    values = jnp.concatenate([halo[HD:, :], kv[HD:, :]], axis=1)
+    allowed = mask[...] > 0.0
+    for head in range(8):
+        source = q_own if head < 4 else q_oth
+        query = source[pl.ds(head % 4 * HD, HD), :]
+        scores = mm(keys, query, 0, 0) * HD**-0.5
+        scores = jnp.where(allowed, scores, -jnp.inf)
+        raised = jnp.exp(scores - jnp.max(scores, axis=0, keepdims=True))
+        prob = raised / jnp.sum(raised, axis=0, keepdims=True)
+        probs[head] = prob
+        mixed[pl.ds(head * HD, HD), :] = mm(values, prob.astype(BF16), 1, 0).astype(BF16)
+
+
+def attend_back_kernel(
+    g_own, g_oth, q_own, q_oth, kv, halo, probs, grad_query, grad_halo, grad_kv
+):
+    keys = jnp.concatenate([halo[:HD, :], kv[:HD, :]], axis=1)
+    values = jnp.concatenate([halo[HD:, :], kv[HD:, :]], axis=1)
+    grad_keys = jnp.zeros(keys.shape, F32)
+    grad_values = jnp.zeros(keys.shape, F32)
+    for head in range(8):
+        rows = pl.ds(head % 4 * HD, HD)
+        query = (q_own if head < 4 else q_oth)[rows, :]
+        grad = (g_own if head < 4 else g_oth)[rows, :]
+        prob = probs[head]
+        grad_values += mm(grad, prob.astype(BF16), 1, 1)
+        grad_prob = mm(values, grad, 0, 0)
+        delta = jnp.sum(prob * grad_prob, axis=0, keepdims=True)
+        grad_scores = (prob * (grad_prob - delta) * HD**-0.5).astype(BF16)
+        grad_query[pl.ds(head * HD, HD), :] = mm(keys, grad_scores, 1, 0).astype(BF16)
+        grad_keys += mm(query, grad_scores, 1, 1)
+    grad_halo[:HD, :] = grad_keys[:, :WIN].astype(BF16)
+    grad_halo[HD:, :] = grad_values[:, :WIN].astype(BF16)
+    grad_kv[:HD, :] = grad_keys[:, WIN:]
+    grad_kv[HD:, :] = grad_values[:, WIN:]
+
+
+def call(kernel, outs, *args):
+    size = sum(a.size * a.dtype.itemsize for a in (*args, *outs))
+    return pl.pallas_call(
+        kernel,
+        out_shape=outs,
+        compiler_params=pltpu.CompilerParams(vmem_limit_bytes=40 * 2**20),
+        cost_estimate=pl.CostEstimate(flops=10**8, bytes_accessed=size, transcendentals=0),
+    )(*args)
 
 
 def shards(
@@ -74,20 +130,19 @@
     start = lax.axis_index(HEAD) * share
 
     padded = lambda w: jnp.pad(w, ((0, PAD - w.shape[0]), (0, 0)))
-    both = jnp.stack([padded(w_query), padded(w_out)])
-    half = both.shape[2] // 2
-    both = both.reshape(2, PAD, 2, half).transpose(2, 0, 1, 3)
-    sent = jnp.broadcast_to(both[None], (4,) + both.shape).reshape((8,) + both.shape[1:])
+    half = w_query.shape[1] // 2
+    query_w, out_w = padded(w_query), padded(w_out)
+    pair = lambda c: jnp.concatenate(
+        [query_w[:, c * half : (c + 1) * half], out_w[:, c * half : (c + 1) * half]], axis=1
+    )
+    sent = jnp.stack([pair(0), pair(1)] * 4)
     near = lax.all_to_all(sent, ("zh", "core"), 0, 0)
-    q_own = lax.all_gather(near[:, 0], "y", axis=0, tiled=True).reshape(-1, half)
-    o_own = lax.all_gather(near[:, 1], "y", axis=0, tiled=True).reshape(-1, half)
+    own = lax.all_gather(near, "y", axis=0, tiled=True).reshape(-1, 2 * half)
     w_kv = padded(jnp.concatenate([w_key, w_value], axis=1))
+    w_kv, near = lax.optimization_barrier((w_kv, near))
     kv_near = lax.all_gather(w_kv, ("zh",), axis=0, tiled=False)
     kv_all = lax.all_gather(kv_near, ("y", "core"), axis=0, tiled=False)
     kv_all = kv_all.reshape(8, 2, 4, PAD, 2 * HD).transpose(0, 2, 1, 3, 4).reshape(-1, 2 * HD)
-    flip = [(0, 1), (1, 0)]
-    q_oth = lax.ppermute(q_own, "core", flip)
-    o_oth = lax.ppermute(o_own, "core", flip)
 
     tok = tokens.T.astype(F32)
     inverse = lax.rsqrt(jnp.mean(tok * tok, axis=0, keepdims=True) + EPSILON)
@@ -113,57 +168,56 @@
     halo_seg = shifted(segment_ids, 1)
     halo_seg = jnp.where(lax.axis_index(SEQ) > 0, halo_seg, -1)
     kv = dot(kv_all, normed_b, ((0,), (0,))).astype(BF16)
-    kv_halo = shifted(kv, 1)
-    wide = jnp.concatenate([kv_halo, kv], axis=1)
-    keys, values = wide[:HD], wide[HD:]
+    halo = shifted(kv, 1)
     wide_seg = jnp.concatenate([halo_seg, segment_ids])
-    query_pos = lax.broadcasted_iota(jnp.int32, (row_count, 2 * row_count), 0)
-    key_pos = lax.broadcasted_iota(jnp.int32, (row_count, 2 * row_count), 1) - WIN
+    key_pos = lax.broadcasted_iota(jnp.int32, (2 * row_count, row_count), 0) - WIN
+    query_pos = lax.broadcasted_iota(jnp.int32, (2 * row_count, row_count), 1)
     distance = query_pos - key_pos
-    mask = (distance >= 0) & (distance < WIN) & (segment_ids[:, None] == wide_seg[None, :])
-    query = jnp.concatenate(
-        [
-            dot(q_own, normed_b, ((0,), (0,))).astype(BF16),
-            dot(q_oth, normed_b, ((0,), (0,))).astype(BF16),
-        ]
-    ).reshape(8, HD, row_count)
-    scores = jnp.einsum("hdq,dk->hqk", query, keys, preferred_element_type=F32) * HD**-0.5
-    scores = jnp.where(mask[None], scores, -jnp.inf)
-    raised = jnp.exp(scores - jnp.max(scores, axis=-1, keepdims=True))
-    probs = raised / jnp.sum(raised, axis=-1, keepdims=True)
-    probs_b = probs.astype(BF16)
-    mixed = jnp.einsum("hqk,dk->hdq", probs_b, values, preferred_element_type=F32)
-    mixed = mixed.astype(BF16).reshape(2, half, row_count)
-    term = dot(o_own, mixed[0], ((1,), (0,))) + dot(o_oth, mixed[1], ((1,), (0,)))
-    attn = lax.all_to_all(for_heads(term.astype(BF16)), HEAD, 0, 0)
-    attn_share = unpadded(jnp.sum(attn.astype(F32), axis=0), share)
-    token_share = lax.dynamic_slice_in_dim(tokens.T, start, share, 0).astype(F32)
-    layer_out = (token_share + attn_share + gate[None, :] * steer_rows).astype(BF16)
-
-    grad_mixed = jnp.concatenate(
-        [
-            dot(o_own, grad_b, ((0,), (0,))).astype(BF16),
-            dot(o_oth, grad_b, ((0,), (0,))).astype(BF16),
-        ]
-    ).reshape(8, HD, row_count)
-    grad_values = jnp.einsum("hqk,hdq->dk", probs_b, grad_mixed, preferred_element_type=F32)
-    grad_prob = jnp.einsum("hdq,dk->hqk", grad_mixed, values, preferred_element_type=F32)
-    delta = jnp.sum(probs * grad_prob, axis=-1, keepdims=True)
-    grad_scores = (probs * (grad_prob - delta) * HD**-0.5).astype(BF16)
-    grad_query = jnp.einsum("hqk,dk->hdq", grad_scores, keys, preferred_element_type=F32)
-    grad_query = grad_query.astype(BF16).reshape(2, half, row_count)
-    grad_keys = jnp.einsum("hqk,hdq->dk", grad_scores, query, preferred_element_type=F32)
-    grad_kv = jnp.concatenate([grad_keys, grad_values])
-    returned = shifted(grad_kv[:, :WIN].astype(BF16), -1)
-    grad_kv = (grad_kv[:, WIN:] + returned.astype(F32)).astype(BF16)
+    mask = (distance >= 0) & (distance < WIN) & (wide_seg[:, None] == segment_ids[None, :])
+    mask = mask.astype(F32)
+    own, halo, mask, steer_grad, normed_b, grad_b, unit_b, kv, kv_all = lax.optimization_barrier(
+        (own, halo, mask, steer_grad, normed_b, grad_b, unit_b, kv, kv_all)
+    )
+    oth = lax.ppermute(own, "core", [(0, 1), (1, 0)])
+    like = jax.ShapeDtypeStruct
+    q_own = dot(own[:, :half], normed_b, ((0,), (0,))).astype(BF16)
+    q_oth = dot(oth[:, :half], normed_b, ((0,), (0,))).astype(BF16)
+    mixed, probs = call(
+        attend_kernel,
+        (like((2 * half, row_count), BF16), like((8, 2 * row_count, row_count), F32)),
+        *(q_own, q_oth, kv, halo, mask),
+    )
+    term = dot(own[:, half:], mixed[:half], ((1,), (0,)))
+    term = term + dot(oth[:, half:], mixed[half:], ((1,), (0,)))
+    blocks = for_heads(term.astype(BF16))
+    g_own = dot(own[:, half:], grad_b, ((0,), (0,))).astype(BF16)
+    blocks, grad_b, own, oth = lax.optimization_barrier((blocks, grad_b, own, oth))
+    attn = lax.all_to_all(blocks, HEAD, 0, 0)
+
+    g_oth = dot(oth[:, half:], grad_b, ((0,), (0,))).astype(BF16)
+    grad_query, grad_halo, grad_kv = call(
+        attend_back_kernel,
+        (
+            like((2 * half, row_count), BF16),
+            like((2 * HD, row_count), BF16),
+            like((2 * HD, row_count), F32),
+        ),
+        *(g_own, g_oth, q_own, q_oth, kv, halo, probs),
+    )
+    returned = shifted(grad_halo, -1)
+    grad_kv = (grad_kv + returned.astype(F32)).astype(BF16)
     terms = (
-        dot(q_own, grad_query[0], ((1,), (0,)))
-        + dot(q_oth, grad_query[1], ((1,), (0,)))
+        dot(own[:, :half], grad_query[:half], ((1,), (0,)))
+        + dot(oth[:, :half], grad_query[half:], ((1,), (0,)))
         + dot(kv_all, grad_kv, ((1,), (0,)))
     ).astype(BF16)
     row_part = split3(jnp.sum(terms.astype(F32) * unit_b, axis=0)).astype(BF16)
     extra = jnp.broadcast_to(jnp.pad(row_part, ((0, 13), (0, 0)))[None], (8, 16, row_count))
     back = lax.all_to_all(jnp.concatenate([for_heads(terms), extra], axis=1), HEAD, 0, 0)
+
+    attn_share = unpadded(jnp.sum(attn.astype(F32), axis=0), share)
+    token_share = lax.dynamic_slice_in_dim(tokens.T, start, share, 0).astype(F32)
+    layer_out = (token_share + attn_share + gate[None, :] * steer_rows).astype(BF16)
     back = jnp.sum(back.astype(F32), axis=0)
     gain_share = lax.dynamic_slice_in_dim(gain, start, share, 0)[:, None]
     gate_share = lax.dynamic_slice_in_dim(w_gate, start, share, 0)[:, None]

time: 242 us -> 167 us (0.69)
  waiting for transfers between devices: 64.5 us -> 19.2 us
  matrix products: 35.3 us -> 12.9 us
  starting transfers between devices: 38.2 us -> 27.7 us
  Pallas kernels: 0 us -> 3.05 us
    all_gather x2 -> x1, waiting for transfers between devices: 29.6 us -> 0.01 us  [shards(): own = lax.all_gather(near, 'y', axis=0, tiled=True).reshape(-1, 2 * half)]
    dot_general x5 -> x0, matrix products: 20.9 us -> none  [the longest x1 7.3 us: shards(): jnp.einsum('hqk,dk->hdq', grad_scores, keys, preferred_element_type=F32)]
    all_to_all x2, waiting for transfers between devices: 14.6 us -> 0.01 us  [gathered(): return lax.all_to_all(spread, axes, 0, 0)]
    ppermute x2 -> x1, starting transfers between devices: 8.85 us -> 2.53 us  [shards(): oth = lax.ppermute(own, 'core', [(0, 1), (1, 0)])]
    all_to_all x1, waiting for transfers between devices: 5.7 us -> 9.48 us  [shards(): lax.all_to_all(jnp.concatenate([for_heads(terms), extra], axis=1), HEAD,...]
    pallas_call x0 -> x2, Pallas kernels: none -> 3.05 us  [call(): pl.pallas_call(kernel, out_shape=outs, compiler_params=pltpu.CompilerPara...]
    all_gather x1, blocking collectives: 10.8 us -> 13.8 us  [shards(): kv_near = lax.all_gather(w_kv, ('zh',), axis=0, tiled=False)]
    all_to_all x1, waiting for transfers between devices: 11.4 us -> 8.54 us  [shards(): attn = lax.all_to_all(blocks, HEAD, 0, 0)]
  transfers between devices with their start and end apart: 11 -> 9, of which waited for: 6 -> 3; matrix products, arithmetic and copies ran while one was open for 13% -> 19% of each run, Pallas kernels for 0% -> 0%
where the time goes in v2:
time: 167 us; the launch traced here: 166 us
  blocking collectives  62.7 us (38%)
  starting transfers between devices  27.7 us (17%)
  waiting for transfers between devices  19.2 us (11%)
  local copies, waits for them, and re-layouts  14.8 us (9%)
  between operations  14.6 us (9%)
  matrix products  12.9 us (8%)
  other arithmetic  11.2 us (7%)
  Pallas kernels  3.05 us (2%)
    all_to_all x1, blocking collectives, shards(): near = lax.all_to_all(sent, ('zh', 'core'), 0, 0)  26.8 us
    all_gather x1, blocking collectives, shards(): kv_all = lax.all_gather(kv_near, ('y', 'core'), axis=0, tiled=False)  22 us
    all_gather x1, blocking collectives, shards(): kv_near = lax.all_gather(w_kv, ('zh',), axis=0, tiled=False)  13.8 us
    dot_general x13, matrix products, dot(): lax.dot_general(left, right, (dims, ((), ())), preferred_element_type=F32...  12.9 us
    all_to_all x2, starting transfers between devices, gathered(): return lax.all_to_all(spread, axes, 0, 0)  9.79 us
    all_to_all x1, waiting for transfers between devices, shards(): lax.all_to_all(jnp.concatenate([for_heads(terms), extra], axis=1), HEAD,...  9.48 us
    all_to_all x1, waiting for transfers between devices, shards(): attn = lax.all_to_all(blocks, HEAD, 0, 0)  8.54 us
    ppermute x3, starting transfers between devices, shifted(): return lax.ppermute(value, SEQ, pairs)  7.41 us
  transfers between devices with their start and end apart: 9, of which 3 were waited for; matrix products, arithmetic and copies ran while one was open for 19% of the time, Pallas kernels for 0%

profile of v2, /device:TPU:1, one launch (start us, length us, event | category | flops | bytes accessed | tf_op | source)
XLA Modules:
  0.0 166.1 jit_solution(13791963327533712264)
XLA Ops:
  8.3 26.8 %all_to_all.25 = bf16[8,48,512]{2,1,0:T(8,128)(2,1)} all-to-all(bf16[8,48,512]{2,1,0:T(8,128)(2,1)S(1)} %constant_dynamic-update-slice_fusion), channel_id=1, replica_groups=mesh['zh'=4,'y'=8,'core'=2,'x'=4,'zl'=2] {'zh','core'}, dimensions={0} | all-to-all | bytes 786432 | tf_op jit(solution)/shard_map/all_to_all | solution.py:139
  35.6 1.5 multiply_reduce_fusion.1
  38.6 3.9 %all-to-all-start.1 = ((f32[8,16,360]{2,1,0:T(8,128)}), f32[8,16,360]{2,1,0:T(8,128)S(1)}, u32[]{:S(2)}, u32[]{:S(2)}) async-start(f32[8,16,360]{2,1,0:T(8,128)} %broadcast_in_dim.14), calls=%async_computation.1 | async-start | bytes 393216 | tf_op jit(solution)/shard_map/all_to_all | solution.py:28
  42.5 3.2 %collective-permute-start.1 = (s32[128]{0:T(128)S(1)}, s32[128]{0:T(128)S(1)}, u32[]{:S(2)}, u32[]{:S(2)}) collective-permute-start(s32[128]{0:T(128)S(1)} %copy-done.20), channel_id=1, source_target_pairs={{0,8},{8,16},{16,24},{24,32},{32,40},{40,48},{48,56},{56,64},{64,7... | collective-permute-start | bytes 1544 | tf_op jit(solution)/shard_map/ppermute | solution.py:22
  45.9 1.0 copy.41
  46.9 3.0 %fusion.17 = (f32[128]{0:T(128)}, f32[2880,128]{1,0:T(8,128)}) fusion(bf16[128,2880]{0,1:T(8,128)(2,1)S(1)} %copy-done.1, f32[2880]{0:T(1024)S(1)} %mul.172, f32[128]{0:T(128)S(1)} %add_rsqrt_fusion, f32[2880]{0:T(1024)S(1)} %copy-done.12), kind=kLoop, calls=%fused_computation.24 | loop fusion | flops 1843072 | bytes 2235904 | tf_op jit(solution)/shard_map/reduce_sum | solution.py:225
  49.9 1.4 reshape.133
  51.3 1.3 copy.35
  54.2 1.0 pad.29
  55.2 1.0 pad.30.clone
  57.7 5.9 %all-to-all-start.2 = ((f32[8,16,360]{2,1,0:T(8,128)}), f32[8,16,360]{2,1,0:T(8,128)S(1)}, u32[]{:S(2)}, u32[]{:S(2)}) async-start(f32[8,16,360]{2,1,0:T(8,128)} %broadcast_in_dim.15), calls=%async_computation.2 | async-start | bytes 393216 | tf_op jit(solution)/shard_map/all_to_all | solution.py:28
  63.6 13.8 %all-gather = bf16[192,128]{1,0:T(8,128)(2,1)S(1)} all-gather(bf16[48,128]{1,0:T(8,128)(2,1)} %fusion.60), channel_id=2, replica_groups=mesh['zh'=4,'y'=8,'core'=2,'x'=4,'zl'=2] {'zh'}, dimensions={0}, use_global_device_ids=true | all-gather | bytes 61440 | tf_op jit(solution)/shard_map/all_gather | solution.py:143
  77.4 22.0 %all-gather.1 = bf16[64,48,128]{2,1,0:T(8,128)(2,1)S(1)} all-gather(bf16[4,48,128]{2,1,0:T(8,128)(2,1)S(1)} %bitcast.125), channel_id=3, replica_groups=mesh['zh'=4,'y'=8,'core'=2,'x'=4,'zl'=2] {'y','core'}, dimensions={0}, use_global_device_ids=true | all-gather | bytes 835584 | tf_op jit(solution)/shard_map/all_gather | solution.py:144
  99.4 1.8 %fusion.37.kv = bf16[128,128]{1,0:T(8,128)(2,1)S(1)} fusion(bf16[8,2,4,48,128]{4,3,2,1,0:T(8,128)(2,1)S(1)} %bitcast.108, bf16[8,4,2,45,128]{4,3,2,1,0:T(8,128)(2,1)} %bitcast.105), kind=kOutput, calls=%fused_computation.39 | convolution fusion | flops 100679680 | bytes 1556480 | tf_op jit(solution)/shard_map/dot_general | solution.py:32
  101.3 1.9 %collective-permute-start = (bf16[128,128]{1,0:T(8,128)(2,1)S(1)}, bf16[128,128]{1,0:T(8,128)(2,1)S(1)}, u32[]{:S(2)}, u32[]{:S(2)}) collective-permute-start(bf16[128,128]{1,0:T(8,128)(2,1)S(1)} %fusion.37.kv), channel_id=1, source_target_pairs={{0,8},{8,16},{16,24},{24,32},{32,40},{40,48},{48,56},{56,64},{64,7... | collective-permute-start | bytes 98312 | tf_op jit(solution)/shard_map/ppermute | solution.py:22
  104.0 2.1 %copy.27 = bf16[8,2,4,48,128]{4,3,1,2,0:T(8,128)(2,1)} copy(bf16[8,2,4,48,128]{4,3,2,1,0:T(8,128)(2,1)} %bitcast.109) | data formatting | bytes 1572864 | tf_op jit(solution)/shard_map/reshape | solution.py:145
  106.1 2.5 %collective-permute-start.2 = (bf16[3072,512]{1,0:T(8,128)(2,1)}, bf16[3072,512]{1,0:T(8,128)(2,1)S(1)}, u32[]{:S(2)}, u32[]{:S(2)}) collective-permute-start(bf16[3072,512]{1,0:T(8,128)(2,1)} %bitcast.113), channel_id=1, source_target_pairs={{0,8},{8,0},{1,9},{9,1},{2,10},{10,2},{3,11},{11,3},{4,12},{12,4},... | collective-permute-start | bytes 9437192 | tf_op jit(solution)/shard_map/ppermute | solution.py:181
  108.6 2.2 %fusion.27.q_own = bf16[256,128]{1,0:T(8,128)(2,1)S(1)} fusion(bf16[3072,128]{1,0:T(8,128)(2,1)} %bitcast.121, bf16[3072,512]{1,0:T(8,128)(2,1)} %bitcast.114), kind=kOutput, calls=%fused_computation.34 | convolution fusion | flops 201359360 | bytes 2424832 | tf_op jit(solution)/shard_map/dot_general | solution.py:32
  110.9 2.1 %fusion.24.g_own = bf16[256,128]{1,0:T(8,128)(2,1)S(1)} fusion(bf16[3072,128]{1,0:T(8,128)(2,1)S(1)} %bitcast.119, bf16[3072,512]{1,0:T(8,128)(2,1)} %bitcast.115), kind=kOutput, calls=%fused_computation.33 | convolution fusion | flops 201359360 | bytes 2424832 | tf_op jit(solution)/shard_map/dot_general | solution.py:32
  113.0 1.1 collective-permute-done.2
  114.7 2.2 %shard_map.130 = (bf16[512,128]{1,0:T(8,128)(2,1)S(1)}, f32[8,256,128]{2,1,0:T(8,128)S(1)}) custom-call(bf16[256,128]{1,0:T(8,128)(2,1)S(1)} %fusion.27.q_own, bf16[256,128]{1,0:T(8,128)(2,1)S(1)} %fusion.33.q_oth, bf16[128,128]{1,0:T(8,128)(2,1)S(1)} %fusion.37.kv, bf16[128,128]{1,0:T(8,128)(2,1)S(1)} %collective-permute-done.halo, f32[256,128]{1,0:T(8,128)S(1)} %fusion.49.mask), custom_call_target="tpu_custom_call" | custom-call | flops 100000000 | bytes 1507328 | tf_op jit(solution)/shard_map/pallas_call | solution.py:107
  117.5 1.3 copy-done.8
  119.4 1.0 copy.31
  121.9 2.3 %collective-permute-start.3 = (bf16[128,128]{1,0:T(8,128)(2,1)S(1)}, bf16[128,128]{1,0:T(8,128)(2,1)S(1)}, u32[]{:S(2)}, u32[]{:S(2)}) collective-permute-start(bf16[128,128]{1,0:T(8,128)(2,1)S(1)} %get-tuple-element.38), channel_id=1, source_target_pairs={{8,0},{16,8},{24,16},{32,24},{40,32},{48,40},{56,48},{64,56},{72,6... | collective-permute-start | bytes 98312 | tf_op jit(solution)/shard_map/ppermute | solution.py:22
  124.2 4.4 %all-to-all-start.3 = ((bf16[8,384,128]{2,1,0:T(8,128)(2,1)}), bf16[8,384,128]{2,1,0:T(8,128)(2,1)}, u32[]{:S(2)}, u32[]{:S(2)}) async-start(bf16[8,384,128]{2,1,0:T(8,128)(2,1)} %bitcast.107), calls=%async_computation.3 | async-start | bytes 1572864 | tf_op jit(solution)/shard_map/all_to_all | solution.py:195
  128.6 2.1 %fusion.9 = f32[3072,128]{1,0:T(8,128)S(1)} fusion(bf16[3072,512]{1,0:T(8,128)(2,1)} %copy-done.4, bf16[512,128]{1,0:T(8,128)(2,1)S(1)} %get-tuple-element.35), kind=kOutput, calls=%fused_computation.15 | convolution fusion | flops 201326592 | bytes 3211264 | tf_op jit(solution)/shard_map/dot_general | solution.py:32
  132.4 0.9 pad_maximum_fusion
  133.3 8.5 %all-to-all-done.3 = bf16[8,384,128]{2,1,0:T(8,128)(2,1)} async-done(((bf16[8,384,128]{2,1,0:T(8,128)(2,1)}), bf16[8,384,128]{2,1,0:T(8,128)(2,1)}, u32[]{:S(2)}, u32[]{:S(2)}) %all-to-all-start.3) | async-done | bytes 786464 | tf_op jit(solution)/shard_map/all_to_all | solution.py:195
  141.8 3.5 %all-to-all-start.4 = ((bf16[8,400,128]{2,1,0:T(8,128)(2,1)}), bf16[8,400,128]{2,1,0:T(8,128)(2,1)S(1)}, u32[]{:S(2)}, u32[]{:S(2)}) async-start(bf16[8,400,128]{2,1,0:T(8,128)(2,1)} %pad_maximum_fusion), calls=%async_computation.4 | async-start | bytes 1638400 | tf_op jit(solution)/shard_map/all_to_all | solution.py:216
  146.5 1.3 convert_reduce_fusion.1
  147.8 1.0 fusion.36
  148.8 9.5 %all-to-all-done.4 = bf16[8,400,128]{2,1,0:T(8,128)(2,1)S(1)} async-done(((bf16[8,400,128]{2,1,0:T(8,128)(2,1)}), bf16[8,400,128]{2,1,0:T(8,128)(2,1)S(1)}, u32[]{:S(2)}, u32[]{:S(2)}) %all-to-all-start.4) | async-done | bytes 819232 | tf_op jit(solution)/shard_map/all_to_all | solution.py:216
  (108 shorter events, 13.8 us)
Async XLA Ops:
  7.2 139.1 %copy-start = (bf16[16,2880]{1,0:T(8,128)(2,1)S(1)}, bf16[16,2880]{1,0:T(8,128)(2,1)}, u32[]{:S(2)}) copy-start(bf16[16,2880]{1,0:T(8,128)(2,1)} %param.18) | copy-start | bytes 276484
  7.2 28.0 %copy-start.1 = (bf16[128,2880]{0,1:T(8,128)(2,1)S(1)}, bf16[128,2880]{0,1:T(8,128)(2,1)}, u32[]{:S(2)}) copy-start(bf16[128,2880]{0,1:T(8,128)(2,1)} %param.11) | copy-start | bytes 2211844
  7.2 28.4 %copy-start.12 = (f32[2880]{0:T(1024)S(1)}, f32[2880]{0:T(1024)}, u32[]{:S(2)}) copy-start(f32[2880]{0:T(1024)} %param.12) | copy-start | bytes 34564
  7.2 28.4 %copy-start.13 = (f32[2880]{0:T(1024)S(1)}, f32[2880]{0:T(1024)}, u32[]{:S(2)}) copy-start(f32[2880]{0:T(1024)} %param.17) | copy-start | bytes 34564
  7.2 98.9 %all-gather.4.cloned.1.call-start = ((), (), s32[]{:S(2)}) async-start(), calls=%async_computation.5 | async-start | bytes 3538944 | tf_op jit(solution)/shard_map/all_gather | solution.py:140
  8.2 29.4 %copy-start.3 = (bf16[128,2880]{0,1:T(8,128)(2,1)S(1)}, bf16[128,2880]{0,1:T(8,128)(2,1)}, u32[]{:S(2)}) copy-start(bf16[128,2880]{0,1:T(8,128)(2,1)} %param.21) | copy-start | bytes 2211844
  8.2 29.4 %copy-start.16 = (s32[128]{0:T(128)S(1)}, s32[128]{0:T(128)}, u32[]{:S(2)}) copy-start(s32[128]{0:T(128)} %param.20) | copy-start | bytes 1540
  35.1 7.3 %copy-start.20 = (s32[128]{0:T(128)S(1)}, s32[128]{0:T(128)}, u32[]{:S(2)}) copy-start(s32[128]{0:T(128)} %param.19) | copy-start | bytes 1540
  37.6 9.3 %copy-start.22 = (f32[128]{0:T(128)}, f32[128]{0:T(128)S(1)}, u32[]{:S(2)}) copy-start(f32[128]{0:T(128)S(1)} %add_divide_fusion) | copy-start | bytes 1540
  38.6 18.4 %all-to-all-start.1 = ((f32[8,16,360]{2,1,0:T(8,128)}), f32[8,16,360]{2,1,0:T(8,128)S(1)}, u32[]{:S(2)}, u32[]{:S(2)}) async-start(f32[8,16,360]{2,1,0:T(8,128)} %broadcast_in_dim.14), calls=%async_computation.1 | async-start | bytes 393216 | tf_op jit(solution)/shard_map/all_to_all | solution.py:28
  42.5 13.9 %collective-permute-start.1 = (s32[128]{0:T(128)S(1)}, s32[128]{0:T(128)S(1)}, u32[]{:S(2)}, u32[]{:S(2)}) collective-permute-start(s32[128]{0:T(128)S(1)} %copy-done.20), channel_id=1, source_target_pairs={{0,8},{8,16},{16,24},{24,32},{32,40},{40,48},{48,56},{56,64},{64,7... | collective-permute-start | bytes 1544 | tf_op jit(solution)/shard_map/ppermute | solution.py:22
  51.3 1.9 %copy-start.14 = (bf16[45,64]{1,0:T(8,128)(2,1)S(1)}, bf16[45,64]{1,0:T(8,128)(2,1)}, u32[]{:S(2)}) copy-start(bf16[45,64]{1,0:T(8,128)(2,1)} %param.15) | copy-start | bytes 17284
  51.3 1.9 %copy-start.15 = (bf16[45,64]{1,0:T(8,128)(2,1)S(1)}, bf16[45,64]{1,0:T(8,128)(2,1)}, u32[]{:S(2)}) copy-start(bf16[45,64]{1,0:T(8,128)(2,1)} %param.14) | copy-start | bytes 17284
  54.2 2.0 %copy-start.2 = (f32[8,4,2,45,128]{4,3,2,1,0:T(8,128)S(1)}, f32[8,4,2,45,128]{4,3,2,1,0:T(8,128)}, u32[]{:S(2)}) copy-start(f32[8,4,2,45,128]{4,3,2,1,0:T(8,128)} %copy.35) | copy-start | bytes 4423684
  57.7 45.7 %all-to-all-start.2 = ((f32[8,16,360]{2,1,0:T(8,128)}), f32[8,16,360]{2,1,0:T(8,128)S(1)}, u32[]{:S(2)}, u32[]{:S(2)}) async-start(f32[8,16,360]{2,1,0:T(8,128)} %broadcast_in_dim.15), calls=%async_computation.2 | async-start | bytes 393216 | tf_op jit(solution)/shard_map/all_to_all | solution.py:28
  77.4 25.8 %copy-start.17 = (s32[256]{0:T(256)S(1)}, s32[256]{0:T(256)}, u32[]{:S(2)}) copy-start(s32[256]{0:T(256)} %pad_add_fusion) | copy-start | bytes 3076
  77.4 25.8 %copy-start.21 = (s32[128]{0:T(128)S(1)}, s32[128]{0:T(128)}, u32[]{:S(2)}) copy-start(s32[128]{0:T(128)} %param.19) | copy-start | bytes 1540
  77.4 25.8 %copy-start.25 = (s32[256]{0:T(256)S(1)}, s32[256]{0:T(256)}, u32[]{:S(2)}) copy-start(s32[256]{0:T(256)} %iota_add_fusion) | copy-start | bytes 3076
  101.3 4.8 %collective-permute-start = (bf16[128,128]{1,0:T(8,128)(2,1)S(1)}, bf16[128,128]{1,0:T(8,128)(2,1)S(1)}, u32[]{:S(2)}, u32[]{:S(2)}) collective-permute-start(bf16[128,128]{1,0:T(8,128)(2,1)S(1)} %fusion.37.kv), channel_id=1, source_target_pairs={{0,8},{8,16},{16,24},{24,32},{32,40},{40,48},{48,56},{56,64},{64,7... | collective-permute-start | bytes 98312 | tf_op jit(solution)/shard_map/ppermute | solution.py:22
  106.1 4.8 %copy-start.10 = (bf16[8,4,2,48,128]{4,3,2,1,0:T(8,128)(2,1)S(1)}, bf16[8,4,2,48,128]{4,3,2,1,0:T(8,128)(2,1)}, u32[]{:S(2)}) copy-start(bf16[8,4,2,48,128]{4,3,2,1,0:T(8,128)(2,1)} %pad.30.clone) | copy-start | bytes 2359300
  106.1 8.0 %collective-permute-start.2 = (bf16[3072,512]{1,0:T(8,128)(2,1)}, bf16[3072,512]{1,0:T(8,128)(2,1)S(1)}, u32[]{:S(2)}, u32[]{:S(2)}) collective-permute-start(bf16[3072,512]{1,0:T(8,128)(2,1)} %bitcast.113), channel_id=1, source_target_pairs={{0,8},{8,0},{1,9},{9,1},{2,10},{10,2},{3,11},{11,3},{4,12},{12,4},... | collective-permute-start | bytes 9437192 | tf_op jit(solution)/shard_map/ppermute | solution.py:181
  110.9 3.2 %copy-start.11 = (bf16[8,4,2,48,128]{4,3,2,1,0:T(8,128)(2,1)S(1)}, bf16[8,4,2,48,128]{4,3,2,1,0:T(8,128)(2,1)}, u32[]{:S(2)}) copy-start(bf16[8,4,2,48,128]{4,3,2,1,0:T(8,128)(2,1)} %pad.29) | copy-start | bytes 2359300
  114.1 6.3 %copy-start.4 = (bf16[3072,512]{1,0:T(8,128)(2,1)}, bf16[3072,512]{1,0:T(8,128)(2,1)S(1)}, u32[]{:S(2)}) copy-start(bf16[3072,512]{1,0:T(8,128)(2,1)S(1)} %collective-permute-done.2) | copy-start | bytes 9437188
  116.9 1.9 %copy-start.8 = (bf16[64,48,512]{2,1,0:T(8,128)(2,1)S(1)}, bf16[64,48,512]{2,1,0:T(8,128)(2,1)}, u32[]{:S(2)}) copy-start(bf16[64,48,512]{2,1,0:T(8,128)(2,1)} %all-gather.4.cloned.1.call-done) | copy-start | bytes 9437188
  121.9 8.8 %collective-permute-start.3 = (bf16[128,128]{1,0:T(8,128)(2,1)S(1)}, bf16[128,128]{1,0:T(8,128)(2,1)S(1)}, u32[]{:S(2)}, u32[]{:S(2)}) collective-permute-start(bf16[128,128]{1,0:T(8,128)(2,1)S(1)} %get-tuple-element.38), channel_id=1, source_target_pairs={{8,0},{16,8},{24,16},{32,24},{40,32},{48,40},{56,48},{64,56},{72,6... | collective-permute-start | bytes 98312 | tf_op jit(solution)/shard_map/ppermute | solution.py:22
  124.2 17.6 %all-to-all-start.3 = ((bf16[8,384,128]{2,1,0:T(8,128)(2,1)}), bf16[8,384,128]{2,1,0:T(8,128)(2,1)}, u32[]{:S(2)}, u32[]{:S(2)}) async-start(bf16[8,384,128]{2,1,0:T(8,128)(2,1)} %bitcast.107), calls=%async_computation.3 | async-start | bytes 1572864 | tf_op jit(solution)/shard_map/all_to_all | solution.py:195
  128.6 2.2 %copy-start.7 = (bf16[8,2,4,48,128]{4,3,1,2,0:T(8,128)(2,1)S(1)}, bf16[8,2,4,48,128]{4,3,1,2,0:T(8,128)(2,1)}, u32[]{:S(2)}) copy-start(bf16[8,2,4,48,128]{4,3,1,2,0:T(8,128)(2,1)} %copy.27) | copy-start | bytes 2359300
  128.6 2.6 %copy-start.9 = (bf16[64,48,512]{2,1,0:T(8,128)(2,1)S(1)}, bf16[64,48,512]{2,1,0:T(8,128)(2,1)}, u32[]{:S(2)}) copy-start(bf16[64,48,512]{2,1,0:T(8,128)(2,1)} %all-gather.4.cloned.1.call-done) | copy-start | bytes 9437188
  133.3 14.5 %copy-start.23 = (f32[128]{0:T(128)S(1)}, f32[128]{0:T(128)}, u32[]{:S(2)}) copy-start(f32[128]{0:T(128)} %copy-done.22) | copy-start | bytes 1540
  141.8 16.4 %all-to-all-start.4 = ((bf16[8,400,128]{2,1,0:T(8,128)(2,1)}), bf16[8,400,128]{2,1,0:T(8,128)(2,1)S(1)}, u32[]{:S(2)}, u32[]{:S(2)}) async-start(bf16[8,400,128]{2,1,0:T(8,128)(2,1)} %pad_maximum_fusion), calls=%async_computation.4 | async-start | bytes 1638400 | tf_op jit(solution)/shard_map/all_to_all | solution.py:216
  146.5 11.9 %copy-start.19 = (f32[128]{0:T(128)S(1)}, f32[128]{0:T(128)}, u32[]{:S(2)}) copy-start(f32[128]{0:T(128)} %copy-done.18) | copy-start | bytes 1540
  146.5 11.9 %copy-start.24 = (f32[128]{0:T(128)S(1)}, f32[128]{0:T(128)}, u32[]{:S(2)}) copy-start(f32[128]{0:T(128)} %get-tuple-element.45) | copy-start | bytes 1540
  (3 other events, 3.9 us)
Sparse Core Ops, SparseCore 0:
  35.2 47.2 all-gather.3

commit v3 on v2

v3 whole, which is shorter than its diff:
```python
import jax
import jax.numpy as jnp
from jax import lax
from jax.experimental import pallas as pl
from jax.experimental.pallas import tpu as pltpu
from jax.sharding import Mesh, PartitionSpec as P

HD = 64
WIN = 128
EPSILON = 1e-05
HIGHEST = lax.Precision.HIGHEST
SEQ = ("zh", "y", "core")
HEAD = ("x", "zl")
F32 = jnp.float32
BF16 = jnp.bfloat16
PAD = 48


def shifted(value, by):
    count = lax.axis_size(SEQ)
    pairs = [(i, i + by) for i in range(count) if 0 <= i + by < count]
    return lax.ppermute(value, SEQ, pairs)


def gathered(value, axes):
    count = lax.axis_size(axes)
    spread = jnp.broadcast_to(value[None], (count,) + value.shape)
    return lax.all_to_all(spread, axes, 0, 0)


def dot(left, right, dims, **kw):
    return lax.dot_general(left, right, (dims, ((), ())), preferred_element_type=F32, **kw)


def blocked(rows):
    width = rows.shape[-1]
    parts = rows.reshape(4, 8, 2, -1, width).transpose(1, 0, 2, 3, 4)
    parts = jnp.pad(parts, ((0, 0), (0, 0), (0, 0), (0, PAD - parts.shape[3]), (0, 0)))
    return parts.reshape(-1, width)


def unpadded(rows, row_count):
    width = rows.shape[-1]
    return rows.reshape(8, PAD, width)[:, : row_count // 8].reshape(row_count, width)


def mm(left, right, left_dim, right_dim):
    dims = (((left_dim,), (right_dim,)), ((), ()))
    return lax.dot_general(left, right, dims, preferred_element_type=F32)


def own_kernel(weight, normed, grads, query, grad):
    half = weight.shape[1] // 2
    query[...] = mm(weight[:, :half], normed[...], 0, 0).astype(BF16)
    grad[...] = mm(weight[:, half:], grads[...], 0, 0).astype(BF16)


def attend_kernel(
    oth, normed, grads, q_own, g_own, kv, halo, mask, mixed, grad_query, grad_halo, grad_kv
):
    half = oth.shape[1] // 2
    q_oth = mm(oth[:, :half], normed[...], 0, 0).astype(BF16)
    g_oth = mm(oth[:, half:], grads[...], 0, 0).astype(BF16)
    keys = jnp.concatenate([halo[:HD, :], kv[:HD, :]], axis=1)
    values = jnp.concatenate([halo[HD:, :], kv[HD:, :]], axis=1)
    allowed = mask[...] > 0.0
    grad_keys = jnp.zeros(keys.shape, F32)
    grad_values = jnp.zeros(keys.shape, F32)
    for head in range(8):
        low = head % 4 * HD
        rows = pl.ds(head * HD, HD)
        query = q_own[low : low + HD, :] if head < 4 else q_oth[low : low + HD]
        grad = g_own[low : low + HD, :] if head < 4 else g_oth[low : low + HD]
        scores = mm(keys, query, 0, 0) * HD**-0.5
        scores = jnp.where(allowed, scores, -jnp.inf)
        raised = jnp.exp(scores - jnp.max(scores, axis=0, keepdims=True))
        prob = raised / jnp.sum(raised, axis=0, keepdims=True)
        prob_b = prob.astype(BF16)
        mixed[rows, :] = mm(values, prob_b, 1, 0).astype(BF16)
        grad_values += mm(grad, prob_b, 1, 1)
        grad_prob = mm(values, grad, 0, 0)
        delta = jnp.sum(prob * grad_prob, axis=0, keepdims=True)
        grad_scores = (prob * (grad_prob - delta) * HD**-0.5).astype(BF16)
        grad_query[rows, :] = mm(keys, grad_scores, 1, 0).astype(BF16)
        grad_keys += mm(query, grad_scores, 1, 1)
    grad_halo[:HD, :] = grad_keys[:, :WIN].astype(BF16)
    grad_halo[HD:, :] = grad_values[:, :WIN].astype(BF16)
    grad_kv[:HD, :] = grad_keys[:, WIN:]
    grad_kv[HD:, :] = grad_values[:, WIN:]


def chunks():
    for group in range(8):
        for part in range(4):
            row = ((group % 2 * 4 + part) * 4 + group // 2) * 2 * PAD
            yield group, part * 2 * PAD, row


def out_kernel(own, oth, mixed, blocks):
    half = own.shape[1] // 2
    for group, place, row in chunks():
        term = mm(own[row : row + 2 * PAD, half:], mixed[:half, :], 1, 0)
        term = term + mm(oth[row : row + 2 * PAD, half:], mixed[half:, :], 1, 0)
        blocks[group, place : place + 2 * PAD, :] = term.astype(BF16)


def back_kernel(own, oth, kv_all, normed, grad_query, grad_kv, returned, blocks):
    half = own.shape[1] // 2
    tokens_here = grad_kv.shape[1]
    kv_grad = (grad_kv[...] + returned[...].astype(F32)).astype(BF16)
    rows = jnp.zeros((2 * PAD, tokens_here), F32)
    for group, place, row in chunks():
        term = mm(own[row : row + 2 * PAD, :half], grad_query[:half, :], 1, 0)
        term = term + mm(oth[row : row + 2 * PAD, :half], grad_query[half:, :], 1, 0)
        term = term + mm(kv_all[row : row + 2 * PAD, :], kv_grad, 1, 0)
        term = term.astype(BF16)
        blocks[group, place : place + 2 * PAD, :] = term
        rows += term.astype(F32) * normed[row : row + 2 * PAD, :].astype(F32)
    total = jnp.sum(rows, axis=0, keepdims=True)
    high = total.astype(BF16).astype(F32)
    mid = (total - high).astype(BF16).astype(F32)
    low = total - high - mid
    line = lax.broadcasted_iota(jnp.int32, (16, tokens_here), 0)
    extra = jnp.where(line == 0, high, jnp.where(line == 1, mid, jnp.where(line == 2, low, 0.0)))
    for group in range(8):
        blocks[group, 8 * PAD :, :] = extra.astype(BF16)


def call(kernel, outs, *args):
    size = sum(a.size * a.dtype.itemsize for a in jax.tree.leaves((args, outs)))
    return pl.pallas_call(
        kernel,
        out_shape=outs,
        compiler_params=pltpu.CompilerParams(vmem_limit_bytes=40 * 2**20),
        cost_estimate=pl.CostEstimate(flops=10**8, bytes_accessed=size, transcendentals=0),
    )(*args)


def shards(
    tokens,
    gain,
    w_query,
    w_key,
    w_value,
    w_out,
    w_gate,
    steering,
    segment_ids,
    steer_index,
    grad_out,
):
    row_count, model_width = tokens.shape
    share = model_width // 8
    start = lax.axis_index(HEAD) * share

    padded = lambda w: jnp.pad(w, ((0, PAD - w.shape[0]), (0, 0)))
    half = w_query.shape[1] // 2
    query_w, out_w = padded(w_query), padded(w_out)
    w_kv = padded(jnp.concatenate([w_key, w_value], axis=1))
    w_kv = w_kv.reshape(2, 6, 4 * 2 * HD)

    def pair(c):
        columns = slice(c * half, (c + 1) * half)
        wide = jnp.concatenate([query_w[:, columns], out_w[:, columns]], axis=1)
        return jnp.concatenate([wide, w_kv[c], jnp.zeros((2, 2 * half), BF16)], axis=0)

    sent = jnp.stack([pair(0), pair(1)] * 4)
    near = lax.all_to_all(sent, ("zh", "core"), 0, 0)
    own = lax.all_gather(near[:, :PAD], "y", axis=0, tiled=True).reshape(-1, 2 * half)
    kv_near = near[:, PAD : PAD + 6].reshape(8, PAD // 2, 2 * HD)
    kv_near = lax.all_gather(kv_near, "y", axis=0, tiled=True)
    kv_all = lax.all_gather(kv_near, "core", axis=1, tiled=True).reshape(-1, 2 * HD)

    tok = tokens.T.astype(F32)
    inverse = lax.rsqrt(jnp.mean(tok * tok, axis=0, keepdims=True) + EPSILON)
    unit = tok * inverse
    normed = (unit * gain[:, None]).astype(BF16)
    normed_b = blocked(normed)
    grad_t = grad_out.T
    grad_b = blocked(grad_t)
    gate = jax.nn.sigmoid(jnp.sum(normed.astype(F32) * w_gate[:, None], axis=0))
    one_hot = steer_index[None, :] == lax.broadcasted_iota(jnp.int32, (16, row_count), 0)
    products = dot(steering, grad_t, ((1,), (0,)))
    grad_logit = gate * (1.0 - gate) * jnp.sum(jnp.where(one_hot, products, 0.0), axis=0)
    steer_share = lax.dynamic_slice_in_dim(steering, start, share, 1)
    steer_rows = dot(steer_share, one_hot.astype(BF16), ((0,), (0,)))
    grad_share = lax.dynamic_slice_in_dim(grad_t, start, share, 0).astype(F32)
    steer_part = dot(
        one_hot.astype(F32), gate[None, :] * grad_share, ((1,), (1,)), precision=HIGHEST
    )
    steer_near = jnp.sum(gathered(steer_part, ("zh", "core")), axis=0)
    steer_grad = jnp.sum(gathered(steer_near, ("y",)), axis=0)

    halo_seg = shifted(segment_ids, 1)
    halo_seg = jnp.where(lax.axis_index(SEQ) > 0, halo_seg, -1)
    kv = dot(kv_all, normed_b, ((0,), (0,))).astype(BF16)
    halo = shifted(kv, 1)
    wide_seg = jnp.concatenate([halo_seg, segment_ids])
    key_pos = lax.broadcasted_iota(jnp.int32, (2 * row_count, row_count), 0) - WIN
    query_pos = lax.broadcasted_iota(jnp.int32, (2 * row_count, row_count), 1)
    distance = query_pos - key_pos
    mask = (distance >= 0) & (distance < WIN) & (wide_seg[:, None] == segment_ids[None, :])
    mask = mask.astype(F32)
    own, halo, mask, steer_grad, normed_b, grad_b, kv, kv_all = lax.optimization_barrier(
        (own, halo, mask, steer_grad, normed_b, grad_b, kv, kv_all)
    )
    oth = lax.ppermute(own, "core", [(0, 1), (1, 0)])
    like = jax.ShapeDtypeStruct
    thin = like((half, row_count), BF16)
    q_own, g_own = call(own_kernel, (thin, thin), own, normed_b, grad_b)
    mixed, grad_query, grad_halo, grad_kv = call(
        attend_kernel,
        (
            like((2 * half, row_count), BF16),
            like((2 * half, row_count), BF16),
            like((2 * HD, row_count), BF16),
            like((2 * HD, row_count), F32),
        ),
        *(oth, normed_b, grad_b, q_own, g_own, kv, halo, mask),
    )
    returned = shifted(grad_halo, -1)
    blocks = call(out_kernel, like((8, 8 * PAD, row_count), BF16), own, oth, mixed)
    attn = lax.all_to_all(blocks, HEAD, 0, 0)
    blocks, grad_query = lax.optimization_barrier((blocks, grad_query))
    back = call(
        back_kernel,
        like((8, 8 * PAD + 16, row_count), BF16),
        *(own, oth, kv_all, normed_b, grad_query, grad_kv, returned),
    )
    back = lax.all_to_all(back, HEAD, 0, 0)

    attn_share = unpadded(jnp.sum(attn.astype(F32), axis=0), share)
    token_share = lax.dynamic_slice_in_dim(tokens.T, start, share, 0).astype(F32)
    layer_out = (token_share + attn_share + gate[None, :] * steer_rows).astype(BF16)
    back = jnp.sum(back.astype(F32), axis=0)
    gain_share = lax.dynamic_slice_in_dim(gain, start, share, 0)[:, None]
    gate_share = lax.dynamic_slice_in_dim(w_gate, start, share, 0)[:, None]
    total = unpadded(back[: 8 * PAD], share) + grad_logit[None, :] * gate_share
    gate_total = jnp.sum(unit * (gain * w_gate)[:, None], axis=0)
    row_total = jnp.sum(back[8 * PAD : 8 * PAD + 3], axis=0) + grad_logit * gate_total
    unit_share = token_share * inverse
    scaled = total * gain_share
    grad_tokens = (
        grad_share + inverse * (scaled - unit_share * (row_total / model_width)[None, :])
    ).astype(BF16)
    return (layer_out.T, grad_tokens.T, steer_grad)


def solution(mesh):
    split = Mesh(mesh.devices.reshape(4, 8, 2, 4, 2), SEQ + HEAD)
    placed = (
        P(SEQ, None),
        P(),
        P(SEQ, HEAD),
        P(SEQ, HEAD),
        P(SEQ, HEAD),
        P(SEQ, HEAD),
        P(),
        P(),
        P(SEQ),
        P(SEQ),
        P(SEQ, None),
    )
    return jax.shard_map(
        shards,
        mesh=split,
        in_specs=placed,
        out_specs=(P(SEQ, HEAD), P(SEQ, HEAD), P(None, HEAD)),
        check_vma=False,
    )
```

time: 167 us -> 167 us (level)
  matrix products: 12.9 us -> 1.81 us
  starting transfers between devices: 27.7 us -> 34.9 us
  Pallas kernels: 3.05 us -> 7.84 us
  other arithmetic: 11.2 us -> 7.63 us
  local copies, waits for them, and re-layouts: 14.8 us -> 18.3 us
  blocking collectives: 62.7 us -> 59.4 us
  waiting for transfers between devices: 19.2 us -> 21.7 us
    dot_general x13 -> x4, matrix products: 12.9 us -> 1.81 us  [dot(): lax.dot_general(left, right, (dims, ((), ())), preferred_element_type=F32...]
    unnamed x54 -> x68, local copies, waits for them, and re-layouts: 3.42 us -> 14.3 us
    all_to_all x1, waiting for transfers between devices: 8.54 us -> 0.01 us  [shards(): attn = lax.all_to_all(blocks, HEAD, 0, 0)]
    pallas_call x2 -> x4, Pallas kernels: 3.05 us -> 7.84 us  [call(): pl.pallas_call(kernel, out_shape=outs, compiler_params=pltpu.CompilerPara...]
    all_to_all x2, waiting for transfers between devices: 0.01 us -> 4.52 us  [gathered(): return lax.all_to_all(spread, axes, 0, 0)]
    ppermute x3, waiting for transfers between devices: 0.01 us -> 4.37 us  [shifted(): return lax.ppermute(value, SEQ, pairs)]
    all_to_all x2, starting transfers between devices: 9.79 us -> 13.7 us  [gathered(): return lax.all_to_all(spread, axes, 0, 0)]
    reshape x3 -> x1, local copies, waits for them, and re-layouts: 3.18 us -> 0.04 us  [shards(): kv_near = near[:, PAD:PAD + 6].reshape(8, PAD // 2, 2 * HD)]
  transfers between devices with their start and end apart: 9 -> 9, of which waited for: 3 -> 5; matrix products, arithmetic and copies ran while one was open for 19% -> 5% of each run, Pallas kernels for 0% -> 1%
where the time goes in v3:
time: 167 us; the launch traced here: 166 us
  blocking collectives  59.4 us (36%)
  starting transfers between devices  34.9 us (21%)
  waiting for transfers between devices  21.7 us (13%)
  local copies, waits for them, and re-layouts  18.3 us (11%)
  between operations  14.6 us (9%)
  Pallas kernels  7.84 us (5%)
  other arithmetic  7.63 us (5%)
  matrix products  1.81 us (1%)
    all_gather x1, blocking collectives, shards(): kv_near = lax.all_gather(kv_near, 'y', axis=0, tiled=True)  26 us
    all_to_all x1, blocking collectives, shards(): near = lax.all_to_all(sent, ('zh', 'core'), 0, 0)  25 us
    unnamed x68, local copies, waits for them, and re-layouts  14.3 us
    all_to_all x2, starting transfers between devices, gathered(): return lax.all_to_all(spread, axes, 0, 0)  13.7 us
    all_to_all x1, waiting for transfers between devices, shards(): back = lax.all_to_all(back, HEAD, 0, 0)  9.93 us
    ppermute x3, starting transfers between devices, shifted(): return lax.ppermute(value, SEQ, pairs)  8.95 us
    all_gather x1, blocking collectives, shards(): lax.all_gather(kv_near, 'core', axis=1, tiled=True).reshape(-1, 2 * HD)  8.36 us
    pallas_call x4, Pallas kernels, call(): pl.pallas_call(kernel, out_shape=outs, compiler_params=pltpu.CompilerPara...  7.84 us
  transfers between devices with their start and end apart: 9, of which 5 were waited for; matrix products, arithmetic and copies ran while one was open for 5% of the time, Pallas kernels for 1%

profile of v3, /device:TPU:1, one launch (start us, length us, event | category | flops | bytes accessed | tf_op | source)
XLA Modules:
  0.0 166.2 jit_solution(1527963110535738008)
XLA Ops:
  10.5 25.0 %all_to_all.25 = bf16[8,56,512]{2,1,0:T(8,128)(2,1)S(1)} all-to-all(bf16[8,56,512]{2,1,0:T(8,128)(2,1)S(1)} %constant_dynamic-update-slice_fusion), channel_id=1, replica_groups=mesh['zh'=4,'y'=8,'core'=2,'x'=4,'zl'=2] {'zh','core'}, dimensions={0} | all-to-all | bytes 917504 | tf_op jit(solution)/shard_map/all_to_all | solution.py:168
  36.8 1.5 multiply_reduce_fusion
  39.8 6.9 %all-to-all-start.1 = ((f32[8,16,360]{2,1,0:T(8,128)}), f32[8,16,360]{2,1,0:T(8,128)S(1)}, u32[]{:S(2)}, u32[]{:S(2)}) async-start(f32[8,16,360]{2,1,0:T(8,128)} %broadcast_in_dim.12), calls=%async_computation.1 | async-start | bytes 393216 | tf_op jit(solution)/shard_map/all_to_all | solution.py:28
  46.7 3.2 %collective-permute-start.1 = (s32[128]{0:T(128)S(1)}, s32[128]{0:T(128)S(1)}, u32[]{:S(2)}, u32[]{:S(2)}) collective-permute-start(s32[128]{0:T(128)S(1)} %copy-done.30), channel_id=1, source_target_pairs={{0,8},{8,16},{16,24},{24,32},{32,40},{40,48},{48,56},{56,64},{64,7... | collective-permute-start | bytes 1544 | tf_op jit(solution)/shard_map/ppermute | solution.py:22
  50.8 4.5 %all-to-all-done.1 = f32[8,16,360]{2,1,0:T(8,128)S(1)} async-done(((f32[8,16,360]{2,1,0:T(8,128)}), f32[8,16,360]{2,1,0:T(8,128)S(1)}, u32[]{:S(2)}, u32[]{:S(2)}) %all-to-all-start.1) | async-done | bytes 184352 | tf_op jit(solution)/shard_map/all_to_all | solution.py:28
  56.1 6.8 %all-to-all-start.2 = ((f32[8,16,360]{2,1,0:T(8,128)}), f32[8,16,360]{2,1,0:T(8,128)S(1)}, u32[]{:S(2)}, u32[]{:S(2)}) async-start(f32[8,16,360]{2,1,0:T(8,128)} %broadcast_in_dim.13), calls=%async_computation.2 | async-start | bytes 393216 | tf_op jit(solution)/shard_map/all_to_all | solution.py:28
  63.0 26.0 %all_gather.10 = bf16[64,24,128]{2,1,0:T(8,128)(2,1)S(1)} all-gather(bf16[8,24,128]{2,1,0:T(8,128)(2,1)S(1)} %reshape.87), channel_id=1, replica_groups=mesh['zh'=4,'y'=8,'core'=2,'x'=4,'zl'=2] {'y'}, dimensions={0}, use_global_device_ids=true | all-gather | bytes 442368 | tf_op jit(solution)/shard_map/all_gather | solution.py:171
  88.9 8.4 %all_gather.11 = bf16[64,48,128]{2,1,0:T(8,128)(2,1)S(1)} all-gather(bf16[64,24,128]{2,1,0:T(8,128)(2,1)S(1)} %all_gather.10), channel_id=1, replica_groups=mesh['zh'=4,'y'=8,'core'=2,'x'=4,'zl'=2] {'core'}, dimensions={1}, use_global_device_ids=true | all-gather | bytes 1179648 | tf_op jit(solution)/shard_map/all_gather | solution.py:172
  97.7 0.9 copy-done.10
  98.6 3.4 %collective-permute-start = (bf16[128,128]{1,0:T(8,128)(2,1)S(1)}, bf16[128,128]{1,0:T(8,128)(2,1)S(1)}, u32[]{:S(2)}, u32[]{:S(2)}) collective-permute-start(bf16[128,128]{1,0:T(8,128)(2,1)S(1)} %convolution_convert_fusion.kv), channel_id=1, source_target_pairs={{0,8},{8,16},{16,24},{24,32},{32,40},{40,48},{48,56},{56,64},{64,7... | collective-permute-start | bytes 98312 | tf_op jit(solution)/shard_map/ppermute | solution.py:22
  103.0 1.9 %collective-permute-start.2 = (bf16[3072,512]{1,0:T(8,128)(2,1)}, bf16[3072,512]{1,0:T(8,128)(2,1)S(1)}, u32[]{:S(2)}, u32[]{:S(2)}) collective-permute-start(bf16[3072,512]{1,0:T(8,128)(2,1)} %bitcast.65), channel_id=1, source_target_pairs={{0,8},{8,0},{1,9},{9,1},{2,10},{10,2},{3,11},{11,3},{4,12},{12,4},... | collective-permute-start | bytes 9437192 | tf_op jit(solution)/shard_map/ppermute | solution.py:207
  104.9 1.9 %copy-done.1 = bf16[64,48,512]{2,1,0:T(8,128)(2,1)S(1)} copy-done((bf16[64,48,512]{2,1,0:T(8,128)(2,1)S(1)}, bf16[64,48,512]{2,1,0:T(8,128)(2,1)}, u32[]{:S(2)}) %copy-start.1) | copy-done | bytes 3145752
  106.8 1.0 shard_map.130
  107.9 2.9 %collective-permute-done.2.oth = bf16[3072,512]{1,0:T(8,128)(2,1)S(1)} collective-permute-done((bf16[3072,512]{1,0:T(8,128)(2,1)}, bf16[3072,512]{1,0:T(8,128)(2,1)S(1)}, u32[]{:S(2)}, u32[]{:S(2)}) %collective-permute-start.2) | collective-permute-done | bytes 3145760 | tf_op jit(solution)/shard_map/ppermute | solution.py:207
  110.8 1.7 %copy-done.6 = bf16[8,4,2,48,128]{4,3,2,1,0:T(8,128)(2,1)S(1)} copy-done((bf16[8,4,2,48,128]{4,3,2,1,0:T(8,128)(2,1)S(1)}, bf16[8,4,2,48,128]{4,3,2,1,0:T(8,128)(2,1)}, u32[]{:S(2)}) %copy-start.6) | copy-done | bytes 786456
  112.4 1.1 copy-done.9
  114.3 4.6 %shard_map.131 = (bf16[512,128]{1,0:T(8,128)(2,1)S(1)}, bf16[512,128]{1,0:T(8,128)(2,1)S(1)}, bf16[128,128]{1,0:T(8,128)(2,1)S(1)}, f32[128,128]{1,0:T(8,128)S(1)}) custom-call(bf16[3072,512]{1,0:T(8,128)(2,1)S(1)} %collective-permute-done.2.oth, bf16[3072,128]{1,0:T(8,128)(2,1)S(1)} %bitcast.71, bf16[3072,128]{1,0:T(8,128)(2,1)S(1)} %bitcast.74, ...), custom_call_target="tpu_custom_call" | custom-call | flops 100000000 | bytes 5406720 | tf_op jit(solution)/shard_map/pallas_call | solution.py:131
  120.2 1.0 shard_map.132
  121.2 0.9 copy-done.13
  122.1 4.8 %all-to-all-start.3 = ((bf16[8,384,128]{2,1,0:T(8,128)(2,1)}), bf16[8,384,128]{2,1,0:T(8,128)(2,1)}, u32[]{:S(2)}, u32[]{:S(2)}) async-start(bf16[8,384,128]{2,1,0:T(8,128)(2,1)} %copy-done.13), calls=%async_computation.3 | async-start | bytes 1572864 | tf_op jit(solution)/shard_map/all_to_all | solution.py:223
  126.8 2.3 %collective-permute-start.3 = (bf16[128,128]{1,0:T(8,128)(2,1)S(1)}, bf16[128,128]{1,0:T(8,128)(2,1)S(1)}, u32[]{:S(2)}, u32[]{:S(2)}) collective-permute-start(bf16[128,128]{1,0:T(8,128)(2,1)S(1)} %copy-done.19), channel_id=1, source_target_pairs={{8,0},{16,8},{24,16},{32,24},{40,32},{48,40},{56,48},{64,56},{72,6... | collective-permute-start | bytes 98312 | tf_op jit(solution)/shard_map/ppermute | solution.py:22
  129.2 4.1 %collective-permute-done.3.returned = bf16[128,128]{1,0:T(8,128)(2,1)S(1)} collective-permute-done((bf16[128,128]{1,0:T(8,128)(2,1)S(1)}, bf16[128,128]{1,0:T(8,128)(2,1)S(1)}, u32[]{:S(2)}, u32[]{:S(2)}) %collective-permute-start.3) | collective-permute-done | bytes 32800 | tf_op jit(solution)/shard_map/ppermute | solution.py:22
  133.3 1.9 %copy-done.4 = bf16[3072,512]{1,0:T(8,128)(2,1)S(1)} copy-done((bf16[3072,512]{1,0:T(8,128)(2,1)S(1)}, bf16[3072,512]{1,0:T(8,128)(2,1)}, u32[]{:S(2)}) %copy-start.4) | copy-done | bytes 3145752
  135.2 1.1 copy-done.7
  136.3 1.1 copy-done.11
  137.5 1.3 shard_map.133
  138.8 0.9 copy-done.12
  139.7 5.6 %all-to-all-start.4 = ((bf16[8,400,128]{2,1,0:T(8,128)(2,1)}), bf16[8,400,128]{2,1,0:T(8,128)(2,1)S(1)}, u32[]{:S(2)}, u32[]{:S(2)}) async-start(bf16[8,400,128]{2,1,0:T(8,128)(2,1)} %copy-done.12), calls=%async_computation.4 | async-start | bytes 1638400 | tf_op jit(solution)/shard_map/all_to_all | solution.py:230
  146.1 1.3 convert_reduce_fusion.1
  147.4 1.0 fusion.7
  148.4 9.9 %all-to-all-done.4 = bf16[8,400,128]{2,1,0:T(8,128)(2,1)S(1)} async-done(((bf16[8,400,128]{2,1,0:T(8,128)(2,1)}), bf16[8,400,128]{2,1,0:T(8,128)(2,1)S(1)}, u32[]{:S(2)}, u32[]{:S(2)}) %all-to-all-start.4) | async-done | bytes 819232 | tf_op jit(solution)/shard_map/all_to_all | solution.py:230
  158.5 0.8 fusion.20
  (113 shorter events, 12.0 us)
Async XLA Ops:
  7.2 138.2 %copy-start = (bf16[16,2880]{1,0:T(8,128)(2,1)S(1)}, bf16[16,2880]{1,0:T(8,128)(2,1)}, u32[]{:S(2)}) copy-start(bf16[16,2880]{1,0:T(8,128)(2,1)} %param.18) | copy-start | bytes 276484
  7.2 95.8 %all-gather.2.cloned.1.call-start = ((), (), s32[]{:S(2)}) async-start(), calls=%async_computation.5 | async-start | bytes 3538944 | tf_op jit(solution)/shard_map/all_gather | solution.py:169
  9.8 26.5 %copy-start.20 = (bf16[128,2880]{0,1:T(8,128)(2,1)S(1)}, bf16[128,2880]{0,1:T(8,128)(2,1)}, u32[]{:S(2)}) copy-start(bf16[128,2880]{0,1:T(8,128)(2,1)} %param.11) | copy-start | bytes 2211844
  10.4 26.4 %copy-start.24 = (f32[2880]{0:T(1024)S(1)}, f32[2880]{0:T(1024)}, u32[]{:S(2)}) copy-start(f32[2880]{0:T(1024)} %param.17) | copy-start | bytes 34564
  10.4 26.4 %copy-start.25 = (f32[2880]{0:T(1024)S(1)}, f32[2880]{0:T(1024)}, u32[]{:S(2)}) copy-start(f32[2880]{0:T(1024)} %param.12) | copy-start | bytes 34564
  36.3 2.6 %copy-start.22 = (bf16[128,2880]{0,1:T(8,128)(2,1)S(1)}, bf16[128,2880]{0,1:T(8,128)(2,1)}, u32[]{:S(2)}) copy-start(bf16[128,2880]{0,1:T(8,128)(2,1)} %param.21) | copy-start | bytes 2211844
  36.3 2.6 %copy-start.27 = (s32[128]{0:T(128)S(1)}, s32[128]{0:T(128)}, u32[]{:S(2)}) copy-start(s32[128]{0:T(128)} %param.20) | copy-start | bytes 1540
  36.3 10.3 %copy-start.30 = (s32[128]{0:T(128)S(1)}, s32[128]{0:T(128)}, u32[]{:S(2)}) copy-start(s32[128]{0:T(128)} %param.19) | copy-start | bytes 1540
  38.9 11.3 %copy-start.31 = (f32[128]{0:T(128)}, f32[128]{0:T(128)S(1)}, u32[]{:S(2)}) copy-start(f32[128]{0:T(128)S(1)} %add_divide_fusion) | copy-start | bytes 1540
  39.8 15.5 %all-to-all-start.1 = ((f32[8,16,360]{2,1,0:T(8,128)}), f32[8,16,360]{2,1,0:T(8,128)S(1)}, u32[]{:S(2)}, u32[]{:S(2)}) async-start(f32[8,16,360]{2,1,0:T(8,128)} %broadcast_in_dim.12), calls=%async_computation.1 | async-start | bytes 393216 | tf_op jit(solution)/shard_map/all_to_all | solution.py:28
  46.7 4.1 %collective-permute-start.1 = (s32[128]{0:T(128)S(1)}, s32[128]{0:T(128)S(1)}, u32[]{:S(2)}, u32[]{:S(2)}) collective-permute-start(s32[128]{0:T(128)S(1)} %copy-done.30), channel_id=1, source_target_pairs={{0,8},{8,16},{16,24},{24,32},{32,40},{40,48},{48,56},{56,64},{64,7... | collective-permute-start | bytes 1544 | tf_op jit(solution)/shard_map/ppermute | solution.py:22
  50.3 54.6 %copy-start.5 = (bf16[8,4,2,48,128]{4,3,2,1,0:T(8,128)(2,1)}, bf16[8,4,2,48,128]{4,3,2,1,0:T(8,128)(2,1)S(1)}, u32[]{:S(2)}) copy-start(bf16[8,4,2,48,128]{4,3,2,1,0:T(8,128)(2,1)S(1)} %pad.21.clone) | copy-start | bytes 2359300
  50.8 54.2 %copy-start.8 = (bf16[8,4,2,48,128]{4,3,2,1,0:T(8,128)(2,1)}, bf16[8,4,2,48,128]{4,3,2,1,0:T(8,128)(2,1)S(1)}, u32[]{:S(2)}) copy-start(bf16[8,4,2,48,128]{4,3,2,1,0:T(8,128)(2,1)S(1)} %pad.22.clone) | copy-start | bytes 2359300
  56.1 46.1 %all-to-all-start.2 = ((f32[8,16,360]{2,1,0:T(8,128)}), f32[8,16,360]{2,1,0:T(8,128)S(1)}, u32[]{:S(2)}, u32[]{:S(2)}) async-start(f32[8,16,360]{2,1,0:T(8,128)} %broadcast_in_dim.13), calls=%async_computation.2 | async-start | bytes 393216 | tf_op jit(solution)/shard_map/all_to_all | solution.py:28
  98.6 4.4 %collective-permute-start = (bf16[128,128]{1,0:T(8,128)(2,1)S(1)}, bf16[128,128]{1,0:T(8,128)(2,1)S(1)}, u32[]{:S(2)}, u32[]{:S(2)}) collective-permute-start(bf16[128,128]{1,0:T(8,128)(2,1)S(1)} %convolution_convert_fusion.kv), channel_id=1, source_target_pairs={{0,8},{8,16},{16,24},{24,32},{32,40},{40,48},{48,56},{56,64},{64,7... | collective-permute-start | bytes 98312 | tf_op jit(solution)/shard_map/ppermute | solution.py:22
  103.0 4.9 %copy-start.16 = (bf16[128,128]{1,0:T(8,128)(2,1)}, bf16[128,128]{1,0:T(8,128)(2,1)S(1)}, u32[]{:S(2)}) copy-start(bf16[128,128]{1,0:T(8,128)(2,1)S(1)} %collective-permute-done.halo) | copy-start | bytes 98308
  103.0 7.8 %collective-permute-start.2 = (bf16[3072,512]{1,0:T(8,128)(2,1)}, bf16[3072,512]{1,0:T(8,128)(2,1)S(1)}, u32[]{:S(2)}, u32[]{:S(2)}) collective-permute-start(bf16[3072,512]{1,0:T(8,128)(2,1)} %bitcast.65), channel_id=1, source_target_pairs={{0,8},{8,0},{1,9},{9,1},{2,10},{10,2},{3,11},{11,3},{4,12},{12,4},... | collective-permute-start | bytes 9437192 | tf_op jit(solution)/shard_map/ppermute | solution.py:207
  104.9 1.9 %copy-start.1 = (bf16[64,48,512]{2,1,0:T(8,128)(2,1)S(1)}, bf16[64,48,512]{2,1,0:T(8,128)(2,1)}, u32[]{:S(2)}) copy-start(bf16[64,48,512]{2,1,0:T(8,128)(2,1)} %all-gather.2.cloned.1.call-done) | copy-start | bytes 9437188
  110.8 9.4 %copy-start.3 = (bf16[3072,512]{1,0:T(8,128)(2,1)}, bf16[3072,512]{1,0:T(8,128)(2,1)S(1)}, u32[]{:S(2)}) copy-start(bf16[3072,512]{1,0:T(8,128)(2,1)S(1)} %collective-permute-done.2.oth) | copy-start | bytes 9437188
  110.8 1.7 %copy-start.6 = (bf16[8,4,2,48,128]{4,3,2,1,0:T(8,128)(2,1)S(1)}, bf16[8,4,2,48,128]{4,3,2,1,0:T(8,128)(2,1)}, u32[]{:S(2)}) copy-start(bf16[8,4,2,48,128]{4,3,2,1,0:T(8,128)(2,1)} %copy-done.5) | copy-start | bytes 2359300
  114.3 5.8 %copy-start.2 = (bf16[64,48,512]{2,1,0:T(8,128)(2,1)S(1)}, bf16[64,48,512]{2,1,0:T(8,128)(2,1)}, u32[]{:S(2)}) copy-start(bf16[64,48,512]{2,1,0:T(8,128)(2,1)} %all-gather.2.cloned.1.call-done) | copy-start | bytes 9437188
  122.1 4.8 %copy-start.19 = (bf16[128,128]{1,0:T(8,128)(2,1)S(1)}, bf16[128,128]{1,0:T(8,128)(2,1)}, u32[]{:S(2)}) copy-start(bf16[128,128]{1,0:T(8,128)(2,1)} %copy-done.18) | copy-start | bytes 98308
  122.1 11.3 %copy-start.15 = (f32[128,128]{1,0:T(8,128)S(1)}, f32[128,128]{1,0:T(8,128)}, u32[]{:S(2)}) copy-start(f32[128,128]{1,0:T(8,128)} %copy-done.14) | copy-start | bytes 196612
  122.1 17.6 %all-to-all-start.3 = ((bf16[8,384,128]{2,1,0:T(8,128)(2,1)}), bf16[8,384,128]{2,1,0:T(8,128)(2,1)}, u32[]{:S(2)}, u32[]{:S(2)}) async-start(bf16[8,384,128]{2,1,0:T(8,128)(2,1)} %copy-done.13), calls=%async_computation.3 | async-start | bytes 1572864 | tf_op jit(solution)/shard_map/all_to_all | solution.py:223
  126.8 6.5 %collective-permute-start.3 = (bf16[128,128]{1,0:T(8,128)(2,1)S(1)}, bf16[128,128]{1,0:T(8,128)(2,1)S(1)}, u32[]{:S(2)}, u32[]{:S(2)}) collective-permute-start(bf16[128,128]{1,0:T(8,128)(2,1)S(1)} %copy-done.19), channel_id=1, source_target_pairs={{8,0},{16,8},{24,16},{32,24},{40,32},{48,40},{56,48},{64,56},{72,6... | collective-permute-start | bytes 98312 | tf_op jit(solution)/shard_map/ppermute | solution.py:22
  133.3 1.9 %copy-start.4 = (bf16[3072,512]{1,0:T(8,128)(2,1)S(1)}, bf16[3072,512]{1,0:T(8,128)(2,1)}, u32[]{:S(2)}) copy-start(bf16[3072,512]{1,0:T(8,128)(2,1)} %copy-done.3) | copy-start | bytes 9437188
  139.7 5.6 %copy-start.26 = (f32[2880]{0:T(1024)S(1)}, f32[2880]{0:T(1024)}, u32[]{:S(2)}) copy-start(f32[2880]{0:T(1024)} %param.12) | copy-start | bytes 34564
  139.7 5.7 %copy-start.23 = (bf16[128,2880]{0,1:T(8,128)(2,1)S(1)}, bf16[128,2880]{0,1:T(8,128)(2,1)}, u32[]{:S(2)}) copy-start(bf16[128,2880]{0,1:T(8,128)(2,1)} %param.21) | copy-start | bytes 2211844
  139.7 6.0 %copy-start.21 = (bf16[128,2880]{0,1:T(8,128)(2,1)S(1)}, bf16[128,2880]{0,1:T(8,128)(2,1)}, u32[]{:S(2)}) copy-start(bf16[128,2880]{0,1:T(8,128)(2,1)} %param.11) | copy-start | bytes 2211844
  139.7 18.6 %all-to-all-start.4 = ((bf16[8,400,128]{2,1,0:T(8,128)(2,1)}), bf16[8,400,128]{2,1,0:T(8,128)(2,1)S(1)}, u32[]{:S(2)}, u32[]{:S(2)}) async-start(bf16[8,400,128]{2,1,0:T(8,128)(2,1)} %copy-done.12), calls=%async_computation.4 | async-start | bytes 1638400 | tf_op jit(solution)/shard_map/all_to_all | solution.py:230
  145.4 2.0 %copy-start.32 = (f32[128]{0:T(128)S(1)}, f32[128]{0:T(128)}, u32[]{:S(2)}) copy-start(f32[128]{0:T(128)} %copy-done.31) | copy-start | bytes 1540
  147.4 11.1 %copy-start.29 = (f32[128]{0:T(128)S(1)}, f32[128]{0:T(128)}, u32[]{:S(2)}) copy-start(f32[128]{0:T(128)} %copy-done.28) | copy-start | bytes 1540
  (10 other events, 8.7 us)
Sparse Core Ops, SparseCore 0:
  36.4 53.4 all-gather.1

commit v4 on v3

--- a/solution.py
+++ b/solution.py
@@ -1,3 +1,5 @@
+import functools
+
 import jax
 import jax.numpy as jnp
 from jax import lax
@@ -49,28 +51,22 @@
     return lax.dot_general(left, right, dims, preferred_element_type=F32)
 
 
-def own_kernel(weight, normed, grads, query, grad):
+def attend_kernel(last, weight, normed, grads, kv, halo, mask, *refs):
+    if last:
+        grad_first, mixed, grad_query, grad_halo, grad_kv = refs
+        grad_keys, grad_values = grad_first[:HD, :], grad_first[HD:, :]
+    else:
+        mixed, grad_query, grad_kv = refs
+        grad_keys = grad_values = jnp.zeros((HD, 2 * WIN), F32)
     half = weight.shape[1] // 2
-    query[...] = mm(weight[:, :half], normed[...], 0, 0).astype(BF16)
-    grad[...] = mm(weight[:, half:], grads[...], 0, 0).astype(BF16)
-
-
-def attend_kernel(
-    oth, normed, grads, q_own, g_own, kv, halo, mask, mixed, grad_query, grad_halo, grad_kv
-):
-    half = oth.shape[1] // 2
-    q_oth = mm(oth[:, :half], normed[...], 0, 0).astype(BF16)
-    g_oth = mm(oth[:, half:], grads[...], 0, 0).astype(BF16)
+    query_all = mm(weight[:, :half], normed[...], 0, 0).astype(BF16)
+    grad_all = mm(weight[:, half:], grads[...], 0, 0).astype(BF16)
     keys = jnp.concatenate([halo[:HD, :], kv[:HD, :]], axis=1)
     values = jnp.concatenate([halo[HD:, :], kv[HD:, :]], axis=1)
     allowed = mask[...] > 0.0
-    grad_keys = jnp.zeros(keys.shape, F32)
-    grad_values = jnp.zeros(keys.shape, F32)
-    for head in range(8):
-        low = head % 4 * HD
-        rows = pl.ds(head * HD, HD)
-        query = q_own[low : low + HD, :] if head < 4 else q_oth[low : low + HD]
-        grad = g_own[low : low + HD, :] if head < 4 else g_oth[low : low + HD]
+    for head in range(4):
+        rows = slice(head * HD, (head + 1) * HD)
+        query, grad = query_all[rows], grad_all[rows]
         scores = mm(keys, query, 0, 0) * HD**-0.5
         scores = jnp.where(allowed, scores, -jnp.inf)
         raised = jnp.exp(scores - jnp.max(scores, axis=0, keepdims=True))
@@ -83,10 +79,14 @@
         grad_scores = (prob * (grad_prob - delta) * HD**-0.5).astype(BF16)
         grad_query[rows, :] = mm(keys, grad_scores, 1, 0).astype(BF16)
         grad_keys += mm(query, grad_scores, 1, 1)
-    grad_halo[:HD, :] = grad_keys[:, :WIN].astype(BF16)
-    grad_halo[HD:, :] = grad_values[:, :WIN].astype(BF16)
-    grad_kv[:HD, :] = grad_keys[:, WIN:]
-    grad_kv[HD:, :] = grad_values[:, WIN:]
+    if last:
+        grad_halo[:HD, :] = grad_keys[:, :WIN].astype(BF16)
+        grad_halo[HD:, :] = grad_values[:, :WIN].astype(BF16)
+        grad_kv[:HD, :] = grad_keys[:, WIN:]
+        grad_kv[HD:, :] = grad_values[:, WIN:]
+    else:
+        grad_kv[:HD, :] = grad_keys
+        grad_kv[HD:, :] = grad_values
 
 
 def chunks():
@@ -96,22 +96,22 @@
             yield group, part * 2 * PAD, row
 
 
-def out_kernel(own, oth, mixed, blocks):
+def out_kernel(own, oth, m_own, m_oth, blocks):
     half = own.shape[1] // 2
     for group, place, row in chunks():
-        term = mm(own[row : row + 2 * PAD, half:], mixed[:half, :], 1, 0)
-        term = term + mm(oth[row : row + 2 * PAD, half:], mixed[half:, :], 1, 0)
+        term = mm(own[row : row + 2 * PAD, half:], m_own[...], 1, 0)
+        term = term + mm(oth[row : row + 2 * PAD, half:], m_oth[...], 1, 0)
         blocks[group, place : place + 2 * PAD, :] = term.astype(BF16)
 
 
-def back_kernel(own, oth, kv_all, normed, grad_query, grad_kv, returned, blocks):
+def back_kernel(own, oth, kv_all, normed, d_own, d_oth, grad_kv, returned, blocks):
     half = own.shape[1] // 2
     tokens_here = grad_kv.shape[1]
     kv_grad = (grad_kv[...] + returned[...].astype(F32)).astype(BF16)
     rows = jnp.zeros((2 * PAD, tokens_here), F32)
     for group, place, row in chunks():
-        term = mm(own[row : row + 2 * PAD, :half], grad_query[:half, :], 1, 0)
-        term = term + mm(oth[row : row + 2 * PAD, :half], grad_query[half:, :], 1, 0)
+        term = mm(own[row : row + 2 * PAD, :half], d_own[...], 1, 0)
+        term = term + mm(oth[row : row + 2 * PAD, :half], d_oth[...], 1, 0)
         term = term + mm(kv_all[row : row + 2 * PAD, :], kv_grad, 1, 0)
         term = term.astype(BF16)
         blocks[group, place : place + 2 * PAD, :] = term
@@ -131,7 +131,7 @@
     return pl.pallas_call(
         kernel,
         out_shape=outs,
-        compiler_params=pltpu.CompilerParams(vmem_limit_bytes=40 * 2**20),
+        compiler_params=pltpu.CompilerParams(vmem_limit_bytes=12 * 2**20),
         cost_estimate=pl.CostEstimate(flops=10**8, bytes_accessed=size, transcendentals=0),
     )(*args)
 
@@ -168,7 +168,7 @@
     near = lax.all_to_all(sent, ("zh", "core"), 0, 0)
     own = lax.all_gather(near[:, :PAD], "y", axis=0, tiled=True).reshape(-1, 2 * half)
     kv_near = near[:, PAD : PAD + 6].reshape(8, PAD // 2, 2 * HD)
-    kv_near = lax.all_gather(kv_near, "y", axis=0, tiled=True)
+    kv_near = gathered(kv_near, ("y",)).reshape(64, PAD // 2, 2 * HD)
     kv_all = lax.all_gather(kv_near, "core", axis=1, tiled=True).reshape(-1, 2 * HD)
 
     tok = tokens.T.astype(F32)
@@ -188,8 +188,10 @@
     steer_part = dot(
         one_hot.astype(F32), gate[None, :] * grad_share, ((1,), (1,)), precision=HIGHEST
     )
-    steer_near = jnp.sum(gathered(steer_part, ("zh", "core")), axis=0)
-    steer_grad = jnp.sum(gathered(steer_near, ("y",)), axis=0)
+    steer_grad = steer_part
+    for axis, step in (("core", 1), ("zh", 1), ("zh", 2), ("y", 1), ("y", 2), ("y", 4)):
+        pairs = [(i, i ^ step) for i in range(lax.axis_size(axis))]
+        steer_grad = steer_grad + lax.ppermute(steer_grad, axis, pairs)
 
     halo_seg = shifted(segment_ids, 1)
     halo_seg = jnp.where(lax.axis_index(SEQ) > 0, halo_seg, -1)
@@ -207,25 +209,24 @@
     oth = lax.ppermute(own, "core", [(0, 1), (1, 0)])
     like = jax.ShapeDtypeStruct
     thin = like((half, row_count), BF16)
-    q_own, g_own = call(own_kernel, (thin, thin), own, normed_b, grad_b)
-    mixed, grad_query, grad_halo, grad_kv = call(
-        attend_kernel,
-        (
-            like((2 * half, row_count), BF16),
-            like((2 * half, row_count), BF16),
-            like((2 * HD, row_count), BF16),
-            like((2 * HD, row_count), F32),
-        ),
-        *(oth, normed_b, grad_b, q_own, g_own, kv, halo, mask),
+    m_own, d_own, grad_first = call(
+        functools.partial(attend_kernel, False),
+        (thin, thin, like((2 * HD, 2 * row_count), F32)),
+        *(own, normed_b, grad_b, kv, halo, mask),
+    )
+    m_oth, d_oth, grad_halo, grad_kv = call(
+        functools.partial(attend_kernel, True),
+        (thin, thin, like((2 * HD, row_count), BF16), like((2 * HD, row_count), F32)),
+        *(oth, normed_b, grad_b, kv, halo, mask, grad_first),
     )
     returned = shifted(grad_halo, -1)
-    blocks = call(out_kernel, like((8, 8 * PAD, row_count), BF16), own, oth, mixed)
+    blocks = call(out_kernel, like((8, 8 * PAD, row_count), BF16), own, oth, m_own, m_oth)
     attn = lax.all_to_all(blocks, HEAD, 0, 0)
-    blocks, grad_query = lax.optimization_barrier((blocks, grad_query))
+    blocks, d_own = lax.optimization_barrier((blocks, d_own))
     back = call(
         back_kernel,
         like((8, 8 * PAD + 16, row_count), BF16),
-        *(own, oth, kv_all, normed_b, grad_query, grad_kv, returned),
+        *(own, oth, kv_all, normed_b, d_own, d_oth, grad_kv, returned),
     )
     back = lax.all_to_all(back, HEAD, 0, 0)
 

time: 167 us -> 159 us (0.952)
  blocking collectives: 59.4 us -> 31 us
  starting transfers between devices: 34.9 us -> 54.5 us
  waiting for transfers between devices: 21.7 us -> 23.8 us
  local copies, waits for them, and re-layouts: 18.3 us -> 16.5 us
    ppermute x0 -> x6, starting transfers between devices: none -> 27.3 us  [shards(): steer_grad = steer_grad + lax.ppermute(steer_grad, axis, pairs)]
    all_gather x1 -> x0, blocking collectives: 26 us -> none  [shards(): kv_near = lax.all_gather(kv_near, 'y', axis=0, tiled=True)]
    ppermute x0 -> x6, waiting for transfers between devices: none -> 8.3 us  [shards(): steer_grad = steer_grad + lax.ppermute(steer_grad, axis, pairs)]
    all_to_all x2 -> x1, starting transfers between devices: 13.7 us -> 6.84 us  [gathered(): return lax.all_to_all(spread, axes, 0, 0)]
    all_to_all x2 -> x1, waiting for transfers between devices: 4.52 us -> 0.01 us  [gathered(): return lax.all_to_all(spread, axes, 0, 0)]
    all_gather x1, blocking collectives: 8.36 us -> 6.03 us  [shards(): lax.all_gather(kv_near, 'core', axis=1, tiled=True).reshape(-1, 2 * HD)]
    ppermute x1, waiting for transfers between devices: 2.89 us -> 1.1 us  [shards(): oth = lax.ppermute(own, 'core', [(0, 1), (1, 0)])]
    unnamed x68 -> x64, local copies, waits for them, and re-layouts: 14.3 us -> 13 us
  transfers between devices with their start and end apart: 9 -> 14, of which waited for: 5 -> 9; matrix products, arithmetic and copies ran while one was open for 5% -> 5% of each run, Pallas kernels for 1% -> 3%
where the time goes in v4:
time: 159 us; the launch traced here: 158 us
  starting transfers between devices  54.5 us (34%)
  blocking collectives  31 us (19%)
  waiting for transfers between devices  23.8 us (15%)
  local copies, waits for them, and re-layouts  16.5 us (10%)
  between operations  14.7 us (9%)
  Pallas kernels  7.88 us (5%)
  other arithmetic  7.62 us (5%)
  matrix products  1.82 us (1%)
    ppermute x6, starting transfers between devices, shards(): steer_grad = steer_grad + lax.ppermute(steer_grad, axis, pairs)  27.3 us
    all_to_all x1, blocking collectives, shards(): near = lax.all_to_all(sent, ('zh', 'core'), 0, 0)  25 us
    unnamed x64, local copies, waits for them, and re-layouts  13 us
    all_to_all x1, waiting for transfers between devices, shards(): back = lax.all_to_all(back, HEAD, 0, 0)  9.93 us
    ppermute x3, starting transfers between devices, shifted(): return lax.ppermute(value, SEQ, pairs)  8.33 us
    ppermute x6, waiting for transfers between devices, shards(): steer_grad = steer_grad + lax.ppermute(steer_grad, axis, pairs)  8.3 us
    pallas_call x4, Pallas kernels, call(): pl.pallas_call(kernel, out_shape=outs, compiler_params=pltpu.CompilerPara...  7.88 us
    all_to_all x1, starting transfers between devices, gathered(): return lax.all_to_all(spread, axes, 0, 0)  6.84 us
  transfers between devices with their start and end apart: 14, of which 9 were waited for; matrix products, arithmetic and copies ran while one was open for 5% of the time, Pallas kernels for 3%

profile of v4, /device:TPU:1, one launch (start us, length us, event | category | flops | bytes accessed | tf_op | source)
XLA Modules:
  0.0 157.7 jit_solution(17381111416685300963)
XLA Ops:
  10.5 25.0 %all_to_all.20 = bf16[8,56,512]{2,1,0:T(8,128)(2,1)S(1)} all-to-all(bf16[8,56,512]{2,1,0:T(8,128)(2,1)S(1)} %constant_dynamic-update-slice_fusion), channel_id=1, replica_groups=mesh['zh'=4,'y'=8,'core'=2,'x'=4,'zl'=2] {'zh','core'}, dimensions={0} | all-to-all | bytes 917504 | tf_op jit(solution)/shard_map/all_to_all | solution.py:168
  36.8 1.5 multiply_reduce_fusion
  39.2 6.8 %all-to-all-start.1 = ((bf16[8,8,24,128]{3,2,1,0:T(8,128)(2,1)}), bf16[8,8,24,128]{3,2,1,0:T(8,128)(2,1)S(1)}, u32[]{:S(2)}, u32[]{:S(2)}) async-start(bf16[8,8,24,128]{3,2,1,0:T(8,128)(2,1)} %broadcast_in_dim.13), calls=%async_computation.1 | async-start | bytes 786432 | tf_op jit(solution)/shard_map/all_to_all | solution.py:30
  46.3 5.7 %collective-permute-start.2 = (f32[16,360]{1,0:T(8,128)S(1)}, f32[16,360]{1,0:T(8,128)S(1)}, u32[]{:S(2)}, u32[]{:S(2)}) collective-permute-start(f32[16,360]{1,0:T(8,128)S(1)} %fusion.10), channel_id=1, source_target_pairs={{0,8},{8,0},{1,9},{9,1},{2,10},{10,2},{3,11},{11,3},{4,12},{12,4},... | collective-permute-start | bytes 69128 | tf_op jit(solution)/shard_map/ppermute | solution.py:194
  52.9 1.9 %collective-permute-start.3 = (f32[16,360]{1,0:T(8,128)S(1)}, f32[16,360]{1,0:T(8,128)S(1)}, u32[]{:S(2)}, u32[]{:S(2)}) collective-permute-start(f32[16,360]{1,0:T(8,128)S(1)} %add.96), channel_id=1, source_target_pairs={{0,128},{128,0},{256,384},{384,256},{1,129},{129,1},{257,385},{385... | collective-permute-start | bytes 69128 | tf_op jit(solution)/shard_map/ppermute | solution.py:194
  54.8 3.9 %collective-permute-start.1 = (s32[128]{0:T(128)S(1)}, s32[128]{0:T(128)S(1)}, u32[]{:S(2)}, u32[]{:S(2)}) collective-permute-start(s32[128]{0:T(128)S(1)} %copy-done.28), channel_id=1, source_target_pairs={{0,8},{8,16},{16,24},{24,32},{32,40},{40,48},{48,56},{56,64},{64,7... | collective-permute-start | bytes 1544 | tf_op jit(solution)/shard_map/ppermute | solution.py:24
  59.0 4.1 %collective-permute-start.4 = (f32[16,360]{1,0:T(8,128)S(1)}, f32[16,360]{1,0:T(8,128)S(1)}, u32[]{:S(2)}, u32[]{:S(2)}) collective-permute-start(f32[16,360]{1,0:T(8,128)S(1)} %add.97), channel_id=1, source_target_pairs={{0,256},{128,384},{256,0},{384,128},{1,257},{129,385},{257,1},{385... | collective-permute-start | bytes 69128 | tf_op jit(solution)/shard_map/ppermute | solution.py:194
  64.0 3.4 %collective-permute-done.4 = f32[16,360]{1,0:T(8,128)S(1)} collective-permute-done((f32[16,360]{1,0:T(8,128)S(1)}, f32[16,360]{1,0:T(8,128)S(1)}, u32[]{:S(2)}, u32[]{:S(2)}) %collective-permute-start.4) | collective-permute-done | bytes 23072 | tf_op jit(solution)/shard_map/ppermute | solution.py:194
  67.5 3.7 %collective-permute-start.5 = (f32[16,360]{1,0:T(8,128)S(1)}, f32[16,360]{1,0:T(8,128)S(1)}, u32[]{:S(2)}, u32[]{:S(2)}) collective-permute-start(f32[16,360]{1,0:T(8,128)S(1)} %add.98), channel_id=1, source_target_pairs={{0,16},{16,0},{32,48},{48,32},{64,80},{80,64},{96,112},{112,96},{1... | collective-permute-start | bytes 69128 | tf_op jit(solution)/shard_map/ppermute | solution.py:194
  71.2 1.8 %collective-permute-done.5 = f32[16,360]{1,0:T(8,128)S(1)} collective-permute-done((f32[16,360]{1,0:T(8,128)S(1)}, f32[16,360]{1,0:T(8,128)S(1)}, u32[]{:S(2)}, u32[]{:S(2)}) %collective-permute-start.5) | collective-permute-done | bytes 23072 | tf_op jit(solution)/shard_map/ppermute | solution.py:194
  73.0 4.3 %collective-permute-start.6 = (f32[16,360]{1,0:T(8,128)S(1)}, f32[16,360]{1,0:T(8,128)S(1)}, u32[]{:S(2)}, u32[]{:S(2)}) collective-permute-start(f32[16,360]{1,0:T(8,128)S(1)} %add.99), channel_id=1, source_target_pairs={{0,32},{16,48},{32,0},{48,16},{64,96},{80,112},{96,64},{112,80},{1... | collective-permute-start | bytes 69128 | tf_op jit(solution)/shard_map/ppermute | solution.py:194
  77.3 1.9 %collective-permute-done.6 = f32[16,360]{1,0:T(8,128)S(1)} collective-permute-done((f32[16,360]{1,0:T(8,128)S(1)}, f32[16,360]{1,0:T(8,128)S(1)}, u32[]{:S(2)}, u32[]{:S(2)}) %collective-permute-start.6) | collective-permute-done | bytes 23072 | tf_op jit(solution)/shard_map/ppermute | solution.py:194
  79.2 7.6 %collective-permute-start.7 = (f32[16,360]{1,0:T(8,128)S(1)}, f32[16,360]{1,0:T(8,128)S(1)}, u32[]{:S(2)}, u32[]{:S(2)}) collective-permute-start(f32[16,360]{1,0:T(8,128)S(1)} %add.100), channel_id=1, source_target_pairs={{0,64},{16,80},{32,96},{48,112},{64,0},{80,16},{96,32},{112,48},{1... | collective-permute-start | bytes 69128 | tf_op jit(solution)/shard_map/ppermute | solution.py:194
  86.8 6.0 %all_gather.7 = bf16[64,48,128]{2,1,0:T(8,128)(2,1)S(1)} all-gather(bf16[64,24,128]{2,1,0:T(8,128)(2,1)S(1)} %bitcast.81), channel_id=1, replica_groups=mesh['zh'=4,'y'=8,'core'=2,'x'=4,'zl'=2] {'core'}, dimensions={1}, use_global_device_ids=true | all-gather | bytes 1179648 | tf_op jit(solution)/shard_map/all_gather | solution.py:172
  94.2 2.1 %collective-permute-start = (bf16[128,128]{1,0:T(8,128)(2,1)S(1)}, bf16[128,128]{1,0:T(8,128)(2,1)S(1)}, u32[]{:S(2)}, u32[]{:S(2)}) collective-permute-start(bf16[128,128]{1,0:T(8,128)(2,1)S(1)} %convolution_convert_fusion.kv), channel_id=1, source_target_pairs={{0,8},{8,16},{16,24},{24,32},{32,40},{40,48},{48,56},{56,64},{64,7... | collective-permute-start | bytes 98312 | tf_op jit(solution)/shard_map/ppermute | solution.py:24
  97.3 2.0 %collective-permute-start.8 = (bf16[3072,512]{1,0:T(8,128)(2,1)}, bf16[3072,512]{1,0:T(8,128)(2,1)S(1)}, u32[]{:S(2)}, u32[]{:S(2)}) collective-permute-start(bf16[3072,512]{1,0:T(8,128)(2,1)} %bitcast.66), channel_id=1, source_target_pairs={{0,8},{8,0},{1,9},{9,1},{2,10},{10,2},{3,11},{11,3},{4,12},{12,4},... | collective-permute-start | bytes 9437192 | tf_op jit(solution)/shard_map/ppermute | solution.py:209
  99.4 1.9 %copy-done.1 = bf16[64,48,512]{2,1,0:T(8,128)(2,1)S(1)} copy-done((bf16[64,48,512]{2,1,0:T(8,128)(2,1)S(1)}, bf16[64,48,512]{2,1,0:T(8,128)(2,1)}, u32[]{:S(2)}) %copy-start.1) | copy-done | bytes 3145752
  101.3 2.7 %shard_map.130 = (bf16[256,128]{1,0:T(8,128)(2,1)S(1)}, bf16[256,128]{1,0:T(8,128)(2,1)S(1)}, f32[128,256]{1,0:T(8,128)S(1)}) custom-call(bf16[3072,512]{1,0:T(8,128)(2,1)S(1)} %bitcast.67, bf16[3072,128]{1,0:T(8,128)(2,1)S(1)} %bitcast.71, bf16[3072,128]{1,0:T(8,128)(2,1)S(1)} %bitcast.74, bf16[128,128]{1,0:T(8,128)(2,1)S(1)} %convolution_convert_fusion.kv, ...), custom_call_target="tpu_custom_call" | custom-call | flops 100000000 | bytes 5177344 | tf_op jit(solution)/shard_map/pallas_call | solution.py:131
  104.0 1.1 collective-permute-done.8.weight.oth
  105.1 1.7 %copy-done.6 = bf16[8,4,2,48,128]{4,3,2,1,0:T(8,128)(2,1)S(1)} copy-done((bf16[8,4,2,48,128]{4,3,2,1,0:T(8,128)(2,1)S(1)}, bf16[8,4,2,48,128]{4,3,2,1,0:T(8,128)(2,1)}, u32[]{:S(2)}) %copy-start.6) | copy-done | bytes 786456
  106.8 1.1 copy-done.9
  107.9 2.9 %shard_map.131 = (bf16[256,128]{1,0:T(8,128)(2,1)S(1)}, bf16[256,128]{1,0:T(8,128)(2,1)S(1)}, bf16[128,128]{1,0:T(8,128)(2,1)S(1)}, f32[128,128]{1,0:T(8,128)S(1)}) custom-call(bf16[3072,512]{1,0:T(8,128)(2,1)S(1)} %collective-permute-done.8.weight.oth, bf16[3072,128]{1,0:T(8,128)(2,1)S(1)} %bitcast.72, bf16[3072,128]{1,0:T(8,128)(2,1)S(1)} %bitcast.75, ...), custom_call_target="tpu_custom_call" | custom-call | flops 100000000 | bytes 5275648 | tf_op jit(solution)/shard_map/pallas_call | solution.py:131
  114.0 4.4 %all-to-all-start.2 = ((bf16[8,384,128]{2,1,0:T(8,128)(2,1)}), bf16[8,384,128]{2,1,0:T(8,128)(2,1)}, u32[]{:S(2)}, u32[]{:S(2)}) async-start(bf16[8,384,128]{2,1,0:T(8,128)(2,1)} %copy-done.13), calls=%async_computation.2 | async-start | bytes 1572864 | tf_op jit(solution)/shard_map/all_to_all | solution.py:224
  118.3 2.3 %collective-permute-start.9 = (bf16[128,128]{1,0:T(8,128)(2,1)S(1)}, bf16[128,128]{1,0:T(8,128)(2,1)S(1)}, u32[]{:S(2)}, u32[]{:S(2)}) collective-permute-start(bf16[128,128]{1,0:T(8,128)(2,1)S(1)} %get-tuple-element.33), channel_id=1, source_target_pairs={{8,0},{16,8},{24,16},{32,24},{40,32},{48,40},{56,48},{64,56},{72,6... | collective-permute-start | bytes 98312 | tf_op jit(solution)/shard_map/ppermute | solution.py:24
  120.7 4.2 %collective-permute-done.9.returned = bf16[128,128]{1,0:T(8,128)(2,1)S(1)} collective-permute-done((bf16[128,128]{1,0:T(8,128)(2,1)S(1)}, bf16[128,128]{1,0:T(8,128)(2,1)S(1)}, u32[]{:S(2)}, u32[]{:S(2)}) %collective-permute-start.9) | collective-permute-done | bytes 32800 | tf_op jit(solution)/shard_map/ppermute | solution.py:24
  124.8 1.9 %copy-done.4 = bf16[3072,512]{1,0:T(8,128)(2,1)S(1)} copy-done((bf16[3072,512]{1,0:T(8,128)(2,1)S(1)}, bf16[3072,512]{1,0:T(8,128)(2,1)}, u32[]{:S(2)}) %copy-start.4) | copy-done | bytes 3145752
  126.7 1.1 copy-done.7
  127.9 1.1 copy-done.11
  129.0 1.3 shard_map.133
  131.2 5.6 %all-to-all-start.3 = ((bf16[8,400,128]{2,1,0:T(8,128)(2,1)}), bf16[8,400,128]{2,1,0:T(8,128)(2,1)S(1)}, u32[]{:S(2)}, u32[]{:S(2)}) async-start(bf16[8,400,128]{2,1,0:T(8,128)(2,1)} %copy-done.12), calls=%async_computation.3 | async-start | bytes 1638400 | tf_op jit(solution)/shard_map/all_to_all | solution.py:231
  137.6 1.3 convert_reduce_fusion.1
  139.9 9.9 %all-to-all-done.3 = bf16[8,400,128]{2,1,0:T(8,128)(2,1)S(1)} async-done(((bf16[8,400,128]{2,1,0:T(8,128)(2,1)}), bf16[8,400,128]{2,1,0:T(8,128)(2,1)S(1)}, u32[]{:S(2)}, u32[]{:S(2)}) %all-to-all-start.3) | async-done | bytes 819232 | tf_op jit(solution)/shard_map/all_to_all | solution.py:231
  (121 shorter events, 16.7 us)
Async XLA Ops:
  7.2 129.8 %copy-start = (bf16[16,2880]{1,0:T(8,128)(2,1)S(1)}, bf16[16,2880]{1,0:T(8,128)(2,1)}, u32[]{:S(2)}) copy-start(bf16[16,2880]{1,0:T(8,128)(2,1)} %param.18) | copy-start | bytes 276484
  7.2 90.1 %all-gather.2.cloned.1.call-start = ((), (), s32[]{:S(2)}) async-start(), calls=%async_computation.4 | async-start | bytes 3538944 | tf_op jit(solution)/shard_map/all_gather | solution.py:169
  9.8 26.5 %copy-start.18 = (bf16[128,2880]{0,1:T(8,128)(2,1)S(1)}, bf16[128,2880]{0,1:T(8,128)(2,1)}, u32[]{:S(2)}) copy-start(bf16[128,2880]{0,1:T(8,128)(2,1)} %param.11) | copy-start | bytes 2211844
  10.4 26.4 %copy-start.22 = (f32[2880]{0:T(1024)S(1)}, f32[2880]{0:T(1024)}, u32[]{:S(2)}) copy-start(f32[2880]{0:T(1024)} %param.17) | copy-start | bytes 34564
  10.4 26.4 %copy-start.23 = (f32[2880]{0:T(1024)S(1)}, f32[2880]{0:T(1024)}, u32[]{:S(2)}) copy-start(f32[2880]{0:T(1024)} %param.12) | copy-start | bytes 34564
  36.8 9.3 %copy-start.20 = (bf16[128,2880]{0,1:T(8,128)(2,1)S(1)}, bf16[128,2880]{0,1:T(8,128)(2,1)}, u32[]{:S(2)}) copy-start(bf16[128,2880]{0,1:T(8,128)(2,1)} %param.21) | copy-start | bytes 2211844
  36.8 9.3 %copy-start.25 = (s32[128]{0:T(128)S(1)}, s32[128]{0:T(128)}, u32[]{:S(2)}) copy-start(s32[128]{0:T(128)} %param.20) | copy-start | bytes 1540
  36.8 18.0 %copy-start.28 = (s32[128]{0:T(128)S(1)}, s32[128]{0:T(128)}, u32[]{:S(2)}) copy-start(s32[128]{0:T(128)} %param.19) | copy-start | bytes 1540
  38.3 24.8 %copy-start.26 = (f32[128]{0:T(128)}, f32[128]{0:T(128)S(1)}, u32[]{:S(2)}) copy-start(f32[128]{0:T(128)S(1)} %get-tuple-element.37) | copy-start | bytes 1540
  38.3 24.8 %copy-start.29 = (f32[128]{0:T(128)}, f32[128]{0:T(128)S(1)}, u32[]{:S(2)}) copy-start(f32[128]{0:T(128)S(1)} %add_divide_fusion) | copy-start | bytes 1540
  39.2 47.6 %all-to-all-start.1 = ((bf16[8,8,24,128]{3,2,1,0:T(8,128)(2,1)}), bf16[8,8,24,128]{3,2,1,0:T(8,128)(2,1)S(1)}, u32[]{:S(2)}, u32[]{:S(2)}) async-start(bf16[8,8,24,128]{3,2,1,0:T(8,128)(2,1)} %broadcast_in_dim.13), calls=%async_computation.1 | async-start | bytes 786432 | tf_op jit(solution)/shard_map/all_to_all | solution.py:30
  46.3 6.6 %collective-permute-start.2 = (f32[16,360]{1,0:T(8,128)S(1)}, f32[16,360]{1,0:T(8,128)S(1)}, u32[]{:S(2)}, u32[]{:S(2)}) collective-permute-start(f32[16,360]{1,0:T(8,128)S(1)} %fusion.10), channel_id=1, source_target_pairs={{0,8},{8,0},{1,9},{9,1},{2,10},{10,2},{3,11},{11,3},{4,12},{12,4},... | collective-permute-start | bytes 69128 | tf_op jit(solution)/shard_map/ppermute | solution.py:194
  52.9 6.1 %collective-permute-start.3 = (f32[16,360]{1,0:T(8,128)S(1)}, f32[16,360]{1,0:T(8,128)S(1)}, u32[]{:S(2)}, u32[]{:S(2)}) collective-permute-start(f32[16,360]{1,0:T(8,128)S(1)} %add.96), channel_id=1, source_target_pairs={{0,128},{128,0},{256,384},{384,256},{1,129},{129,1},{257,385},{385... | collective-permute-start | bytes 69128 | tf_op jit(solution)/shard_map/ppermute | solution.py:194
  54.8 16.4 %collective-permute-start.1 = (s32[128]{0:T(128)S(1)}, s32[128]{0:T(128)S(1)}, u32[]{:S(2)}, u32[]{:S(2)}) collective-permute-start(s32[128]{0:T(128)S(1)} %copy-done.28), channel_id=1, source_target_pairs={{0,8},{8,16},{16,24},{24,32},{32,40},{40,48},{48,56},{56,64},{64,7... | collective-permute-start | bytes 1544 | tf_op jit(solution)/shard_map/ppermute | solution.py:24
  59.0 8.5 %collective-permute-start.4 = (f32[16,360]{1,0:T(8,128)S(1)}, f32[16,360]{1,0:T(8,128)S(1)}, u32[]{:S(2)}, u32[]{:S(2)}) collective-permute-start(f32[16,360]{1,0:T(8,128)S(1)} %add.97), channel_id=1, source_target_pairs={{0,256},{128,384},{256,0},{384,128},{1,257},{129,385},{257,1},{385... | collective-permute-start | bytes 69128 | tf_op jit(solution)/shard_map/ppermute | solution.py:194
  63.6 35.8 %copy-start.5 = (bf16[8,4,2,48,128]{4,3,2,1,0:T(8,128)(2,1)}, bf16[8,4,2,48,128]{4,3,2,1,0:T(8,128)(2,1)S(1)}, u32[]{:S(2)}) copy-start(bf16[8,4,2,48,128]{4,3,2,1,0:T(8,128)(2,1)S(1)} %pad.21.clone) | copy-start | bytes 2359300
  64.0 35.3 %copy-start.8 = (bf16[8,4,2,48,128]{4,3,2,1,0:T(8,128)(2,1)}, bf16[8,4,2,48,128]{4,3,2,1,0:T(8,128)(2,1)S(1)}, u32[]{:S(2)}) copy-start(bf16[8,4,2,48,128]{4,3,2,1,0:T(8,128)(2,1)S(1)} %pad.22.clone) | copy-start | bytes 2359300
  67.5 5.6 %collective-permute-start.5 = (f32[16,360]{1,0:T(8,128)S(1)}, f32[16,360]{1,0:T(8,128)S(1)}, u32[]{:S(2)}, u32[]{:S(2)}) collective-permute-start(f32[16,360]{1,0:T(8,128)S(1)} %add.98), channel_id=1, source_target_pairs={{0,16},{16,0},{32,48},{48,32},{64,80},{80,64},{96,112},{112,96},{1... | collective-permute-start | bytes 69128 | tf_op jit(solution)/shard_map/ppermute | solution.py:194
  73.0 6.2 %collective-permute-start.6 = (f32[16,360]{1,0:T(8,128)S(1)}, f32[16,360]{1,0:T(8,128)S(1)}, u32[]{:S(2)}, u32[]{:S(2)}) collective-permute-start(f32[16,360]{1,0:T(8,128)S(1)} %add.99), channel_id=1, source_target_pairs={{0,32},{16,48},{32,0},{48,16},{64,96},{80,112},{96,64},{112,80},{1... | collective-permute-start | bytes 69128 | tf_op jit(solution)/shard_map/ppermute | solution.py:194
  79.2 17.2 %collective-permute-start.7 = (f32[16,360]{1,0:T(8,128)S(1)}, f32[16,360]{1,0:T(8,128)S(1)}, u32[]{:S(2)}, u32[]{:S(2)}) collective-permute-start(f32[16,360]{1,0:T(8,128)S(1)} %add.100), channel_id=1, source_target_pairs={{0,64},{16,80},{32,96},{48,112},{64,0},{80,16},{96,32},{112,48},{1... | collective-permute-start | bytes 69128 | tf_op jit(solution)/shard_map/ppermute | solution.py:194
  94.2 3.1 %collective-permute-start = (bf16[128,128]{1,0:T(8,128)(2,1)S(1)}, bf16[128,128]{1,0:T(8,128)(2,1)S(1)}, u32[]{:S(2)}, u32[]{:S(2)}) collective-permute-start(bf16[128,128]{1,0:T(8,128)(2,1)S(1)} %convolution_convert_fusion.kv), channel_id=1, source_target_pairs={{0,8},{8,16},{16,24},{24,32},{32,40},{40,48},{48,56},{56,64},{64,7... | collective-permute-start | bytes 98312 | tf_op jit(solution)/shard_map/ppermute | solution.py:24
  97.3 7.8 %collective-permute-start.8 = (bf16[3072,512]{1,0:T(8,128)(2,1)}, bf16[3072,512]{1,0:T(8,128)(2,1)S(1)}, u32[]{:S(2)}, u32[]{:S(2)}) collective-permute-start(bf16[3072,512]{1,0:T(8,128)(2,1)} %bitcast.66), channel_id=1, source_target_pairs={{0,8},{8,0},{1,9},{9,1},{2,10},{10,2},{3,11},{11,3},{4,12},{12,4},... | collective-permute-start | bytes 9437192 | tf_op jit(solution)/shard_map/ppermute | solution.py:209
  105.1 7.0 %copy-start.3 = (bf16[3072,512]{1,0:T(8,128)(2,1)}, bf16[3072,512]{1,0:T(8,128)(2,1)S(1)}, u32[]{:S(2)}) copy-start(bf16[3072,512]{1,0:T(8,128)(2,1)S(1)} %collective-permute-done.8.weight.oth) | copy-start | bytes 9437188
  114.0 10.9 %copy-start.15 = (bf16[256,128]{1,0:T(8,128)(2,1)S(1)}, bf16[256,128]{1,0:T(8,128)(2,1)}, u32[]{:S(2)}) copy-start(bf16[256,128]{1,0:T(8,128)(2,1)} %copy-done.14) | copy-start | bytes 196612
  114.0 10.9 %copy-start.17 = (f32[128,128]{1,0:T(8,128)S(1)}, f32[128,128]{1,0:T(8,128)}, u32[]{:S(2)}) copy-start(f32[128,128]{1,0:T(8,128)} %copy-done.16) | copy-start | bytes 196612
  114.0 17.2 %all-to-all-start.2 = ((bf16[8,384,128]{2,1,0:T(8,128)(2,1)}), bf16[8,384,128]{2,1,0:T(8,128)(2,1)}, u32[]{:S(2)}, u32[]{:S(2)}) async-start(bf16[8,384,128]{2,1,0:T(8,128)(2,1)} %copy-done.13), calls=%async_computation.2 | async-start | bytes 1572864 | tf_op jit(solution)/shard_map/all_to_all | solution.py:224
  118.3 6.5 %collective-permute-start.9 = (bf16[128,128]{1,0:T(8,128)(2,1)S(1)}, bf16[128,128]{1,0:T(8,128)(2,1)S(1)}, u32[]{:S(2)}, u32[]{:S(2)}) collective-permute-start(bf16[128,128]{1,0:T(8,128)(2,1)S(1)} %get-tuple-element.33), channel_id=1, source_target_pairs={{8,0},{16,8},{24,16},{32,24},{40,32},{48,40},{56,48},{64,56},{72,6... | collective-permute-start | bytes 98312 | tf_op jit(solution)/shard_map/ppermute | solution.py:24
  131.2 5.6 %copy-start.24 = (f32[2880]{0:T(1024)S(1)}, f32[2880]{0:T(1024)}, u32[]{:S(2)}) copy-start(f32[2880]{0:T(1024)} %param.12) | copy-start | bytes 34564
  131.2 5.8 %copy-start.21 = (bf16[128,2880]{0,1:T(8,128)(2,1)S(1)}, bf16[128,2880]{0,1:T(8,128)(2,1)}, u32[]{:S(2)}) copy-start(bf16[128,2880]{0,1:T(8,128)(2,1)} %param.21) | copy-start | bytes 2211844
  131.2 6.0 %copy-start.19 = (bf16[128,2880]{0,1:T(8,128)(2,1)S(1)}, bf16[128,2880]{0,1:T(8,128)(2,1)}, u32[]{:S(2)}) copy-start(bf16[128,2880]{0,1:T(8,128)(2,1)} %param.11) | copy-start | bytes 2211844
  131.2 18.7 %all-to-all-start.3 = ((bf16[8,400,128]{2,1,0:T(8,128)(2,1)}), bf16[8,400,128]{2,1,0:T(8,128)(2,1)S(1)}, u32[]{:S(2)}, u32[]{:S(2)}) async-start(bf16[8,400,128]{2,1,0:T(8,128)(2,1)} %copy-done.12), calls=%async_computation.3 | async-start | bytes 1638400 | tf_op jit(solution)/shard_map/all_to_all | solution.py:231
  138.9 11.1 %copy-start.27 = (f32[128]{0:T(128)S(1)}, f32[128]{0:T(128)}, u32[]{:S(2)}) copy-start(f32[128]{0:T(128)} %copy-done.26) | copy-start | bytes 1540
  (13 other events, 19.0 us)
Sparse Core Ops, SparseCore 0:
  36.4 53.1 all-gather.1

commit v5 on v3

v5 whole, which is shorter than its diff:
```python
import functools

import jax
import jax.numpy as jnp
from jax import lax
from jax.experimental import pallas as pl
from jax.experimental.pallas import tpu as pltpu
from jax.sharding import Mesh, PartitionSpec as P

HD = 64
WIN = 128
EPSILON = 1e-05
HIGHEST = lax.Precision.HIGHEST
SEQ = ("zh", "y", "core")
HEAD = ("x", "zl")
F32 = jnp.float32
BF16 = jnp.bfloat16
PAD = 48


def shifted(value, by):
    count = lax.axis_size(SEQ)
    pairs = [(i, i + by) for i in range(count) if 0 <= i + by < count]
    return lax.ppermute(value, SEQ, pairs)


def gathered(value, axes):
    count = lax.axis_size(axes)
    spread = jnp.broadcast_to(value[None], (count,) + value.shape)
    return lax.all_to_all(spread, axes, 0, 0)


def dot(left, right, dims, **kw):
    return lax.dot_general(left, right, (dims, ((), ())), preferred_element_type=F32, **kw)


def blocked(rows):
    width = rows.shape[-1]
    parts = rows.reshape(4, 8, 2, -1, width).transpose(1, 2, 0, 3, 4)
    parts = jnp.pad(parts, ((0, 0), (0, 0), (0, 0), (0, PAD - parts.shape[3]), (0, 0)))
    return parts.reshape(-1, width)


def unpadded(rows, row_count):
    width = rows.shape[-1]
    return rows.reshape(8, PAD, width)[:, : row_count // 8].reshape(row_count, width)


def mm(left, right, left_dim, right_dim):
    dims = (((left_dim,), (right_dim,)), ((), ()))
    return lax.dot_general(left, right, dims, preferred_element_type=F32)


def pack_kernel(w_query, w_out, w_key, w_value, out):
    rows = w_query.shape[0]
    width = w_query.shape[1]
    out[...] = jnp.zeros(out.shape, BF16)
    for place in range(out.shape[0]):
        out[place, :rows, :width] = w_query[...]
        out[place, :rows, width : 2 * width] = w_out[...]
        out[place, :rows, 2 * width : 2 * width + HD] = w_key[...]
        out[place, :rows, 2 * width + HD :] = w_value[...]


def pieces():
    for group in range(8):
        for part in range(8):
            row = ((group % 2 * 8 + part) * 4 + group // 2) * PAD
            yield group, part * PAD, row


def attend_kernel(
    w_hbm, x_hbm, g_hbm, kv, halo, mask, blocks_hbm, grad_query, grad_halo, grad_kv, *scratch
):
    weight, normed, grads, blocks, sems, out_sems = scratch
    count = sems.shape[0]
    size = weight.shape[0] // count
    width = weight.shape[1] // 2
    copies = []
    for step in range(count):
        rows = pl.ds(step * size, size)
        trio = ((w_hbm, weight), (x_hbm, normed), (g_hbm, grads))
        copies.append(
            [
                pltpu.make_async_copy(a.at[rows, :], b.at[rows, :], sems.at[step, k])
                for k, (a, b) in enumerate(trio)
            ]
        )
        for copy in copies[-1]:
            copy.start()
    keys = jnp.concatenate([halo[:HD, :], kv[:HD, :]], axis=1)
    values = jnp.concatenate([halo[HD:, :], kv[HD:, :]], axis=1)
    allowed = mask[...] > 0.0
    query_sum = jnp.zeros((width, WIN), F32)
    grad_sum = jnp.zeros((width, WIN), F32)
    for step in range(count):
        for copy in copies[step]:
            copy.wait()
        rows = slice(step * size, (step + 1) * size)
        query_sum += mm(weight[rows, :width], normed[rows, :], 0, 0)
        grad_sum += mm(weight[rows, width:], grads[rows, :], 0, 0)
    query_all = query_sum.astype(BF16)
    grad_all = grad_sum.astype(BF16)
    grad_keys = grad_values = jnp.zeros((HD, 2 * WIN), F32)
    mixed = []
    for head in range(8):
        rows = slice(head * HD, (head + 1) * HD)
        query, grad = query_all[rows], grad_all[rows]
        scores = mm(keys, query, 0, 0) * HD**-0.5
        scores = jnp.where(allowed, scores, -jnp.inf)
        raised = jnp.exp(scores - jnp.max(scores, axis=0, keepdims=True))
        prob = raised / jnp.sum(raised, axis=0, keepdims=True)
        prob_b = prob.astype(BF16)
        mixed.append(mm(values, prob_b, 1, 0).astype(BF16))
        grad_values += mm(grad, prob_b, 1, 1)
        grad_prob = mm(values, grad, 0, 0)
        delta = jnp.sum(prob * grad_prob, axis=0, keepdims=True)
        grad_scores = (prob * (grad_prob - delta) * HD**-0.5).astype(BF16)
        grad_query[rows, :] = mm(keys, grad_scores, 1, 0).astype(BF16)
        grad_keys += mm(query, grad_scores, 1, 1)
    grad_halo[:HD, :] = grad_keys[:, :WIN].astype(BF16)
    grad_halo[HD:, :] = grad_values[:, :WIN].astype(BF16)
    grad_kv[:HD, :] = grad_keys[:, WIN:]
    grad_kv[HD:, :] = grad_values[:, WIN:]
    mixed = jnp.concatenate(mixed, axis=0)
    sent = []
    for group, place, row in pieces():
        term = mm(weight[row : row + PAD, width:], mixed, 1, 0)
        blocks[group, place : place + PAD, :] = term.astype(BF16)
        if place == 7 * PAD:
            copy = pltpu.make_async_copy(
                blocks.at[group], blocks_hbm.at[group], out_sems.at[group]
            )
            copy.start()
            sent.append(copy)
    for copy in sent:
        copy.wait()


def back_kernel(w_hbm, kv_hbm, x_hbm, grad_query, grad_kv, returned, blocks_hbm, *scratch):
    weight, kv_all, normed, blocks, sems, out_sems = scratch
    width = weight.shape[1]
    size = weight.shape[0] // 2
    copies = []
    for step in range(2):
        rows = pl.ds(step * size, size)
        copies.append(
            [
                pltpu.make_async_copy(
                    w_hbm.at[rows, pl.ds(0, width)], weight.at[rows, :], sems.at[step, 0]
                ),
                pltpu.make_async_copy(kv_hbm.at[rows, :], kv_all.at[rows, :], sems.at[step, 1]),
                pltpu.make_async_copy(x_hbm.at[rows, :], normed.at[rows, :], sems.at[step, 2]),
            ]
        )
        for copy in copies[-1]:
            copy.start()
    tokens_here = grad_kv.shape[1]
    kv_grad = (grad_kv[...] + returned[...].astype(F32)).astype(BF16)
    rows_sum = jnp.zeros((PAD, tokens_here), F32)
    ordered = sorted(pieces(), key=lambda piece: piece[2] >= size)
    ready = 0
    for group, place, row in ordered:
        if ready < 1 + (row >= size):
            for copy in copies[ready]:
                copy.wait()
            ready += 1
        term = mm(weight[row : row + PAD, :], grad_query[...], 1, 0)
        term = term + mm(kv_all[row : row + PAD, :], kv_grad, 1, 0)
        term = term.astype(BF16)
        blocks[group, place : place + PAD, :] = term
        rows_sum += term.astype(F32) * normed[row : row + PAD, :].astype(F32)
    total = jnp.sum(rows_sum, axis=0, keepdims=True)
    high = total.astype(BF16).astype(F32)
    mid = (total - high).astype(BF16).astype(F32)
    low = total - high - mid
    line = lax.broadcasted_iota(jnp.int32, (16, tokens_here), 0)
    extra = jnp.where(line == 0, high, jnp.where(line == 1, mid, jnp.where(line == 2, low, 0.0)))
    sent = []
    for group in range(8):
        blocks[group, 8 * PAD :, :] = extra.astype(BF16)
        copy = pltpu.make_async_copy(blocks.at[group], blocks_hbm.at[group], out_sems.at[group])
        copy.start()
        sent.append(copy)
    for copy in sent:
        copy.wait()


ANY = pl.BlockSpec(memory_space=pltpu.MemorySpace.HBM)
FULL = pl.BlockSpec(memory_space=pltpu.MemorySpace.VMEM)


def call(kernel, outs, in_specs, out_specs, scratch, *args):
    size = sum(a.size * a.dtype.itemsize for a in jax.tree.leaves((args, outs)))
    return pl.pallas_call(
        kernel,
        out_shape=outs,
        in_specs=in_specs,
        out_specs=out_specs,
        scratch_shapes=scratch,
        compiler_params=pltpu.CompilerParams(vmem_limit_bytes=58 * 2**20),
        cost_estimate=pl.CostEstimate(flops=10**8, bytes_accessed=size, transcendentals=0),
    )(*args)


def shards(
    tokens,
    gain,
    w_query,
    w_key,
    w_value,
    w_out,
    w_gate,
    steering,
    segment_ids,
    steer_index,
    grad_out,
):
    row_count, model_width = tokens.shape
    share = model_width // 8
    start = lax.axis_index(HEAD) * share

    width = w_query.shape[1]
    like = jax.ShapeDtypeStruct
    sent = call(
        pack_kernel,
        like((4, PAD, 2 * width + 2 * HD), BF16),
        [FULL] * 4,
        FULL,
        [],
        *(w_query, w_out, w_key, w_value),
    )
    near = lax.all_to_all(sent, "zh", 0, 0)
    whole = lax.all_gather(near[:, :, : 2 * width], ("y", "core"), axis=0, tiled=True)
    whole = whole.reshape(-1, 2 * width)
    kv_near = gathered(near[:, :, 2 * width :], ("y",))
    kv_all = lax.all_gather(kv_near[:, None], "core", axis=1, tiled=True).reshape(-1, 2 * HD)

    tok = tokens.T.astype(F32)
    inverse = lax.rsqrt(jnp.mean(tok * tok, axis=0, keepdims=True) + EPSILON)
    unit = tok * inverse
    normed = (unit * gain[:, None]).astype(BF16)
    normed_b = blocked(normed)
    grad_t = grad_out.T
    grad_b = blocked(grad_t)
    gate = jax.nn.sigmoid(jnp.sum(normed.astype(F32) * w_gate[:, None], axis=0))
    one_hot = steer_index[None, :] == lax.broadcasted_iota(jnp.int32, (16, row_count), 0)
    products = dot(steering, grad_t, ((1,), (0,)))
    grad_logit = gate * (1.0 - gate) * jnp.sum(jnp.where(one_hot, products, 0.0), axis=0)
    steer_share = lax.dynamic_slice_in_dim(steering, start, share, 1)
    steer_rows = dot(steer_share, one_hot.astype(BF16), ((0,), (0,)))
    grad_share = lax.dynamic_slice_in_dim(grad_t, start, share, 0).astype(F32)
    steer_part = dot(
        one_hot.astype(F32), gate[None, :] * grad_share, ((1,), (1,)), precision=HIGHEST
    )

    def exchanged(value, *steps):
        for axis, step in steps:
            pairs = [(i, i ^ step) for i in range(lax.axis_size(axis))]
            value = value + lax.ppermute(value, axis, pairs)
        return value

    steer = exchanged(steer_part, ("core", 1), ("zh", 1))

    halo_seg = shifted(segment_ids, 1)
    halo_seg = jnp.where(lax.axis_index(SEQ) > 0, halo_seg, -1)
    kv = dot(kv_all, normed_b, ((0,), (0,))).astype(BF16)
    halo = shifted(kv, 1)
    wide_seg = jnp.concatenate([halo_seg, segment_ids])
    key_pos = lax.broadcasted_iota(jnp.int32, (2 * row_count, row_count), 0) - WIN
    query_pos = lax.broadcasted_iota(jnp.int32, (2 * row_count, row_count), 1)
    distance = query_pos - key_pos
    mask = (distance >= 0) & (distance < WIN) & (wide_seg[:, None] == segment_ids[None, :])
    mask = mask.astype(F32)
    steer, halo, kv, mask = lax.optimization_barrier((steer, halo, kv, mask))
    steer = exchanged(steer, ("zh", 2), ("y", 1))
    whole, halo, mask, steer, normed_b, grad_b, kv, kv_all = lax.optimization_barrier(
        (whole, halo, mask, steer, normed_b, grad_b, kv, kv_all)
    )
    total_rows = whole.shape[0]
    dma = pltpu.SemaphoreType.DMA
    blocks, grad_query, grad_halo, grad_kv = call(
        attend_kernel,
        (
            like((8, 8 * PAD, row_count), BF16),
            like((width, row_count), BF16),
            like((2 * HD, row_count), BF16),
            like((2 * HD, row_count), F32),
        ),
        [ANY, ANY, ANY, FULL, FULL, FULL],
        [ANY, FULL, FULL, FULL],
        [
            pltpu.VMEM((total_rows, 2 * width), BF16),
            pltpu.VMEM((total_rows, row_count), BF16),
            pltpu.VMEM((total_rows, row_count), BF16),
            pltpu.VMEM((8, 8 * PAD, row_count), BF16),
            dma((6, 3)),
            dma((8,)),
        ],
        *(whole, normed_b, grad_b, kv, halo, mask),
    )
    returned = shifted(grad_halo, -1)
    attn = lax.all_to_all(blocks, HEAD, 0, 0)
    back = call(
        back_kernel,
        like((8, 8 * PAD + 16, row_count), BF16),
        [ANY, ANY, ANY, FULL, FULL, FULL],
        ANY,
        [
            pltpu.VMEM((total_rows, width), BF16),
            pltpu.VMEM((total_rows, 2 * HD), BF16),
            pltpu.VMEM((total_rows, row_count), BF16),
            pltpu.VMEM((8, 8 * PAD + 16, row_count), BF16),
            dma((2, 3)),
            dma((8,)),
        ],
        *(whole, kv_all, normed_b, grad_query, grad_kv, returned),
    )
    steer, back = lax.optimization_barrier((steer, back))
    steer_grad = exchanged(steer, ("y", 2), ("y", 4))
    back = lax.all_to_all(back, HEAD, 0, 0)

    attn_share = unpadded(jnp.sum(attn.astype(F32), axis=0), share)
    token_share = lax.dynamic_slice_in_dim(tokens.T, start, share, 0).astype(F32)
    layer_out = (token_share + attn_share + gate[None, :] * steer_rows).astype(BF16)
    back = jnp.sum(back.astype(F32), axis=0)
    gain_share = lax.dynamic_slice_in_dim(gain, start, share, 0)[:, None]
    gate_share = lax.dynamic_slice_in_dim(w_gate, start, share, 0)[:, None]
    total = unpadded(back[: 8 * PAD], share) + grad_logit[None, :] * gate_share
    gate_total = jnp.sum(unit * (gain * w_gate)[:, None], axis=0)
    row_total = jnp.sum(back[8 * PAD : 8 * PAD + 3], axis=0) + grad_logit * gate_total
    unit_share = token_share * inverse
    scaled = total * gain_share
    grad_tokens = (
        grad_share + inverse * (scaled - unit_share * (row_total / model_width)[None, :])
    ).astype(BF16)
    return (layer_out.T, grad_tokens.T, steer_grad)


def solution(mesh):
    split = Mesh(mesh.devices.reshape(4, 8, 2, 4, 2), SEQ + HEAD)
    placed = (
        P(SEQ, None),
        P(),
        P(SEQ, HEAD),
        P(SEQ, HEAD),
        P(SEQ, HEAD),
        P(SEQ, HEAD),
        P(),
        P(),
        P(SEQ),
        P(SEQ),
        P(SEQ, None),
    )
    return jax.shard_map(
        shards,
        mesh=split,
        in_specs=placed,
        out_specs=(P(SEQ, HEAD), P(SEQ, HEAD), P(None, HEAD)),
        check_vma=False,
    )
```

time: 167 us -> 148 us (0.89); the launches traced: 166 us -> 145 us
  blocking collectives: 59.4 us -> 28.9 us
  starting transfers between devices: 34.9 us -> 49.9 us
  local copies, waits for them, and re-layouts: 18.3 us -> 5.24 us
  Pallas kernels: 7.84 us -> 18.3 us
  waiting for transfers between devices: 21.7 us -> 18 us
    all_gather x2 -> x1, blocking collectives: 34.3 us -> 6.24 us  [shards(): lax.all_gather(kv_near[:, None], 'core', axis=1, tiled=True)]
    ppermute x1 -> x6, starting transfers between devices: 1.91 us -> 23.7 us  [exchanged(): value = value + lax.ppermute(value, axis, pairs)]
    unnamed x68 -> x35, local copies, waits for them, and re-layouts: 14.3 us -> 0.77 us
    pallas_call x4 -> x3, Pallas kernels: 7.84 us -> 18.3 us  [call(): pl.pallas_call(kernel, out_shape=outs, in_specs=in_specs, out_specs=out_s...]
    all_to_all x1, waiting for transfers between devices: 9.93 us -> 0.01 us  [shards(): back = lax.all_to_all(back, HEAD, 0, 0)]
    ppermute x1 -> x6, waiting for transfers between devices: 2.89 us -> 10.1 us  [exchanged(): value = value + lax.ppermute(value, axis, pairs)]
    all_to_all x2 -> x1, starting transfers between devices: 13.7 us -> 6.82 us  [gathered(): return lax.all_to_all(spread, axes, 0, 0)]
    all_to_all x2 -> x1, waiting for transfers between devices: 4.52 us -> 0.01 us  [gathered(): return lax.all_to_all(spread, axes, 0, 0)]
  transfers between devices with their start and end apart: 9 -> 13, of which waited for: 5 -> 7; matrix products, arithmetic and copies ran while one was open for 5% -> 9% of each run, Pallas kernels for 1% -> 4%
where the time goes in v5:
time: 148 us; the launch traced here: 145 us
  starting transfers between devices  49.9 us (34%)
  blocking collectives  28.9 us (20%)
  Pallas kernels  18.3 us (12%)
  waiting for transfers between devices  18 us (12%)
  between operations  14.5 us (10%)
  other arithmetic  8.19 us (6%)
  local copies, waits for them, and re-layouts  5.24 us (4%)
  matrix products  2.44 us (2%)
    ppermute x6, starting transfers between devices, exchanged(): value = value + lax.ppermute(value, axis, pairs)  23.7 us
    all_to_all x1, blocking collectives, shards(): near = lax.all_to_all(sent, 'zh', 0, 0)  22.7 us
    pallas_call x3, Pallas kernels, call(): pl.pallas_call(kernel, out_shape=outs, in_specs=in_specs, out_specs=out_s...  18.3 us
    ppermute x6, waiting for transfers between devices, exchanged(): value = value + lax.ppermute(value, axis, pairs)  10.1 us
    ppermute x3, starting transfers between devices, shifted(): return lax.ppermute(value, SEQ, pairs)  8.53 us
    all_to_all x1, starting transfers between devices, gathered(): return lax.all_to_all(spread, axes, 0, 0)  6.82 us
    all_to_all x1, starting transfers between devices, shards(): attn = lax.all_to_all(blocks, HEAD, 0, 0)  6.38 us
    all_gather x1, blocking collectives, shards(): lax.all_gather(kv_near[:, None], 'core', axis=1, tiled=True)  6.24 us
  transfers between devices with their start and end apart: 13, of which 7 were waited for; matrix products, arithmetic and copies ran while one was open for 9% of the time, Pallas kernels for 4%

profile of v5, /device:TPU:1, one launch (start us, length us, event | category | flops | bytes accessed | tf_op | source)
XLA Modules:
  0.0 145.4 jit_solution(4175187482406055886)
XLA Ops:
  7.2 1.8 %shard_map.130 = bf16[4,48,1152]{2,1,0:T(8,128)(2,1)} custom-call(bf16[45,512]{1,0:T(8,128)(2,1)} %w_query.1, bf16[45,512]{1,0:T(8,128)(2,1)} %w_out.1, bf16[45,64]{1,0:T(8,128)(2,1)} %w_key.1, bf16[45,64]{1,0:T(8,128)(2,1)} %w_value.1), custom_call_target="tpu_custom_call" | custom-call | flops 100000000 | bytes 546048 | tf_op jit(solution)/shard_map/pallas_call | solution.py:195
  9.0 22.7 %all_to_all.20 = bf16[4,48,1152]{2,1,0:T(8,128)(2,1)S(1)} all-to-all(bf16[4,48,1152]{2,1,0:T(8,128)(2,1)} %shard_map.130), channel_id=1, replica_groups=mesh['zh'=4,'y'=8,'core'=2,'x'=4,'zl'=2] {'zh'}, dimensions={0} | all-to-all | bytes 884736 | tf_op jit(solution)/shard_map/all_to_all | solution.py:233
  31.7 0.8 slice.24
  33.0 1.5 %multiply_reduce_fusion = (f32[128]{0:T(128)S(1)}, bf16[2880,128]{1,0:T(8,128)(2,1)S(1)}) fusion(f32[2880]{0:T(1024)S(1)} %copy-done.4, f32[2880]{0:T(1024)S(1)} %copy-done.5, f32[128]{0:T(128)S(1)} %add_rsqrt_fusion, bf16[128,2880]{0,1:T(8,128)(2,1)S(1)} %copy-done.1), kind=kLoop, calls=%fused_computation.9 | loop fusion | flops 2580352 | bytes 1498624 | tf_op jit(solution)/shard_map/reduce_sum | solution.py:246
  34.5 0.8 broadcast_in_dim.11
  35.3 6.8 %all-to-all-start.1 = ((bf16[8,4,48,128]{3,2,1,0:T(8,128)(2,1)}), bf16[8,4,48,128]{3,2,1,0:T(8,128)(2,1)S(1)}, u32[]{:S(2)}, u32[]{:S(2)}) async-start(bf16[8,4,48,128]{3,2,1,0:T(8,128)(2,1)} %broadcast_in_dim.11), calls=%async_computation.1 | async-start | bytes 786432 | tf_op jit(solution)/shard_map/all_to_all | solution.py:30
  42.2 0.9 fusion.11
  43.1 7.0 %collective-permute-start = (f32[16,360]{1,0:T(8,128)}, f32[16,360]{1,0:T(8,128)}, u32[]{:S(2)}, u32[]{:S(2)}) collective-permute-start(f32[16,360]{1,0:T(8,128)} %fusion.11), channel_id=1, source_target_pairs={{0,8},{8,0},{1,9},{9,1},{2,10},{10,2},{3,11},{11,3},{4,12},{12,4},... | collective-permute-start | bytes 69128 | tf_op jit(solution)/shard_map/ppermute | solution.py:260
  50.1 3.5 %collective-permute-start.3 = (s32[128]{0:T(128)}, s32[128]{0:T(128)}, u32[]{:S(2)}, u32[]{:S(2)}) collective-permute-start(s32[128]{0:T(128)} %param.19), channel_id=1, source_target_pairs={{0,8},{8,16},{16,24},{24,32},{32,40},{40,48},{48,56},{56,64},{64,7... | collective-permute-start | bytes 1544 | tf_op jit(solution)/shard_map/ppermute | solution.py:24
  56.7 2.3 %collective-permute-start.1 = (f32[16,360]{1,0:T(8,128)S(1)}, f32[16,360]{1,0:T(8,128)S(1)}, u32[]{:S(2)}, u32[]{:S(2)}) collective-permute-start(f32[16,360]{1,0:T(8,128)S(1)} %add.88), channel_id=1, source_target_pairs={{0,128},{128,0},{256,384},{384,256},{1,129},{129,1},{257,385},{385... | collective-permute-start | bytes 69128 | tf_op jit(solution)/shard_map/ppermute | solution.py:260
  59.0 6.2 %all-gather = bf16[8,8,48,128]{3,2,1,0:T(8,128)(2,1)S(1)} all-gather(bf16[8,4,48,128]{3,2,1,0:T(8,128)(2,1)S(1)} %all-to-all-done.1), channel_id=2, replica_groups=mesh['zh'=4,'y'=8,'core'=2,'x'=4,'zl'=2] {'core'}, dimensions={1}, use_global_device_ids=true | all-gather | bytes 1179648 | tf_op jit(solution)/shard_map/all_gather | solution.py:237
  65.7 2.5 %collective-permute-start.2 = (bf16[128,128]{1,0:T(8,128)(2,1)S(1)}, bf16[128,128]{1,0:T(8,128)(2,1)S(1)}, u32[]{:S(2)}, u32[]{:S(2)}) collective-permute-start(bf16[128,128]{1,0:T(8,128)(2,1)S(1)} %fusion.8.kv), channel_id=1, source_target_pairs={{0,8},{8,16},{16,24},{24,32},{32,40},{40,48},{48,56},{56,64},{64,7... | collective-permute-start | bytes 98312 | tf_op jit(solution)/shard_map/ppermute | solution.py:24
  68.2 1.4 fusion.20.mask
  69.7 3.2 %collective-permute-start.4 = (f32[16,360]{1,0:T(8,128)S(1)}, f32[16,360]{1,0:T(8,128)S(1)}, u32[]{:S(2)}, u32[]{:S(2)}) collective-permute-start(f32[16,360]{1,0:T(8,128)S(1)} %add.89), channel_id=1, source_target_pairs={{0,256},{128,384},{256,0},{384,128},{1,257},{129,385},{257,1},{385... | collective-permute-start | bytes 69128 | tf_op jit(solution)/shard_map/ppermute | solution.py:260
  72.9 5.2 %collective-permute-done.4 = f32[16,360]{1,0:T(8,128)S(1)} collective-permute-done((f32[16,360]{1,0:T(8,128)S(1)}, f32[16,360]{1,0:T(8,128)S(1)}, u32[]{:S(2)}, u32[]{:S(2)}) %collective-permute-start.4) | collective-permute-done | bytes 23072 | tf_op jit(solution)/shard_map/ppermute | solution.py:260
  78.2 1.9 %collective-permute-start.5 = (f32[16,360]{1,0:T(8,128)S(1)}, f32[16,360]{1,0:T(8,128)S(1)}, u32[]{:S(2)}, u32[]{:S(2)}) collective-permute-start(f32[16,360]{1,0:T(8,128)S(1)} %add.92), channel_id=1, source_target_pairs={{0,16},{16,0},{32,48},{48,32},{64,80},{80,64},{96,112},{112,96},{1... | collective-permute-start | bytes 69128 | tf_op jit(solution)/shard_map/ppermute | solution.py:260
  80.1 1.1 pad.7
  81.5 1.0 pad.8.clone
  83.2 4.1 %all-gather.3.cloned.1.call-done = bf16[64,48,1024]{2,1,0:T(8,128)(2,1)} async-done(((bf16[4,48,1024]{2,1,0:T(8,128)(2,1)}), bf16[64,48,1024]{2,1,0:T(8,128)(2,1)}) %all-gather.3.cloned.1.call-update) | async-done | bytes 6291472 | tf_op jit(solution)/shard_map/all_gather | solution.py:234
  87.3 11.0 %shard_map.131 = (bf16[8,384,128]{2,1,0:T(8,128)(2,1)}, bf16[512,128]{1,0:T(8,128)(2,1)}, bf16[128,128]{1,0:T(8,128)(2,1)}, f32[128,128]{1,0:T(8,128)}) custom-call(bf16[3072,1024]{1,0:T(8,128)(2,1)} %bitcast.53, bf16[3072,128]{1,0:T(8,128)(2,1)} %bitcast.55, bf16[3072,128]{1,0:T(8,128)(2,1)} %bitcast.63, bf16[128,128]{1,0:T(8,128)(2,1)} %copy-done.7, ...), custom_call_target="tpu_custom_call" | custom-call | flops 100000000 | bytes 9076736 | tf_op jit(solution)/shard_map/pallas_call | solution.py:195
  98.3 6.4 %all-to-all-start.2 = ((bf16[8,384,128]{2,1,0:T(8,128)(2,1)}), bf16[8,384,128]{2,1,0:T(8,128)(2,1)S(1)}, u32[]{:S(2)}, u32[]{:S(2)}) async-start(bf16[8,384,128]{2,1,0:T(8,128)(2,1)} %get-tuple-element.31), calls=%async_computation.2 | async-start | bytes 1572864 | tf_op jit(solution)/shard_map/all_to_all | solution.py:303
  104.7 2.4 %collective-permute-start.6 = (bf16[128,128]{1,0:T(8,128)(2,1)S(1)}, bf16[128,128]{1,0:T(8,128)(2,1)S(1)}, u32[]{:S(2)}, u32[]{:S(2)}) collective-permute-start(bf16[128,128]{1,0:T(8,128)(2,1)S(1)} %copy-done.16), channel_id=1, source_target_pairs={{8,0},{16,8},{24,16},{32,24},{40,32},{48,40},{56,48},{64,56},{72,6... | collective-permute-start | bytes 98312 | tf_op jit(solution)/shard_map/ppermute | solution.py:24
  107.1 3.1 %collective-permute-done.6.returned = bf16[128,128]{1,0:T(8,128)(2,1)S(1)} collective-permute-done((bf16[128,128]{1,0:T(8,128)(2,1)S(1)}, bf16[128,128]{1,0:T(8,128)(2,1)S(1)}, u32[]{:S(2)}, u32[]{:S(2)}) %collective-permute-start.6) | collective-permute-done | bytes 32800 | tf_op jit(solution)/shard_map/ppermute | solution.py:24
  110.8 5.5 %shard_map.132 = bf16[8,400,128]{2,1,0:T(8,128)(2,1)} custom-call(bf16[3072,1024]{1,0:T(8,128)(2,1)} %bitcast.54, bf16[3072,128]{1,0:T(8,128)(2,1)} %bitcast.59, bf16[3072,128]{1,0:T(8,128)(2,1)} %bitcast.56, bf16[512,128]{1,0:T(8,128)(2,1)} %get-tuple-element.34.grad_query, f32[128,128]{1,0:T(8,128)} %get-tuple-element.35.grad_kv, bf16[128,128]{1,0:T(8,128)(2,1)} %copy-done.9), custom_call_target="tpu_custom_call" | custom-call | flops 100000000 | bytes 8912896 | tf_op jit(solution)/shard_map/pallas_call | solution.py:195
  116.4 0.8 all-to-all-done.2
  117.2 4.4 %all-to-all-start.3 = ((bf16[8,400,128]{2,1,0:T(8,128)(2,1)}), bf16[8,400,128]{2,1,0:T(8,128)(2,1)S(1)}, u32[]{:S(2)}, u32[]{:S(2)}) async-start(bf16[8,400,128]{2,1,0:T(8,128)(2,1)} %shard_map.132), calls=%async_computation.3 | async-start | bytes 1638400 | tf_op jit(solution)/shard_map/all_to_all | solution.py:321
  121.6 3.7 %collective-permute-start.7 = (f32[16,360]{1,0:T(8,128)S(1)}, f32[16,360]{1,0:T(8,128)S(1)}, u32[]{:S(2)}, u32[]{:S(2)}) collective-permute-start(f32[16,360]{1,0:T(8,128)S(1)} %add.93), channel_id=1, source_target_pairs={{0,32},{16,48},{32,0},{48,16},{64,96},{80,112},{96,64},{112,80},{1... | collective-permute-start | bytes 69128 | tf_op jit(solution)/shard_map/ppermute | solution.py:260
  125.8 1.6 %collective-permute-done.7 = f32[16,360]{1,0:T(8,128)S(1)} collective-permute-done((f32[16,360]{1,0:T(8,128)S(1)}, f32[16,360]{1,0:T(8,128)S(1)}, u32[]{:S(2)}, u32[]{:S(2)}) %collective-permute-start.7) | collective-permute-done | bytes 23072 | tf_op jit(solution)/shard_map/ppermute | solution.py:260
  127.3 5.6 %collective-permute-start.8 = (f32[16,360]{1,0:T(8,128)S(1)}, f32[16,360]{1,0:T(8,128)S(1)}, u32[]{:S(2)}, u32[]{:S(2)}) collective-permute-start(f32[16,360]{1,0:T(8,128)S(1)} %add.99), channel_id=1, source_target_pairs={{0,64},{16,80},{32,96},{48,112},{64,0},{80,16},{96,32},{112,48},{1... | collective-permute-start | bytes 69128 | tf_op jit(solution)/shard_map/ppermute | solution.py:260
  133.3 2.5 %collective-permute-done.8 = f32[16,360]{1,0:T(8,128)S(1)} collective-permute-done((f32[16,360]{1,0:T(8,128)S(1)}, f32[16,360]{1,0:T(8,128)S(1)}, u32[]{:S(2)}, u32[]{:S(2)}) %collective-permute-start.8) | collective-permute-done | bytes 23072 | tf_op jit(solution)/shard_map/ppermute | solution.py:260
  136.6 1.0 fusion.7
  137.7 0.8 fusion.21
  (73 shorter events, 7.4 us)
Async XLA Ops:
  7.2 125.7 %copy-start = (bf16[16,2880]{1,0:T(8,128)(2,1)S(1)}, bf16[16,2880]{1,0:T(8,128)(2,1)}, u32[]{:S(2)}) copy-start(bf16[16,2880]{1,0:T(8,128)(2,1)} %param.18) | copy-start | bytes 276484
  7.2 25.3 %copy-start.1 = (bf16[128,2880]{0,1:T(8,128)(2,1)S(1)}, bf16[128,2880]{0,1:T(8,128)(2,1)}, u32[]{:S(2)}) copy-start(bf16[128,2880]{0,1:T(8,128)(2,1)} %param.11) | copy-start | bytes 2211844
  7.2 80.1 %all-gather.3.cloned.1.call-start = ((), (), s32[]{:S(2)}) async-start(), calls=%async_computation.4 | async-start | bytes 6684672 | tf_op jit(solution)/shard_map/all_gather | solution.py:234
  9.0 24.0 %copy-start.4 = (f32[2880]{0:T(1024)S(1)}, f32[2880]{0:T(1024)}, u32[]{:S(2)}) copy-start(f32[2880]{0:T(1024)} %param.17) | copy-start | bytes 34564
  9.0 24.0 %copy-start.5 = (f32[2880]{0:T(1024)S(1)}, f32[2880]{0:T(1024)}, u32[]{:S(2)}) copy-start(f32[2880]{0:T(1024)} %param.12) | copy-start | bytes 34564
  32.9 9.3 %copy-start.2 = (bf16[128,2880]{0,1:T(8,128)(2,1)S(1)}, bf16[128,2880]{0,1:T(8,128)(2,1)}, u32[]{:S(2)}) copy-start(bf16[128,2880]{0,1:T(8,128)(2,1)} %param.21) | copy-start | bytes 2211844
  32.9 9.3 %copy-start.10 = (s32[128]{0:T(128)S(1)}, s32[128]{0:T(128)}, u32[]{:S(2)}) copy-start(s32[128]{0:T(128)} %param.20) | copy-start | bytes 1540
  34.5 19.8 %copy-start.11 = (f32[128]{0:T(128)}, f32[128]{0:T(128)S(1)}, u32[]{:S(2)}) copy-start(f32[128]{0:T(128)S(1)} %get-tuple-element.41) | copy-start | bytes 1540
  35.3 23.6 %all-to-all-start.1 = ((bf16[8,4,48,128]{3,2,1,0:T(8,128)(2,1)}), bf16[8,4,48,128]{3,2,1,0:T(8,128)(2,1)S(1)}, u32[]{:S(2)}, u32[]{:S(2)}) async-start(bf16[8,4,48,128]{3,2,1,0:T(8,128)(2,1)} %broadcast_in_dim.11), calls=%async_computation.1 | async-start | bytes 786432 | tf_op jit(solution)/shard_map/all_to_all | solution.py:30
  42.2 12.1 %copy-start.13 = (f32[128]{0:T(128)}, f32[128]{0:T(128)S(1)}, u32[]{:S(2)}) copy-start(f32[128]{0:T(128)S(1)} %add_divide_fusion) | copy-start | bytes 1540
  43.1 12.9 %collective-permute-start = (f32[16,360]{1,0:T(8,128)}, f32[16,360]{1,0:T(8,128)}, u32[]{:S(2)}, u32[]{:S(2)}) collective-permute-start(f32[16,360]{1,0:T(8,128)} %fusion.11), channel_id=1, source_target_pairs={{0,8},{8,0},{1,9},{9,1},{2,10},{10,2},{3,11},{11,3},{4,12},{12,4},... | collective-permute-start | bytes 69128 | tf_op jit(solution)/shard_map/ppermute | solution.py:260
  50.1 4.5 %collective-permute-start.3 = (s32[128]{0:T(128)}, s32[128]{0:T(128)}, u32[]{:S(2)}, u32[]{:S(2)}) collective-permute-start(s32[128]{0:T(128)} %param.19), channel_id=1, source_target_pairs={{0,8},{8,16},{16,24},{24,32},{32,40},{40,48},{48,56},{56,64},{64,7... | collective-permute-start | bytes 1544 | tf_op jit(solution)/shard_map/ppermute | solution.py:24
  56.7 11.5 %copy-start.15 = (s32[256]{0:T(256)S(1)}, s32[256]{0:T(256)}, u32[]{:S(2)}) copy-start(s32[256]{0:T(256)} %iota_add_fusion) | copy-start | bytes 3076
  56.7 13.0 %collective-permute-start.1 = (f32[16,360]{1,0:T(8,128)S(1)}, f32[16,360]{1,0:T(8,128)S(1)}, u32[]{:S(2)}, u32[]{:S(2)}) collective-permute-start(f32[16,360]{1,0:T(8,128)S(1)} %add.88), channel_id=1, source_target_pairs={{0,128},{128,0},{256,384},{384,256},{1,129},{129,1},{257,385},{385... | collective-permute-start | bytes 69128 | tf_op jit(solution)/shard_map/ppermute | solution.py:260
  65.2 15.9 %copy-start.3 = (bf16[8,8,48,128]{3,2,1,0:T(8,128)(2,1)}, bf16[8,8,48,128]{3,2,1,0:T(8,128)(2,1)S(1)}, u32[]{:S(2)}) copy-start(bf16[8,8,48,128]{3,2,1,0:T(8,128)(2,1)S(1)} %all-gather) | copy-start | bytes 2359300
  65.6 15.7 %copy-start.7 = (bf16[128,128]{1,0:T(8,128)(2,1)}, bf16[128,128]{1,0:T(8,128)(2,1)S(1)}, u32[]{:S(2)}) copy-start(bf16[128,128]{1,0:T(8,128)(2,1)S(1)} %fusion.8.kv) | copy-start | bytes 98308
  65.7 4.0 %collective-permute-start.2 = (bf16[128,128]{1,0:T(8,128)(2,1)S(1)}, bf16[128,128]{1,0:T(8,128)(2,1)S(1)}, u32[]{:S(2)}, u32[]{:S(2)}) collective-permute-start(bf16[128,128]{1,0:T(8,128)(2,1)S(1)} %fusion.8.kv), channel_id=1, source_target_pairs={{0,8},{8,16},{16,24},{24,32},{32,40},{40,48},{48,56},{56,64},{64,7... | collective-permute-start | bytes 98312 | tf_op jit(solution)/shard_map/ppermute | solution.py:24
  69.7 11.7 %copy-start.8 = (bf16[128,128]{1,0:T(8,128)(2,1)}, bf16[128,128]{1,0:T(8,128)(2,1)S(1)}, u32[]{:S(2)}) copy-start(bf16[128,128]{1,0:T(8,128)(2,1)S(1)} %collective-permute-done.2.halo) | copy-start | bytes 98308
  69.7 8.5 %collective-permute-start.4 = (f32[16,360]{1,0:T(8,128)S(1)}, f32[16,360]{1,0:T(8,128)S(1)}, u32[]{:S(2)}, u32[]{:S(2)}) collective-permute-start(f32[16,360]{1,0:T(8,128)S(1)} %add.89), channel_id=1, source_target_pairs={{0,256},{128,384},{256,0},{384,128},{1,257},{129,385},{257,1},{385... | collective-permute-start | bytes 69128 | tf_op jit(solution)/shard_map/ppermute | solution.py:260
  78.2 5.1 %collective-permute-start.5 = (f32[16,360]{1,0:T(8,128)S(1)}, f32[16,360]{1,0:T(8,128)S(1)}, u32[]{:S(2)}, u32[]{:S(2)}) collective-permute-start(f32[16,360]{1,0:T(8,128)S(1)} %add.92), channel_id=1, source_target_pairs={{0,16},{16,0},{32,48},{48,32},{64,80},{80,64},{96,112},{112,96},{1... | collective-permute-start | bytes 69128 | tf_op jit(solution)/shard_map/ppermute | solution.py:260
  98.3 6.4 %copy-start.16 = (bf16[128,128]{1,0:T(8,128)(2,1)S(1)}, bf16[128,128]{1,0:T(8,128)(2,1)}, u32[]{:S(2)}) copy-start(bf16[128,128]{1,0:T(8,128)(2,1)} %get-tuple-element.36) | copy-start | bytes 98308
  98.3 18.9 %all-to-all-start.2 = ((bf16[8,384,128]{2,1,0:T(8,128)(2,1)}), bf16[8,384,128]{2,1,0:T(8,128)(2,1)S(1)}, u32[]{:S(2)}, u32[]{:S(2)}) async-start(bf16[8,384,128]{2,1,0:T(8,128)(2,1)} %get-tuple-element.31), calls=%async_computation.2 | async-start | bytes 1572864 | tf_op jit(solution)/shard_map/all_to_all | solution.py:303
  104.7 5.5 %collective-permute-start.6 = (bf16[128,128]{1,0:T(8,128)(2,1)S(1)}, bf16[128,128]{1,0:T(8,128)(2,1)S(1)}, u32[]{:S(2)}, u32[]{:S(2)}) collective-permute-start(bf16[128,128]{1,0:T(8,128)(2,1)S(1)} %copy-done.16), channel_id=1, source_target_pairs={{8,0},{16,8},{24,16},{32,24},{40,32},{48,40},{56,48},{64,56},{72,6... | collective-permute-start | bytes 98312 | tf_op jit(solution)/shard_map/ppermute | solution.py:24
  110.2 0.6 copy-start.9
  116.4 5.2 %copy-start.6 = (f32[2880]{0:T(1024)S(1)}, f32[2880]{0:T(1024)}, u32[]{:S(2)}) copy-start(f32[2880]{0:T(1024)} %param.12) | copy-start | bytes 34564
  117.2 20.3 %all-to-all-start.3 = ((bf16[8,400,128]{2,1,0:T(8,128)(2,1)}), bf16[8,400,128]{2,1,0:T(8,128)(2,1)S(1)}, u32[]{:S(2)}, u32[]{:S(2)}) async-start(bf16[8,400,128]{2,1,0:T(8,128)(2,1)} %shard_map.132), calls=%async_computation.3 | async-start | bytes 1638400 | tf_op jit(solution)/shard_map/all_to_all | solution.py:321
  121.6 15.0 %copy-start.14 = (f32[128]{0:T(128)S(1)}, f32[128]{0:T(128)}, u32[]{:S(2)}) copy-start(f32[128]{0:T(128)} %copy-done.13) | copy-start | bytes 1540
  121.6 5.8 %collective-permute-start.7 = (f32[16,360]{1,0:T(8,128)S(1)}, f32[16,360]{1,0:T(8,128)S(1)}, u32[]{:S(2)}, u32[]{:S(2)}) collective-permute-start(f32[16,360]{1,0:T(8,128)S(1)} %add.93), channel_id=1, source_target_pairs={{0,32},{16,48},{32,0},{48,16},{64,96},{80,112},{96,64},{112,80},{1... | collective-permute-start | bytes 69128 | tf_op jit(solution)/shard_map/ppermute | solution.py:260
  127.3 8.5 %collective-permute-start.8 = (f32[16,360]{1,0:T(8,128)S(1)}, f32[16,360]{1,0:T(8,128)S(1)}, u32[]{:S(2)}, u32[]{:S(2)}) collective-permute-start(f32[16,360]{1,0:T(8,128)S(1)} %add.99), channel_id=1, source_target_pairs={{0,64},{16,80},{32,96},{48,112},{64,0},{80,16},{96,32},{112,48},{1... | collective-permute-start | bytes 69128 | tf_op jit(solution)/shard_map/ppermute | solution.py:260
  136.5 1.2 copy-start.12
Sparse Core Ops, SparseCore 0:
  32.6 54.6 all-gather.2

commit v6 on v5

--- a/solution.py
+++ b/solution.py
@@ -46,6 +46,13 @@
     return rows.reshape(8, PAD, width)[:, : row_count // 8].reshape(row_count, width)
 
 
+def split3(value):
+    high = lax.reduce_precision(value, 8, 7)
+    rest = value - high
+    mid = lax.reduce_precision(rest, 8, 7)
+    return jnp.stack([high, mid, lax.reduce_precision(rest - mid, 8, 7)])
+
+
 def mm(left, right, left_dim, right_dim):
     dims = (((left_dim,), (right_dim,)), ((), ()))
     return lax.dot_general(left, right, dims, preferred_element_type=F32)
@@ -62,60 +69,93 @@
         out[place, :rows, 2 * width + HD :] = w_value[...]
 
 
-def pieces():
-    for group in range(8):
-        for part in range(8):
-            row = ((group % 2 * 8 + part) * 4 + group // 2) * PAD
-            yield group, part * PAD, row
+CHUNK = 8 * PAD
+
+
+def scatter_rows(blocks, row, term):
+    for piece in range(CHUNK // PAD):
+        number = row // PAD + piece
+        z, line = number % 4, number // 4
+        place = line % 8 * PAD
+        group = z * 2 + line // 8
+        blocks[group, place : place + PAD, :] = term[piece * PAD : (piece + 1) * PAD]
+
+
+def send_blocks(blocks, blocks_hbm, sems, groups):
+    sent = []
+    for group in groups:
+        copy = pltpu.make_async_copy(blocks.at[group], blocks_hbm.at[group], sems.at[group])
+        copy.start()
+        sent.append(copy)
+    return sent
 
 
 def attend_kernel(
     w_hbm, x_hbm, g_hbm, kv, halo, mask, blocks_hbm, grad_query, grad_halo, grad_kv, *scratch
 ):
     weight, normed, grads, blocks, sems, out_sems = scratch
-    count = sems.shape[0]
-    size = weight.shape[0] // count
+    rows_all = weight.shape[0]
     width = weight.shape[1] // 2
-    copies = []
-    for step in range(count):
-        rows = pl.ds(step * size, size)
-        trio = ((w_hbm, weight), (x_hbm, normed), (g_hbm, grads))
-        copies.append(
-            [
-                pltpu.make_async_copy(a.at[rows, :], b.at[rows, :], sems.at[step, k])
-                for k, (a, b) in enumerate(trio)
-            ]
-        )
-        for copy in copies[-1]:
-            copy.start()
+    two = 2 * HD
+    x_copy = pltpu.make_async_copy(x_hbm, normed, sems.at[0])
+    g_copy = pltpu.make_async_copy(g_hbm, grads, sems.at[1])
+
+    def fetch(column, sem):
+        part = pl.ds(column, two)
+        return pltpu.make_async_copy(w_hbm.at[:, part], weight.at[:, part], sems.at[sem])
+
+    q_copies = [fetch(two * pair, 2 + 2 * pair) for pair in range(4)]
+    o_copies = [fetch(width + two * pair, 3 + 2 * pair) for pair in range(4)]
+    x_copy.start()
+    q_copies[0].start()
+    g_copy.start()
+    o_copies[0].start()
+    for pair in range(1, 4):
+        q_copies[pair].start()
+        o_copies[pair].start()
     keys = jnp.concatenate([halo[:HD, :], kv[:HD, :]], axis=1)
     values = jnp.concatenate([halo[HD:, :], kv[HD:, :]], axis=1)
     allowed = mask[...] > 0.0
-    query_sum = jnp.zeros((width, WIN), F32)
-    grad_sum = jnp.zeros((width, WIN), F32)
-    for step in range(count):
-        for copy in copies[step]:
-            copy.wait()
-        rows = slice(step * size, (step + 1) * size)
-        query_sum += mm(weight[rows, :width], normed[rows, :], 0, 0)
-        grad_sum += mm(weight[rows, width:], grads[rows, :], 0, 0)
-    query_all = query_sum.astype(BF16)
-    grad_all = grad_sum.astype(BF16)
+    late = lax.broadcasted_iota(jnp.int32, (WIN, WIN), 0) > lax.broadcasted_iota(
+        jnp.int32, (WIN, WIN), 1
+    )
+
+    def folded(wide):
+        return jnp.where(late, wide[:WIN], wide[WIN:])
+
+    def unfolded(value):
+        zero = jnp.zeros_like(value)
+        parts = [jnp.where(late, value, zero), jnp.where(late, zero, value)]
+        return jnp.concatenate(parts, axis=0).astype(BF16)
+
     grad_keys = grad_values = jnp.zeros((HD, 2 * WIN), F32)
     mixed = []
     for head in range(8):
-        rows = slice(head * HD, (head + 1) * HD)
-        query, grad = query_all[rows], grad_all[rows]
-        scores = mm(keys, query, 0, 0) * HD**-0.5
+        pair = head // 2
+        if head % 2 == 0:
+            if head == 0:
+                x_copy.wait()
+            q_copies[pair].wait()
+            columns = slice(two * pair, two * (pair + 1))
+            query_two = mm(weight[:, columns], normed[...], 0, 0).astype(BF16)
+            if head == 0:
+                g_copy.wait()
+            o_copies[pair].wait()
+            columns = slice(width + two * pair, width + two * (pair + 1))
+            grad_two = mm(weight[:, columns], grads[...], 0, 0).astype(BF16)
+        rows = slice(head % 2 * HD, (head % 2 + 1) * HD)
+        query, grad = query_two[rows], grad_two[rows]
+        scores = folded(mm(keys, query, 0, 0)) * HD**-0.5
         scores = jnp.where(allowed, scores, -jnp.inf)
         raised = jnp.exp(scores - jnp.max(scores, axis=0, keepdims=True))
-        prob = raised / jnp.sum(raised, axis=0, keepdims=True)
-        prob_b = prob.astype(BF16)
+        prob = raised * (1.0 / jnp.sum(raised, axis=0, keepdims=True))
+        prob_b = unfolded(prob)
         mixed.append(mm(values, prob_b, 1, 0).astype(BF16))
         grad_values += mm(grad, prob_b, 1, 1)
-        grad_prob = mm(values, grad, 0, 0)
+        grad_prob = folded(mm(values, grad, 0, 0))
         delta = jnp.sum(prob * grad_prob, axis=0, keepdims=True)
-        grad_scores = (prob * (grad_prob - delta) * HD**-0.5).astype(BF16)
+        grad_scores = unfolded(prob * (grad_prob - delta) * HD**-0.5)
+        rows = slice(head * HD, (head + 1) * HD)
         grad_query[rows, :] = mm(keys, grad_scores, 1, 0).astype(BF16)
         grad_keys += mm(query, grad_scores, 1, 1)
     grad_halo[:HD, :] = grad_keys[:, :WIN].astype(BF16)
@@ -124,15 +164,12 @@
     grad_kv[HD:, :] = grad_values[:, WIN:]
     mixed = jnp.concatenate(mixed, axis=0)
     sent = []
-    for group, place, row in pieces():
-        term = mm(weight[row : row + PAD, width:], mixed, 1, 0)
-        blocks[group, place : place + PAD, :] = term.astype(BF16)
-        if place == 7 * PAD:
-            copy = pltpu.make_async_copy(
-                blocks.at[group], blocks_hbm.at[group], out_sems.at[group]
-            )
-            copy.start()
-            sent.append(copy)
+    for row in range(0, rows_all, CHUNK):
+        term = mm(weight[row : row + CHUNK, width:], mixed, 1, 0).astype(BF16)
+        scatter_rows(blocks, row, term)
+        if row + CHUNK == rows_all // 2:
+            sent += send_blocks(blocks, blocks_hbm, out_sems, range(0, 8, 2))
+    sent += send_blocks(blocks, blocks_hbm, out_sems, range(1, 8, 2))
     for copy in sent:
         copy.wait()
 
@@ -140,49 +177,43 @@
 def back_kernel(w_hbm, kv_hbm, x_hbm, grad_query, grad_kv, returned, blocks_hbm, *scratch):
     weight, kv_all, normed, blocks, sems, out_sems = scratch
     width = weight.shape[1]
-    size = weight.shape[0] // 2
+    rows_all = weight.shape[0]
+    size = 2 * CHUNK
     copies = []
-    for step in range(2):
+    for step in range(rows_all // size):
         rows = pl.ds(step * size, size)
+        trio = (
+            (w_hbm.at[rows, pl.ds(0, width)], weight.at[rows, :]),
+            (kv_hbm.at[rows, :], kv_all.at[rows, :]),
+            (x_hbm.at[rows, :], normed.at[rows, :]),
+        )
         copies.append(
-            [
-                pltpu.make_async_copy(
-                    w_hbm.at[rows, pl.ds(0, width)], weight.at[rows, :], sems.at[step, 0]
-                ),
-                pltpu.make_async_copy(kv_hbm.at[rows, :], kv_all.at[rows, :], sems.at[step, 1]),
-                pltpu.make_async_copy(x_hbm.at[rows, :], normed.at[rows, :], sems.at[step, 2]),
-            ]
+            [pltpu.make_async_copy(a, b, sems.at[step, k]) for k, (a, b) in enumerate(trio)]
         )
         for copy in copies[-1]:
             copy.start()
     tokens_here = grad_kv.shape[1]
     kv_grad = (grad_kv[...] + returned[...].astype(F32)).astype(BF16)
-    rows_sum = jnp.zeros((PAD, tokens_here), F32)
-    ordered = sorted(pieces(), key=lambda piece: piece[2] >= size)
-    ready = 0
-    for group, place, row in ordered:
-        if ready < 1 + (row >= size):
-            for copy in copies[ready]:
+    grads = grad_query[...]
+    total = jnp.zeros((1, tokens_here), F32)
+    for row in range(0, rows_all, CHUNK):
+        if row % size == 0:
+            for copy in copies[row // size]:
                 copy.wait()
-            ready += 1
-        term = mm(weight[row : row + PAD, :], grad_query[...], 1, 0)
-        term = term + mm(kv_all[row : row + PAD, :], kv_grad, 1, 0)
+        rows = slice(row, row + CHUNK)
+        term = mm(weight[rows, :], grads, 1, 0) + mm(kv_all[rows, :], kv_grad, 1, 0)
         term = term.astype(BF16)
-        blocks[group, place : place + PAD, :] = term
-        rows_sum += term.astype(F32) * normed[row : row + PAD, :].astype(F32)
-    total = jnp.sum(rows_sum, axis=0, keepdims=True)
+        scatter_rows(blocks, row, term)
+        products = term.astype(F32) * normed[rows, :].astype(F32)
+        total = total + jnp.sum(products, axis=0, keepdims=True)
     high = total.astype(BF16).astype(F32)
     mid = (total - high).astype(BF16).astype(F32)
     low = total - high - mid
     line = lax.broadcasted_iota(jnp.int32, (16, tokens_here), 0)
     extra = jnp.where(line == 0, high, jnp.where(line == 1, mid, jnp.where(line == 2, low, 0.0)))
-    sent = []
     for group in range(8):
         blocks[group, 8 * PAD :, :] = extra.astype(BF16)
-        copy = pltpu.make_async_copy(blocks.at[group], blocks_hbm.at[group], out_sems.at[group])
-        copy.start()
-        sent.append(copy)
-    for copy in sent:
+    for copy in send_blocks(blocks, blocks_hbm, out_sems, range(8)):
         copy.wait()
 
 
@@ -233,8 +264,7 @@
     near = lax.all_to_all(sent, "zh", 0, 0)
     whole = lax.all_gather(near[:, :, : 2 * width], ("y", "core"), axis=0, tiled=True)
     whole = whole.reshape(-1, 2 * width)
-    kv_near = gathered(near[:, :, 2 * width :], ("y",))
-    kv_all = lax.all_gather(kv_near[:, None], "core", axis=1, tiled=True).reshape(-1, 2 * HD)
+    kv_near = near[:, :, 2 * width :].reshape(-1, 2 * HD)
 
     tok = tokens.T.astype(F32)
     inverse = lax.rsqrt(jnp.mean(tok * tok, axis=0, keepdims=True) + EPSILON)
@@ -254,28 +284,28 @@
         one_hot.astype(F32), gate[None, :] * grad_share, ((1,), (1,)), precision=HIGHEST
     )
 
-    def exchanged(value, *steps):
-        for axis, step in steps:
-            pairs = [(i, i ^ step) for i in range(lax.axis_size(axis))]
-            value = value + lax.ppermute(value, axis, pairs)
-        return value
-
-    steer = exchanged(steer_part, ("core", 1), ("zh", 1))
+    steer = jnp.sum(gathered(steer_part, ("zh", "core")), axis=0)
+    lanes = 3 * 128
+    parts = jnp.pad(split3(steer), ((0, 0), (0, 0), (0, lanes - share))).astype(BF16)
+    parts = parts.reshape(-1, lanes)
+    parts = [parts[:, k : k + 128] for k in range(0, lanes, 128)]
+    kv_rows = kv_near.shape[0]
+    both = gathered(jnp.concatenate([kv_near, *parts], axis=0), ("y",))
+    kv_all = both[:, :kv_rows].reshape(8, 1, kv_rows, 2 * HD)
+    kv_all = lax.all_gather(kv_all, "core", axis=1, tiled=True).reshape(-1, 2 * HD)
+    steer = jnp.sum(both[:, kv_rows:].astype(F32), axis=0).reshape(3, 3, 16, 128)
+    steer_grad = jnp.sum(steer, axis=1).transpose(1, 0, 2).reshape(16, lanes)[:, :share]
 
     halo_seg = shifted(segment_ids, 1)
     halo_seg = jnp.where(lax.axis_index(SEQ) > 0, halo_seg, -1)
     kv = dot(kv_all, normed_b, ((0,), (0,))).astype(BF16)
     halo = shifted(kv, 1)
-    wide_seg = jnp.concatenate([halo_seg, segment_ids])
-    key_pos = lax.broadcasted_iota(jnp.int32, (2 * row_count, row_count), 0) - WIN
-    query_pos = lax.broadcasted_iota(jnp.int32, (2 * row_count, row_count), 1)
-    distance = query_pos - key_pos
-    mask = (distance >= 0) & (distance < WIN) & (wide_seg[:, None] == segment_ids[None, :])
-    mask = mask.astype(F32)
-    steer, halo, kv, mask = lax.optimization_barrier((steer, halo, kv, mask))
-    steer = exchanged(steer, ("zh", 2), ("y", 1))
-    whole, halo, mask, steer, normed_b, grad_b, kv, kv_all = lax.optimization_barrier(
-        (whole, halo, mask, steer, normed_b, grad_b, kv, kv_all)
+    key_pos = lax.broadcasted_iota(jnp.int32, (row_count, row_count), 0)
+    query_pos = lax.broadcasted_iota(jnp.int32, (row_count, row_count), 1)
+    key_seg = jnp.where(key_pos > query_pos, halo_seg[:, None], segment_ids[:, None])
+    mask = (key_seg == segment_ids[None, :]).astype(F32)
+    whole, halo, mask, steer_grad, normed_b, grad_b, kv, kv_all = lax.optimization_barrier(
+        (whole, halo, mask, steer_grad, normed_b, grad_b, kv, kv_all)
     )
     total_rows = whole.shape[0]
     dma = pltpu.SemaphoreType.DMA
@@ -294,7 +324,7 @@
             pltpu.VMEM((total_rows, row_count), BF16),
             pltpu.VMEM((total_rows, row_count), BF16),
             pltpu.VMEM((8, 8 * PAD, row_count), BF16),
-            dma((6, 3)),
+            dma((10,)),
             dma((8,)),
         ],
         *(whole, normed_b, grad_b, kv, halo, mask),
@@ -311,13 +341,11 @@
             pltpu.VMEM((total_rows, 2 * HD), BF16),
             pltpu.VMEM((total_rows, row_count), BF16),
             pltpu.VMEM((8, 8 * PAD + 16, row_count), BF16),
-            dma((2, 3)),
+            dma((4, 3)),
             dma((8,)),
         ],
         *(whole, kv_all, normed_b, grad_query, grad_kv, returned),
     )
-    steer, back = lax.optimization_barrier((steer, back))
-    steer_grad = exchanged(steer, ("y", 2), ("y", 4))
     back = lax.all_to_all(back, HEAD, 0, 0)
 
     attn_share = unpadded(jnp.sum(attn.astype(F32), axis=0), share)

time: 148 us -> 153 us (1.034); the launches traced: 145 us -> 152 us
  starting transfers between devices: 49.9 us -> 26.3 us
  waiting for transfers between devices: 18 us -> 34.7 us
  blocking collectives: 28.9 us -> 43.2 us
  local copies, waits for them, and re-layouts: 5.24 us -> 7.02 us
    ppermute x6 -> x0, starting transfers between devices: 23.7 us -> none  [exchanged(): value = value + lax.ppermute(value, axis, pairs)]
    all_to_all x0 -> x1, blocking collectives: none -> 15.9 us  [gathered(): return lax.all_to_all(spread, axes, 0, 0)]
    ppermute x3, waiting for transfers between devices: 3.08 us -> 15.7 us  [shifted(): return lax.ppermute(value, SEQ, pairs)]
    all_to_all x1, waiting for transfers between devices: 0.01 us -> 11 us  [shards(): back = lax.all_to_all(back, HEAD, 0, 0)]
    ppermute x6 -> x0, waiting for transfers between devices: 10.1 us -> none  [exchanged(): value = value + lax.ppermute(value, axis, pairs)]
    all_to_all x1, waiting for transfers between devices: 0.01 us -> 6.05 us  [gathered(): return lax.all_to_all(spread, axes, 0, 0)]
    all_gather x1, waiting for transfers between devices: 4.08 us -> 0.01 us  [shards(): lax.all_gather(near[:, :, :2 * width], ('y', 'core'), axis=0, tiled=True)]
    ppermute x3, starting transfers between devices: 8.53 us -> 11 us  [shifted(): return lax.ppermute(value, SEQ, pairs)]
  transfers between devices with their start and end apart: 13 -> 7, of which waited for: 7 -> 5; matrix products, arithmetic and copies ran while one was open for 9% -> 8% of each run, Pallas kernels for 4% -> 3%
where the time goes in v6:
time: 153 us; the launch traced here: 152 us
  blocking collectives  43.2 us (28%)
  waiting for transfers between devices  34.7 us (23%)
  starting transfers between devices  26.3 us (17%)
  Pallas kernels  18.2 us (12%)
  between operations  14.4 us (9%)
  local copies, waits for them, and re-layouts  7.02 us (5%)
  other arithmetic  6.67 us (4%)
  matrix products  1.81 us (1%)
    all_to_all x1, blocking collectives, shards(): near = lax.all_to_all(sent, 'zh', 0, 0)  22.7 us
    pallas_call x3, Pallas kernels, call(): pl.pallas_call(kernel, out_shape=outs, in_specs=in_specs, out_specs=out_s...  18.2 us
    all_to_all x1, blocking collectives, gathered(): return lax.all_to_all(spread, axes, 0, 0)  15.9 us
    ppermute x3, waiting for transfers between devices, shifted(): return lax.ppermute(value, SEQ, pairs)  15.7 us
    ppermute x3, starting transfers between devices, shifted(): return lax.ppermute(value, SEQ, pairs)  11 us
    all_to_all x1, waiting for transfers between devices, shards(): back = lax.all_to_all(back, HEAD, 0, 0)  11 us
    all_to_all x1, starting transfers between devices, gathered(): return lax.all_to_all(spread, axes, 0, 0)  6.82 us
    all_to_all x1, waiting for transfers between devices, gathered(): return lax.all_to_all(spread, axes, 0, 0)  6.05 us
  transfers between devices with their start and end apart: 7, of which 5 were waited for; matrix products, arithmetic and copies ran while one was open for 8% of the time, Pallas kernels for 3%

profile of v6, /device:TPU:1, one launch (start us, length us, event | category | flops | bytes accessed | tf_op | source)
XLA Modules:
  0.0 152.3 jit_solution(6595509515387528319)
XLA Ops:
  7.2 1.8 %shard_map.130 = bf16[4,48,1152]{2,1,0:T(8,128)(2,1)} custom-call(bf16[45,512]{1,0:T(8,128)(2,1)} %w_query.1, bf16[45,512]{1,0:T(8,128)(2,1)} %w_out.1, bf16[45,64]{1,0:T(8,128)(2,1)} %w_key.1, bf16[45,64]{1,0:T(8,128)(2,1)} %w_value.1), custom_call_target="tpu_custom_call" | custom-call | flops 100000000 | bytes 546048 | tf_op jit(solution)/shard_map/pallas_call | solution.py:226
  9.0 22.7 %all_to_all.25 = bf16[4,48,1152]{2,1,0:T(8,128)(2,1)S(1)} all-to-all(bf16[4,48,1152]{2,1,0:T(8,128)(2,1)} %shard_map.130), channel_id=1, replica_groups=mesh['zh'=4,'y'=8,'core'=2,'x'=4,'zl'=2] {'zh'}, dimensions={0} | all-to-all | bytes 884736 | tf_op jit(solution)/shard_map/all_to_all | solution.py:264
  31.7 0.8 slice.48
  32.9 1.5 multiply_reduce_fusion
  35.0 15.9 %all_to_all.26 = f32[8,16,360]{2,1,0:T(8,128)S(1)} all-to-all(f32[8,16,360]{2,1,0:T(8,128)S(1)} %broadcast_in_dim.22), channel_id=1, replica_groups=mesh['zh'=4,'y'=8,'core'=2,'x'=4,'zl'=2] {'zh','core'}, dimensions={0} | all-to-all | bytes 368640 | tf_op jit(solution)/shard_map/all_to_all | solution.py:30
  51.1 1.0 broadcast_in_dim.23
  52.1 6.8 %all-to-all-start.2 = ((bf16[8,336,128]{2,1,0:T(8,128)(2,1)}), bf16[8,336,128]{2,1,0:T(8,128)(2,1)}, u32[]{:S(2)}, u32[]{:S(2)}) async-start(bf16[8,336,128]{2,1,0:T(8,128)(2,1)} %broadcast_in_dim.23), calls=%async_computation.2 | async-start | bytes 1376256 | tf_op jit(solution)/shard_map/all_to_all | solution.py:30
  58.9 6.1 %collective-permute-start.1 = (s32[128]{0:T(128)}, s32[128]{0:T(128)}, u32[]{:S(2)}, u32[]{:S(2)}) collective-permute-start(s32[128]{0:T(128)} %param.19), channel_id=1, source_target_pairs={{0,8},{8,16},{16,24},{24,32},{32,40},{40,48},{48,56},{56,64},{64,7... | collective-permute-start | bytes 1544 | tf_op jit(solution)/shard_map/ppermute | solution.py:24
  65.7 1.1 pad.14.clone
  66.8 11.9 %collective-permute-done.1 = s32[128]{0:T(128)} collective-permute-done((s32[128]{0:T(128)}, s32[128]{0:T(128)}, u32[]{:S(2)}, u32[]{:S(2)}) %collective-permute-start.1) | collective-permute-done | bytes 544 | tf_op jit(solution)/shard_map/ppermute | solution.py:24
  78.7 0.7 broadcast_select_fusion
  79.4 1.5 fusion.21.mask
  80.8 6.0 %all-to-all-done.2 = bf16[8,336,128]{2,1,0:T(8,128)(2,1)} async-done(((bf16[8,336,128]{2,1,0:T(8,128)(2,1)}), bf16[8,336,128]{2,1,0:T(8,128)(2,1)}, u32[]{:S(2)}, u32[]{:S(2)}) %all-to-all-start.2) | async-done | bytes 688160 | tf_op jit(solution)/shard_map/all_to_all | solution.py:30
  86.9 1.0 slice.53
  87.9 4.6 %all-gather = bf16[8,384,128]{2,1,0:T(8,128)(2,1)S(1)} all-gather(bf16[8,192,128]{2,1,0:T(8,128)(2,1)S(1)} %slice.53), channel_id=2, replica_groups=mesh['zh'=4,'y'=8,'core'=2,'x'=4,'zl'=2] {'core'}, dimensions={1}, use_global_device_ids=true | all-gather | bytes 1179648 | tf_op jit(solution)/shard_map/all_gather | solution.py:295
  92.5 0.4 convolution_convert_fusion.kv
  93.0 3.0 %collective-permute-start = (bf16[128,128]{1,0:T(8,128)(2,1)S(1)}, bf16[128,128]{1,0:T(8,128)(2,1)S(1)}, u32[]{:S(2)}, u32[]{:S(2)}) collective-permute-start(bf16[128,128]{1,0:T(8,128)(2,1)S(1)} %convolution_convert_fusion.kv), channel_id=1, source_target_pairs={{0,8},{8,16},{16,24},{24,32},{32,40},{40,48},{48,56},{56,64},{64,7... | collective-permute-start | bytes 98312 | tf_op jit(solution)/shard_map/ppermute | solution.py:24
  96.0 1.0 convert_reduce_fusion.2
  97.1 0.6 copy_bitcast_fusion
  97.7 0.6 copy-done.9
  98.3 11.4 %shard_map.131 = (bf16[8,384,128]{2,1,0:T(8,128)(2,1)}, bf16[512,128]{1,0:T(8,128)(2,1)}, bf16[128,128]{1,0:T(8,128)(2,1)}, f32[128,128]{1,0:T(8,128)}) custom-call(bf16[3072,1024]{1,0:T(8,128)(2,1)} %bitcast.62, bf16[3072,128]{1,0:T(8,128)(2,1)} %bitcast.65, bf16[3072,128]{1,0:T(8,128)(2,1)} %bitcast.72, bf16[128,128]{1,0:T(8,128)(2,1)} %copy-done.5, ...), custom_call_target="tpu_custom_call" | custom-call | flops 100000000 | bytes 9011200 | tf_op jit(solution)/shard_map/pallas_call | solution.py:226
  109.7 4.8 %all-to-all-start.3 = ((bf16[8,384,128]{2,1,0:T(8,128)(2,1)}), bf16[8,384,128]{2,1,0:T(8,128)(2,1)S(1)}, u32[]{:S(2)}, u32[]{:S(2)}) async-start(bf16[8,384,128]{2,1,0:T(8,128)(2,1)} %get-tuple-element.21), calls=%async_computation.3 | async-start | bytes 1572864 | tf_op jit(solution)/shard_map/all_to_all | solution.py:333
  114.5 1.9 %collective-permute-start.2 = (bf16[128,128]{1,0:T(8,128)(2,1)S(1)}, bf16[128,128]{1,0:T(8,128)(2,1)S(1)}, u32[]{:S(2)}, u32[]{:S(2)}) collective-permute-start(bf16[128,128]{1,0:T(8,128)(2,1)S(1)} %copy-done.16), channel_id=1, source_target_pairs={{8,0},{16,8},{24,16},{32,24},{40,32},{48,40},{56,48},{64,56},{72,6... | collective-permute-start | bytes 98312 | tf_op jit(solution)/shard_map/ppermute | solution.py:24
  116.5 3.8 %collective-permute-done.2.returned = bf16[128,128]{1,0:T(8,128)(2,1)S(1)} collective-permute-done((bf16[128,128]{1,0:T(8,128)(2,1)S(1)}, bf16[128,128]{1,0:T(8,128)(2,1)S(1)}, u32[]{:S(2)}, u32[]{:S(2)}) %collective-permute-start.2) | collective-permute-done | bytes 32800 | tf_op jit(solution)/shard_map/ppermute | solution.py:24
  120.3 0.6 copy-done.10
  120.9 5.0 %shard_map.132 = bf16[8,400,128]{2,1,0:T(8,128)(2,1)} custom-call(bf16[3072,1024]{1,0:T(8,128)(2,1)} %bitcast.63, bf16[3072,128]{1,0:T(8,128)(2,1)} %bitcast.68, bf16[3072,128]{1,0:T(8,128)(2,1)} %bitcast.66, bf16[512,128]{1,0:T(8,128)(2,1)} %get-tuple-element.23.grad_query, f32[128,128]{1,0:T(8,128)} %get-tuple-element.24.grad_kv, bf16[128,128]{1,0:T(8,128)(2,1)} %copy-done.10), custom_call_target="tpu_custom_call" | custom-call | flops 100000000 | bytes 8912896 | tf_op jit(solution)/shard_map/pallas_call | solution.py:226
  125.9 2.0 %all-to-all-done.3 = bf16[8,384,128]{2,1,0:T(8,128)(2,1)S(1)} async-done(((bf16[8,384,128]{2,1,0:T(8,128)(2,1)}), bf16[8,384,128]{2,1,0:T(8,128)(2,1)S(1)}, u32[]{:S(2)}, u32[]{:S(2)}) %all-to-all-start.3) | async-done | bytes 786464 | tf_op jit(solution)/shard_map/all_to_all | solution.py:333
  127.9 3.5 %all-to-all-start.4 = ((bf16[8,400,128]{2,1,0:T(8,128)(2,1)}), bf16[8,400,128]{2,1,0:T(8,128)(2,1)S(1)}, u32[]{:S(2)}, u32[]{:S(2)}) async-start(bf16[8,400,128]{2,1,0:T(8,128)(2,1)} %shard_map.132), calls=%async_computation.4 | async-start | bytes 1638400 | tf_op jit(solution)/shard_map/all_to_all | solution.py:349
  131.9 0.5 fusion.3
  132.5 1.0 fusion.7
  133.5 11.0 %all-to-all-done.4 = bf16[8,400,128]{2,1,0:T(8,128)(2,1)S(1)} async-done(((bf16[8,400,128]{2,1,0:T(8,128)(2,1)}), bf16[8,400,128]{2,1,0:T(8,128)(2,1)S(1)}, u32[]{:S(2)}, u32[]{:S(2)}) %all-to-all-start.4) | async-done | bytes 819232 | tf_op jit(solution)/shard_map/all_to_all | solution.py:349
  144.6 0.8 fusion.15
  (64 shorter events, 2.5 us)
Async XLA Ops:
  7.2 124.5 %copy-start = (bf16[16,2880]{1,0:T(8,128)(2,1)S(1)}, bf16[16,2880]{1,0:T(8,128)(2,1)}, u32[]{:S(2)}) copy-start(bf16[16,2880]{1,0:T(8,128)(2,1)} %param.18) | copy-start | bytes 276484
  7.2 25.3 %copy-start.2 = (bf16[128,2880]{0,1:T(8,128)(2,1)S(1)}, bf16[128,2880]{0,1:T(8,128)(2,1)}, u32[]{:S(2)}) copy-start(bf16[128,2880]{0,1:T(8,128)(2,1)} %param.11) | copy-start | bytes 2211844
  7.2 90.5 %all-gather.3.cloned.1.call-start = ((), (), s32[]{:S(2)}) async-start(), calls=%async_computation.5 | async-start | bytes 6684672 | tf_op jit(solution)/shard_map/all_gather | solution.py:265
  9.0 23.9 %copy-start.6 = (f32[2880]{0:T(1024)S(1)}, f32[2880]{0:T(1024)}, u32[]{:S(2)}) copy-start(f32[2880]{0:T(1024)} %param.17) | copy-start | bytes 34564
  9.0 23.9 %copy-start.7 = (f32[2880]{0:T(1024)S(1)}, f32[2880]{0:T(1024)}, u32[]{:S(2)}) copy-start(f32[2880]{0:T(1024)} %param.12) | copy-start | bytes 34564
  32.4 2.0 %copy-start.4 = (bf16[128,2880]{0,1:T(8,128)(2,1)S(1)}, bf16[128,2880]{0,1:T(8,128)(2,1)}, u32[]{:S(2)}) copy-start(bf16[128,2880]{0,1:T(8,128)(2,1)} %param.21) | copy-start | bytes 2211844
  32.4 2.0 %copy-start.11 = (s32[128]{0:T(128)S(1)}, s32[128]{0:T(128)}, u32[]{:S(2)}) copy-start(s32[128]{0:T(128)} %param.20) | copy-start | bytes 1540
  34.4 0.6 copy-start.12
  34.5 0.5 copy-start.14
  52.1 34.8 %all-to-all-start.2 = ((bf16[8,336,128]{2,1,0:T(8,128)(2,1)}), bf16[8,336,128]{2,1,0:T(8,128)(2,1)}, u32[]{:S(2)}, u32[]{:S(2)}) async-start(bf16[8,336,128]{2,1,0:T(8,128)(2,1)} %broadcast_in_dim.23), calls=%async_computation.2 | async-start | bytes 1376256 | tf_op jit(solution)/shard_map/all_to_all | solution.py:30
  58.9 19.8 %collective-permute-start.1 = (s32[128]{0:T(128)}, s32[128]{0:T(128)}, u32[]{:S(2)}, u32[]{:S(2)}) collective-permute-start(s32[128]{0:T(128)} %param.19), channel_id=1, source_target_pairs={{0,8},{8,16},{16,24},{24,32},{32,40},{40,48},{48,56},{56,64},{64,7... | collective-permute-start | bytes 1544 | tf_op jit(solution)/shard_map/ppermute | solution.py:24
  65.7 26.8 %copy-start.1 = (bf16[8,2,4,48,128]{4,3,2,1,0:T(8,128)(2,1)}, bf16[8,2,4,48,128]{4,3,2,1,0:T(8,128)(2,1)S(1)}, u32[]{:S(2)}) copy-start(bf16[8,2,4,48,128]{4,3,2,1,0:T(8,128)(2,1)S(1)} %pad.13.clone) | copy-start | bytes 2359300
  92.5 17.2 %copy-start.3 = (bf16[8,384,128]{2,1,0:T(8,128)(2,1)}, bf16[8,384,128]{2,1,0:T(8,128)(2,1)S(1)}, u32[]{:S(2)}) copy-start(bf16[8,384,128]{2,1,0:T(8,128)(2,1)S(1)} %all-gather) | copy-start | bytes 2359300
  93.0 4.7 %copy-start.5 = (bf16[128,128]{1,0:T(8,128)(2,1)}, bf16[128,128]{1,0:T(8,128)(2,1)S(1)}, u32[]{:S(2)}) copy-start(bf16[128,128]{1,0:T(8,128)(2,1)S(1)} %convolution_convert_fusion.kv) | copy-start | bytes 98308
  93.0 4.7 %collective-permute-start = (bf16[128,128]{1,0:T(8,128)(2,1)S(1)}, bf16[128,128]{1,0:T(8,128)(2,1)S(1)}, u32[]{:S(2)}, u32[]{:S(2)}) collective-permute-start(bf16[128,128]{1,0:T(8,128)(2,1)S(1)} %convolution_convert_fusion.kv), channel_id=1, source_target_pairs={{0,8},{8,16},{16,24},{24,32},{32,40},{40,48},{48,56},{56,64},{64,7... | collective-permute-start | bytes 98312 | tf_op jit(solution)/shard_map/ppermute | solution.py:24
  97.7 0.6 copy-start.9
  109.7 4.8 %copy-start.16 = (bf16[128,128]{1,0:T(8,128)(2,1)S(1)}, bf16[128,128]{1,0:T(8,128)(2,1)}, u32[]{:S(2)}) copy-start(bf16[128,128]{1,0:T(8,128)(2,1)} %get-tuple-element.25) | copy-start | bytes 98308
  109.7 18.2 %all-to-all-start.3 = ((bf16[8,384,128]{2,1,0:T(8,128)(2,1)}), bf16[8,384,128]{2,1,0:T(8,128)(2,1)S(1)}, u32[]{:S(2)}, u32[]{:S(2)}) async-start(bf16[8,384,128]{2,1,0:T(8,128)(2,1)} %get-tuple-element.21), calls=%async_computation.3 | async-start | bytes 1572864 | tf_op jit(solution)/shard_map/all_to_all | solution.py:333
  114.5 5.7 %collective-permute-start.2 = (bf16[128,128]{1,0:T(8,128)(2,1)S(1)}, bf16[128,128]{1,0:T(8,128)(2,1)S(1)}, u32[]{:S(2)}, u32[]{:S(2)}) collective-permute-start(bf16[128,128]{1,0:T(8,128)(2,1)S(1)} %copy-done.16), channel_id=1, source_target_pairs={{8,0},{16,8},{24,16},{32,24},{40,32},{48,40},{56,48},{64,56},{72,6... | collective-permute-start | bytes 98312 | tf_op jit(solution)/shard_map/ppermute | solution.py:24
  120.3 0.6 copy-start.10
  125.9 5.6 %copy-start.8 = (f32[2880]{0:T(1024)S(1)}, f32[2880]{0:T(1024)}, u32[]{:S(2)}) copy-start(f32[2880]{0:T(1024)} %param.12) | copy-start | bytes 34564
  127.9 16.5 %all-to-all-start.4 = ((bf16[8,400,128]{2,1,0:T(8,128)(2,1)}), bf16[8,400,128]{2,1,0:T(8,128)(2,1)S(1)}, u32[]{:S(2)}, u32[]{:S(2)}) async-start(bf16[8,400,128]{2,1,0:T(8,128)(2,1)} %shard_map.132), calls=%async_computation.4 | async-start | bytes 1638400 | tf_op jit(solution)/shard_map/all_to_all | solution.py:349
  131.7 0.8 copy-start.15
  132.5 12.1 %copy-start.13 = (f32[128]{0:T(128)S(1)}, f32[128]{0:T(128)}, u32[]{:S(2)}) copy-start(f32[128]{0:T(128)} %copy-done.12) | copy-start | bytes 1540
Sparse Core Ops, SparseCore 0:
  32.6 64.1 all-gather.2

commit v7 on v6

--- a/solution.py
+++ b/solution.py
@@ -46,27 +46,24 @@
     return rows.reshape(8, PAD, width)[:, : row_count // 8].reshape(row_count, width)
 
 
-def split3(value):
-    high = lax.reduce_precision(value, 8, 7)
-    rest = value - high
-    mid = lax.reduce_precision(rest, 8, 7)
-    return jnp.stack([high, mid, lax.reduce_precision(rest - mid, 8, 7)])
-
-
 def mm(left, right, left_dim, right_dim):
     dims = (((left_dim,), (right_dim,)), ((), ()))
     return lax.dot_general(left, right, dims, preferred_element_type=F32)
 
 
-def pack_kernel(w_query, w_out, w_key, w_value, out):
-    rows = w_query.shape[0]
-    width = w_query.shape[1]
-    out[...] = jnp.zeros(out.shape, BF16)
-    for place in range(out.shape[0]):
-        out[place, :rows, :width] = w_query[...]
-        out[place, :rows, width : 2 * width] = w_out[...]
-        out[place, :rows, 2 * width : 2 * width + HD] = w_key[...]
-        out[place, :rows, 2 * width + HD :] = w_value[...]
+def pack_kernel(q_hbm, o_hbm, k_hbm, v_hbm, out_hbm, query, out, key, value, packed, sems):
+    pairs = ((q_hbm, query), (o_hbm, out), (k_hbm, key), (v_hbm, value))
+    copies = start_all(pairs, sems)
+    rows, width = query.shape
+    packed[rows // 8 * 8 :, :] = jnp.zeros((PAD - rows // 8 * 8, packed.shape[1]), BF16)
+    for copy in copies:
+        copy.wait()
+    packed[:rows, :width] = query[...]
+    packed[:rows, width : 2 * width] = out[...]
+    packed[:rows, 2 * width :] = jnp.concatenate([key[...], value[...]], axis=1)
+    places = [(packed, out_hbm.at[place]) for place in range(out_hbm.shape[0])]
+    for copy in start_all(places, sems):
+        copy.wait()
 
 
 CHUNK = 8 * PAD
@@ -90,35 +87,35 @@
     return sent
 
 
+def start_all(pairs, sems):
+    copies = [pltpu.make_async_copy(a, b, sems.at[k]) for k, (a, b) in enumerate(pairs)]
+    for copy in copies:
+        copy.start()
+    return copies
+
+
 def attend_kernel(
-    w_hbm, x_hbm, g_hbm, kv, halo, mask, blocks_hbm, grad_query, grad_halo, grad_kv, *scratch
+    w_hbm, x_hbm, g_hbm, kv_hbm, halo_hbm, mask_hbm, blocks_hbm, dq_hbm, dh_hbm, dkv_hbm, *scratch
 ):
-    weight, normed, grads, blocks, sems, out_sems = scratch
+    weight, normed, grads, kv, halo, mask, blocks, grad_query, grad_halo, grad_kv = scratch[:10]
+    sems, out_sems = scratch[10:]
     rows_all = weight.shape[0]
     width = weight.shape[1] // 2
-    two = 2 * HD
-    x_copy = pltpu.make_async_copy(x_hbm, normed, sems.at[0])
-    g_copy = pltpu.make_async_copy(g_hbm, grads, sems.at[1])
-
-    def fetch(column, sem):
-        part = pl.ds(column, two)
-        return pltpu.make_async_copy(w_hbm.at[:, part], weight.at[:, part], sems.at[sem])
-
-    q_copies = [fetch(two * pair, 2 + 2 * pair) for pair in range(4)]
-    o_copies = [fetch(width + two * pair, 3 + 2 * pair) for pair in range(4)]
-    x_copy.start()
-    q_copies[0].start()
-    g_copy.start()
-    o_copies[0].start()
-    for pair in range(1, 4):
-        q_copies[pair].start()
-        o_copies[pair].start()
-    keys = jnp.concatenate([halo[:HD, :], kv[:HD, :]], axis=1)
-    values = jnp.concatenate([halo[HD:, :], kv[HD:, :]], axis=1)
-    allowed = mask[...] > 0.0
+    together = 4
+    span = together * HD
+    pairs = [(x_hbm, normed)]
+    for column in range(0, width, span):
+        for first in (column, width + column):
+            part = pl.ds(first, span)
+            pairs.append((w_hbm.at[:, part], weight.at[:, part]))
+        if column == 0:
+            pairs.insert(2, (g_hbm, grads))
+            pairs += [(kv_hbm, kv), (halo_hbm, halo), (mask_hbm, mask)]
+    copies = start_all(pairs, sems)
     late = lax.broadcasted_iota(jnp.int32, (WIN, WIN), 0) > lax.broadcasted_iota(
         jnp.int32, (WIN, WIN), 1
     )
+    late = jnp.concatenate([late] * together, axis=1)
 
     def folded(wide):
         return jnp.where(late, wide[:WIN], wide[WIN:])
@@ -128,42 +125,51 @@
         parts = [jnp.where(late, value, zero), jnp.where(late, zero, value)]
         return jnp.concatenate(parts, axis=0).astype(BF16)
 
+    def beside(rows):
+        return jnp.concatenate([rows[k : k + HD] for k in range(0, span, HD)], axis=1)
+
+    def stacked(lanes):
+        return jnp.concatenate([lanes[:, k * WIN : (k + 1) * WIN] for k in range(together)], axis=0)
+
     grad_keys = grad_values = jnp.zeros((HD, 2 * WIN), F32)
     mixed = []
-    for head in range(8):
-        pair = head // 2
-        if head % 2 == 0:
-            if head == 0:
-                x_copy.wait()
-            q_copies[pair].wait()
-            columns = slice(two * pair, two * (pair + 1))
-            query_two = mm(weight[:, columns], normed[...], 0, 0).astype(BF16)
-            if head == 0:
-                g_copy.wait()
-            o_copies[pair].wait()
-            columns = slice(width + two * pair, width + two * (pair + 1))
-            grad_two = mm(weight[:, columns], grads[...], 0, 0).astype(BF16)
-        rows = slice(head % 2 * HD, (head % 2 + 1) * HD)
-        query, grad = query_two[rows], grad_two[rows]
+    for column in range(0, width, span):
+        if column == 0:
+            for copy in copies[:2]:
+                copy.wait()
+        else:
+            copies[5 + 2 * column // span].wait()
+        query = mm(weight[:, column : column + span], normed[...], 0, 0).astype(BF16)
+        if column == 0:
+            for copy in copies[2:7]:
+                copy.wait()
+            keys = jnp.concatenate([halo[:HD, :], kv[:HD, :]], axis=1)
+            values = jnp.concatenate([halo[HD:, :], kv[HD:, :]], axis=1)
+            allowed = jnp.concatenate([mask[...] > 0.0] * together, axis=1)
+        else:
+            copies[6 + 2 * column // span].wait()
+        first = width + column
+        grad = mm(weight[:, first : first + span], grads[...], 0, 0).astype(BF16)
+        query, grad = beside(query), beside(grad)
         scores = folded(mm(keys, query, 0, 0)) * HD**-0.5
         scores = jnp.where(allowed, scores, -jnp.inf)
         raised = jnp.exp(scores - jnp.max(scores, axis=0, keepdims=True))
         prob = raised * (1.0 / jnp.sum(raised, axis=0, keepdims=True))
         prob_b = unfolded(prob)
-        mixed.append(mm(values, prob_b, 1, 0).astype(BF16))
+        mixed.append(stacked(mm(values, prob_b, 1, 0).astype(BF16)))
         grad_values += mm(grad, prob_b, 1, 1)
         grad_prob = folded(mm(values, grad, 0, 0))
         delta = jnp.sum(prob * grad_prob, axis=0, keepdims=True)
         grad_scores = unfolded(prob * (grad_prob - delta) * HD**-0.5)
-        rows = slice(head * HD, (head + 1) * HD)
-        grad_query[rows, :] = mm(keys, grad_scores, 1, 0).astype(BF16)
+        grad_query[column : column + span, :] = stacked(mm(keys, grad_scores, 1, 0).astype(BF16))
         grad_keys += mm(query, grad_scores, 1, 1)
     grad_halo[:HD, :] = grad_keys[:, :WIN].astype(BF16)
     grad_halo[HD:, :] = grad_values[:, :WIN].astype(BF16)
     grad_kv[:HD, :] = grad_keys[:, WIN:]
     grad_kv[HD:, :] = grad_values[:, WIN:]
+    results = ((grad_query, dq_hbm), (grad_halo, dh_hbm), (grad_kv, dkv_hbm))
+    sent = start_all(results, out_sems.at[pl.ds(8, 3)])
     mixed = jnp.concatenate(mixed, axis=0)
-    sent = []
     for row in range(0, rows_all, CHUNK):
         term = mm(weight[row : row + CHUNK, width:], mixed, 1, 0).astype(BF16)
         scatter_rows(blocks, row, term)
@@ -174,8 +180,10 @@
         copy.wait()
 
 
-def back_kernel(w_hbm, kv_hbm, x_hbm, grad_query, grad_kv, returned, blocks_hbm, *scratch):
-    weight, kv_all, normed, blocks, sems, out_sems = scratch
+def back_kernel(w_hbm, kv_hbm, x_hbm, dq_hbm, dkv_hbm, ret_hbm, blocks_hbm, *scratch):
+    weight, kv_all, normed, grad_query, grad_kv, returned, blocks, sems, out_sems = scratch
+    results = ((dq_hbm, grad_query), (dkv_hbm, grad_kv), (ret_hbm, returned))
+    small = start_all(results, sems.at[weight.shape[0] // (2 * CHUNK)])
     width = weight.shape[1]
     rows_all = weight.shape[0]
     size = 2 * CHUNK
@@ -192,6 +200,8 @@
         )
         for copy in copies[-1]:
             copy.start()
+    for copy in small:
+        copy.wait()
     tokens_here = grad_kv.shape[1]
     kv_grad = (grad_kv[...] + returned[...].astype(F32)).astype(BF16)
     grads = grad_query[...]
@@ -209,7 +219,7 @@
     high = total.astype(BF16).astype(F32)
     mid = (total - high).astype(BF16).astype(F32)
     low = total - high - mid
-    line = lax.broadcasted_iota(jnp.int32, (16, tokens_here), 0)
+    line = lax.broadcasted_iota(jnp.int32, (8, tokens_here), 0)
     extra = jnp.where(line == 0, high, jnp.where(line == 1, mid, jnp.where(line == 2, low, 0.0)))
     for group in range(8):
         blocks[group, 8 * PAD :, :] = extra.astype(BF16)
@@ -217,8 +227,8 @@
         copy.wait()
 
 
-ANY = pl.BlockSpec(memory_space=pltpu.MemorySpace.HBM)
-FULL = pl.BlockSpec(memory_space=pltpu.MemorySpace.VMEM)
+HBM = pl.BlockSpec(memory_space=pltpu.MemorySpace.HBM)
+ANY = pl.BlockSpec(memory_space=pl.ANY)
 
 
 def call(kernel, outs, in_specs, out_specs, scratch, *args):
@@ -256,15 +266,20 @@
     sent = call(
         pack_kernel,
         like((4, PAD, 2 * width + 2 * HD), BF16),
-        [FULL] * 4,
-        FULL,
-        [],
+        [ANY] * 4,
+        HBM,
+        [
+            *[pltpu.VMEM(w.shape, BF16) for w in (w_query, w_out, w_key, w_value)],
+            pltpu.VMEM((PAD, 2 * width + 2 * HD), BF16),
+            pltpu.SemaphoreType.DMA((4,)),
+        ],
         *(w_query, w_out, w_key, w_value),
     )
     near = lax.all_to_all(sent, "zh", 0, 0)
     whole = lax.all_gather(near[:, :, : 2 * width], ("y", "core"), axis=0, tiled=True)
     whole = whole.reshape(-1, 2 * width)
-    kv_near = near[:, :, 2 * width :].reshape(-1, 2 * HD)
+    kv_near = gathered(near[:, :, 2 * width :], ("y",))
+    kv_all = lax.all_gather(kv_near[:, None], "core", axis=1, tiled=True).reshape(-1, 2 * HD)
 
     tok = tokens.T.astype(F32)
     inverse = lax.rsqrt(jnp.mean(tok * tok, axis=0, keepdims=True) + EPSILON)
@@ -284,17 +299,14 @@
         one_hot.astype(F32), gate[None, :] * grad_share, ((1,), (1,)), precision=HIGHEST
     )
 
-    steer = jnp.sum(gathered(steer_part, ("zh", "core")), axis=0)
-    lanes = 3 * 128
-    parts = jnp.pad(split3(steer), ((0, 0), (0, 0), (0, lanes - share))).astype(BF16)
-    parts = parts.reshape(-1, lanes)
-    parts = [parts[:, k : k + 128] for k in range(0, lanes, 128)]
-    kv_rows = kv_near.shape[0]
-    both = gathered(jnp.concatenate([kv_near, *parts], axis=0), ("y",))
-    kv_all = both[:, :kv_rows].reshape(8, 1, kv_rows, 2 * HD)
-    kv_all = lax.all_gather(kv_all, "core", axis=1, tiled=True).reshape(-1, 2 * HD)
-    steer = jnp.sum(both[:, kv_rows:].astype(F32), axis=0).reshape(3, 3, 16, 128)
-    steer_grad = jnp.sum(steer, axis=1).transpose(1, 0, 2).reshape(16, lanes)[:, :share]
+
+    def exchanged(value, *steps):
+        for axis, step in steps:
+            pairs = [(i, i ^ step) for i in range(lax.axis_size(axis))]
+            value = value + lax.ppermute(value, axis, pairs)
+        return value
+
+    steer = exchanged(steer_part, ("core", 1), ("zh", 1))
 
     halo_seg = shifted(segment_ids, 1)
     halo_seg = jnp.where(lax.axis_index(SEQ) > 0, halo_seg, -1)
@@ -304,8 +316,10 @@
     query_pos = lax.broadcasted_iota(jnp.int32, (row_count, row_count), 1)
     key_seg = jnp.where(key_pos > query_pos, halo_seg[:, None], segment_ids[:, None])
     mask = (key_seg == segment_ids[None, :]).astype(F32)
-    whole, halo, mask, steer_grad, normed_b, grad_b, kv, kv_all = lax.optimization_barrier(
-        (whole, halo, mask, steer_grad, normed_b, grad_b, kv, kv_all)
+    steer, halo, kv, mask = lax.optimization_barrier((steer, halo, kv, mask))
+    steer = exchanged(steer, ("zh", 2), ("y", 1))
+    whole, halo, mask, steer, normed_b, grad_b, kv, kv_all = lax.optimization_barrier(
+        (whole, halo, mask, steer, normed_b, grad_b, kv, kv_all)
     )
     total_rows = whole.shape[0]
     dma = pltpu.SemaphoreType.DMA
@@ -317,36 +331,50 @@
             like((2 * HD, row_count), BF16),
             like((2 * HD, row_count), F32),
         ),
-        [ANY, ANY, ANY, FULL, FULL, FULL],
-        [ANY, FULL, FULL, FULL],
+        [HBM] * 3 + [ANY] * 3,
+        [HBM] + [ANY] * 3,
         [
             pltpu.VMEM((total_rows, 2 * width), BF16),
             pltpu.VMEM((total_rows, row_count), BF16),
             pltpu.VMEM((total_rows, row_count), BF16),
+            pltpu.VMEM((2 * HD, row_count), BF16),
+            pltpu.VMEM((2 * HD, row_count), BF16),
+            pltpu.VMEM((row_count, row_count), F32),
             pltpu.VMEM((8, 8 * PAD, row_count), BF16),
-            dma((10,)),
-            dma((8,)),
+            pltpu.VMEM((width, row_count), BF16),
+            pltpu.VMEM((2 * HD, row_count), BF16),
+            pltpu.VMEM((2 * HD, row_count), F32),
+            dma((9,)),
+            dma((11,)),
         ],
         *(whole, normed_b, grad_b, kv, halo, mask),
     )
     returned = shifted(grad_halo, -1)
     attn = lax.all_to_all(blocks, HEAD, 0, 0)
+    steer, grad_kv = lax.optimization_barrier((steer, grad_kv))
+    steer = exchanged(steer, ("y", 2))
+    steer, returned, grad_kv = lax.optimization_barrier((steer, returned, grad_kv))
     back = call(
         back_kernel,
-        like((8, 8 * PAD + 16, row_count), BF16),
-        [ANY, ANY, ANY, FULL, FULL, FULL],
-        ANY,
+        like((8, 8 * PAD + 8, row_count), BF16),
+        [HBM] * 3 + [ANY] * 3,
+        HBM,
         [
             pltpu.VMEM((total_rows, width), BF16),
             pltpu.VMEM((total_rows, 2 * HD), BF16),
             pltpu.VMEM((total_rows, row_count), BF16),
-            pltpu.VMEM((8, 8 * PAD + 16, row_count), BF16),
-            dma((4, 3)),
+            pltpu.VMEM((width, row_count), BF16),
+            pltpu.VMEM((2 * HD, row_count), F32),
+            pltpu.VMEM((2 * HD, row_count), BF16),
+            pltpu.VMEM((8, 8 * PAD + 8, row_count), BF16),
+            dma((5, 3)),
             dma((8,)),
         ],
         *(whole, kv_all, normed_b, grad_query, grad_kv, returned),
     )
+    steer, back = lax.optimization_barrier((steer, back))
     back = lax.all_to_all(back, HEAD, 0, 0)
+    steer_grad = exchanged(steer, ("y", 4))
 
     attn_share = unpadded(jnp.sum(attn.astype(F32), axis=0), share)
     token_share = lax.dynamic_slice_in_dim(tokens.T, start, share, 0).astype(F32)

time: 153 us -> 139 us (0.908)
  starting transfers between devices: 26.3 us -> 49 us
  waiting for transfers between devices: 34.7 us -> 18.1 us
  blocking collectives: 43.2 us -> 29 us
  Pallas kernels: 18.2 us -> 13.5 us
  local copies, waits for them, and re-layouts: 7.02 us -> 5.23 us
    ppermute x0 -> x6, starting transfers between devices: none -> 23.6 us  [exchanged(): value = value + lax.ppermute(value, axis, pairs)]
    all_to_all x1 -> x0, blocking collectives: 15.9 us -> none  [gathered(): return lax.all_to_all(spread, axes, 0, 0)]
    ppermute x3, waiting for transfers between devices: 15.7 us -> 0.49 us  [shifted(): return lax.ppermute(value, SEQ, pairs)]
    ppermute x0 -> x6, waiting for transfers between devices: none -> 11 us  [exchanged(): value = value + lax.ppermute(value, axis, pairs)]
    all_to_all x1, waiting for transfers between devices: 11 us -> 1.98 us  [shards(): back = lax.all_to_all(back, HEAD, 0, 0)]
    all_to_all x1, waiting for transfers between devices: 6.05 us -> 0.01 us  [gathered(): return lax.all_to_all(spread, axes, 0, 0)]
    pallas_call x3, Pallas kernels: 18.2 us -> 13.5 us  [call(): pl.pallas_call(kernel, out_shape=outs, in_specs=in_specs, out_specs=out_s...]
    all_gather x1, waiting for transfers between devices: 0.01 us -> 4.6 us  [shards(): lax.all_gather(near[:, :, :2 * width], ('y', 'core'), axis=0, tiled=True)]
  transfers between devices with their start and end apart: 7 -> 13, of which waited for: 5 -> 7; matrix products, arithmetic and copies ran while one was open for 8% -> 9% of each run, Pallas kernels for 3% -> 3%
where the time goes in v7:
time: 139 us
  starting transfers between devices  49 us (35%)
  blocking collectives  29 us (21%)
  waiting for transfers between devices  18.1 us (13%)
  between operations  14.5 us (10%)
  Pallas kernels  13.5 us (10%)
  other arithmetic  6.91 us (5%)
  local copies, waits for them, and re-layouts  5.23 us (4%)
  matrix products  2.44 us (2%)
    ppermute x6, starting transfers between devices, exchanged(): value = value + lax.ppermute(value, axis, pairs)  23.6 us
    all_to_all x1, blocking collectives, shards(): near = lax.all_to_all(sent, 'zh', 0, 0)  22.5 us
    pallas_call x3, Pallas kernels, call(): pl.pallas_call(kernel, out_shape=outs, in_specs=in_specs, out_specs=out_s...  13.5 us
    ppermute x6, waiting for transfers between devices, exchanged(): value = value + lax.ppermute(value, axis, pairs)  11 us
    ppermute x3, starting transfers between devices, shifted(): return lax.ppermute(value, SEQ, pairs)  7.91 us
    all_to_all x1, starting transfers between devices, gathered(): return lax.all_to_all(spread, axes, 0, 0)  6.82 us
    all_gather x1, blocking collectives, shards(): lax.all_gather(kv_near[:, None], 'core', axis=1, tiled=True)  6.47 us
    all_to_all x1, starting transfers between devices, shards(): attn = lax.all_to_all(blocks, HEAD, 0, 0)  5.49 us
  transfers between devices with their start and end apart: 13, of which 7 were waited for; matrix products, arithmetic and copies ran while one was open for 9% of the time, Pallas kernels for 3%

profile of v7, /device:TPU:1, one launch (start us, length us, event | category | flops | bytes accessed | tf_op | source)
XLA Modules:
  0.0 138.7 jit_solution(4756314585142587535)
XLA Ops:
  7.2 1.8 %shard_map.130 = bf16[4,48,1152]{2,1,0:T(8,128)(2,1)} custom-call(bf16[45,512]{1,0:T(8,128)(2,1)} %q_hbm.1, bf16[45,512]{1,0:T(8,128)(2,1)} %o_hbm.1, bf16[45,64]{1,0:T(8,128)(2,1)} %k_hbm.1, bf16[45,64]{1,0:T(8,128)(2,1)} %v_hbm.1), custom_call_target="tpu_custom_call" | custom-call | flops 100000000 | bytes 546048 | tf_op jit(solution)/shard_map/pallas_call | solution.py:236
  9.0 22.5 %all_to_all.20 = bf16[4,48,1152]{2,1,0:T(8,128)(2,1)S(1)} all-to-all(bf16[4,48,1152]{2,1,0:T(8,128)(2,1)} %shard_map.130), channel_id=1, replica_groups=mesh['zh'=4,'y'=8,'core'=2,'x'=4,'zl'=2] {'zh'}, dimensions={0} | all-to-all | bytes 884736 | tf_op jit(solution)/shard_map/all_to_all | solution.py:278
  31.5 0.8 slice.24
  32.9 0.8 broadcast_in_dim.28
  33.7 6.8 %all-to-all-start.1 = ((bf16[8,4,48,128]{3,2,1,0:T(8,128)(2,1)}), bf16[8,4,48,128]{3,2,1,0:T(8,128)(2,1)S(1)}, u32[]{:S(2)}, u32[]{:S(2)}) async-start(bf16[8,4,48,128]{3,2,1,0:T(8,128)(2,1)} %broadcast_in_dim.28), calls=%async_computation.1 | async-start | bytes 786432 | tf_op jit(solution)/shard_map/all_to_all | solution.py:30
  40.5 1.5 %multiply_reduce_fusion = (f32[128]{0:T(128)S(1)}, bf16[2880,128]{1,0:T(8,128)(2,1)S(1)}) fusion(f32[2880]{0:T(1024)S(1)} %copy-done.4, f32[2880]{0:T(1024)S(1)} %copy-done.5, f32[128]{0:T(128)S(1)} %add_rsqrt_fusion, bf16[128,2880]{0,1:T(8,128)(2,1)S(1)} %copy-done.1), kind=kLoop, calls=%fused_computation.9 | loop fusion | flops 2580352 | bytes 1498624 | tf_op jit(solution)/shard_map/reduce_sum | solution.py:291
  42.1 0.9 fusion.11
  42.9 7.0 %collective-permute-start = (f32[16,360]{1,0:T(8,128)}, f32[16,360]{1,0:T(8,128)}, u32[]{:S(2)}, u32[]{:S(2)}) collective-permute-start(f32[16,360]{1,0:T(8,128)} %fusion.11), channel_id=1, source_target_pairs={{0,8},{8,0},{1,9},{9,1},{2,10},{10,2},{3,11},{11,3},{4,12},{12,4},... | collective-permute-start | bytes 69128 | tf_op jit(solution)/shard_map/ppermute | solution.py:306
  50.0 3.5 %collective-permute-start.3 = (s32[128]{0:T(128)}, s32[128]{0:T(128)}, u32[]{:S(2)}, u32[]{:S(2)}) collective-permute-start(s32[128]{0:T(128)} %param.19), channel_id=1, source_target_pairs={{0,8},{8,16},{16,24},{24,32},{32,40},{40,48},{48,56},{56,64},{64,7... | collective-permute-start | bytes 1544 | tf_op jit(solution)/shard_map/ppermute | solution.py:24
  55.0 0.8 add.86
  55.8 2.1 %collective-permute-start.1 = (f32[16,360]{1,0:T(8,128)S(1)}, f32[16,360]{1,0:T(8,128)S(1)}, u32[]{:S(2)}, u32[]{:S(2)}) collective-permute-start(f32[16,360]{1,0:T(8,128)S(1)} %add.86), channel_id=1, source_target_pairs={{0,128},{128,0},{256,384},{384,256},{1,129},{129,1},{257,385},{385... | collective-permute-start | bytes 69128 | tf_op jit(solution)/shard_map/ppermute | solution.py:306
  57.9 6.5 %all-gather = bf16[8,8,48,128]{3,2,1,0:T(8,128)(2,1)S(1)} all-gather(bf16[8,4,48,128]{3,2,1,0:T(8,128)(2,1)S(1)} %all-to-all-done.1), channel_id=2, replica_groups=mesh['zh'=4,'y'=8,'core'=2,'x'=4,'zl'=2] {'core'}, dimensions={1}, use_global_device_ids=true | all-gather | bytes 1179648 | tf_op jit(solution)/shard_map/all_gather | solution.py:282
  64.8 1.9 %collective-permute-start.2 = (bf16[128,128]{1,0:T(8,128)(2,1)S(1)}, bf16[128,128]{1,0:T(8,128)(2,1)S(1)}, u32[]{:S(2)}, u32[]{:S(2)}) collective-permute-start(bf16[128,128]{1,0:T(8,128)(2,1)S(1)} %fusion.8.kv_hbm), channel_id=1, source_target_pairs={{0,8},{8,16},{16,24},{24,32},{32,40},{40,48},{48,56},{56,64},{64,7... | collective-permute-start | bytes 98312 | tf_op jit(solution)/shard_map/ppermute | solution.py:24
  66.7 1.5 %fusion.19.mask_hbm = f32[128,128]{1,0:T(8,128)} fusion(s32[128]{0:T(128)} %param.19, s32[128]{0:T(128)S(1)} %broadcast_select_fusion), kind=kLoop, calls=%fused_computation.34 | loop fusion | flops 65536 | bytes 66560 | tf_op jit(solution)/shard_map/convert_element_type | solution.py:318
  68.2 3.8 %collective-permute-start.4 = (f32[16,360]{1,0:T(8,128)S(1)}, f32[16,360]{1,0:T(8,128)S(1)}, u32[]{:S(2)}, u32[]{:S(2)}) collective-permute-start(f32[16,360]{1,0:T(8,128)S(1)} %add.87), channel_id=1, source_target_pairs={{0,256},{128,384},{256,0},{384,128},{1,257},{129,385},{257,1},{385... | collective-permute-start | bytes 69128 | tf_op jit(solution)/shard_map/ppermute | solution.py:306
  72.1 4.6 %collective-permute-done.4 = f32[16,360]{1,0:T(8,128)S(1)} collective-permute-done((f32[16,360]{1,0:T(8,128)S(1)}, f32[16,360]{1,0:T(8,128)S(1)}, u32[]{:S(2)}, u32[]{:S(2)}) %collective-permute-start.4) | collective-permute-done | bytes 23072 | tf_op jit(solution)/shard_map/ppermute | solution.py:306
  76.7 2.0 %collective-permute-start.5 = (f32[16,360]{1,0:T(8,128)S(1)}, f32[16,360]{1,0:T(8,128)S(1)}, u32[]{:S(2)}, u32[]{:S(2)}) collective-permute-start(f32[16,360]{1,0:T(8,128)S(1)} %add.90), channel_id=1, source_target_pairs={{0,16},{16,0},{32,48},{48,32},{64,80},{80,64},{96,112},{112,96},{1... | collective-permute-start | bytes 69128 | tf_op jit(solution)/shard_map/ppermute | solution.py:306
  78.8 1.1 pad.7
  80.2 1.0 pad.8.clone
  81.9 4.6 %all-gather.3.cloned.1.call-done = bf16[64,48,1024]{2,1,0:T(8,128)(2,1)} async-done(((bf16[4,48,1024]{2,1,0:T(8,128)(2,1)}), bf16[64,48,1024]{2,1,0:T(8,128)(2,1)}) %all-gather.3.cloned.1.call-update) | async-done | bytes 6291472 | tf_op jit(solution)/shard_map/all_gather | solution.py:279
  86.5 7.5 %shard_map.131 = (bf16[8,384,128]{2,1,0:T(8,128)(2,1)}, bf16[512,128]{1,0:T(8,128)(2,1)}, bf16[128,128]{1,0:T(8,128)(2,1)}, f32[128,128]{1,0:T(8,128)}) custom-call(bf16[3072,1024]{1,0:T(8,128)(2,1)} %bitcast.53, bf16[3072,128]{1,0:T(8,128)(2,1)} %bitcast.55, bf16[3072,128]{1,0:T(8,128)(2,1)} %bitcast.63, bf16[128,128]{1,0:T(8,128)(2,1)} %copy-done.7, ...), custom_call_target="tpu_custom_call" | custom-call | flops 100000000 | bytes 9011200 | tf_op jit(solution)/shard_map/pallas_call | solution.py:236
  94.1 5.5 %all-to-all-start.2 = ((bf16[8,384,128]{2,1,0:T(8,128)(2,1)}), bf16[8,384,128]{2,1,0:T(8,128)(2,1)S(1)}, u32[]{:S(2)}, u32[]{:S(2)}) async-start(bf16[8,384,128]{2,1,0:T(8,128)(2,1)} %get-tuple-element.36), calls=%async_computation.2 | async-start | bytes 1572864 | tf_op jit(solution)/shard_map/all_to_all | solution.py:353
  99.6 2.5 %collective-permute-start.7 = (bf16[128,128]{1,0:T(8,128)(2,1)S(1)}, bf16[128,128]{1,0:T(8,128)(2,1)S(1)}, u32[]{:S(2)}, u32[]{:S(2)}) collective-permute-start(bf16[128,128]{1,0:T(8,128)(2,1)S(1)} %copy-done.15), channel_id=1, source_target_pairs={{8,0},{16,8},{24,16},{32,24},{40,32},{48,40},{56,48},{64,56},{72,6... | collective-permute-start | bytes 98312 | tf_op jit(solution)/shard_map/ppermute | solution.py:24
  102.0 3.8 %collective-permute-start.6 = (f32[16,360]{1,0:T(8,128)S(1)}, f32[16,360]{1,0:T(8,128)S(1)}, u32[]{:S(2)}, u32[]{:S(2)}) collective-permute-start(f32[16,360]{1,0:T(8,128)S(1)} %add.91), channel_id=1, source_target_pairs={{0,32},{16,48},{32,0},{48,16},{64,96},{80,112},{96,64},{112,80},{1... | collective-permute-start | bytes 69128 | tf_op jit(solution)/shard_map/ppermute | solution.py:306
  105.8 2.4 %collective-permute-done.6 = f32[16,360]{1,0:T(8,128)S(1)} collective-permute-done((f32[16,360]{1,0:T(8,128)S(1)}, f32[16,360]{1,0:T(8,128)S(1)}, u32[]{:S(2)}, u32[]{:S(2)}) %collective-permute-start.6) | collective-permute-done | bytes 23072 | tf_op jit(solution)/shard_map/ppermute | solution.py:306
  108.8 4.2 %shard_map.132 = bf16[8,392,128]{2,1,0:T(8,128)(2,1)} custom-call(bf16[3072,1024]{1,0:T(8,128)(2,1)} %bitcast.54, bf16[3072,128]{1,0:T(8,128)(2,1)} %bitcast.59, bf16[3072,128]{1,0:T(8,128)(2,1)} %bitcast.56, bf16[512,128]{1,0:T(8,128)(2,1)} %get-tuple-element.44.dq_hbm, f32[128,128]{1,0:T(8,128)} %get-tuple-element.45.dkv_hbm, bf16[128,128]{1,0:T(8,128)(2,1)} %copy-done.9), custom_call_target="tpu_custom_call" | custom-call | flops 100000000 | bytes 8896512 | tf_op jit(solution)/shard_map/pallas_call | solution.py:236
  113.0 5.1 %all-to-all-start.3 = ((bf16[8,392,128]{2,1,0:T(8,128)(2,1)}), bf16[8,392,128]{2,1,0:T(8,128)(2,1)S(1)}, u32[]{:S(2)}, u32[]{:S(2)}) async-start(bf16[8,392,128]{2,1,0:T(8,128)(2,1)} %shard_map.132), calls=%async_computation.3 | async-start | bytes 1605632 | tf_op jit(solution)/shard_map/all_to_all | solution.py:376
  118.7 4.8 %collective-permute-start.8 = (f32[16,360]{1,0:T(8,128)S(1)}, f32[16,360]{1,0:T(8,128)S(1)}, u32[]{:S(2)}, u32[]{:S(2)}) collective-permute-start(f32[16,360]{1,0:T(8,128)S(1)} %add.94), channel_id=1, source_target_pairs={{0,64},{16,80},{32,96},{48,112},{64,0},{80,16},{96,32},{112,48},{1... | collective-permute-start | bytes 69128 | tf_op jit(solution)/shard_map/ppermute | solution.py:306
  123.9 3.3 %collective-permute-done.8 = f32[16,360]{1,0:T(8,128)S(1)} collective-permute-done((f32[16,360]{1,0:T(8,128)S(1)}, f32[16,360]{1,0:T(8,128)S(1)}, u32[]{:S(2)}, u32[]{:S(2)}) %collective-permute-start.8) | collective-permute-done | bytes 23072 | tf_op jit(solution)/shard_map/ppermute | solution.py:306
  127.9 1.0 fusion.7
  128.8 2.0 %all-to-all-done.3 = bf16[8,392,128]{2,1,0:T(8,128)(2,1)S(1)} async-done(((bf16[8,392,128]{2,1,0:T(8,128)(2,1)}), bf16[8,392,128]{2,1,0:T(8,128)(2,1)S(1)}, u32[]{:S(2)}, u32[]{:S(2)}) %all-to-all-start.3) | async-done | bytes 802848 | tf_op jit(solution)/shard_map/all_to_all | solution.py:376
  131.0 0.8 fusion.16
  (69 shorter events, 5.8 us)
Async XLA Ops:
  7.2 116.3 %copy-start = (bf16[16,2880]{1,0:T(8,128)(2,1)S(1)}, bf16[16,2880]{1,0:T(8,128)(2,1)}, u32[]{:S(2)}) copy-start(bf16[16,2880]{1,0:T(8,128)(2,1)} %param.18) | copy-start | bytes 276484
  7.2 25.2 %copy-start.1 = (bf16[128,2880]{0,1:T(8,128)(2,1)S(1)}, bf16[128,2880]{0,1:T(8,128)(2,1)}, u32[]{:S(2)}) copy-start(bf16[128,2880]{0,1:T(8,128)(2,1)} %param.11) | copy-start | bytes 2211844
  7.2 79.3 %all-gather.3.cloned.1.call-start = ((), (), s32[]{:S(2)}) async-start(), calls=%async_computation.4 | async-start | bytes 6684672 | tf_op jit(solution)/shard_map/all_gather | solution.py:279
  31.5 9.0 %copy-start.4 = (f32[2880]{0:T(1024)S(1)}, f32[2880]{0:T(1024)}, u32[]{:S(2)}) copy-start(f32[2880]{0:T(1024)} %param.17) | copy-start | bytes 34564
  31.5 9.0 %copy-start.5 = (f32[2880]{0:T(1024)S(1)}, f32[2880]{0:T(1024)}, u32[]{:S(2)}) copy-start(f32[2880]{0:T(1024)} %param.12) | copy-start | bytes 34564
  32.8 9.2 %copy-start.2 = (bf16[128,2880]{0,1:T(8,128)(2,1)S(1)}, bf16[128,2880]{0,1:T(8,128)(2,1)}, u32[]{:S(2)}) copy-start(bf16[128,2880]{0,1:T(8,128)(2,1)} %param.21) | copy-start | bytes 2211844
  32.8 9.3 %copy-start.10 = (s32[128]{0:T(128)S(1)}, s32[128]{0:T(128)}, u32[]{:S(2)}) copy-start(s32[128]{0:T(128)} %param.20) | copy-start | bytes 1540
  33.7 24.2 %all-to-all-start.1 = ((bf16[8,4,48,128]{3,2,1,0:T(8,128)(2,1)}), bf16[8,4,48,128]{3,2,1,0:T(8,128)(2,1)S(1)}, u32[]{:S(2)}, u32[]{:S(2)}) async-start(bf16[8,4,48,128]{3,2,1,0:T(8,128)(2,1)} %broadcast_in_dim.28), calls=%async_computation.1 | async-start | bytes 786432 | tf_op jit(solution)/shard_map/all_to_all | solution.py:30
  42.0 11.5 %copy-start.11 = (f32[128]{0:T(128)}, f32[128]{0:T(128)S(1)}, u32[]{:S(2)}) copy-start(f32[128]{0:T(128)S(1)} %get-tuple-element.51) | copy-start | bytes 1540
  42.1 11.5 %copy-start.13 = (f32[128]{0:T(128)}, f32[128]{0:T(128)S(1)}, u32[]{:S(2)}) copy-start(f32[128]{0:T(128)S(1)} %add_divide_fusion) | copy-start | bytes 1540
  42.9 12.1 %collective-permute-start = (f32[16,360]{1,0:T(8,128)}, f32[16,360]{1,0:T(8,128)}, u32[]{:S(2)}, u32[]{:S(2)}) collective-permute-start(f32[16,360]{1,0:T(8,128)} %fusion.11), channel_id=1, source_target_pairs={{0,8},{8,0},{1,9},{9,1},{2,10},{10,2},{3,11},{11,3},{4,12},{12,4},... | collective-permute-start | bytes 69128 | tf_op jit(solution)/shard_map/ppermute | solution.py:306
  50.0 4.4 %collective-permute-start.3 = (s32[128]{0:T(128)}, s32[128]{0:T(128)}, u32[]{:S(2)}, u32[]{:S(2)}) collective-permute-start(s32[128]{0:T(128)} %param.19), channel_id=1, source_target_pairs={{0,8},{8,16},{16,24},{24,32},{32,40},{40,48},{48,56},{56,64},{64,7... | collective-permute-start | bytes 1544 | tf_op jit(solution)/shard_map/ppermute | solution.py:24
  55.8 12.5 %collective-permute-start.1 = (f32[16,360]{1,0:T(8,128)S(1)}, f32[16,360]{1,0:T(8,128)S(1)}, u32[]{:S(2)}, u32[]{:S(2)}) collective-permute-start(f32[16,360]{1,0:T(8,128)S(1)} %add.86), channel_id=1, source_target_pairs={{0,128},{128,0},{256,384},{384,256},{1,129},{129,1},{257,385},{385... | collective-permute-start | bytes 69128 | tf_op jit(solution)/shard_map/ppermute | solution.py:306
  64.4 15.4 %copy-start.3 = (bf16[8,8,48,128]{3,2,1,0:T(8,128)(2,1)}, bf16[8,8,48,128]{3,2,1,0:T(8,128)(2,1)S(1)}, u32[]{:S(2)}) copy-start(bf16[8,8,48,128]{3,2,1,0:T(8,128)(2,1)S(1)} %all-gather) | copy-start | bytes 2359300
  64.8 15.3 %copy-start.7 = (bf16[128,128]{1,0:T(8,128)(2,1)}, bf16[128,128]{1,0:T(8,128)(2,1)S(1)}, u32[]{:S(2)}) copy-start(bf16[128,128]{1,0:T(8,128)(2,1)S(1)} %fusion.8.kv_hbm) | copy-start | bytes 98308
  64.8 3.4 %collective-permute-start.2 = (bf16[128,128]{1,0:T(8,128)(2,1)S(1)}, bf16[128,128]{1,0:T(8,128)(2,1)S(1)}, u32[]{:S(2)}, u32[]{:S(2)}) collective-permute-start(bf16[128,128]{1,0:T(8,128)(2,1)S(1)} %fusion.8.kv_hbm), channel_id=1, source_target_pairs={{0,8},{8,16},{16,24},{24,32},{32,40},{40,48},{48,56},{56,64},{64,7... | collective-permute-start | bytes 98312 | tf_op jit(solution)/shard_map/ppermute | solution.py:24
  68.2 11.9 %copy-start.8 = (bf16[128,128]{1,0:T(8,128)(2,1)}, bf16[128,128]{1,0:T(8,128)(2,1)S(1)}, u32[]{:S(2)}) copy-start(bf16[128,128]{1,0:T(8,128)(2,1)S(1)} %collective-permute-done.2.halo_hbm) | copy-start | bytes 98308
  68.2 8.5 %collective-permute-start.4 = (f32[16,360]{1,0:T(8,128)S(1)}, f32[16,360]{1,0:T(8,128)S(1)}, u32[]{:S(2)}, u32[]{:S(2)}) collective-permute-start(f32[16,360]{1,0:T(8,128)S(1)} %add.87), channel_id=1, source_target_pairs={{0,256},{128,384},{256,0},{384,128},{1,257},{129,385},{257,1},{385... | collective-permute-start | bytes 69128 | tf_op jit(solution)/shard_map/ppermute | solution.py:306
  76.7 5.2 %collective-permute-start.5 = (f32[16,360]{1,0:T(8,128)S(1)}, f32[16,360]{1,0:T(8,128)S(1)}, u32[]{:S(2)}, u32[]{:S(2)}) collective-permute-start(f32[16,360]{1,0:T(8,128)S(1)} %add.90), channel_id=1, source_target_pairs={{0,16},{16,0},{32,48},{48,32},{64,80},{80,64},{96,112},{112,96},{1... | collective-permute-start | bytes 69128 | tf_op jit(solution)/shard_map/ppermute | solution.py:306
  94.1 5.5 %copy-start.15 = (bf16[128,128]{1,0:T(8,128)(2,1)S(1)}, bf16[128,128]{1,0:T(8,128)(2,1)}, u32[]{:S(2)}) copy-start(bf16[128,128]{1,0:T(8,128)(2,1)} %get-tuple-element.40) | copy-start | bytes 98308
  94.1 19.0 %all-to-all-start.2 = ((bf16[8,384,128]{2,1,0:T(8,128)(2,1)}), bf16[8,384,128]{2,1,0:T(8,128)(2,1)S(1)}, u32[]{:S(2)}, u32[]{:S(2)}) async-start(bf16[8,384,128]{2,1,0:T(8,128)(2,1)} %get-tuple-element.36), calls=%async_computation.2 | async-start | bytes 1572864 | tf_op jit(solution)/shard_map/all_to_all | solution.py:353
  99.6 8.6 %collective-permute-start.7 = (bf16[128,128]{1,0:T(8,128)(2,1)S(1)}, bf16[128,128]{1,0:T(8,128)(2,1)S(1)}, u32[]{:S(2)}, u32[]{:S(2)}) collective-permute-start(bf16[128,128]{1,0:T(8,128)(2,1)S(1)} %copy-done.15), channel_id=1, source_target_pairs={{8,0},{16,8},{24,16},{32,24},{40,32},{48,40},{56,48},{64,56},{72,6... | collective-permute-start | bytes 98312 | tf_op jit(solution)/shard_map/ppermute | solution.py:24
  102.0 6.1 %collective-permute-start.6 = (f32[16,360]{1,0:T(8,128)S(1)}, f32[16,360]{1,0:T(8,128)S(1)}, u32[]{:S(2)}, u32[]{:S(2)}) collective-permute-start(f32[16,360]{1,0:T(8,128)S(1)} %add.91), channel_id=1, source_target_pairs={{0,32},{16,48},{32,0},{48,16},{64,96},{80,112},{96,64},{112,80},{1... | collective-permute-start | bytes 69128 | tf_op jit(solution)/shard_map/ppermute | solution.py:306
  108.2 0.6 copy-start.9
  113.0 5.2 %copy-start.6 = (f32[2880]{0:T(1024)S(1)}, f32[2880]{0:T(1024)}, u32[]{:S(2)}) copy-start(f32[2880]{0:T(1024)} %param.12) | copy-start | bytes 34564
  113.0 17.8 %all-to-all-start.3 = ((bf16[8,392,128]{2,1,0:T(8,128)(2,1)}), bf16[8,392,128]{2,1,0:T(8,128)(2,1)S(1)}, u32[]{:S(2)}, u32[]{:S(2)}) async-start(bf16[8,392,128]{2,1,0:T(8,128)(2,1)} %shard_map.132), calls=%async_computation.3 | async-start | bytes 1605632 | tf_op jit(solution)/shard_map/all_to_all | solution.py:376
  118.2 9.7 %copy-start.14 = (f32[128]{0:T(128)S(1)}, f32[128]{0:T(128)}, u32[]{:S(2)}) copy-start(f32[128]{0:T(128)} %copy-done.13) | copy-start | bytes 1540
  118.7 8.5 %collective-permute-start.8 = (f32[16,360]{1,0:T(8,128)S(1)}, f32[16,360]{1,0:T(8,128)S(1)}, u32[]{:S(2)}, u32[]{:S(2)}) collective-permute-start(f32[16,360]{1,0:T(8,128)S(1)} %add.94), channel_id=1, source_target_pairs={{0,64},{16,80},{32,96},{48,112},{64,0},{80,16},{96,32},{112,48},{1... | collective-permute-start | bytes 69128 | tf_op jit(solution)/shard_map/ppermute | solution.py:306
  127.8 3.1 %copy-start.12 = (f32[128]{0:T(128)S(1)}, f32[128]{0:T(128)}, u32[]{:S(2)}) copy-start(f32[128]{0:T(128)} %copy-done.11) | copy-start | bytes 1540
Sparse Core Ops, SparseCore 0:
  32.5 53.9 all-gather.2

commit v8 on v7

--- a/solution.py
+++ b/solution.py
@@ -144,7 +144,7 @@
             for copy in copies[2:7]:
                 copy.wait()
             keys = jnp.concatenate([halo[:HD, :], kv[:HD, :]], axis=1)
-            values = jnp.concatenate([halo[HD:, :], kv[HD:, :]], axis=1)
+            values = jnp.concatenate([halo[HD : 2 * HD, :], kv[HD:, :]], axis=1)
             allowed = jnp.concatenate([mask[...] > 0.0] * together, axis=1)
         else:
             copies[6 + 2 * column // span].wait()
@@ -308,16 +308,17 @@
 
     steer = exchanged(steer_part, ("core", 1), ("zh", 1))
 
-    halo_seg = shifted(segment_ids, 1)
+    kv = dot(kv_all, normed_b, ((0,), (0,))).astype(BF16)
+    ids = jnp.broadcast_to(segment_ids.astype(BF16)[None], (8, row_count))
+    halo = shifted(jnp.concatenate([kv, ids], axis=0), 1)
+    halo_seg = halo[2 * HD].astype(jnp.int32)
     halo_seg = jnp.where(lax.axis_index(SEQ) > 0, halo_seg, -1)
-    kv = dot(kv_all, normed_b, ((0,), (0,))).astype(BF16)
-    halo = shifted(kv, 1)
     key_pos = lax.broadcasted_iota(jnp.int32, (row_count, row_count), 0)
     query_pos = lax.broadcasted_iota(jnp.int32, (row_count, row_count), 1)
     key_seg = jnp.where(key_pos > query_pos, halo_seg[:, None], segment_ids[:, None])
     mask = (key_seg == segment_ids[None, :]).astype(F32)
     steer, halo, kv, mask = lax.optimization_barrier((steer, halo, kv, mask))
-    steer = exchanged(steer, ("zh", 2), ("y", 1))
+    steer = exchanged(steer, ("zh", 2), ("y", 1), ("y", 2))
     whole, halo, mask, steer, normed_b, grad_b, kv, kv_all = lax.optimization_barrier(
         (whole, halo, mask, steer, normed_b, grad_b, kv, kv_all)
     )
@@ -338,7 +339,7 @@
             pltpu.VMEM((total_rows, row_count), BF16),
             pltpu.VMEM((total_rows, row_count), BF16),
             pltpu.VMEM((2 * HD, row_count), BF16),
-            pltpu.VMEM((2 * HD, row_count), BF16),
+            pltpu.VMEM((2 * HD + 8, row_count), BF16),
             pltpu.VMEM((row_count, row_count), F32),
             pltpu.VMEM((8, 8 * PAD, row_count), BF16),
             pltpu.VMEM((width, row_count), BF16),
@@ -351,9 +352,6 @@
     )
     returned = shifted(grad_halo, -1)
     attn = lax.all_to_all(blocks, HEAD, 0, 0)
-    steer, grad_kv = lax.optimization_barrier((steer, grad_kv))
-    steer = exchanged(steer, ("y", 2))
-    steer, returned, grad_kv = lax.optimization_barrier((steer, returned, grad_kv))
     back = call(
         back_kernel,
         like((8, 8 * PAD + 8, row_count), BF16),

time: 139 us -> 147 us (1.058)
  blocking collectives: 29 us -> 34.8 us
  waiting for transfers between devices: 18.1 us -> 23.7 us
  starting transfers between devices: 49 us -> 44.9 us
    ppermute x6, waiting for transfers between devices: 11 us -> 19.5 us  [exchanged(): value = value + lax.ppermute(value, axis, pairs)]
    all_gather x1, blocking collectives: 6.47 us -> 12.3 us  [shards(): lax.all_gather(kv_near[:, None], 'core', axis=1, tiled=True)]
    ppermute x6, starting transfers between devices: 23.6 us -> 18 us  [exchanged(): value = value + lax.ppermute(value, axis, pairs)]
    all_gather x1, waiting for transfers between devices: 4.6 us -> 0.01 us  [shards(): lax.all_gather(near[:, :, :2 * width], ('y', 'core'), axis=0, tiled=True)]
    ppermute x3 -> x2, starting transfers between devices: 7.91 us -> 8.56 us  [shifted(): return lax.ppermute(value, SEQ, pairs)]
  transfers between devices with their start and end apart: 13 -> 12, of which waited for: 7 -> 7; matrix products, arithmetic and copies ran while one was open for 9% -> 8% of each run, Pallas kernels for 3% -> 3%
where the time goes in v8:
time: 147 us
  starting transfers between devices  44.9 us (31%)
  blocking collectives  34.8 us (24%)
  waiting for transfers between devices  23.7 us (16%)
  between operations  14.5 us (10%)
  Pallas kernels  13.5 us (9%)
  other arithmetic  6.83 us (5%)
  local copies, waits for them, and re-layouts  5.75 us (4%)
  matrix products  2.44 us (2%)
    all_to_all x1, blocking collectives, shards(): near = lax.all_to_all(sent, 'zh', 0, 0)  22.5 us
    ppermute x6, waiting for transfers between devices, exchanged(): value = value + lax.ppermute(value, axis, pairs)  19.5 us
    ppermute x6, starting transfers between devices, exchanged(): value = value + lax.ppermute(value, axis, pairs)  18 us
    pallas_call x3, Pallas kernels, call(): pl.pallas_call(kernel, out_shape=outs, in_specs=in_specs, out_specs=out_s...  13.5 us
    all_gather x1, blocking collectives, shards(): lax.all_gather(kv_near[:, None], 'core', axis=1, tiled=True)  12.3 us
    ppermute x2, starting transfers between devices, shifted(): return lax.ppermute(value, SEQ, pairs)  8.56 us
    all_to_all x1, starting transfers between devices, gathered(): return lax.all_to_all(spread, axes, 0, 0)  6.82 us
    all_to_all x1, starting transfers between devices, shards(): attn = lax.all_to_all(blocks, HEAD, 0, 0)  6.08 us
  transfers between devices with their start and end apart: 12, of which 7 were waited for; matrix products, arithmetic and copies ran while one was open for 8% of the time, Pallas kernels for 3%

profile of v8, /device:TPU:1, one launch (start us, length us, event | category | flops | bytes accessed | tf_op | source)
XLA Modules:
  0.0 146.5 jit_solution(16466193190778215840)
XLA Ops:
  7.2 1.8 %shard_map.130 = bf16[4,48,1152]{2,1,0:T(8,128)(2,1)} custom-call(bf16[45,512]{1,0:T(8,128)(2,1)} %q_hbm.1, bf16[45,512]{1,0:T(8,128)(2,1)} %o_hbm.1, bf16[45,64]{1,0:T(8,128)(2,1)} %k_hbm.1, bf16[45,64]{1,0:T(8,128)(2,1)} %v_hbm.1), custom_call_target="tpu_custom_call" | custom-call | flops 100000000 | bytes 546048 | tf_op jit(solution)/shard_map/pallas_call | solution.py:236
  9.0 22.5 %all_to_all.20 = bf16[4,48,1152]{2,1,0:T(8,128)(2,1)S(1)} all-to-all(bf16[4,48,1152]{2,1,0:T(8,128)(2,1)} %shard_map.130), channel_id=1, replica_groups=mesh['zh'=4,'y'=8,'core'=2,'x'=4,'zl'=2] {'zh'}, dimensions={0} | all-to-all | bytes 884736 | tf_op jit(solution)/shard_map/all_to_all | solution.py:278
  31.6 0.8 slice.28
  32.9 0.8 broadcast_in_dim.24
  33.7 6.8 %all-to-all-start.1 = ((bf16[8,4,48,128]{3,2,1,0:T(8,128)(2,1)}), bf16[8,4,48,128]{3,2,1,0:T(8,128)(2,1)S(1)}, u32[]{:S(2)}, u32[]{:S(2)}) async-start(bf16[8,4,48,128]{3,2,1,0:T(8,128)(2,1)} %broadcast_in_dim.24), calls=%async_computation.1 | async-start | bytes 786432 | tf_op jit(solution)/shard_map/all_to_all | solution.py:30
  40.5 1.5 %multiply_reduce_fusion = (f32[128]{0:T(128)S(1)}, bf16[2880,128]{1,0:T(8,128)(2,1)S(1)}) fusion(f32[2880]{0:T(1024)S(1)} %copy-done.5, f32[2880]{0:T(1024)S(1)} %copy-done.6, f32[128]{0:T(128)S(1)} %add_rsqrt_fusion, bf16[128,2880]{0,1:T(8,128)(2,1)S(1)} %copy-done.1), kind=kLoop, calls=%fused_computation.9 | loop fusion | flops 2580352 | bytes 1498624 | tf_op jit(solution)/shard_map/reduce_sum | solution.py:291
  42.1 0.9 fusion.11
  43.0 7.0 %collective-permute-start = (f32[16,360]{1,0:T(8,128)}, f32[16,360]{1,0:T(8,128)}, u32[]{:S(2)}, u32[]{:S(2)}) collective-permute-start(f32[16,360]{1,0:T(8,128)} %fusion.11), channel_id=1, source_target_pairs={{0,8},{8,0},{1,9},{9,1},{2,10},{10,2},{3,11},{11,3},{4,12},{12,4},... | collective-permute-start | bytes 69128 | tf_op jit(solution)/shard_map/ppermute | solution.py:306
  51.4 12.3 %all-gather = bf16[8,8,48,128]{3,2,1,0:T(8,128)(2,1)S(1)} all-gather(bf16[8,4,48,128]{3,2,1,0:T(8,128)(2,1)S(1)} %all-to-all-done.1), channel_id=2, replica_groups=mesh['zh'=4,'y'=8,'core'=2,'x'=4,'zl'=2] {'core'}, dimensions={1}, use_global_device_ids=true | all-gather | bytes 1179648 | tf_op jit(solution)/shard_map/all_gather | solution.py:282
  64.2 2.1 %collective-permute-start.2 = (bf16[136,128]{1,0:T(8,128)(2,1)S(1)}, bf16[136,128]{1,0:T(8,128)(2,1)S(1)}, u32[]{:S(2)}, u32[]{:S(2)}) collective-permute-start(bf16[136,128]{1,0:T(8,128)(2,1)S(1)} %pad_maximum_fusion), channel_id=1, source_target_pairs={{0,8},{8,16},{16,24},{24,32},{32,40},{40,48},{48,56},{56,64},{64,7... | collective-permute-start | bytes 104456 | tf_op jit(solution)/shard_map/ppermute | solution.py:24
  67.1 1.9 %collective-permute-start.1 = (f32[16,360]{1,0:T(8,128)S(1)}, f32[16,360]{1,0:T(8,128)S(1)}, u32[]{:S(2)}, u32[]{:S(2)}) collective-permute-start(f32[16,360]{1,0:T(8,128)S(1)} %add.86), channel_id=1, source_target_pairs={{0,128},{128,0},{256,384},{384,256},{1,129},{129,1},{257,385},{385... | collective-permute-start | bytes 69128 | tf_op jit(solution)/shard_map/ppermute | solution.py:306
  69.0 3.9 %collective-permute-done.1 = f32[16,360]{1,0:T(8,128)S(1)} collective-permute-done((f32[16,360]{1,0:T(8,128)S(1)}, f32[16,360]{1,0:T(8,128)S(1)}, u32[]{:S(2)}, u32[]{:S(2)}) %collective-permute-start.1) | collective-permute-done | bytes 23072 | tf_op jit(solution)/shard_map/ppermute | solution.py:306
  73.0 1.5 fusion.19.mask_hbm
  74.4 1.9 %collective-permute-start.3 = (f32[16,360]{1,0:T(8,128)S(1)}, f32[16,360]{1,0:T(8,128)S(1)}, u32[]{:S(2)}, u32[]{:S(2)}) collective-permute-start(f32[16,360]{1,0:T(8,128)S(1)} %add.87), channel_id=1, source_target_pairs={{0,256},{128,384},{256,0},{384,128},{1,257},{129,385},{257,1},{385... | collective-permute-start | bytes 69128 | tf_op jit(solution)/shard_map/ppermute | solution.py:306
  76.4 6.5 %collective-permute-done.3 = f32[16,360]{1,0:T(8,128)S(1)} collective-permute-done((f32[16,360]{1,0:T(8,128)S(1)}, f32[16,360]{1,0:T(8,128)S(1)}, u32[]{:S(2)}, u32[]{:S(2)}) %collective-permute-start.3) | collective-permute-done | bytes 23072 | tf_op jit(solution)/shard_map/ppermute | solution.py:306
  82.9 1.9 %collective-permute-start.4 = (f32[16,360]{1,0:T(8,128)S(1)}, f32[16,360]{1,0:T(8,128)S(1)}, u32[]{:S(2)}, u32[]{:S(2)}) collective-permute-start(f32[16,360]{1,0:T(8,128)S(1)} %add.90), channel_id=1, source_target_pairs={{0,16},{16,0},{32,48},{48,32},{64,80},{80,64},{96,112},{112,96},{1... | collective-permute-start | bytes 69128 | tf_op jit(solution)/shard_map/ppermute | solution.py:306
  84.8 2.6 %collective-permute-done.4 = f32[16,360]{1,0:T(8,128)S(1)} collective-permute-done((f32[16,360]{1,0:T(8,128)S(1)}, f32[16,360]{1,0:T(8,128)S(1)}, u32[]{:S(2)}, u32[]{:S(2)}) %collective-permute-start.4) | collective-permute-done | bytes 23072 | tf_op jit(solution)/shard_map/ppermute | solution.py:306
  87.5 2.0 %collective-permute-start.5 = (f32[16,360]{1,0:T(8,128)S(1)}, f32[16,360]{1,0:T(8,128)S(1)}, u32[]{:S(2)}, u32[]{:S(2)}) collective-permute-start(f32[16,360]{1,0:T(8,128)S(1)} %add.91), channel_id=1, source_target_pairs={{0,32},{16,48},{32,0},{48,16},{64,96},{80,112},{96,64},{112,80},{1... | collective-permute-start | bytes 69128 | tf_op jit(solution)/shard_map/ppermute | solution.py:306
  89.4 1.0 pad.7
  90.8 1.0 pad.8.clone
  91.8 1.1 collective-permute-done.5
  92.9 7.5 %shard_map.131 = (bf16[8,384,128]{2,1,0:T(8,128)(2,1)}, bf16[512,128]{1,0:T(8,128)(2,1)}, bf16[128,128]{1,0:T(8,128)(2,1)}, f32[128,128]{1,0:T(8,128)}) custom-call(bf16[3072,1024]{1,0:T(8,128)(2,1)} %bitcast.55, bf16[3072,128]{1,0:T(8,128)(2,1)} %bitcast.57, bf16[3072,128]{1,0:T(8,128)(2,1)} %bitcast.62, bf16[128,128]{1,0:T(8,128)(2,1)} %copy-done.4, ...), custom_call_target="tpu_custom_call" | custom-call | flops 100000000 | bytes 9013248 | tf_op jit(solution)/shard_map/pallas_call | solution.py:236
  100.5 6.1 %all-to-all-start.2 = ((bf16[8,384,128]{2,1,0:T(8,128)(2,1)}), bf16[8,384,128]{2,1,0:T(8,128)(2,1)S(1)}, u32[]{:S(2)}, u32[]{:S(2)}) async-start(bf16[8,384,128]{2,1,0:T(8,128)(2,1)} %get-tuple-element.31), calls=%async_computation.2 | async-start | bytes 1572864 | tf_op jit(solution)/shard_map/all_to_all | solution.py:354
  106.6 6.5 %collective-permute-start.6 = (bf16[128,128]{1,0:T(8,128)(2,1)S(1)}, bf16[128,128]{1,0:T(8,128)(2,1)S(1)}, u32[]{:S(2)}, u32[]{:S(2)}) collective-permute-start(bf16[128,128]{1,0:T(8,128)(2,1)S(1)} %copy-done.17), channel_id=1, source_target_pairs={{8,0},{16,8},{24,16},{32,24},{40,32},{48,40},{56,48},{64,56},{72,6... | collective-permute-start | bytes 98312 | tf_op jit(solution)/shard_map/ppermute | solution.py:24
  113.0 1.8 %collective-permute-done.6.ret_hbm = bf16[128,128]{1,0:T(8,128)(2,1)S(1)} collective-permute-done((bf16[128,128]{1,0:T(8,128)(2,1)S(1)}, bf16[128,128]{1,0:T(8,128)(2,1)S(1)}, u32[]{:S(2)}, u32[]{:S(2)}) %collective-permute-start.6) | collective-permute-done | bytes 32800 | tf_op jit(solution)/shard_map/ppermute | solution.py:24
  115.5 4.2 %shard_map.132 = bf16[8,392,128]{2,1,0:T(8,128)(2,1)} custom-call(bf16[3072,1024]{1,0:T(8,128)(2,1)} %bitcast.56, bf16[3072,128]{1,0:T(8,128)(2,1)} %bitcast.61, bf16[3072,128]{1,0:T(8,128)(2,1)} %bitcast.58, bf16[512,128]{1,0:T(8,128)(2,1)} %get-tuple-element.34.dq_hbm, f32[128,128]{1,0:T(8,128)} %get-tuple-element.35.dkv_hbm, bf16[128,128]{1,0:T(8,128)(2,1)} %copy-done.9), custom_call_target="tpu_custom_call" | custom-call | flops 100000000 | bytes 8896512 | tf_op jit(solution)/shard_map/pallas_call | solution.py:236
  119.7 5.4 %all-to-all-start.3 = ((bf16[8,392,128]{2,1,0:T(8,128)(2,1)}), bf16[8,392,128]{2,1,0:T(8,128)(2,1)S(1)}, u32[]{:S(2)}, u32[]{:S(2)}) async-start(bf16[8,392,128]{2,1,0:T(8,128)(2,1)} %shard_map.132), calls=%async_computation.3 | async-start | bytes 1605632 | tf_op jit(solution)/shard_map/all_to_all | solution.py:374
  125.6 3.3 %collective-permute-start.7 = (f32[16,360]{1,0:T(8,128)S(1)}, f32[16,360]{1,0:T(8,128)S(1)}, u32[]{:S(2)}, u32[]{:S(2)}) collective-permute-start(f32[16,360]{1,0:T(8,128)S(1)} %add.92), channel_id=1, source_target_pairs={{0,64},{16,80},{32,96},{48,112},{64,0},{80,16},{96,32},{112,48},{1... | collective-permute-start | bytes 69128 | tf_op jit(solution)/shard_map/ppermute | solution.py:306
  129.3 5.2 %collective-permute-done.7 = f32[16,360]{1,0:T(8,128)S(1)} collective-permute-done((f32[16,360]{1,0:T(8,128)S(1)}, f32[16,360]{1,0:T(8,128)S(1)}, u32[]{:S(2)}, u32[]{:S(2)}) %collective-permute-start.7) | collective-permute-done | bytes 23072 | tf_op jit(solution)/shard_map/ppermute | solution.py:306
  135.3 1.0 fusion.7
  136.2 2.5 %all-to-all-done.3 = bf16[8,392,128]{2,1,0:T(8,128)(2,1)S(1)} async-done(((bf16[8,392,128]{2,1,0:T(8,128)(2,1)}), bf16[8,392,128]{2,1,0:T(8,128)(2,1)S(1)}, u32[]{:S(2)}, u32[]{:S(2)}) %all-to-all-start.3) | async-done | bytes 802848 | tf_op jit(solution)/shard_map/all_to_all | solution.py:374
  138.9 0.8 fusion.16
  (74 shorter events, 5.8 us)
Async XLA Ops:
  7.2 121.7 %copy-start = (bf16[16,2880]{1,0:T(8,128)(2,1)S(1)}, bf16[16,2880]{1,0:T(8,128)(2,1)}, u32[]{:S(2)}) copy-start(bf16[16,2880]{1,0:T(8,128)(2,1)} %param.18) | copy-start | bytes 276484
  7.2 25.3 %copy-start.1 = (bf16[128,2880]{0,1:T(8,128)(2,1)S(1)}, bf16[128,2880]{0,1:T(8,128)(2,1)}, u32[]{:S(2)}) copy-start(bf16[128,2880]{0,1:T(8,128)(2,1)} %param.11) | copy-start | bytes 2211844
  7.2 85.8 %all-gather.3.cloned.1.call-start = ((), (), s32[]{:S(2)}) async-start(), calls=%async_computation.4 | async-start | bytes 6684672 | tf_op jit(solution)/shard_map/all_gather | solution.py:279
  31.5 9.0 %copy-start.5 = (f32[2880]{0:T(1024)S(1)}, f32[2880]{0:T(1024)}, u32[]{:S(2)}) copy-start(f32[2880]{0:T(1024)} %param.17) | copy-start | bytes 34564
  31.5 9.0 %copy-start.6 = (f32[2880]{0:T(1024)S(1)}, f32[2880]{0:T(1024)}, u32[]{:S(2)}) copy-start(f32[2880]{0:T(1024)} %param.12) | copy-start | bytes 34564
  32.8 9.2 %copy-start.2 = (bf16[128,2880]{0,1:T(8,128)(2,1)S(1)}, bf16[128,2880]{0,1:T(8,128)(2,1)}, u32[]{:S(2)}) copy-start(bf16[128,2880]{0,1:T(8,128)(2,1)} %param.21) | copy-start | bytes 2211844
  32.8 9.2 %copy-start.10 = (s32[128]{0:T(128)S(1)}, s32[128]{0:T(128)}, u32[]{:S(2)}) copy-start(s32[128]{0:T(128)} %param.20) | copy-start | bytes 1540
  33.7 17.7 %all-to-all-start.1 = ((bf16[8,4,48,128]{3,2,1,0:T(8,128)(2,1)}), bf16[8,4,48,128]{3,2,1,0:T(8,128)(2,1)S(1)}, u32[]{:S(2)}, u32[]{:S(2)}) async-start(bf16[8,4,48,128]{3,2,1,0:T(8,128)(2,1)} %broadcast_in_dim.24), calls=%async_computation.1 | async-start | bytes 786432 | tf_op jit(solution)/shard_map/all_to_all | solution.py:30
  42.0 8.0 %copy-start.11 = (f32[128]{0:T(128)}, f32[128]{0:T(128)S(1)}, u32[]{:S(2)}) copy-start(f32[128]{0:T(128)S(1)} %get-tuple-element.41) | copy-start | bytes 1540
  42.1 7.9 %copy-start.14 = (f32[128]{0:T(128)}, f32[128]{0:T(128)S(1)}, u32[]{:S(2)}) copy-start(f32[128]{0:T(128)S(1)} %add_divide_fusion) | copy-start | bytes 1540
  43.0 23.4 %collective-permute-start = (f32[16,360]{1,0:T(8,128)}, f32[16,360]{1,0:T(8,128)}, u32[]{:S(2)}, u32[]{:S(2)}) collective-permute-start(f32[16,360]{1,0:T(8,128)} %fusion.11), channel_id=1, source_target_pairs={{0,8},{8,0},{1,9},{9,1},{2,10},{10,2},{3,11},{11,3},{4,12},{12,4},... | collective-permute-start | bytes 69128 | tf_op jit(solution)/shard_map/ppermute | solution.py:306
  50.3 0.7 copy-start.13
  51.4 12.7 %copy-start.16 = (bf16[128]{0:T(256)(128)(2,1)S(1)}, bf16[128]{0:T(256)(128)(2,1)}, u32[]{:S(2)}) copy-start(bf16[128]{0:T(256)(128)(2,1)} %convert_element_type.68) | copy-start | bytes 772
  63.8 26.7 %copy-start.3 = (bf16[8,8,48,128]{3,2,1,0:T(8,128)(2,1)}, bf16[8,8,48,128]{3,2,1,0:T(8,128)(2,1)S(1)}, u32[]{:S(2)}) copy-start(bf16[8,8,48,128]{3,2,1,0:T(8,128)(2,1)S(1)} %all-gather) | copy-start | bytes 2359300
  64.2 26.5 %copy-start.4 = (bf16[128,128]{1,0:T(8,128)(2,1)}, bf16[128,128]{1,0:T(8,128)(2,1)S(1)}, u32[]{:S(2)}) copy-start(bf16[128,128]{1,0:T(8,128)(2,1)S(1)} %fusion.8.kv_hbm) | copy-start | bytes 98308
  64.2 8.7 %collective-permute-start.2 = (bf16[136,128]{1,0:T(8,128)(2,1)S(1)}, bf16[136,128]{1,0:T(8,128)(2,1)S(1)}, u32[]{:S(2)}, u32[]{:S(2)}) collective-permute-start(bf16[136,128]{1,0:T(8,128)(2,1)S(1)} %pad_maximum_fusion), channel_id=1, source_target_pairs={{0,8},{8,16},{16,24},{24,32},{32,40},{40,48},{48,56},{56,64},{64,7... | collective-permute-start | bytes 104456 | tf_op jit(solution)/shard_map/ppermute | solution.py:24
  67.1 5.9 %collective-permute-start.1 = (f32[16,360]{1,0:T(8,128)S(1)}, f32[16,360]{1,0:T(8,128)S(1)}, u32[]{:S(2)}, u32[]{:S(2)}) collective-permute-start(f32[16,360]{1,0:T(8,128)S(1)} %add.86), channel_id=1, source_target_pairs={{0,128},{128,0},{256,384},{384,256},{1,129},{129,1},{257,385},{385... | collective-permute-start | bytes 69128 | tf_op jit(solution)/shard_map/ppermute | solution.py:306
  73.0 17.7 %copy-start.8 = (bf16[136,128]{1,0:T(8,128)(2,1)}, bf16[136,128]{1,0:T(8,128)(2,1)S(1)}, u32[]{:S(2)}) copy-start(bf16[136,128]{1,0:T(8,128)(2,1)S(1)} %collective-permute-done.2.halo_hbm) | copy-start | bytes 104452
  74.4 8.5 %collective-permute-start.3 = (f32[16,360]{1,0:T(8,128)S(1)}, f32[16,360]{1,0:T(8,128)S(1)}, u32[]{:S(2)}, u32[]{:S(2)}) collective-permute-start(f32[16,360]{1,0:T(8,128)S(1)} %add.87), channel_id=1, source_target_pairs={{0,256},{128,384},{256,0},{384,128},{1,257},{129,385},{257,1},{385... | collective-permute-start | bytes 69128 | tf_op jit(solution)/shard_map/ppermute | solution.py:306
  82.9 4.6 %collective-permute-start.4 = (f32[16,360]{1,0:T(8,128)S(1)}, f32[16,360]{1,0:T(8,128)S(1)}, u32[]{:S(2)}, u32[]{:S(2)}) collective-permute-start(f32[16,360]{1,0:T(8,128)S(1)} %add.90), channel_id=1, source_target_pairs={{0,16},{16,0},{32,48},{48,32},{64,80},{80,64},{96,112},{112,96},{1... | collective-permute-start | bytes 69128 | tf_op jit(solution)/shard_map/ppermute | solution.py:306
  87.5 5.5 %collective-permute-start.5 = (f32[16,360]{1,0:T(8,128)S(1)}, f32[16,360]{1,0:T(8,128)S(1)}, u32[]{:S(2)}, u32[]{:S(2)}) collective-permute-start(f32[16,360]{1,0:T(8,128)S(1)} %add.91), channel_id=1, source_target_pairs={{0,32},{16,48},{32,0},{48,16},{64,96},{80,112},{96,64},{112,80},{1... | collective-permute-start | bytes 69128 | tf_op jit(solution)/shard_map/ppermute | solution.py:306
  100.5 6.1 %copy-start.17 = (bf16[128,128]{1,0:T(8,128)(2,1)S(1)}, bf16[128,128]{1,0:T(8,128)(2,1)}, u32[]{:S(2)}) copy-start(bf16[128,128]{1,0:T(8,128)(2,1)} %get-tuple-element.36) | copy-start | bytes 98308
  100.5 19.2 %all-to-all-start.2 = ((bf16[8,384,128]{2,1,0:T(8,128)(2,1)}), bf16[8,384,128]{2,1,0:T(8,128)(2,1)S(1)}, u32[]{:S(2)}, u32[]{:S(2)}) async-start(bf16[8,384,128]{2,1,0:T(8,128)(2,1)} %get-tuple-element.31), calls=%async_computation.2 | async-start | bytes 1572864 | tf_op jit(solution)/shard_map/all_to_all | solution.py:354
  106.6 8.3 %collective-permute-start.6 = (bf16[128,128]{1,0:T(8,128)(2,1)S(1)}, bf16[128,128]{1,0:T(8,128)(2,1)S(1)}, u32[]{:S(2)}, u32[]{:S(2)}) collective-permute-start(bf16[128,128]{1,0:T(8,128)(2,1)S(1)} %copy-done.17), channel_id=1, source_target_pairs={{8,0},{16,8},{24,16},{32,24},{40,32},{48,40},{56,48},{64,56},{72,6... | collective-permute-start | bytes 98312 | tf_op jit(solution)/shard_map/ppermute | solution.py:24
  114.8 0.6 copy-start.9
  119.7 5.4 %copy-start.7 = (f32[2880]{0:T(1024)S(1)}, f32[2880]{0:T(1024)}, u32[]{:S(2)}) copy-start(f32[2880]{0:T(1024)} %param.12) | copy-start | bytes 34564
  119.7 19.0 %all-to-all-start.3 = ((bf16[8,392,128]{2,1,0:T(8,128)(2,1)}), bf16[8,392,128]{2,1,0:T(8,128)(2,1)S(1)}, u32[]{:S(2)}, u32[]{:S(2)}) async-start(bf16[8,392,128]{2,1,0:T(8,128)(2,1)} %shard_map.132), calls=%async_computation.3 | async-start | bytes 1605632 | tf_op jit(solution)/shard_map/all_to_all | solution.py:374
  125.2 10.1 %copy-start.15 = (f32[128]{0:T(128)S(1)}, f32[128]{0:T(128)}, u32[]{:S(2)}) copy-start(f32[128]{0:T(128)} %copy-done.14) | copy-start | bytes 1540
  125.6 8.9 %collective-permute-start.7 = (f32[16,360]{1,0:T(8,128)S(1)}, f32[16,360]{1,0:T(8,128)S(1)}, u32[]{:S(2)}, u32[]{:S(2)}) collective-permute-start(f32[16,360]{1,0:T(8,128)S(1)} %add.92), channel_id=1, source_target_pairs={{0,64},{16,80},{32,96},{48,112},{64,0},{80,16},{96,32},{112,48},{1... | collective-permute-start | bytes 69128 | tf_op jit(solution)/shard_map/ppermute | solution.py:306
  135.2 3.6 %copy-start.12 = (f32[128]{0:T(128)S(1)}, f32[128]{0:T(128)}, u32[]{:S(2)}) copy-start(f32[128]{0:T(128)} %copy-done.11) | copy-start | bytes 1540
Sparse Core Ops, SparseCore 0:
  32.5 53.9 all-gather.2

commit v9 on v8

--- a/solution.py
+++ b/solution.py
@@ -279,8 +279,6 @@
     whole = lax.all_gather(near[:, :, : 2 * width], ("y", "core"), axis=0, tiled=True)
     whole = whole.reshape(-1, 2 * width)
     kv_near = gathered(near[:, :, 2 * width :], ("y",))
-    kv_all = lax.all_gather(kv_near[:, None], "core", axis=1, tiled=True).reshape(-1, 2 * HD)
-
     tok = tokens.T.astype(F32)
     inverse = lax.rsqrt(jnp.mean(tok * tok, axis=0, keepdims=True) + EPSILON)
     unit = tok * inverse
@@ -307,8 +305,11 @@
         return value
 
     steer = exchanged(steer_part, ("core", 1), ("zh", 1))
+    steer, kv_near = lax.optimization_barrier((steer, kv_near))
+    kv_all = lax.all_gather(kv_near[:, None], "core", axis=1, tiled=True).reshape(-1, 2 * HD)
 
     kv = dot(kv_all, normed_b, ((0,), (0,))).astype(BF16)
+    steer, kv = lax.optimization_barrier((steer, kv))
     ids = jnp.broadcast_to(segment_ids.astype(BF16)[None], (8, row_count))
     halo = shifted(jnp.concatenate([kv, ids], axis=0), 1)
     halo_seg = halo[2 * HD].astype(jnp.int32)
@@ -317,7 +318,6 @@
     query_pos = lax.broadcasted_iota(jnp.int32, (row_count, row_count), 1)
     key_seg = jnp.where(key_pos > query_pos, halo_seg[:, None], segment_ids[:, None])
     mask = (key_seg == segment_ids[None, :]).astype(F32)
-    steer, halo, kv, mask = lax.optimization_barrier((steer, halo, kv, mask))
     steer = exchanged(steer, ("zh", 2), ("y", 1), ("y", 2))
     whole, halo, mask, steer, normed_b, grad_b, kv, kv_all = lax.optimization_barrier(
         (whole, halo, mask, steer, normed_b, grad_b, kv, kv_all)

time: 147 us -> 140 us (0.952)
  blocking collectives: 34.8 us -> 26.6 us
  waiting for transfers between devices: 23.7 us -> 18.2 us
  starting transfers between devices: 44.9 us -> 49.6 us
    all_gather x1, blocking collectives: 12.3 us -> 4.06 us  [shards(): lax.all_gather(kv_near[:, None], 'core', axis=1, tiled=True)]
    ppermute x6, starting transfers between devices: 18 us -> 24.6 us  [exchanged(): value = value + lax.ppermute(value, axis, pairs)]
    ppermute x6, waiting for transfers between devices: 19.5 us -> 13.6 us  [exchanged(): value = value + lax.ppermute(value, axis, pairs)]
    all_to_all x1, starting transfers between devices: 6.08 us -> 4.05 us  [shards(): attn = lax.all_to_all(blocks, HEAD, 0, 0)]
    add x6, other arithmetic: 1.39 us -> 3.34 us  [exchanged(): value = value + lax.ppermute(value, axis, pairs)]
  transfers between devices with their start and end apart: 12 -> 12, of which waited for: 7 -> 8; matrix products, arithmetic and copies ran while one was open for 8% -> 9% of each run, Pallas kernels for 3% -> 3%
where the time goes in v9:
time: 140 us; the launch traced here: 139 us
  starting transfers between devices  49.6 us (35%)
  blocking collectives  26.6 us (19%)
  waiting for transfers between devices  18.2 us (13%)
  between operations  14.5 us (10%)
  Pallas kernels  13.5 us (10%)
  other arithmetic  8.04 us (6%)
  local copies, waits for them, and re-layouts  6.91 us (5%)
  matrix products  1.81 us (1%)
    ppermute x6, starting transfers between devices, exchanged(): value = value + lax.ppermute(value, axis, pairs)  24.6 us
    all_to_all x1, blocking collectives, shards(): near = lax.all_to_all(sent, 'zh', 0, 0)  22.5 us
    ppermute x6, waiting for transfers between devices, exchanged(): value = value + lax.ppermute(value, axis, pairs)  13.6 us
    pallas_call x3, Pallas kernels, call(): pl.pallas_call(kernel, out_shape=outs, in_specs=in_specs, out_specs=out_s...  13.5 us
    ppermute x2, starting transfers between devices, shifted(): return lax.ppermute(value, SEQ, pairs)  8.75 us
    all_to_all x1, starting transfers between devices, gathered(): return lax.all_to_all(spread, axes, 0, 0)  6.82 us
    all_to_all x1, starting transfers between devices, shards(): back = lax.all_to_all(back, HEAD, 0, 0)  5.42 us
    all_gather x1, blocking collectives, shards(): lax.all_gather(kv_near[:, None], 'core', axis=1, tiled=True)  4.06 us
  transfers between devices with their start and end apart: 12, of which 8 were waited for; matrix products, arithmetic and copies ran while one was open for 9% of the time, Pallas kernels for 3%

profile of v9, /device:TPU:1, one launch (start us, length us, event | category | flops | bytes accessed | tf_op | source)
XLA Modules:
  0.0 139.2 jit_solution(6362515531299034732)
XLA Ops:
  7.2 1.8 %shard_map.130 = bf16[4,48,1152]{2,1,0:T(8,128)(2,1)} custom-call(bf16[45,512]{1,0:T(8,128)(2,1)} %q_hbm.1, bf16[45,512]{1,0:T(8,128)(2,1)} %o_hbm.1, bf16[45,64]{1,0:T(8,128)(2,1)} %k_hbm.1, bf16[45,64]{1,0:T(8,128)(2,1)} %v_hbm.1), custom_call_target="tpu_custom_call" | custom-call | flops 100000000 | bytes 546048 | tf_op jit(solution)/shard_map/pallas_call | solution.py:236
  9.0 22.5 %all_to_all.20 = bf16[4,48,1152]{2,1,0:T(8,128)(2,1)S(1)} all-to-all(bf16[4,48,1152]{2,1,0:T(8,128)(2,1)} %shard_map.130), channel_id=1, replica_groups=mesh['zh'=4,'y'=8,'core'=2,'x'=4,'zl'=2] {'zh'}, dimensions={0} | all-to-all | bytes 884736 | tf_op jit(solution)/shard_map/all_to_all | solution.py:278
  31.5 0.8 slice.28
  32.9 0.8 broadcast_in_dim.24
  33.7 6.8 %all-to-all-start.1 = ((bf16[8,4,48,128]{3,2,1,0:T(8,128)(2,1)}), bf16[8,4,48,128]{3,2,1,0:T(8,128)(2,1)S(1)}, u32[]{:S(2)}, u32[]{:S(2)}) async-start(bf16[8,4,48,128]{3,2,1,0:T(8,128)(2,1)} %broadcast_in_dim.24), calls=%async_computation.1 | async-start | bytes 786432 | tf_op jit(solution)/shard_map/all_to_all | solution.py:30
  40.5 1.5 %multiply_reduce_fusion = (f32[128]{0:T(128)S(1)}, bf16[2880,128]{1,0:T(8,128)(2,1)S(1)}) fusion(f32[2880]{0:T(1024)S(1)} %copy-done.5, f32[2880]{0:T(1024)S(1)} %copy-done.6, f32[128]{0:T(128)S(1)} %add_rsqrt_fusion, bf16[128,2880]{0,1:T(8,128)(2,1)S(1)} %copy-done.1), kind=kLoop, calls=%fused_computation.9 | loop fusion | flops 2580352 | bytes 1498624 | tf_op jit(solution)/shard_map/reduce_sum | solution.py:289
  43.5 7.1 %collective-permute-start = (f32[16,360]{1,0:T(8,128)S(1)}, f32[16,360]{1,0:T(8,128)S(1)}, u32[]{:S(2)}, u32[]{:S(2)}) collective-permute-start(f32[16,360]{1,0:T(8,128)S(1)} %fusion.11), channel_id=1, source_target_pairs={{0,8},{8,0},{1,9},{9,1},{2,10},{10,2},{3,11},{11,3},{4,12},{12,4},... | collective-permute-start | bytes 69128 | tf_op jit(solution)/shard_map/ppermute | solution.py:304
  50.5 0.8 collective-permute-done
  52.0 2.1 %collective-permute-start.1 = (f32[16,360]{1,0:T(8,128)}, f32[16,360]{1,0:T(8,128)}, u32[]{:S(2)}, u32[]{:S(2)}) collective-permute-start(f32[16,360]{1,0:T(8,128)} %add.86), channel_id=1, source_target_pairs={{0,128},{128,0},{256,384},{384,256},{1,129},{129,1},{257,385},{385... | collective-permute-start | bytes 69128 | tf_op jit(solution)/shard_map/ppermute | solution.py:304
  55.5 2.8 %collective-permute-done.1 = f32[16,360]{1,0:T(8,128)} collective-permute-done((f32[16,360]{1,0:T(8,128)}, f32[16,360]{1,0:T(8,128)}, u32[]{:S(2)}, u32[]{:S(2)}) %collective-permute-start.1) | collective-permute-done | bytes 23072 | tf_op jit(solution)/shard_map/ppermute | solution.py:304
  58.3 1.4 add.87
  59.7 4.1 %all-gather = bf16[8,8,48,128]{3,2,1,0:T(8,128)(2,1)S(1)} all-gather(bf16[8,4,48,128]{3,2,1,0:T(8,128)(2,1)S(1)} %all-to-all-done.1), channel_id=2, replica_groups=mesh['zh'=4,'y'=8,'core'=2,'x'=4,'zl'=2] {'core'}, dimensions={1}, use_global_device_ids=true | all-gather | bytes 1179648 | tf_op jit(solution)/shard_map/all_gather | solution.py:309
  64.2 3.2 %collective-permute-start.2 = (bf16[136,128]{1,0:T(8,128)(2,1)S(1)}, bf16[136,128]{1,0:T(8,128)(2,1)S(1)}, u32[]{:S(2)}, u32[]{:S(2)}) collective-permute-start(bf16[136,128]{1,0:T(8,128)(2,1)S(1)} %pad_maximum_fusion), channel_id=1, source_target_pairs={{0,8},{8,16},{16,24},{24,32},{32,40},{40,48},{48,56},{56,64},{64,7... | collective-permute-start | bytes 104456 | tf_op jit(solution)/shard_map/ppermute | solution.py:24
  67.4 2.0 %collective-permute-start.3 = (f32[16,360]{1,0:T(8,128)}, f32[16,360]{1,0:T(8,128)S(1)}, u32[]{:S(2)}, u32[]{:S(2)}) collective-permute-start(f32[16,360]{1,0:T(8,128)} %add.87), channel_id=1, source_target_pairs={{0,256},{128,384},{256,0},{384,128},{1,257},{129,385},{257,1},{385... | collective-permute-start | bytes 69128 | tf_op jit(solution)/shard_map/ppermute | solution.py:304
  69.4 1.0 pad.7
  70.8 1.0 pad.8.clone
  71.7 4.7 %collective-permute-done.3 = f32[16,360]{1,0:T(8,128)S(1)} collective-permute-done((f32[16,360]{1,0:T(8,128)}, f32[16,360]{1,0:T(8,128)S(1)}, u32[]{:S(2)}, u32[]{:S(2)}) %collective-permute-start.3) | collective-permute-done | bytes 23072 | tf_op jit(solution)/shard_map/ppermute | solution.py:304
  76.5 0.7 add.90
  77.2 3.1 %collective-permute-start.4 = (f32[16,360]{1,0:T(8,128)S(1)}, f32[16,360]{1,0:T(8,128)S(1)}, u32[]{:S(2)}, u32[]{:S(2)}) collective-permute-start(f32[16,360]{1,0:T(8,128)S(1)} %add.90), channel_id=1, source_target_pairs={{0,16},{16,0},{32,48},{48,32},{64,80},{80,64},{96,112},{112,96},{1... | collective-permute-start | bytes 69128 | tf_op jit(solution)/shard_map/ppermute | solution.py:304
  80.3 2.1 %collective-permute-done.4 = f32[16,360]{1,0:T(8,128)S(1)} collective-permute-done((f32[16,360]{1,0:T(8,128)S(1)}, f32[16,360]{1,0:T(8,128)S(1)}, u32[]{:S(2)}, u32[]{:S(2)}) %collective-permute-start.4) | collective-permute-done | bytes 23072 | tf_op jit(solution)/shard_map/ppermute | solution.py:304
  82.4 4.9 %collective-permute-start.5 = (f32[16,360]{1,0:T(8,128)S(1)}, f32[16,360]{1,0:T(8,128)S(1)}, u32[]{:S(2)}, u32[]{:S(2)}) collective-permute-start(f32[16,360]{1,0:T(8,128)S(1)} %add.91), channel_id=1, source_target_pairs={{0,32},{16,48},{32,0},{48,16},{64,96},{80,112},{96,64},{112,80},{1... | collective-permute-start | bytes 69128 | tf_op jit(solution)/shard_map/ppermute | solution.py:304
  88.6 7.5 %shard_map.131 = (bf16[8,384,128]{2,1,0:T(8,128)(2,1)}, bf16[512,128]{1,0:T(8,128)(2,1)}, bf16[128,128]{1,0:T(8,128)(2,1)}, f32[128,128]{1,0:T(8,128)}) custom-call(bf16[3072,1024]{1,0:T(8,128)(2,1)} %bitcast.55, bf16[3072,128]{1,0:T(8,128)(2,1)} %bitcast.57, bf16[3072,128]{1,0:T(8,128)(2,1)} %bitcast.62, bf16[128,128]{1,0:T(8,128)(2,1)} %copy-done.4, ...), custom_call_target="tpu_custom_call" | custom-call | flops 100000000 | bytes 9013248 | tf_op jit(solution)/shard_map/pallas_call | solution.py:236
  96.1 4.1 %all-to-all-start.2 = ((bf16[8,384,128]{2,1,0:T(8,128)(2,1)}), bf16[8,384,128]{2,1,0:T(8,128)(2,1)S(1)}, u32[]{:S(2)}, u32[]{:S(2)}) async-start(bf16[8,384,128]{2,1,0:T(8,128)(2,1)} %get-tuple-element.31), calls=%async_computation.2 | async-start | bytes 1572864 | tf_op jit(solution)/shard_map/all_to_all | solution.py:354
  100.2 5.6 %collective-permute-start.6 = (bf16[128,128]{1,0:T(8,128)(2,1)S(1)}, bf16[128,128]{1,0:T(8,128)(2,1)S(1)}, u32[]{:S(2)}, u32[]{:S(2)}) collective-permute-start(bf16[128,128]{1,0:T(8,128)(2,1)S(1)} %copy-done.18), channel_id=1, source_target_pairs={{8,0},{16,8},{24,16},{32,24},{40,32},{48,40},{56,48},{64,56},{72,6... | collective-permute-start | bytes 98312 | tf_op jit(solution)/shard_map/ppermute | solution.py:24
  105.8 2.0 %collective-permute-done.6.ret_hbm = bf16[128,128]{1,0:T(8,128)(2,1)S(1)} collective-permute-done((bf16[128,128]{1,0:T(8,128)(2,1)S(1)}, bf16[128,128]{1,0:T(8,128)(2,1)S(1)}, u32[]{:S(2)}, u32[]{:S(2)}) %collective-permute-start.6) | collective-permute-done | bytes 32800 | tf_op jit(solution)/shard_map/ppermute | solution.py:24
  108.4 4.2 %shard_map.132 = bf16[8,392,128]{2,1,0:T(8,128)(2,1)} custom-call(bf16[3072,1024]{1,0:T(8,128)(2,1)} %bitcast.56, bf16[3072,128]{1,0:T(8,128)(2,1)} %bitcast.61, bf16[3072,128]{1,0:T(8,128)(2,1)} %bitcast.58, bf16[512,128]{1,0:T(8,128)(2,1)} %get-tuple-element.34.dq_hbm, f32[128,128]{1,0:T(8,128)} %get-tuple-element.35.dkv_hbm, bf16[128,128]{1,0:T(8,128)(2,1)} %copy-done.9), custom_call_target="tpu_custom_call" | custom-call | flops 100000000 | bytes 8896512 | tf_op jit(solution)/shard_map/pallas_call | solution.py:236
  112.6 5.4 %all-to-all-start.3 = ((bf16[8,392,128]{2,1,0:T(8,128)(2,1)}), bf16[8,392,128]{2,1,0:T(8,128)(2,1)S(1)}, u32[]{:S(2)}, u32[]{:S(2)}) async-start(bf16[8,392,128]{2,1,0:T(8,128)(2,1)} %shard_map.132), calls=%async_computation.3 | async-start | bytes 1605632 | tf_op jit(solution)/shard_map/all_to_all | solution.py:374
  118.5 5.3 %collective-permute-start.7 = (f32[16,360]{1,0:T(8,128)S(1)}, f32[16,360]{1,0:T(8,128)S(1)}, u32[]{:S(2)}, u32[]{:S(2)}) collective-permute-start(f32[16,360]{1,0:T(8,128)S(1)} %add.92), channel_id=1, source_target_pairs={{0,64},{16,80},{32,96},{48,112},{64,0},{80,16},{96,32},{112,48},{1... | collective-permute-start | bytes 69128 | tf_op jit(solution)/shard_map/ppermute | solution.py:304
  124.3 2.7 %collective-permute-done.7 = f32[16,360]{1,0:T(8,128)S(1)} collective-permute-done((f32[16,360]{1,0:T(8,128)S(1)}, f32[16,360]{1,0:T(8,128)S(1)}, u32[]{:S(2)}, u32[]{:S(2)}) %collective-permute-start.7) | collective-permute-done | bytes 23072 | tf_op jit(solution)/shard_map/ppermute | solution.py:304
  127.7 1.0 fusion.7
  128.7 2.7 %all-to-all-done.3 = bf16[8,392,128]{2,1,0:T(8,128)(2,1)S(1)} async-done(((bf16[8,392,128]{2,1,0:T(8,128)(2,1)}), bf16[8,392,128]{2,1,0:T(8,128)(2,1)S(1)}, u32[]{:S(2)}, u32[]{:S(2)}) %all-to-all-start.3) | async-done | bytes 802848 | tf_op jit(solution)/shard_map/all_to_all | solution.py:374
  131.6 0.8 fusion.16
  (76 shorter events, 8.2 us)
Async XLA Ops:
  7.2 116.7 %copy-start = (bf16[16,2880]{1,0:T(8,128)(2,1)S(1)}, bf16[16,2880]{1,0:T(8,128)(2,1)}, u32[]{:S(2)}) copy-start(bf16[16,2880]{1,0:T(8,128)(2,1)} %param.18) | copy-start | bytes 276484
  7.2 25.2 %copy-start.1 = (bf16[128,2880]{0,1:T(8,128)(2,1)S(1)}, bf16[128,2880]{0,1:T(8,128)(2,1)}, u32[]{:S(2)}) copy-start(bf16[128,2880]{0,1:T(8,128)(2,1)} %param.11) | copy-start | bytes 2211844
  7.2 81.4 %all-gather.3.cloned.1.call-start = ((), (), s32[]{:S(2)}) async-start(), calls=%async_computation.4 | async-start | bytes 6684672 | tf_op jit(solution)/shard_map/all_gather | solution.py:279
  31.5 9.0 %copy-start.5 = (f32[2880]{0:T(1024)S(1)}, f32[2880]{0:T(1024)}, u32[]{:S(2)}) copy-start(f32[2880]{0:T(1024)} %param.17) | copy-start | bytes 34564
  31.5 9.0 %copy-start.6 = (f32[2880]{0:T(1024)S(1)}, f32[2880]{0:T(1024)}, u32[]{:S(2)}) copy-start(f32[2880]{0:T(1024)} %param.12) | copy-start | bytes 34564
  32.8 10.4 %copy-start.2 = (bf16[128,2880]{0,1:T(8,128)(2,1)S(1)}, bf16[128,2880]{0,1:T(8,128)(2,1)}, u32[]{:S(2)}) copy-start(bf16[128,2880]{0,1:T(8,128)(2,1)} %param.21) | copy-start | bytes 2211844
  32.8 10.4 %copy-start.10 = (s32[128]{0:T(128)S(1)}, s32[128]{0:T(128)}, u32[]{:S(2)}) copy-start(s32[128]{0:T(128)} %param.20) | copy-start | bytes 1540
  33.7 26.0 %all-to-all-start.1 = ((bf16[8,4,48,128]{3,2,1,0:T(8,128)(2,1)}), bf16[8,4,48,128]{3,2,1,0:T(8,128)(2,1)S(1)}, u32[]{:S(2)}, u32[]{:S(2)}) async-start(bf16[8,4,48,128]{3,2,1,0:T(8,128)(2,1)} %broadcast_in_dim.24), calls=%async_computation.1 | async-start | bytes 786432 | tf_op jit(solution)/shard_map/all_to_all | solution.py:30
  42.0 0.6 copy-start.11
  42.6 0.6 copy-start.15
  43.5 7.9 %collective-permute-start = (f32[16,360]{1,0:T(8,128)S(1)}, f32[16,360]{1,0:T(8,128)S(1)}, u32[]{:S(2)}, u32[]{:S(2)}) collective-permute-start(f32[16,360]{1,0:T(8,128)S(1)} %fusion.11), channel_id=1, source_target_pairs={{0,8},{8,0},{1,9},{9,1},{2,10},{10,2},{3,11},{11,3},{4,12},{12,4},... | collective-permute-start | bytes 69128 | tf_op jit(solution)/shard_map/ppermute | solution.py:304
  52.0 6.3 %collective-permute-start.1 = (f32[16,360]{1,0:T(8,128)}, f32[16,360]{1,0:T(8,128)}, u32[]{:S(2)}, u32[]{:S(2)}) collective-permute-start(f32[16,360]{1,0:T(8,128)} %add.86), channel_id=1, source_target_pairs={{0,128},{128,0},{256,384},{384,256},{1,129},{129,1},{257,385},{385... | collective-permute-start | bytes 69128 | tf_op jit(solution)/shard_map/ppermute | solution.py:304
  54.4 0.7 copy-start.13
  59.7 4.5 %copy-start.17 = (bf16[128]{0:T(256)(128)(2,1)S(1)}, bf16[128]{0:T(256)(128)(2,1)}, u32[]{:S(2)}) copy-start(bf16[128]{0:T(256)(128)(2,1)} %convert_element_type.68) | copy-start | bytes 772
  63.7 6.7 %copy-start.3 = (bf16[8,8,48,128]{3,2,1,0:T(8,128)(2,1)}, bf16[8,8,48,128]{3,2,1,0:T(8,128)(2,1)S(1)}, u32[]{:S(2)}) copy-start(bf16[8,8,48,128]{3,2,1,0:T(8,128)(2,1)S(1)} %all-gather) | copy-start | bytes 2359300
  64.2 6.5 %copy-start.4 = (bf16[128,128]{1,0:T(8,128)(2,1)}, bf16[128,128]{1,0:T(8,128)(2,1)S(1)}, u32[]{:S(2)}) copy-start(bf16[128,128]{1,0:T(8,128)(2,1)S(1)} %fusion.8.kv_hbm) | copy-start | bytes 98308
  64.2 16.1 %collective-permute-start.2 = (bf16[136,128]{1,0:T(8,128)(2,1)S(1)}, bf16[136,128]{1,0:T(8,128)(2,1)S(1)}, u32[]{:S(2)}, u32[]{:S(2)}) collective-permute-start(bf16[136,128]{1,0:T(8,128)(2,1)S(1)} %pad_maximum_fusion), channel_id=1, source_target_pairs={{0,8},{8,16},{16,24},{24,32},{32,40},{40,48},{48,56},{56,64},{64,7... | collective-permute-start | bytes 104456 | tf_op jit(solution)/shard_map/ppermute | solution.py:24
  67.4 9.1 %collective-permute-start.3 = (f32[16,360]{1,0:T(8,128)}, f32[16,360]{1,0:T(8,128)S(1)}, u32[]{:S(2)}, u32[]{:S(2)}) collective-permute-start(f32[16,360]{1,0:T(8,128)} %add.87), channel_id=1, source_target_pairs={{0,256},{128,384},{256,0},{384,128},{1,257},{129,385},{257,1},{385... | collective-permute-start | bytes 69128 | tf_op jit(solution)/shard_map/ppermute | solution.py:304
  70.7 16.7 %copy-start.14 = (s32[128]{0:T(128)S(1)}, s32[128]{0:T(128)}, u32[]{:S(2)}) copy-start(s32[128]{0:T(128)} %param.19) | copy-start | bytes 1540
  77.2 5.2 %collective-permute-start.4 = (f32[16,360]{1,0:T(8,128)S(1)}, f32[16,360]{1,0:T(8,128)S(1)}, u32[]{:S(2)}, u32[]{:S(2)}) collective-permute-start(f32[16,360]{1,0:T(8,128)S(1)} %add.90), channel_id=1, source_target_pairs={{0,16},{16,0},{32,48},{48,32},{64,80},{80,64},{96,112},{112,96},{1... | collective-permute-start | bytes 69128 | tf_op jit(solution)/shard_map/ppermute | solution.py:304
  80.3 8.3 %copy-start.8 = (bf16[136,128]{1,0:T(8,128)(2,1)}, bf16[136,128]{1,0:T(8,128)(2,1)S(1)}, u32[]{:S(2)}) copy-start(bf16[136,128]{1,0:T(8,128)(2,1)S(1)} %collective-permute-done.2.halo_hbm) | copy-start | bytes 104452
  82.4 6.1 %collective-permute-start.5 = (f32[16,360]{1,0:T(8,128)S(1)}, f32[16,360]{1,0:T(8,128)S(1)}, u32[]{:S(2)}, u32[]{:S(2)}) collective-permute-start(f32[16,360]{1,0:T(8,128)S(1)} %add.91), channel_id=1, source_target_pairs={{0,32},{16,48},{32,0},{48,16},{64,96},{80,112},{96,64},{112,80},{1... | collective-permute-start | bytes 69128 | tf_op jit(solution)/shard_map/ppermute | solution.py:304
  96.1 4.1 %copy-start.18 = (bf16[128,128]{1,0:T(8,128)(2,1)S(1)}, bf16[128,128]{1,0:T(8,128)(2,1)}, u32[]{:S(2)}) copy-start(bf16[128,128]{1,0:T(8,128)(2,1)} %get-tuple-element.36) | copy-start | bytes 98308
  96.1 16.5 %all-to-all-start.2 = ((bf16[8,384,128]{2,1,0:T(8,128)(2,1)}), bf16[8,384,128]{2,1,0:T(8,128)(2,1)S(1)}, u32[]{:S(2)}, u32[]{:S(2)}) async-start(bf16[8,384,128]{2,1,0:T(8,128)(2,1)} %get-tuple-element.31), calls=%async_computation.2 | async-start | bytes 1572864 | tf_op jit(solution)/shard_map/all_to_all | solution.py:354
  100.2 7.6 %collective-permute-start.6 = (bf16[128,128]{1,0:T(8,128)(2,1)S(1)}, bf16[128,128]{1,0:T(8,128)(2,1)S(1)}, u32[]{:S(2)}, u32[]{:S(2)}) collective-permute-start(bf16[128,128]{1,0:T(8,128)(2,1)S(1)} %copy-done.18), channel_id=1, source_target_pairs={{8,0},{16,8},{24,16},{32,24},{40,32},{48,40},{56,48},{64,56},{72,6... | collective-permute-start | bytes 98312 | tf_op jit(solution)/shard_map/ppermute | solution.py:24
  107.7 0.6 copy-start.9
  112.6 5.4 %copy-start.7 = (f32[2880]{0:T(1024)S(1)}, f32[2880]{0:T(1024)}, u32[]{:S(2)}) copy-start(f32[2880]{0:T(1024)} %param.12) | copy-start | bytes 34564
  112.6 18.8 %all-to-all-start.3 = ((bf16[8,392,128]{2,1,0:T(8,128)(2,1)}), bf16[8,392,128]{2,1,0:T(8,128)(2,1)S(1)}, u32[]{:S(2)}, u32[]{:S(2)}) async-start(bf16[8,392,128]{2,1,0:T(8,128)(2,1)} %shard_map.132), calls=%async_computation.3 | async-start | bytes 1605632 | tf_op jit(solution)/shard_map/all_to_all | solution.py:374
  118.0 9.7 %copy-start.16 = (f32[128]{0:T(128)S(1)}, f32[128]{0:T(128)}, u32[]{:S(2)}) copy-start(f32[128]{0:T(128)} %copy-done.15) | copy-start | bytes 1540
  118.5 8.5 %collective-permute-start.7 = (f32[16,360]{1,0:T(8,128)S(1)}, f32[16,360]{1,0:T(8,128)S(1)}, u32[]{:S(2)}, u32[]{:S(2)}) collective-permute-start(f32[16,360]{1,0:T(8,128)S(1)} %add.92), channel_id=1, source_target_pairs={{0,64},{16,80},{32,96},{48,112},{64,0},{80,16},{96,32},{112,48},{1... | collective-permute-start | bytes 69128 | tf_op jit(solution)/shard_map/ppermute | solution.py:304
  127.7 3.8 %copy-start.12 = (f32[128]{0:T(128)S(1)}, f32[128]{0:T(128)}, u32[]{:S(2)}) copy-start(f32[128]{0:T(128)} %copy-done.11) | copy-start | bytes 1540
Sparse Core Ops, SparseCore 0:
  32.5 53.9 all-gather.2

commit v10 on v9

--- a/solution.py
+++ b/solution.py
@@ -232,6 +232,7 @@
 
 
 def call(kernel, outs, in_specs, out_specs, scratch, *args):
+    limit = 48 if kernel is back_kernel else 58
     size = sum(a.size * a.dtype.itemsize for a in jax.tree.leaves((args, outs)))
     return pl.pallas_call(
         kernel,
@@ -239,7 +240,7 @@
         in_specs=in_specs,
         out_specs=out_specs,
         scratch_shapes=scratch,
-        compiler_params=pltpu.CompilerParams(vmem_limit_bytes=58 * 2**20),
+        compiler_params=pltpu.CompilerParams(vmem_limit_bytes=limit * 2**20),
         cost_estimate=pl.CostEstimate(flops=10**8, bytes_accessed=size, transcendentals=0),
     )(*args)
 
@@ -318,7 +319,7 @@
     query_pos = lax.broadcasted_iota(jnp.int32, (row_count, row_count), 1)
     key_seg = jnp.where(key_pos > query_pos, halo_seg[:, None], segment_ids[:, None])
     mask = (key_seg == segment_ids[None, :]).astype(F32)
-    steer = exchanged(steer, ("zh", 2), ("y", 1), ("y", 2))
+    steer = exchanged(steer, ("zh", 2), ("y", 1))
     whole, halo, mask, steer, normed_b, grad_b, kv, kv_all = lax.optimization_barrier(
         (whole, halo, mask, steer, normed_b, grad_b, kv, kv_all)
     )
@@ -351,6 +352,8 @@
         *(whole, normed_b, grad_b, kv, halo, mask),
     )
     returned = shifted(grad_halo, -1)
+    steer, returned = lax.optimization_barrier((steer, returned))
+    steer = exchanged(steer, ("y", 2))
     attn = lax.all_to_all(blocks, HEAD, 0, 0)
     back = call(
         back_kernel,

time: 140 us -> 141 us (level)
  starting transfers between devices: 49.6 us -> 45.4 us
  waiting for transfers between devices: 18.2 us -> 22.1 us
    all_gather x1, waiting for transfers between devices: 0.01 us -> 4.2 us  [shards(): lax.all_gather(near[:, :, :2 * width], ('y', 'core'), axis=0, tiled=True)]
    ppermute x2, starting transfers between devices: 8.75 us -> 5.61 us  [shifted(): return lax.ppermute(value, SEQ, pairs)]
    ppermute x6, starting transfers between devices: 24.6 us -> 22.2 us  [exchanged(): value = value + lax.ppermute(value, axis, pairs)]
    all_to_all x1, starting transfers between devices: 4.05 us -> 5.61 us  [shards(): attn = lax.all_to_all(blocks, HEAD, 0, 0)]
  transfers between devices with their start and end apart: 12 -> 12, of which waited for: 8 -> 8; matrix products, arithmetic and copies ran while one was open for 9% -> 10% of each run, Pallas kernels for 3% -> 4%
where the time goes in v10:
time: 141 us
  starting transfers between devices  45.4 us (32%)
  blocking collectives  26.7 us (19%)
  waiting for transfers between devices  22.1 us (16%)
  Pallas kernels  14.5 us (10%)
  between operations  14.5 us (10%)
  other arithmetic  9.19 us (7%)
  local copies, waits for them, and re-layouts  6.18 us (4%)
  matrix products  1.81 us (1%)
    all_to_all x1, blocking collectives, shards(): near = lax.all_to_all(sent, 'zh', 0, 0)  22.5 us
    ppermute x6, starting transfers between devices, exchanged(): value = value + lax.ppermute(value, axis, pairs)  22.2 us
    pallas_call x3, Pallas kernels, call(): pl.pallas_call(kernel, out_shape=outs, in_specs=in_specs, out_specs=out_s...  14.5 us
    ppermute x6, waiting for transfers between devices, exchanged(): value = value + lax.ppermute(value, axis, pairs)  13.5 us
    all_to_all x1, starting transfers between devices, gathered(): return lax.all_to_all(spread, axes, 0, 0)  6.82 us
    all_to_all x1, starting transfers between devices, shards(): attn = lax.all_to_all(blocks, HEAD, 0, 0)  5.61 us
    ppermute x2, starting transfers between devices, shifted(): return lax.ppermute(value, SEQ, pairs)  5.61 us
    all_to_all x1, starting transfers between devices, shards(): back = lax.all_to_all(back, HEAD, 0, 0)  5.14 us
  transfers between devices with their start and end apart: 12, of which 8 were waited for; matrix products, arithmetic and copies ran while one was open for 10% of the time, Pallas kernels for 4%

profile of v10, /device:TPU:1, one launch (start us, length us, event | category | flops | bytes accessed | tf_op | source)
XLA Modules:
  0.0 140.5 jit_solution(7623891522682414115)
XLA Ops:
  7.2 1.8 %shard_map.130 = bf16[4,48,1152]{2,1,0:T(8,128)(2,1)} custom-call(bf16[45,512]{1,0:T(8,128)(2,1)} %q_hbm.1, bf16[45,512]{1,0:T(8,128)(2,1)} %o_hbm.1, bf16[45,64]{1,0:T(8,128)(2,1)} %k_hbm.1, bf16[45,64]{1,0:T(8,128)(2,1)} %v_hbm.1), custom_call_target="tpu_custom_call" | custom-call | flops 100000000 | bytes 546048 | tf_op jit(solution)/shard_map/pallas_call | solution.py:237
  9.0 22.5 %all_to_all.20 = bf16[4,48,1152]{2,1,0:T(8,128)(2,1)S(1)} all-to-all(bf16[4,48,1152]{2,1,0:T(8,128)(2,1)} %shard_map.130), channel_id=1, replica_groups=mesh['zh'=4,'y'=8,'core'=2,'x'=4,'zl'=2] {'zh'}, dimensions={0} | all-to-all | bytes 884736 | tf_op jit(solution)/shard_map/all_to_all | solution.py:279
  32.8 0.8 broadcast_in_dim.24
  33.6 6.8 %all-to-all-start.1 = ((bf16[8,4,48,128]{3,2,1,0:T(8,128)(2,1)}), bf16[8,4,48,128]{3,2,1,0:T(8,128)(2,1)S(1)}, u32[]{:S(2)}, u32[]{:S(2)}) async-start(bf16[8,4,48,128]{3,2,1,0:T(8,128)(2,1)} %broadcast_in_dim.24), calls=%async_computation.1 | async-start | bytes 786432 | tf_op jit(solution)/shard_map/all_to_all | solution.py:30
  40.5 1.5 %multiply_reduce_fusion = (f32[128]{0:T(128)S(1)}, bf16[2880,128]{1,0:T(8,128)(2,1)S(1)}) fusion(f32[2880]{0:T(1024)S(1)} %copy-done.7, f32[2880]{0:T(1024)S(1)} %copy-done.8, f32[128]{0:T(128)S(1)} %add_rsqrt_fusion, bf16[128,2880]{0,1:T(8,128)(2,1)S(1)} %copy-done.4), kind=kLoop, calls=%fused_computation.9 | loop fusion | flops 2580352 | bytes 1498624 | tf_op jit(solution)/shard_map/reduce_sum | solution.py:290
  43.2 7.1 %collective-permute-start = (f32[16,360]{1,0:T(8,128)S(1)}, f32[16,360]{1,0:T(8,128)S(1)}, u32[]{:S(2)}, u32[]{:S(2)}) collective-permute-start(f32[16,360]{1,0:T(8,128)S(1)} %fusion.11), channel_id=1, source_target_pairs={{0,8},{8,0},{1,9},{9,1},{2,10},{10,2},{3,11},{11,3},{4,12},{12,4},... | collective-permute-start | bytes 69128 | tf_op jit(solution)/shard_map/ppermute | solution.py:305
  50.3 0.8 collective-permute-done
  51.8 2.1 %collective-permute-start.1 = (f32[16,360]{1,0:T(8,128)}, f32[16,360]{1,0:T(8,128)}, u32[]{:S(2)}, u32[]{:S(2)}) collective-permute-start(f32[16,360]{1,0:T(8,128)} %add.86), channel_id=1, source_target_pairs={{0,128},{128,0},{256,384},{384,256},{1,129},{129,1},{257,385},{385... | collective-permute-start | bytes 69128 | tf_op jit(solution)/shard_map/ppermute | solution.py:305
  55.3 2.8 %collective-permute-done.1 = f32[16,360]{1,0:T(8,128)} collective-permute-done((f32[16,360]{1,0:T(8,128)}, f32[16,360]{1,0:T(8,128)}, u32[]{:S(2)}, u32[]{:S(2)}) %collective-permute-start.1) | collective-permute-done | bytes 23072 | tf_op jit(solution)/shard_map/ppermute | solution.py:305
  58.1 1.4 add.87
  59.5 4.2 %all-gather = bf16[8,8,48,128]{3,2,1,0:T(8,128)(2,1)S(1)} all-gather(bf16[8,4,48,128]{3,2,1,0:T(8,128)(2,1)S(1)} %all-to-all-done.1), channel_id=2, replica_groups=mesh['zh'=4,'y'=8,'core'=2,'x'=4,'zl'=2] {'core'}, dimensions={1}, use_global_device_ids=true | all-gather | bytes 1179648 | tf_op jit(solution)/shard_map/all_gather | solution.py:310
  64.1 3.1 %collective-permute-start.2 = (bf16[136,128]{1,0:T(8,128)(2,1)S(1)}, bf16[136,128]{1,0:T(8,128)(2,1)S(1)}, u32[]{:S(2)}, u32[]{:S(2)}) collective-permute-start(bf16[136,128]{1,0:T(8,128)(2,1)S(1)} %pad_maximum_fusion), channel_id=1, source_target_pairs={{0,8},{8,16},{16,24},{24,32},{32,40},{40,48},{48,56},{56,64},{64,7... | collective-permute-start | bytes 104456 | tf_op jit(solution)/shard_map/ppermute | solution.py:24
  67.3 1.9 %collective-permute-start.3 = (f32[16,360]{1,0:T(8,128)}, f32[16,360]{1,0:T(8,128)S(1)}, u32[]{:S(2)}, u32[]{:S(2)}) collective-permute-start(f32[16,360]{1,0:T(8,128)} %add.87), channel_id=1, source_target_pairs={{0,256},{128,384},{256,0},{384,128},{1,257},{129,385},{257,1},{385... | collective-permute-start | bytes 69128 | tf_op jit(solution)/shard_map/ppermute | solution.py:305
  69.2 1.0 pad.7
  70.6 1.0 pad.8.clone
  71.7 4.7 %collective-permute-done.3 = f32[16,360]{1,0:T(8,128)S(1)} collective-permute-done((f32[16,360]{1,0:T(8,128)}, f32[16,360]{1,0:T(8,128)S(1)}, u32[]{:S(2)}, u32[]{:S(2)}) %collective-permute-start.3) | collective-permute-done | bytes 23072 | tf_op jit(solution)/shard_map/ppermute | solution.py:305
  77.1 3.0 %collective-permute-start.4 = (f32[16,360]{1,0:T(8,128)S(1)}, f32[16,360]{1,0:T(8,128)S(1)}, u32[]{:S(2)}, u32[]{:S(2)}) collective-permute-start(f32[16,360]{1,0:T(8,128)S(1)} %add.90), channel_id=1, source_target_pairs={{0,16},{16,0},{32,48},{48,32},{64,80},{80,64},{96,112},{112,96},{1... | collective-permute-start | bytes 69128 | tf_op jit(solution)/shard_map/ppermute | solution.py:305
  80.9 1.4 collective-permute-done.4
  82.3 4.2 %all-gather.3.cloned.1.call-done = bf16[64,48,1024]{2,1,0:T(8,128)(2,1)} async-done(((bf16[4,48,1024]{2,1,0:T(8,128)(2,1)}), bf16[64,48,1024]{2,1,0:T(8,128)(2,1)}) %all-gather.3.cloned.1.call-update) | async-done | bytes 6291472 | tf_op jit(solution)/shard_map/all_gather | solution.py:280
  86.5 7.5 %shard_map.131 = (bf16[8,384,128]{2,1,0:T(8,128)(2,1)}, bf16[512,128]{1,0:T(8,128)(2,1)}, bf16[128,128]{1,0:T(8,128)(2,1)}, f32[128,128]{1,0:T(8,128)}) custom-call(bf16[3072,1024]{1,0:T(8,128)(2,1)} %bitcast.59, bf16[3072,128]{1,0:T(8,128)(2,1)} %bitcast.55, bf16[3072,128]{1,0:T(8,128)(2,1)} %bitcast.62, bf16[128,128]{1,0:T(8,128)(2,1)} %copy-done.6, ...), custom_call_target="tpu_custom_call" | custom-call | flops 100000000 | bytes 9013248 | tf_op jit(solution)/shard_map/pallas_call | solution.py:237
  94.1 5.6 %all-to-all-start.2 = ((bf16[8,384,128]{2,1,0:T(8,128)(2,1)}), bf16[8,384,128]{2,1,0:T(8,128)(2,1)}, u32[]{:S(2)}, u32[]{:S(2)}) async-start(bf16[8,384,128]{2,1,0:T(8,128)(2,1)} %get-tuple-element.33), calls=%async_computation.2 | async-start | bytes 1572864 | tf_op jit(solution)/shard_map/all_to_all | solution.py:357
  99.7 2.5 %collective-permute-start.5 = (bf16[128,128]{1,0:T(8,128)(2,1)S(1)}, bf16[128,128]{1,0:T(8,128)(2,1)S(1)}, u32[]{:S(2)}, u32[]{:S(2)}) collective-permute-start(bf16[128,128]{1,0:T(8,128)(2,1)S(1)} %copy-done.19), channel_id=1, source_target_pairs={{8,0},{16,8},{24,16},{32,24},{40,32},{48,40},{56,48},{64,56},{72,6... | collective-permute-start | bytes 98312 | tf_op jit(solution)/shard_map/ppermute | solution.py:24
  102.2 3.2 %collective-permute-done.5.ret_hbm = bf16[128,128]{1,0:T(8,128)(2,1)S(1)} collective-permute-done((bf16[128,128]{1,0:T(8,128)(2,1)S(1)}, bf16[128,128]{1,0:T(8,128)(2,1)S(1)}, u32[]{:S(2)}, u32[]{:S(2)}) %collective-permute-start.5) | collective-permute-done | bytes 32800 | tf_op jit(solution)/shard_map/ppermute | solution.py:24
  105.4 3.7 %collective-permute-start.6 = (f32[16,360]{1,0:T(8,128)S(1)}, f32[16,360]{1,0:T(8,128)S(1)}, u32[]{:S(2)}, u32[]{:S(2)}) collective-permute-start(f32[16,360]{1,0:T(8,128)S(1)} %add.91), channel_id=1, source_target_pairs={{0,32},{16,48},{32,0},{48,16},{64,96},{80,112},{96,64},{112,80},{1... | collective-permute-start | bytes 69128 | tf_op jit(solution)/shard_map/ppermute | solution.py:305
  109.1 5.2 %shard_map.132 = bf16[8,392,128]{2,1,0:T(8,128)(2,1)} custom-call(bf16[3072,1024]{1,0:T(8,128)(2,1)} %bitcast.60, bf16[3072,128]{1,0:T(8,128)(2,1)S(1)} %bitcast.58, bf16[3072,128]{1,0:T(8,128)(2,1)S(1)} %bitcast.56, bf16[512,128]{1,0:T(8,128)(2,1)S(1)} %copy-done.2, f32[128,128]{1,0:T(8,128)S(1)} %copy-done.3, ...), custom_call_target="tpu_custom_call" | custom-call | flops 100000000 | bytes 8896512 | tf_op jit(solution)/shard_map/pallas_call | solution.py:237
  114.4 5.1 %all-to-all-start.3 = ((bf16[8,392,128]{2,1,0:T(8,128)(2,1)}), bf16[8,392,128]{2,1,0:T(8,128)(2,1)S(1)}, u32[]{:S(2)}, u32[]{:S(2)}) async-start(bf16[8,392,128]{2,1,0:T(8,128)(2,1)} %shard_map.132), calls=%async_computation.3 | async-start | bytes 1605632 | tf_op jit(solution)/shard_map/all_to_all | solution.py:377
  120.0 4.2 %collective-permute-start.7 = (f32[16,360]{1,0:T(8,128)S(1)}, f32[16,360]{1,0:T(8,128)S(1)}, u32[]{:S(2)}, u32[]{:S(2)}) collective-permute-start(f32[16,360]{1,0:T(8,128)S(1)} %add.94), channel_id=1, source_target_pairs={{0,64},{16,80},{32,96},{48,112},{64,0},{80,16},{96,32},{112,48},{1... | collective-permute-start | bytes 69128 | tf_op jit(solution)/shard_map/ppermute | solution.py:305
  124.7 3.8 %collective-permute-done.7 = f32[16,360]{1,0:T(8,128)S(1)} collective-permute-done((f32[16,360]{1,0:T(8,128)S(1)}, f32[16,360]{1,0:T(8,128)S(1)}, u32[]{:S(2)}, u32[]{:S(2)}) %collective-permute-start.7) | collective-permute-done | bytes 23072 | tf_op jit(solution)/shard_map/ppermute | solution.py:305
  129.2 1.3 convert_reduce_fusion.1
  130.4 1.0 fusion.7
  131.4 1.3 all-to-all-done.3
  132.9 0.8 fusion.16
  (78 shorter events, 8.4 us)
Async XLA Ops:
  7.2 117.1 %copy-start = (bf16[16,2880]{1,0:T(8,128)(2,1)S(1)}, bf16[16,2880]{1,0:T(8,128)(2,1)}, u32[]{:S(2)}) copy-start(bf16[16,2880]{1,0:T(8,128)(2,1)} %param.18) | copy-start | bytes 276484
  7.2 25.2 %copy-start.4 = (bf16[128,2880]{0,1:T(8,128)(2,1)S(1)}, bf16[128,2880]{0,1:T(8,128)(2,1)}, u32[]{:S(2)}) copy-start(bf16[128,2880]{0,1:T(8,128)(2,1)} %param.11) | copy-start | bytes 2211844
  7.2 79.3 %all-gather.3.cloned.1.call-start = ((), (), s32[]{:S(2)}) async-start(), calls=%async_computation.4 | async-start | bytes 6684672 | tf_op jit(solution)/shard_map/all_gather | solution.py:280
  31.5 8.9 %copy-start.7 = (f32[2880]{0:T(1024)S(1)}, f32[2880]{0:T(1024)}, u32[]{:S(2)}) copy-start(f32[2880]{0:T(1024)} %param.17) | copy-start | bytes 34564
  31.5 8.9 %copy-start.8 = (f32[2880]{0:T(1024)S(1)}, f32[2880]{0:T(1024)}, u32[]{:S(2)}) copy-start(f32[2880]{0:T(1024)} %param.12) | copy-start | bytes 34564
  32.8 10.3 %copy-start.5 = (bf16[128,2880]{0,1:T(8,128)(2,1)S(1)}, bf16[128,2880]{0,1:T(8,128)(2,1)}, u32[]{:S(2)}) copy-start(bf16[128,2880]{0,1:T(8,128)(2,1)} %param.21) | copy-start | bytes 2211844
  32.8 10.3 %copy-start.11 = (s32[128]{0:T(128)S(1)}, s32[128]{0:T(128)}, u32[]{:S(2)}) copy-start(s32[128]{0:T(128)} %param.20) | copy-start | bytes 1540
  33.6 25.8 %all-to-all-start.1 = ((bf16[8,4,48,128]{3,2,1,0:T(8,128)(2,1)}), bf16[8,4,48,128]{3,2,1,0:T(8,128)(2,1)S(1)}, u32[]{:S(2)}, u32[]{:S(2)}) async-start(bf16[8,4,48,128]{3,2,1,0:T(8,128)(2,1)} %broadcast_in_dim.24), calls=%async_computation.1 | async-start | bytes 786432 | tf_op jit(solution)/shard_map/all_to_all | solution.py:30
  42.0 0.5 copy-start.12
  42.5 0.5 copy-start.16
  43.2 7.9 %collective-permute-start = (f32[16,360]{1,0:T(8,128)S(1)}, f32[16,360]{1,0:T(8,128)S(1)}, u32[]{:S(2)}, u32[]{:S(2)}) collective-permute-start(f32[16,360]{1,0:T(8,128)S(1)} %fusion.11), channel_id=1, source_target_pairs={{0,8},{8,0},{1,9},{9,1},{2,10},{10,2},{3,11},{11,3},{4,12},{12,4},... | collective-permute-start | bytes 69128 | tf_op jit(solution)/shard_map/ppermute | solution.py:305
  51.8 6.3 %collective-permute-start.1 = (f32[16,360]{1,0:T(8,128)}, f32[16,360]{1,0:T(8,128)}, u32[]{:S(2)}, u32[]{:S(2)}) collective-permute-start(f32[16,360]{1,0:T(8,128)} %add.86), channel_id=1, source_target_pairs={{0,128},{128,0},{256,384},{384,256},{1,129},{129,1},{257,385},{385... | collective-permute-start | bytes 69128 | tf_op jit(solution)/shard_map/ppermute | solution.py:305
  54.2 0.7 copy-start.14
  59.5 4.6 %copy-start.18 = (bf16[128]{0:T(256)(128)(2,1)S(1)}, bf16[128]{0:T(256)(128)(2,1)}, u32[]{:S(2)}) copy-start(bf16[128]{0:T(256)(128)(2,1)} %convert_element_type.68) | copy-start | bytes 772
  64.1 6.4 %copy-start.6 = (bf16[128,128]{1,0:T(8,128)(2,1)}, bf16[128,128]{1,0:T(8,128)(2,1)S(1)}, u32[]{:S(2)}) copy-start(bf16[128,128]{1,0:T(8,128)(2,1)S(1)} %fusion.8.kv_hbm) | copy-start | bytes 98308
  64.1 16.0 %collective-permute-start.2 = (bf16[136,128]{1,0:T(8,128)(2,1)S(1)}, bf16[136,128]{1,0:T(8,128)(2,1)S(1)}, u32[]{:S(2)}, u32[]{:S(2)}) collective-permute-start(bf16[136,128]{1,0:T(8,128)(2,1)S(1)} %pad_maximum_fusion), channel_id=1, source_target_pairs={{0,8},{8,16},{16,24},{24,32},{32,40},{40,48},{48,56},{56,64},{64,7... | collective-permute-start | bytes 104456 | tf_op jit(solution)/shard_map/ppermute | solution.py:24
  67.3 9.1 %collective-permute-start.3 = (f32[16,360]{1,0:T(8,128)}, f32[16,360]{1,0:T(8,128)S(1)}, u32[]{:S(2)}, u32[]{:S(2)}) collective-permute-start(f32[16,360]{1,0:T(8,128)} %add.87), channel_id=1, source_target_pairs={{0,256},{128,384},{256,0},{384,128},{1,257},{129,385},{257,1},{385... | collective-permute-start | bytes 69128 | tf_op jit(solution)/shard_map/ppermute | solution.py:305
  70.5 9.7 %copy-start.15 = (s32[128]{0:T(128)S(1)}, s32[128]{0:T(128)}, u32[]{:S(2)}) copy-start(s32[128]{0:T(128)} %param.19) | copy-start | bytes 1540
  77.1 5.2 %collective-permute-start.4 = (f32[16,360]{1,0:T(8,128)S(1)}, f32[16,360]{1,0:T(8,128)S(1)}, u32[]{:S(2)}, u32[]{:S(2)}) collective-permute-start(f32[16,360]{1,0:T(8,128)S(1)} %add.90), channel_id=1, source_target_pairs={{0,16},{16,0},{32,48},{48,32},{64,80},{80,64},{96,112},{112,96},{1... | collective-permute-start | bytes 69128 | tf_op jit(solution)/shard_map/ppermute | solution.py:305
  80.2 6.3 %copy-start.10 = (bf16[136,128]{1,0:T(8,128)(2,1)}, bf16[136,128]{1,0:T(8,128)(2,1)S(1)}, u32[]{:S(2)}) copy-start(bf16[136,128]{1,0:T(8,128)(2,1)S(1)} %collective-permute-done.2.halo_hbm) | copy-start | bytes 104452
  94.1 5.7 %copy-start.19 = (bf16[128,128]{1,0:T(8,128)(2,1)S(1)}, bf16[128,128]{1,0:T(8,128)(2,1)}, u32[]{:S(2)}) copy-start(bf16[128,128]{1,0:T(8,128)(2,1)} %get-tuple-element.35) | copy-start | bytes 98308
  94.1 15.0 %copy-start.1 = (bf16[8,2,4,48,128]{4,3,2,1,0:T(8,128)(2,1)S(1)}, bf16[8,2,4,48,128]{4,3,2,1,0:T(8,128)(2,1)}, u32[]{:S(2)}) copy-start(bf16[8,2,4,48,128]{4,3,2,1,0:T(8,128)(2,1)} %pad.7) | copy-start | bytes 2359300
  94.1 15.0 %copy-start.2 = (bf16[512,128]{1,0:T(8,128)(2,1)S(1)}, bf16[512,128]{1,0:T(8,128)(2,1)}, u32[]{:S(2)}) copy-start(bf16[512,128]{1,0:T(8,128)(2,1)} %get-tuple-element.38.dq_hbm) | copy-start | bytes 393220
  94.1 15.0 %copy-start.3 = (f32[128,128]{1,0:T(8,128)S(1)}, f32[128,128]{1,0:T(8,128)}, u32[]{:S(2)}) copy-start(f32[128,128]{1,0:T(8,128)} %get-tuple-element.39.dkv_hbm) | copy-start | bytes 196612
  94.1 20.3 %all-to-all-start.2 = ((bf16[8,384,128]{2,1,0:T(8,128)(2,1)}), bf16[8,384,128]{2,1,0:T(8,128)(2,1)}, u32[]{:S(2)}, u32[]{:S(2)}) async-start(bf16[8,384,128]{2,1,0:T(8,128)(2,1)} %get-tuple-element.33), calls=%async_computation.2 | async-start | bytes 1572864 | tf_op jit(solution)/shard_map/all_to_all | solution.py:357
  99.7 5.6 %collective-permute-start.5 = (bf16[128,128]{1,0:T(8,128)(2,1)S(1)}, bf16[128,128]{1,0:T(8,128)(2,1)S(1)}, u32[]{:S(2)}, u32[]{:S(2)}) collective-permute-start(bf16[128,128]{1,0:T(8,128)(2,1)S(1)} %copy-done.19), channel_id=1, source_target_pairs={{8,0},{16,8},{24,16},{32,24},{40,32},{48,40},{56,48},{64,56},{72,6... | collective-permute-start | bytes 98312 | tf_op jit(solution)/shard_map/ppermute | solution.py:24
  105.4 9.0 %collective-permute-start.6 = (f32[16,360]{1,0:T(8,128)S(1)}, f32[16,360]{1,0:T(8,128)S(1)}, u32[]{:S(2)}, u32[]{:S(2)}) collective-permute-start(f32[16,360]{1,0:T(8,128)S(1)} %add.91), channel_id=1, source_target_pairs={{0,32},{16,48},{32,0},{48,16},{64,96},{80,112},{96,64},{112,80},{1... | collective-permute-start | bytes 69128 | tf_op jit(solution)/shard_map/ppermute | solution.py:305
  114.4 5.2 %copy-start.9 = (f32[2880]{0:T(1024)S(1)}, f32[2880]{0:T(1024)}, u32[]{:S(2)}) copy-start(f32[2880]{0:T(1024)} %param.12) | copy-start | bytes 34564
  114.4 18.3 %all-to-all-start.3 = ((bf16[8,392,128]{2,1,0:T(8,128)(2,1)}), bf16[8,392,128]{2,1,0:T(8,128)(2,1)S(1)}, u32[]{:S(2)}, u32[]{:S(2)}) async-start(bf16[8,392,128]{2,1,0:T(8,128)(2,1)} %shard_map.132), calls=%async_computation.3 | async-start | bytes 1605632 | tf_op jit(solution)/shard_map/all_to_all | solution.py:377
  119.6 10.9 %copy-start.17 = (f32[128]{0:T(128)S(1)}, f32[128]{0:T(128)}, u32[]{:S(2)}) copy-start(f32[128]{0:T(128)} %copy-done.16) | copy-start | bytes 1540
  120.0 8.5 %collective-permute-start.7 = (f32[16,360]{1,0:T(8,128)S(1)}, f32[16,360]{1,0:T(8,128)S(1)}, u32[]{:S(2)}, u32[]{:S(2)}) collective-permute-start(f32[16,360]{1,0:T(8,128)S(1)} %add.94), channel_id=1, source_target_pairs={{0,64},{16,80},{32,96},{48,112},{64,0},{80,16},{96,32},{112,48},{1... | collective-permute-start | bytes 69128 | tf_op jit(solution)/shard_map/ppermute | solution.py:305
  130.4 2.4 %copy-start.13 = (f32[128]{0:T(128)S(1)}, f32[128]{0:T(128)}, u32[]{:S(2)}) copy-start(f32[128]{0:T(128)} %copy-done.12) | copy-start | bytes 1540
Sparse Core Ops, SparseCore 0:
  32.5 53.9 all-gather.2

commit v11 on v10

--- a/solution.py
+++ b/solution.py
@@ -232,7 +232,6 @@
 
 
 def call(kernel, outs, in_specs, out_specs, scratch, *args):
-    limit = 48 if kernel is back_kernel else 58
     size = sum(a.size * a.dtype.itemsize for a in jax.tree.leaves((args, outs)))
     return pl.pallas_call(
         kernel,
@@ -240,7 +239,7 @@
         in_specs=in_specs,
         out_specs=out_specs,
         scratch_shapes=scratch,
-        compiler_params=pltpu.CompilerParams(vmem_limit_bytes=limit * 2**20),
+        compiler_params=pltpu.CompilerParams(vmem_limit_bytes=58 * 2**20),
         cost_estimate=pl.CostEstimate(flops=10**8, bytes_accessed=size, transcendentals=0),
     )(*args)
 

time: 141 us -> 140 us (level)
  transfers between devices with their start and end apart: 12 -> 12, of which waited for: 8 -> 8; matrix products, arithmetic and copies ran while one was open for 10% -> 9% of each run, Pallas kernels for 4% -> 3%
where the time goes in v11:
time: 140 us; the launch traced here: 139 us
  starting transfers between devices  45.4 us (32%)
  blocking collectives  26.6 us (19%)
  waiting for transfers between devices  23.4 us (17%)
  between operations  14.5 us (10%)
  Pallas kernels  13.5 us (10%)
  other arithmetic  8.04 us (6%)
  local copies, waits for them, and re-layouts  6.3 us (4%)
  matrix products  1.81 us (1%)
    all_to_all x1, blocking collectives, shards(): near = lax.all_to_all(sent, 'zh', 0, 0)  22.5 us
    ppermute x6, starting transfers between devices, exchanged(): value = value + lax.ppermute(value, axis, pairs)  22.3 us
    ppermute x6, waiting for transfers between devices, exchanged(): value = value + lax.ppermute(value, axis, pairs)  13.7 us
    pallas_call x3, Pallas kernels, call(): pl.pallas_call(kernel, out_shape=outs, in_specs=in_specs, out_specs=out_s...  13.5 us
    all_to_all x1, starting transfers between devices, gathered(): return lax.all_to_all(spread, axes, 0, 0)  6.82 us
    ppermute x2, starting transfers between devices, shifted(): return lax.ppermute(value, SEQ, pairs)  5.6 us
    all_to_all x1, starting transfers between devices, shards(): attn = lax.all_to_all(blocks, HEAD, 0, 0)  5.5 us
    all_to_all x1, starting transfers between devices, shards(): back = lax.all_to_all(back, HEAD, 0, 0)  5.14 us
  transfers between devices with their start and end apart: 12, of which 8 were waited for; matrix products, arithmetic and copies ran while one was open for 9% of the time, Pallas kernels for 3%

profile of v11, /device:TPU:1, one launch (start us, length us, event | category | flops | bytes accessed | tf_op | source)
XLA Modules:
  0.0 139.5 jit_solution(6654676040098149512)
XLA Ops:
  7.2 1.8 %shard_map.130 = bf16[4,48,1152]{2,1,0:T(8,128)(2,1)} custom-call(bf16[45,512]{1,0:T(8,128)(2,1)} %q_hbm.1, bf16[45,512]{1,0:T(8,128)(2,1)} %o_hbm.1, bf16[45,64]{1,0:T(8,128)(2,1)} %k_hbm.1, bf16[45,64]{1,0:T(8,128)(2,1)} %v_hbm.1), custom_call_target="tpu_custom_call" | custom-call | flops 100000000 | bytes 546048 | tf_op jit(solution)/shard_map/pallas_call | solution.py:236
  9.0 22.5 %all_to_all.20 = bf16[4,48,1152]{2,1,0:T(8,128)(2,1)S(1)} all-to-all(bf16[4,48,1152]{2,1,0:T(8,128)(2,1)} %shard_map.130), channel_id=1, replica_groups=mesh['zh'=4,'y'=8,'core'=2,'x'=4,'zl'=2] {'zh'}, dimensions={0} | all-to-all | bytes 884736 | tf_op jit(solution)/shard_map/all_to_all | solution.py:278
  31.5 0.8 slice.28
  32.9 0.8 broadcast_in_dim.24
  33.7 6.8 %all-to-all-start.1 = ((bf16[8,4,48,128]{3,2,1,0:T(8,128)(2,1)}), bf16[8,4,48,128]{3,2,1,0:T(8,128)(2,1)S(1)}, u32[]{:S(2)}, u32[]{:S(2)}) async-start(bf16[8,4,48,128]{3,2,1,0:T(8,128)(2,1)} %broadcast_in_dim.24), calls=%async_computation.1 | async-start | bytes 786432 | tf_op jit(solution)/shard_map/all_to_all | solution.py:30
  40.5 1.5 %multiply_reduce_fusion = (f32[128]{0:T(128)S(1)}, bf16[2880,128]{1,0:T(8,128)(2,1)S(1)}) fusion(f32[2880]{0:T(1024)S(1)} %copy-done.5, f32[2880]{0:T(1024)S(1)} %copy-done.6, f32[128]{0:T(128)S(1)} %add_rsqrt_fusion, bf16[128,2880]{0,1:T(8,128)(2,1)S(1)} %copy-done.1), kind=kLoop, calls=%fused_computation.9 | loop fusion | flops 2580352 | bytes 1498624 | tf_op jit(solution)/shard_map/reduce_sum | solution.py:289
  43.5 7.1 %collective-permute-start = (f32[16,360]{1,0:T(8,128)S(1)}, f32[16,360]{1,0:T(8,128)S(1)}, u32[]{:S(2)}, u32[]{:S(2)}) collective-permute-start(f32[16,360]{1,0:T(8,128)S(1)} %fusion.11), channel_id=1, source_target_pairs={{0,8},{8,0},{1,9},{9,1},{2,10},{10,2},{3,11},{11,3},{4,12},{12,4},... | collective-permute-start | bytes 69128 | tf_op jit(solution)/shard_map/ppermute | solution.py:304
  50.5 0.8 collective-permute-done
  52.0 2.1 %collective-permute-start.1 = (f32[16,360]{1,0:T(8,128)}, f32[16,360]{1,0:T(8,128)}, u32[]{:S(2)}, u32[]{:S(2)}) collective-permute-start(f32[16,360]{1,0:T(8,128)} %add.86), channel_id=1, source_target_pairs={{0,128},{128,0},{256,384},{384,256},{1,129},{129,1},{257,385},{385... | collective-permute-start | bytes 69128 | tf_op jit(solution)/shard_map/ppermute | solution.py:304
  55.5 2.8 %collective-permute-done.1 = f32[16,360]{1,0:T(8,128)} collective-permute-done((f32[16,360]{1,0:T(8,128)}, f32[16,360]{1,0:T(8,128)}, u32[]{:S(2)}, u32[]{:S(2)}) %collective-permute-start.1) | collective-permute-done | bytes 23072 | tf_op jit(solution)/shard_map/ppermute | solution.py:304
  58.3 1.4 add.87
  59.7 4.1 %all-gather = bf16[8,8,48,128]{3,2,1,0:T(8,128)(2,1)S(1)} all-gather(bf16[8,4,48,128]{3,2,1,0:T(8,128)(2,1)S(1)} %all-to-all-done.1), channel_id=2, replica_groups=mesh['zh'=4,'y'=8,'core'=2,'x'=4,'zl'=2] {'core'}, dimensions={1}, use_global_device_ids=true | all-gather | bytes 1179648 | tf_op jit(solution)/shard_map/all_gather | solution.py:309
  64.2 3.2 %collective-permute-start.2 = (bf16[136,128]{1,0:T(8,128)(2,1)S(1)}, bf16[136,128]{1,0:T(8,128)(2,1)S(1)}, u32[]{:S(2)}, u32[]{:S(2)}) collective-permute-start(bf16[136,128]{1,0:T(8,128)(2,1)S(1)} %pad_maximum_fusion), channel_id=1, source_target_pairs={{0,8},{8,16},{16,24},{24,32},{32,40},{40,48},{48,56},{56,64},{64,7... | collective-permute-start | bytes 104456 | tf_op jit(solution)/shard_map/ppermute | solution.py:24
  67.4 2.0 %collective-permute-start.3 = (f32[16,360]{1,0:T(8,128)}, f32[16,360]{1,0:T(8,128)S(1)}, u32[]{:S(2)}, u32[]{:S(2)}) collective-permute-start(f32[16,360]{1,0:T(8,128)} %add.87), channel_id=1, source_target_pairs={{0,256},{128,384},{256,0},{384,128},{1,257},{129,385},{257,1},{385... | collective-permute-start | bytes 69128 | tf_op jit(solution)/shard_map/ppermute | solution.py:304
  69.4 1.0 pad.7
  70.8 1.0 pad.8.clone
  71.7 4.7 %collective-permute-done.3 = f32[16,360]{1,0:T(8,128)S(1)} collective-permute-done((f32[16,360]{1,0:T(8,128)}, f32[16,360]{1,0:T(8,128)S(1)}, u32[]{:S(2)}, u32[]{:S(2)}) %collective-permute-start.3) | collective-permute-done | bytes 23072 | tf_op jit(solution)/shard_map/ppermute | solution.py:304
  77.2 3.1 %collective-permute-start.4 = (f32[16,360]{1,0:T(8,128)S(1)}, f32[16,360]{1,0:T(8,128)S(1)}, u32[]{:S(2)}, u32[]{:S(2)}) collective-permute-start(f32[16,360]{1,0:T(8,128)S(1)} %add.90), channel_id=1, source_target_pairs={{0,16},{16,0},{32,48},{48,32},{64,80},{80,64},{96,112},{112,96},{1... | collective-permute-start | bytes 69128 | tf_op jit(solution)/shard_map/ppermute | solution.py:304
  81.1 1.3 collective-permute-done.4
  82.4 4.1 %all-gather.3.cloned.1.call-done = bf16[64,48,1024]{2,1,0:T(8,128)(2,1)} async-done(((bf16[4,48,1024]{2,1,0:T(8,128)(2,1)}), bf16[64,48,1024]{2,1,0:T(8,128)(2,1)}) %all-gather.3.cloned.1.call-update) | async-done | bytes 6291472 | tf_op jit(solution)/shard_map/all_gather | solution.py:279
  86.6 7.6 %shard_map.131 = (bf16[8,384,128]{2,1,0:T(8,128)(2,1)}, bf16[512,128]{1,0:T(8,128)(2,1)}, bf16[128,128]{1,0:T(8,128)(2,1)}, f32[128,128]{1,0:T(8,128)}) custom-call(bf16[3072,1024]{1,0:T(8,128)(2,1)} %bitcast.55, bf16[3072,128]{1,0:T(8,128)(2,1)} %bitcast.57, bf16[3072,128]{1,0:T(8,128)(2,1)} %bitcast.62, bf16[128,128]{1,0:T(8,128)(2,1)} %copy-done.4, ...), custom_call_target="tpu_custom_call" | custom-call | flops 100000000 | bytes 9013248 | tf_op jit(solution)/shard_map/pallas_call | solution.py:236
  94.1 5.5 %all-to-all-start.2 = ((bf16[8,384,128]{2,1,0:T(8,128)(2,1)}), bf16[8,384,128]{2,1,0:T(8,128)(2,1)S(1)}, u32[]{:S(2)}, u32[]{:S(2)}) async-start(bf16[8,384,128]{2,1,0:T(8,128)(2,1)} %get-tuple-element.33), calls=%async_computation.2 | async-start | bytes 1572864 | tf_op jit(solution)/shard_map/all_to_all | solution.py:356
  99.7 2.4 %collective-permute-start.5 = (bf16[128,128]{1,0:T(8,128)(2,1)S(1)}, bf16[128,128]{1,0:T(8,128)(2,1)S(1)}, u32[]{:S(2)}, u32[]{:S(2)}) collective-permute-start(bf16[128,128]{1,0:T(8,128)(2,1)S(1)} %copy-done.18), channel_id=1, source_target_pairs={{8,0},{16,8},{24,16},{32,24},{40,32},{48,40},{56,48},{64,56},{72,6... | collective-permute-start | bytes 98312 | tf_op jit(solution)/shard_map/ppermute | solution.py:24
  102.1 3.1 %collective-permute-done.5.ret_hbm = bf16[128,128]{1,0:T(8,128)(2,1)S(1)} collective-permute-done((bf16[128,128]{1,0:T(8,128)(2,1)S(1)}, bf16[128,128]{1,0:T(8,128)(2,1)S(1)}, u32[]{:S(2)}, u32[]{:S(2)}) %collective-permute-start.5) | collective-permute-done | bytes 32800 | tf_op jit(solution)/shard_map/ppermute | solution.py:24
  105.2 3.7 %collective-permute-start.6 = (f32[16,360]{1,0:T(8,128)S(1)}, f32[16,360]{1,0:T(8,128)S(1)}, u32[]{:S(2)}, u32[]{:S(2)}) collective-permute-start(f32[16,360]{1,0:T(8,128)S(1)} %add.91), channel_id=1, source_target_pairs={{0,32},{16,48},{32,0},{48,16},{64,96},{80,112},{96,64},{112,80},{1... | collective-permute-start | bytes 69128 | tf_op jit(solution)/shard_map/ppermute | solution.py:304
  108.9 4.2 %shard_map.132 = bf16[8,392,128]{2,1,0:T(8,128)(2,1)} custom-call(bf16[3072,1024]{1,0:T(8,128)(2,1)} %bitcast.56, bf16[3072,128]{1,0:T(8,128)(2,1)} %bitcast.61, bf16[3072,128]{1,0:T(8,128)(2,1)} %bitcast.58, bf16[512,128]{1,0:T(8,128)(2,1)} %get-tuple-element.38.dq_hbm, f32[128,128]{1,0:T(8,128)} %get-tuple-element.39.dkv_hbm, bf16[128,128]{1,0:T(8,128)(2,1)} %copy-done.9), custom_call_target="tpu_custom_call" | custom-call | flops 100000000 | bytes 8896512 | tf_op jit(solution)/shard_map/pallas_call | solution.py:236
  113.2 5.1 %all-to-all-start.3 = ((bf16[8,392,128]{2,1,0:T(8,128)(2,1)}), bf16[8,392,128]{2,1,0:T(8,128)(2,1)S(1)}, u32[]{:S(2)}, u32[]{:S(2)}) async-start(bf16[8,392,128]{2,1,0:T(8,128)(2,1)} %shard_map.132), calls=%async_computation.3 | async-start | bytes 1605632 | tf_op jit(solution)/shard_map/all_to_all | solution.py:376
  118.8 4.3 %collective-permute-start.7 = (f32[16,360]{1,0:T(8,128)S(1)}, f32[16,360]{1,0:T(8,128)S(1)}, u32[]{:S(2)}, u32[]{:S(2)}) collective-permute-start(f32[16,360]{1,0:T(8,128)S(1)} %add.94), channel_id=1, source_target_pairs={{0,64},{16,80},{32,96},{48,112},{64,0},{80,16},{96,32},{112,48},{1... | collective-permute-start | bytes 69128 | tf_op jit(solution)/shard_map/ppermute | solution.py:304
  123.5 4.0 %collective-permute-done.7 = f32[16,360]{1,0:T(8,128)S(1)} collective-permute-done((f32[16,360]{1,0:T(8,128)S(1)}, f32[16,360]{1,0:T(8,128)S(1)}, u32[]{:S(2)}, u32[]{:S(2)}) %collective-permute-start.7) | collective-permute-done | bytes 23072 | tf_op jit(solution)/shard_map/ppermute | solution.py:304
  128.2 1.0 fusion.7
  129.2 2.4 %all-to-all-done.3 = bf16[8,392,128]{2,1,0:T(8,128)(2,1)S(1)} async-done(((bf16[8,392,128]{2,1,0:T(8,128)(2,1)}), bf16[8,392,128]{2,1,0:T(8,128)(2,1)S(1)}, u32[]{:S(2)}, u32[]{:S(2)}) %all-to-all-start.3) | async-done | bytes 802848 | tf_op jit(solution)/shard_map/all_to_all | solution.py:376
  131.8 0.8 fusion.16
  (76 shorter events, 7.9 us)
Async XLA Ops:
  7.2 115.9 %copy-start = (bf16[16,2880]{1,0:T(8,128)(2,1)S(1)}, bf16[16,2880]{1,0:T(8,128)(2,1)}, u32[]{:S(2)}) copy-start(bf16[16,2880]{1,0:T(8,128)(2,1)} %param.18) | copy-start | bytes 276484
  7.2 25.2 %copy-start.1 = (bf16[128,2880]{0,1:T(8,128)(2,1)S(1)}, bf16[128,2880]{0,1:T(8,128)(2,1)}, u32[]{:S(2)}) copy-start(bf16[128,2880]{0,1:T(8,128)(2,1)} %param.11) | copy-start | bytes 2211844
  7.2 79.4 %all-gather.3.cloned.1.call-start = ((), (), s32[]{:S(2)}) async-start(), calls=%async_computation.4 | async-start | bytes 6684672 | tf_op jit(solution)/shard_map/all_gather | solution.py:279
  31.5 9.0 %copy-start.5 = (f32[2880]{0:T(1024)S(1)}, f32[2880]{0:T(1024)}, u32[]{:S(2)}) copy-start(f32[2880]{0:T(1024)} %param.17) | copy-start | bytes 34564
  31.5 9.0 %copy-start.6 = (f32[2880]{0:T(1024)S(1)}, f32[2880]{0:T(1024)}, u32[]{:S(2)}) copy-start(f32[2880]{0:T(1024)} %param.12) | copy-start | bytes 34564
  32.8 10.4 %copy-start.2 = (bf16[128,2880]{0,1:T(8,128)(2,1)S(1)}, bf16[128,2880]{0,1:T(8,128)(2,1)}, u32[]{:S(2)}) copy-start(bf16[128,2880]{0,1:T(8,128)(2,1)} %param.21) | copy-start | bytes 2211844
  32.8 10.4 %copy-start.10 = (s32[128]{0:T(128)S(1)}, s32[128]{0:T(128)}, u32[]{:S(2)}) copy-start(s32[128]{0:T(128)} %param.20) | copy-start | bytes 1540
  33.7 26.0 %all-to-all-start.1 = ((bf16[8,4,48,128]{3,2,1,0:T(8,128)(2,1)}), bf16[8,4,48,128]{3,2,1,0:T(8,128)(2,1)S(1)}, u32[]{:S(2)}, u32[]{:S(2)}) async-start(bf16[8,4,48,128]{3,2,1,0:T(8,128)(2,1)} %broadcast_in_dim.24), calls=%async_computation.1 | async-start | bytes 786432 | tf_op jit(solution)/shard_map/all_to_all | solution.py:30
  42.0 0.6 copy-start.11
  42.6 0.6 copy-start.15
  43.5 7.9 %collective-permute-start = (f32[16,360]{1,0:T(8,128)S(1)}, f32[16,360]{1,0:T(8,128)S(1)}, u32[]{:S(2)}, u32[]{:S(2)}) collective-permute-start(f32[16,360]{1,0:T(8,128)S(1)} %fusion.11), channel_id=1, source_target_pairs={{0,8},{8,0},{1,9},{9,1},{2,10},{10,2},{3,11},{11,3},{4,12},{12,4},... | collective-permute-start | bytes 69128 | tf_op jit(solution)/shard_map/ppermute | solution.py:304
  52.0 6.3 %collective-permute-start.1 = (f32[16,360]{1,0:T(8,128)}, f32[16,360]{1,0:T(8,128)}, u32[]{:S(2)}, u32[]{:S(2)}) collective-permute-start(f32[16,360]{1,0:T(8,128)} %add.86), channel_id=1, source_target_pairs={{0,128},{128,0},{256,384},{384,256},{1,129},{129,1},{257,385},{385... | collective-permute-start | bytes 69128 | tf_op jit(solution)/shard_map/ppermute | solution.py:304
  54.4 0.7 copy-start.13
  59.7 4.5 %copy-start.17 = (bf16[128]{0:T(256)(128)(2,1)S(1)}, bf16[128]{0:T(256)(128)(2,1)}, u32[]{:S(2)}) copy-start(bf16[128]{0:T(256)(128)(2,1)} %convert_element_type.68) | copy-start | bytes 772
  63.7 6.7 %copy-start.3 = (bf16[8,8,48,128]{3,2,1,0:T(8,128)(2,1)}, bf16[8,8,48,128]{3,2,1,0:T(8,128)(2,1)S(1)}, u32[]{:S(2)}) copy-start(bf16[8,8,48,128]{3,2,1,0:T(8,128)(2,1)S(1)} %all-gather) | copy-start | bytes 2359300
  64.2 6.5 %copy-start.4 = (bf16[128,128]{1,0:T(8,128)(2,1)}, bf16[128,128]{1,0:T(8,128)(2,1)S(1)}, u32[]{:S(2)}) copy-start(bf16[128,128]{1,0:T(8,128)(2,1)S(1)} %fusion.8.kv_hbm) | copy-start | bytes 98308
  64.2 16.1 %collective-permute-start.2 = (bf16[136,128]{1,0:T(8,128)(2,1)S(1)}, bf16[136,128]{1,0:T(8,128)(2,1)S(1)}, u32[]{:S(2)}, u32[]{:S(2)}) collective-permute-start(bf16[136,128]{1,0:T(8,128)(2,1)S(1)} %pad_maximum_fusion), channel_id=1, source_target_pairs={{0,8},{8,16},{16,24},{24,32},{32,40},{40,48},{48,56},{56,64},{64,7... | collective-permute-start | bytes 104456 | tf_op jit(solution)/shard_map/ppermute | solution.py:24
  67.4 9.1 %collective-permute-start.3 = (f32[16,360]{1,0:T(8,128)}, f32[16,360]{1,0:T(8,128)S(1)}, u32[]{:S(2)}, u32[]{:S(2)}) collective-permute-start(f32[16,360]{1,0:T(8,128)} %add.87), channel_id=1, source_target_pairs={{0,256},{128,384},{256,0},{384,128},{1,257},{129,385},{257,1},{385... | collective-permute-start | bytes 69128 | tf_op jit(solution)/shard_map/ppermute | solution.py:304
  70.7 9.7 %copy-start.14 = (s32[128]{0:T(128)S(1)}, s32[128]{0:T(128)}, u32[]{:S(2)}) copy-start(s32[128]{0:T(128)} %param.19) | copy-start | bytes 1540
  77.2 5.2 %collective-permute-start.4 = (f32[16,360]{1,0:T(8,128)S(1)}, f32[16,360]{1,0:T(8,128)S(1)}, u32[]{:S(2)}, u32[]{:S(2)}) collective-permute-start(f32[16,360]{1,0:T(8,128)S(1)} %add.90), channel_id=1, source_target_pairs={{0,16},{16,0},{32,48},{48,32},{64,80},{80,64},{96,112},{112,96},{1... | collective-permute-start | bytes 69128 | tf_op jit(solution)/shard_map/ppermute | solution.py:304
  80.3 6.3 %copy-start.8 = (bf16[136,128]{1,0:T(8,128)(2,1)}, bf16[136,128]{1,0:T(8,128)(2,1)S(1)}, u32[]{:S(2)}) copy-start(bf16[136,128]{1,0:T(8,128)(2,1)S(1)} %collective-permute-done.2.halo_hbm) | copy-start | bytes 104452
  94.1 5.5 %copy-start.18 = (bf16[128,128]{1,0:T(8,128)(2,1)S(1)}, bf16[128,128]{1,0:T(8,128)(2,1)}, u32[]{:S(2)}) copy-start(bf16[128,128]{1,0:T(8,128)(2,1)} %get-tuple-element.35) | copy-start | bytes 98308
  94.1 19.0 %all-to-all-start.2 = ((bf16[8,384,128]{2,1,0:T(8,128)(2,1)}), bf16[8,384,128]{2,1,0:T(8,128)(2,1)S(1)}, u32[]{:S(2)}, u32[]{:S(2)}) async-start(bf16[8,384,128]{2,1,0:T(8,128)(2,1)} %get-tuple-element.33), calls=%async_computation.2 | async-start | bytes 1572864 | tf_op jit(solution)/shard_map/all_to_all | solution.py:356
  99.7 5.5 %collective-permute-start.5 = (bf16[128,128]{1,0:T(8,128)(2,1)S(1)}, bf16[128,128]{1,0:T(8,128)(2,1)S(1)}, u32[]{:S(2)}, u32[]{:S(2)}) collective-permute-start(bf16[128,128]{1,0:T(8,128)(2,1)S(1)} %copy-done.18), channel_id=1, source_target_pairs={{8,0},{16,8},{24,16},{32,24},{40,32},{48,40},{56,48},{64,56},{72,6... | collective-permute-start | bytes 98312 | tf_op jit(solution)/shard_map/ppermute | solution.py:24
  105.2 3.7 %copy-start.9 = (bf16[128,128]{1,0:T(8,128)(2,1)}, bf16[128,128]{1,0:T(8,128)(2,1)S(1)}, u32[]{:S(2)}) copy-start(bf16[128,128]{1,0:T(8,128)(2,1)S(1)} %collective-permute-done.5.ret_hbm) | copy-start | bytes 98308
  105.2 8.0 %collective-permute-start.6 = (f32[16,360]{1,0:T(8,128)S(1)}, f32[16,360]{1,0:T(8,128)S(1)}, u32[]{:S(2)}, u32[]{:S(2)}) collective-permute-start(f32[16,360]{1,0:T(8,128)S(1)} %add.91), channel_id=1, source_target_pairs={{0,32},{16,48},{32,0},{48,16},{64,96},{80,112},{96,64},{112,80},{1... | collective-permute-start | bytes 69128 | tf_op jit(solution)/shard_map/ppermute | solution.py:304
  113.1 5.2 %copy-start.7 = (f32[2880]{0:T(1024)S(1)}, f32[2880]{0:T(1024)}, u32[]{:S(2)}) copy-start(f32[2880]{0:T(1024)} %param.12) | copy-start | bytes 34564
  113.2 18.5 %all-to-all-start.3 = ((bf16[8,392,128]{2,1,0:T(8,128)(2,1)}), bf16[8,392,128]{2,1,0:T(8,128)(2,1)S(1)}, u32[]{:S(2)}, u32[]{:S(2)}) async-start(bf16[8,392,128]{2,1,0:T(8,128)(2,1)} %shard_map.132), calls=%async_computation.3 | async-start | bytes 1605632 | tf_op jit(solution)/shard_map/all_to_all | solution.py:376
  118.3 9.9 %copy-start.16 = (f32[128]{0:T(128)S(1)}, f32[128]{0:T(128)}, u32[]{:S(2)}) copy-start(f32[128]{0:T(128)} %copy-done.15) | copy-start | bytes 1540
  118.8 8.7 %collective-permute-start.7 = (f32[16,360]{1,0:T(8,128)S(1)}, f32[16,360]{1,0:T(8,128)S(1)}, u32[]{:S(2)}, u32[]{:S(2)}) collective-permute-start(f32[16,360]{1,0:T(8,128)S(1)} %add.94), channel_id=1, source_target_pairs={{0,64},{16,80},{32,96},{48,112},{64,0},{80,16},{96,32},{112,48},{1... | collective-permute-start | bytes 69128 | tf_op jit(solution)/shard_map/ppermute | solution.py:304
  128.2 3.6 %copy-start.12 = (f32[128]{0:T(128)S(1)}, f32[128]{0:T(128)}, u32[]{:S(2)}) copy-start(f32[128]{0:T(128)} %copy-done.11) | copy-start | bytes 1540
Sparse Core Ops, SparseCore 0:
  32.5 53.9 all-gather.2
